TPU v7x, 128 devices: a whole 4x4x4 slice. The times are simulated.
128 devices in a mesh: row: 16 (over z, x_hi, core), col: 8 (over y, x_lo).
Axes of the slice: x: 4 (x_hi: 2, x_lo: 2; x = x_hi * 2 + x_lo), y: 4, z: 4, core: 2. Of those that a mesh axis runs over, the one named last changes fastest.
Arguments:
- queries: bfloat16 [1024, 8192], P('col', 'row'), may hold values from -8 to 8
- cache_keys: bfloat16 [8, 131072, 128], P(None, ('row', 'col')), may hold values from -8 to 8
- cache_values: bfloat16 [8, 131072, 128], P(None, ('row', 'col')), may hold values from -6 to 6
- stretch_keys: bfloat16 [8, 1024, 128], P(None, 'col'), may hold values from -8 to 8
- stretch_values: bfloat16 [8, 1024, 128], P(None, 'col'), may hold values from -6 to 6
- block_lists: int32 [8, 8, 64], replicated, may hold values from 0 to 1023, as said below
- out_weight: bfloat16 [8192, 8192], P('row', 'col'), may hold values from -0.5 to 0.5
- residual: bfloat16 [1024, 8192], P('row', 'col'), may hold values from -6 to 6
- norm_gain: bfloat16 [8192], P('col'), may hold values from 0.25 to 1.75
- gate_weight: bfloat16 [8192, 28672], P('col', 'row'), may hold values from -0.0625 to 0.0625
- up_weight: bfloat16 [8192, 28672], P('col', 'row'), may hold values from -0.0625 to 0.0625
- down_weight: bfloat16 [28672, 8192], P('row', 'col'), may hold values from -0.03125 to 0.03125
Outputs:
- layer_out: bfloat16 [1024, 8192], P('row', 'col')
Inputs may be any that keep to these rules, and one draw needn't show every extreme that they name: `block_lists`: each list names 64 different cache blocks; device k of row+col holds cache blocks k * (8) to (k + 1) * 8 - 1, and no two blocks of one list lie on the same device. Every list holds block 0 and block 1023.
All inputs are finite; a program needn't handle non-finite values.
Results may differ from a plain program's by a relative error of at most 0.0085.
Values may be sent and summed in bfloat16 or wider, within the bound.
No kernel may reach another device: no remote copies, remote signals or barrier semaphores. Data moves between devices by JAX's collectives and lax.ppermute only.
A program may use at most 128 MiB of HBM per device.

v0:
```python
import math

import jax
import jax.numpy as jnp
from jax import lax
from jax.sharding import PartitionSpec as P

D = 8192
KV_HEADS = 8
HEAD_DIM = 128
BLK = 128
GROUP = 8


def local(
    queries,
    cache_keys,
    cache_values,
    stretch_keys,
    stretch_values,
    block_lists,
    out_weight,
    residual,
    norm_gain,
    gate_weight,
    up_weight,
    down_weight,
):
    row_count = lax.axis_size("row")
    col_count = lax.axis_size("col")
    row_index = lax.axis_index("row")
    col_index = lax.axis_index("col")
    device_count = row_count * col_count
    my_index = row_index * col_count + col_index
    local_blocks = cache_keys.shape[1] // BLK
    heads_here = queries.shape[1] // HEAD_DIM
    list_length = block_lists.shape[2]
    my_group = row_index * heads_here // GROUP
    scaling = 1.0 / math.sqrt(HEAD_DIM)
    targets = jnp.arange(device_count, dtype=jnp.int32)
    target_group = targets // col_count * heads_here // GROUP
    target_lists = block_lists[targets % col_count, target_group]
    holders = target_lists // local_blocks
    matched = holders == my_index
    found_any = jnp.any(matched, axis=1)
    within = jnp.sum(jnp.where(matched, target_lists % local_blocks, 0), axis=1)
    source_rows = target_group * local_blocks + within
    flat_keys = cache_keys.reshape(KV_HEADS * local_blocks, BLK, HEAD_DIM)
    flat_values = cache_values.reshape(KV_HEADS * local_blocks, BLK, HEAD_DIM)
    outgoing = jnp.concatenate([flat_keys[source_rows], flat_values[source_rows]], axis=2)
    outgoing = jnp.where(found_any[:, None, None], outgoing, jnp.zeros_like(outgoing))
    arrived = lax.all_to_all(outgoing, ("row", "col"), split_axis=0, concat_axis=0, tiled=True)
    my_list = block_lists[col_index, my_group]
    fetched = arrived[my_list // local_blocks].reshape(list_length * BLK, 2 * HEAD_DIM)
    far_keys = fetched[:, :HEAD_DIM]
    far_values = fetched[:, HEAD_DIM:]
    query_rows = queries.reshape(BLK * heads_here, HEAD_DIM)
    far_scores = jnp.dot(query_rows, far_keys.T, preferred_element_type=jnp.float32) * scaling
    run_max = jnp.max(far_scores, axis=1)
    far_exp = jnp.exp(far_scores - run_max[:, None])
    run_sum = jnp.sum(far_exp, axis=1)
    run_acc = jnp.dot(far_exp.astype(jnp.bfloat16), far_values, preferred_element_type=jnp.float32)
    query_pos = col_index * BLK + jnp.arange(BLK * heads_here, dtype=jnp.int32) // heads_here
    own_keys = lax.dynamic_index_in_dim(stretch_keys, my_group, 0, keepdims=False)
    own_values = lax.dynamic_index_in_dim(stretch_values, my_group, 0, keepdims=False)
    piece_keys = lax.all_gather(own_keys, "col", axis=0, tiled=True)
    piece_values = lax.all_gather(own_values, "col", axis=0, tiled=True)
    scores = jnp.dot(query_rows, piece_keys.T, preferred_element_type=jnp.float32) * scaling
    key_pos = jnp.arange(piece_keys.shape[0], dtype=jnp.int32)
    allowed = key_pos[None, :] <= query_pos[:, None]
    scores = jnp.where(allowed, scores, -1e30)
    new_max = jnp.maximum(run_max, jnp.max(scores, axis=1))
    decays = jnp.exp(run_max - new_max)
    weights = jnp.where(allowed, jnp.exp(scores - new_max[:, None]), 0.0)
    new_sum = run_sum * decays + jnp.sum(weights, axis=1)
    new_acc = run_acc * decays[:, None] + jnp.dot(
        weights.astype(jnp.bfloat16), piece_values, preferred_element_type=jnp.float32
    )
    attended = (new_acc / new_sum[:, None]).astype(jnp.bfloat16).reshape(BLK, heads_here * HEAD_DIM)
    all_attended = lax.all_gather(attended, "col", axis=0, tiled=True)
    projected = lax.psum_scatter(
        jnp.dot(all_attended, out_weight, preferred_element_type=jnp.float32),
        "row",
        scatter_dimension=0,
        tiled=True,
    )
    stream = residual.astype(jnp.float32) + projected
    squares = lax.psum(jnp.sum(stream * stream, axis=1), "col")
    normed = (
        stream * lax.rsqrt(squares / D + 1e-05)[:, None] * norm_gain.astype(jnp.float32)
    ).astype(jnp.bfloat16)
    block_piece = lax.all_gather(normed, "row", axis=0, tiled=True)
    gate_part = jnp.dot(block_piece, gate_weight, preferred_element_type=jnp.float32)
    up_part = jnp.dot(block_piece, up_weight, preferred_element_type=jnp.float32)
    partials = jnp.concatenate([gate_part, up_part], axis=1)
    hidden_width = gate_weight.shape[1]
    summed = lax.psum(partials, "col")
    hidden = (jax.nn.silu(summed[:, :hidden_width]) * summed[:, hidden_width:]).astype(jnp.bfloat16)
    down_terms = jnp.dot(hidden, down_weight, preferred_element_type=jnp.float32)
    mlp_part = lax.psum_scatter(down_terms, "row", scatter_dimension=0, tiled=True)
    return (stream + mlp_part).astype(jnp.bfloat16)


def solution(mesh):
    in_specs = (
        P("col", "row"),
        P(None, ("row", "col"), None),
        P(None, ("row", "col"), None),
        P(None, "col", None),
        P(None, "col", None),
        P(),
        P("row", "col"),
        P("row", "col"),
        P("col"),
        P("col", "row"),
        P("col", "row"),
        P("row", "col"),
    )
    out_specs = P("row", "col")
    return jax.shard_map(local, mesh=mesh, in_specs=in_specs, out_specs=out_specs, check_vma=False)
```

profile of v0, /device:TPU:0, one launch (start us, length us, event | category | flops | bytes accessed | tf_op | source)
XLA Modules:
  0.0 1105.7 jit_solution(4571468520694999564)
XLA Ops:
  6.6 1.9 gather_fusion
  8.7 3.1 gather_fusion.2
  11.8 4.6 gather_fusion.1
  16.4 8.2 maximum_select_fusion
  24.6 11.7 %all-to-all-start = ((bf16[128,128,256]{2,1,0:T(8,128)(2,1)}), bf16[128,128,256]{2,1,0:T(8,128)(2,1)}, u32[]{:S(2)}, u32[]{:S(2)}) async-start(bf16[128,128,256]{2,1,0:T(8,128)(2,1)} %maximum_select_fusion), calls=%async_computation | async-start | bytes 16777216 | tf_op jit(solution)/shard_map/all_to_all | solution.py:52
  36.5 0.7 fusion.41
  37.2 0.8 constant_dynamic-slice_fusion.1
  38.0 0.8 constant_dynamic-slice_fusion
  38.7 118.4 %all-gather.1 = bf16[1,1024,128]{2,1,0:T(8,128)(2,1)S(1)} all-gather(bf16[1,128,128]{2,1,0:T(8,128)(2,1)S(1)} %constant_dynamic-slice_fusion), channel_id=3, replica_groups=mesh['row'=16,'col'=8] {'col'}, dimensions={1}, use_global_device_ids=true | all-gather | bytes 294912 | tf_op jit(solution)/shard_map/all_gather | solution.py:67
  157.1 28.9 %all-gather = bf16[1,1024,128]{2,1,0:T(8,128)(2,1)S(1)} all-gather(bf16[1,128,128]{2,1,0:T(8,128)(2,1)S(1)} %constant_dynamic-slice_fusion.1), channel_id=2, replica_groups=mesh['row'=16,'col'=8] {'col'}, dimensions={1}, use_global_device_ids=true | all-gather | bytes 294912 | tf_op jit(solution)/shard_map/all_gather | solution.py:66
  186.5 6.1 gather_fusion.3
  192.6 9.6 multiply_reduce_fusion
  202.2 8.8 fusion
  211.0 0.6 fusion.11
  211.6 7.7 fusion.15
  219.3 0.8 fusion.14
  220.1 0.7 reshape.273
  220.9 39.3 %all-gather.5.cloned.1.call-done = bf16[1024,512]{1,0:T(8,128)(2,1)} async-done(((bf16[128,512]{1,0:T(8,128)(2,1)}), bf16[1024,512]{1,0:T(8,128)(2,1)}) %all-gather.5.cloned.1.call-update) | async-done | bytes 1048592 | tf_op jit(solution)/shard_map/all_gather | solution.py:80
  260.3 4.7 fusion.50
  265.1 0.6 copy-done.6
  265.7 79.7 %reduce-scatter.3.cloned.1.call-done = f32[64,1024]{1,0:T(8,128)} async-done(((f32[1024,1024]{1,0:T(8,128)}), f32[64,1024]{1,0:T(8,128)}) %reduce-scatter.3.cloned.1.call-update) | async-done | bytes 262160 | tf_op jit(solution)/shard_map/reduce_scatter | solution.py:81
  345.4 1.1 multiply_reduce_fusion.1
  346.4 18.8 %psum.14 = f32[64]{0:T(128)S(1)} all-reduce(f32[64]{0:T(128)S(1)} %multiply_reduce_fusion.1), channel_id=1, replica_groups=mesh['row'=16,'col'=8] {'col'}, use_global_device_ids=true, to_apply=%region_8.9 | all-reduce | flops 64 | bytes 512 | tf_op jit(solution)/shard_map/psum | solution.py:88
  365.2 1.7 multiply_convert_fusion
  367.2 44.7 %all-gather.7.cloned.1.call-done = bf16[1024,1024]{1,0:T(8,128)(2,1)} async-done(((bf16[64,1024]{1,0:T(8,128)(2,1)}), bf16[1024,1024]{1,0:T(8,128)(2,1)}) %all-gather.7.cloned.1.call-update) | async-done | bytes 2097168 | tf_op jit(solution)/shard_map/all_gather | solution.py:92
  412.0 6.8 fusion.52
  418.8 4.0 fusion.51
  422.7 5.7 pad_maximum_fusion
  428.5 574.8 %all-reduce.2.cloned.1.call-done = f32[1024,3584]{1,0:T(8,128)} async-done(((f32[1024,3584]{1,0:T(8,128)}), f32[1024,3584]{1,0:T(8,128)}) %all-reduce.2.cloned.1.call-update) | async-done | bytes 14680080 | tf_op jit(solution)/shard_map/psum | solution.py:97
  1003.3 12.3 %fusion.5 = f32[1024,1024]{1,0:T(8,128)} fusion(bf16[1792,1024]{1,0:T(8,128)(2,1)} %param.23, f32[1024,3584]{1,0:T(8,128)} %all-reduce.2.cloned.1.call-done), kind=kOutput, calls=%fused_computation.13 | convolution fusion | flops 3769106432 | bytes 22544384 | tf_op jit(solution)/shard_map/dot_general | solution.py:99
  1015.7 81.9 %reduce-scatter.5.cloned.1.call-done = f32[64,1024]{1,0:T(8,128)} async-done(((f32[1024,1024]{1,0:T(8,128)}), f32[64,1024]{1,0:T(8,128)}) %reduce-scatter.5.cloned.1.call-update) | async-done | bytes 262160 | tf_op jit(solution)/shard_map/reduce_scatter | solution.py:100
  1097.5 1.6 add_convert_fusion
  (41 shorter events, 1.4 us)
Async XLA Ops:
  6.5 2.2 copy-start
  24.6 11.8 %copy-start.5 = (bf16[128,512]{1,0:T(8,128)(2,1)S(1)}, bf16[128,512]{1,0:T(8,128)(2,1)}, u32[]{:S(2)}) copy-start(bf16[128,512]{1,0:T(8,128)(2,1)} %param.12) | copy-start | bytes 393220
  24.6 161.9 %all-to-all-start = ((bf16[128,128,256]{2,1,0:T(8,128)(2,1)}), bf16[128,128,256]{2,1,0:T(8,128)(2,1)}, u32[]{:S(2)}, u32[]{:S(2)}) async-start(bf16[128,128,256]{2,1,0:T(8,128)(2,1)} %maximum_select_fusion), calls=%async_computation | async-start | bytes 16777216 | tf_op jit(solution)/shard_map/all_to_all | solution.py:52
  36.3 224.0 %all-gather.5.cloned.1.call-start = ((), (), s32[]{:S(2)}) async-start(), calls=%async_computation.3 | async-start | bytes 1179648 | tf_op jit(solution)/shard_map/all_gather | solution.py:80
  202.2 9.4 copy-start.2
  220.9 124.5 %reduce-scatter.3.cloned.1.call-start = ((), (), s32[]{:S(2)}) async-start(), calls=%async_computation.4 | async-start | bytes 4456448 | tf_op jit(solution)/shard_map/reduce_scatter | solution.py:81
  265.0 0.7 copy-start.6
  265.0 80.4 %copy-start.4 = (bf16[64,1024]{1,0:T(8,128)(2,1)S(1)}, bf16[64,1024]{1,0:T(8,128)(2,1)}, u32[]{:S(2)}) copy-start(bf16[64,1024]{1,0:T(8,128)(2,1)} %param.19) | copy-start | bytes 393220
  265.0 147.0 %all-gather.7.cloned.1.call-start = ((), (), s32[]{:S(2)}) async-start(), calls=%async_computation.5 | async-start | bytes 2228224 | tf_op jit(solution)/shard_map/all_gather | solution.py:92
  367.0 636.4 %all-reduce.2.cloned.1.call-start = ((), (), s32[]{:S(2)}) async-start(), calls=%async_computation.6 | async-start | bytes 29360128 | tf_op jit(solution)/shard_map/psum | solution.py:97
  412.0 6.8 copy-start.7
  412.0 6.8 copy-start.8
  428.5 669.0 %reduce-scatter.5.cloned.1.call-start = ((), (), s32[]{:S(2)}) async-start(), calls=%async_computation.7 | async-start | bytes 4456448 | tf_op jit(solution)/shard_map/reduce_scatter | solution.py:100
  1003.3 95.9 %copy-start.1 = (bf16[8,1024,128]{2,1,0:T(8,128)(2,1)S(1)}, bf16[8,1024,128]{2,1,0:T(8,128)(2,1)}, u32[]{:S(2)}) copy-start(bf16[8,1024,128]{2,1,0:T(8,128)(2,1)} %param.14) | copy-start | bytes 6291460
  1015.6 81.9 %copy-start.3 = (f32[64,1024]{1,0:T(8,128)S(1)}, f32[64,1024]{1,0:T(8,128)}, u32[]{:S(2)}) copy-start(f32[64,1024]{1,0:T(8,128)} %reduce-scatter.3.cloned.1.call-done) | copy-start | bytes 786436
Sparse Core Ops, SparseCore 0:
  221.0 39.2 all-gather.4
  265.1 80.1 reduce-scatter.2
  367.1 44.8 all-gather.6
  428.6 574.6 all-reduce.1
  1015.8 81.6 reduce-scatter.4
where the time goes:
time: 1110 us
  waiting for transfers between devices  820 us (74%)
  blocking collectives  166 us (15%)
  matrix products  46.4 us (4%)
  other arithmetic  28.8 us (3%)
  local copies, waits for them, and re-layouts  18.7 us (2%)
  between operations  13.3 us (1%)
  starting transfers between devices  12.1 us (1%)
    psum x1, waiting for transfers between devices, local(): summed = lax.psum(partials, 'col')  575 us
    all_gather x1, blocking collectives, local(): piece_values = lax.all_gather(own_values, 'col', axis=0, tiled=True)  118 us
    reduce_scatter x1, waiting for transfers between devices, local(): lax.psum_scatter(down_terms, 'row', scatter_dimension=0, tiled=True)  81.9 us
    reduce_scatter x1, waiting for transfers between devices, local(): lax.psum_scatter(jnp.dot(all_attended, out_weight, preferred_element_type...  79.7 us
    all_gather x1, waiting for transfers between devices, local(): block_piece = lax.all_gather(normed, 'row', axis=0, tiled=True)  44.7 us
    all_gather x1, waiting for transfers between devices, local(): all_attended = lax.all_gather(attended, 'col', axis=0, tiled=True)  39.3 us
    all_gather x1, blocking collectives, local(): piece_keys = lax.all_gather(own_keys, 'col', axis=0, tiled=True)  28.9 us
  transfers between devices with their start and end apart: 6, of which 5 were waited for; matrix products, arithmetic and copies ran while one was open for 0% of the time, Pallas kernels for 0%

commit v1 on v0

v1 whole, which is shorter than its diff:
```python
import functools
import math

import jax
import jax.numpy as jnp
from jax import lax
from jax.experimental import pallas as pl
from jax.experimental.pallas import tpu as pltpu
from jax.sharding import Mesh, PartitionSpec as P

D = 8192
KV_HEADS = 8
HEAD_DIM = 128
BLK = 128
GROUP = 8
AXES = ("z", "xh", "core", "y", "xl")
ROW = ("z", "xh", "core")
ZXH = ("z", "xh")
COL = ("y", "xl")
CHIP = ("z", "xh", "y", "xl")
NEG = -1e30
bf16 = jnp.bfloat16
f32 = jnp.float32


def nt_dot(a, b):
    return lax.dot_general(a, b, (((1,), (1,)), ((), ())), preferred_element_type=f32)


def tn_dot(a, b):
    return lax.dot_general(a, b, (((0,), (0,)), ((), ())), preferred_element_type=f32)


def attend_kernel(
    scale,
    per_step,
    local_blocks,
    list_ref,
    place_ref,
    own_q_ref,
    other_q_ref,
    keys_ref,
    values_ref,
    near_keys_ref,
    near_values_ref,
    own_ref,
    send_ref,
    order_ref,
    q_ref,
    top_ref,
    sum_ref,
    acc_ref,
):
    core = place_ref[0]
    block = place_ref[1]
    length = list_ref.shape[0]
    heads = own_q_ref.shape[1] // HEAD_DIM
    rows = heads * BLK
    for h in range(heads):
        cols = pl.ds(h * HEAD_DIM, HEAD_DIM)
        q_ref[pl.ds(h * BLK, BLK), :] = own_q_ref[:, cols]
        q_ref[pl.ds(rows + h * BLK, BLK), :] = other_q_ref[:, cols]
    top_ref[...] = jnp.full_like(top_ref, NEG)
    sum_ref[...] = jnp.zeros_like(sum_ref)
    acc_ref[...] = jnp.zeros_like(acc_ref)

    def collect(i, count):
        device = list_ref[i] // local_blocks
        row = device // 8
        order_ref[count] = (row // 2) * 8 + device % 8
        return count + jnp.where(row % 2 == core, 1, 0)

    count = lax.fori_loop(0, length, collect, jnp.int32(0))

    def update(half, keys, values, bias):
        part = pl.ds(half * rows, rows)
        scores = nt_dot(keys, q_ref[part, :]) * scale
        if bias is not None:
            scores = scores + bias
        old = top_ref[half]
        new = jnp.maximum(old, jnp.max(scores, axis=0, keepdims=True))
        weights = jnp.exp(scores - new)
        decay = jnp.exp(old - new)
        top_ref[half] = new
        sum_ref[half] = sum_ref[half] * decay + jnp.sum(weights, axis=0, keepdims=True)
        acc_ref[half] = acc_ref[half] * decay + tn_dot(values, weights.astype(bf16))

    def far(step, carry):
        slots = [jnp.minimum(step * per_step + i, count - 1) for i in range(per_step)]
        keys = jnp.concatenate([keys_ref[order_ref[s]] for s in slots], axis=0)
        values = jnp.concatenate([values_ref[order_ref[s]] for s in slots], axis=0)
        bias = jnp.concatenate(
            [
                jnp.full((BLK, 1), jnp.where(step * per_step + i < count, 0.0, NEG), f32)
                for i in range(per_step)
            ],
            axis=0,
        )
        for half in range(2):
            update(half, keys, values, bias)
        return carry

    lax.fori_loop(0, (count + per_step - 1) // per_step, far, 0)

    def near(j, carry):
        which = core + 2 * j
        shift = (block - which) * BLK
        key_pos = lax.broadcasted_iota(jnp.int32, (BLK, rows), 0)
        token = lax.broadcasted_iota(jnp.int32, (BLK, rows), 1) % BLK
        bias = jnp.where(key_pos <= token + shift, 0.0, NEG)
        for half in range(2):
            update(half, near_keys_ref[which], near_values_ref[which], bias)
        return carry

    lax.fori_loop(0, (block - core + 2) // 2, near, 0)
    own_ref[0:HEAD_DIM, :] = acc_ref[0]
    own_ref[HEAD_DIM : HEAD_DIM + 1, :] = top_ref[0]
    own_ref[HEAD_DIM + 1 : HEAD_DIM + 2, :] = sum_ref[0]
    send_ref[0:HEAD_DIM, :] = acc_ref[1]
    send_ref[HEAD_DIM : HEAD_DIM + 1, :] = top_ref[1]
    send_ref[HEAD_DIM + 1 : HEAD_DIM + 2, :] = sum_ref[1]


def attend(my_list, place, own_q, other_q, keys, values, near_keys, near_values, local_blocks):
    heads = own_q.shape[1] // HEAD_DIM
    rows = heads * BLK
    packed = jax.ShapeDtypeStruct((HEAD_DIM + 8, rows), f32)
    smem = pl.BlockSpec(memory_space=pltpu.SMEM)
    vmem = pl.BlockSpec(memory_space=pltpu.VMEM)
    return pl.pallas_call(
        functools.partial(attend_kernel, 1.0 / math.sqrt(HEAD_DIM), 2, local_blocks),
        out_shape=(packed, packed),
        in_specs=[smem, smem] + [vmem] * 6,
        out_specs=(vmem, vmem),
        scratch_shapes=[
            pltpu.SMEM((my_list.shape[0] + 1,), jnp.int32),
            pltpu.VMEM((2 * rows, HEAD_DIM), bf16),
            pltpu.VMEM((2, 1, rows), f32),
            pltpu.VMEM((2, 1, rows), f32),
            pltpu.VMEM((2, HEAD_DIM, rows), f32),
        ],
        compiler_params=pltpu.CompilerParams(vmem_limit_bytes=48 * 1024 * 1024),
        cost_estimate=pl.CostEstimate(
            flops=4 * 2 * rows * 40 * BLK * HEAD_DIM,
            bytes_accessed=2 * keys.size * 2,
            transcendentals=2 * rows * 40 * BLK,
        ),
    )(my_list, place, own_q, other_q, keys, values, near_keys, near_values)


def merge_kernel(own_ref, got_ref, out_ref):
    own_top = own_ref[HEAD_DIM : HEAD_DIM + 1, :]
    got_top = got_ref[HEAD_DIM : HEAD_DIM + 1, :]
    top = jnp.maximum(own_top, got_top)
    own_w = jnp.exp(own_top - top)
    got_w = jnp.exp(got_top - top)
    total = own_w * own_ref[HEAD_DIM + 1 : HEAD_DIM + 2, :] + got_w * got_ref[HEAD_DIM + 1 : HEAD_DIM + 2, :]
    mixed = (own_ref[0:HEAD_DIM, :] * own_w + got_ref[0:HEAD_DIM, :] * got_w) / total
    heads = mixed.shape[1] // BLK
    for h in range(heads):
        piece = mixed[:, h * BLK : (h + 1) * BLK].T.astype(bf16)
        for i in range(out_ref.shape[0]):
            out_ref[i, :, pl.ds(h * HEAD_DIM, HEAD_DIM)] = piece


def merge(own, got, copies):
    heads = own.shape[1] // BLK
    vmem = pl.BlockSpec(memory_space=pltpu.VMEM)
    return pl.pallas_call(
        merge_kernel,
        out_shape=jax.ShapeDtypeStruct((copies, BLK, heads * HEAD_DIM), bf16),
        in_specs=[vmem, vmem],
        out_specs=vmem,
    )(own, got)


def exchange(x, axes):
    return lax.all_to_all(x, axes, split_axis=0, concat_axis=0, tiled=True)


def swap(x):
    return lax.ppermute(x, "core", [(0, 1), (1, 0)])


def spread(x, copies):
    return jnp.broadcast_to(x[None], (copies,) + x.shape)


def mm(a, b):
    return jnp.dot(a, b, preferred_element_type=f32)


def local(
    queries,
    cache_keys,
    cache_values,
    stretch_keys,
    stretch_values,
    block_lists,
    out_weight,
    residual,
    norm_gain,
    gate_weight,
    up_weight,
    down_weight,
):
    core = lax.axis_index("core")
    col = lax.axis_index(COL)
    row = lax.axis_index(ROW)
    group = lax.axis_index(ZXH)
    me = row * 8 + col
    local_blocks = cache_keys.shape[1] // BLK
    tokens_here = residual.shape[0]

    matched = block_lists // local_blocks == me
    within = jnp.sum(jnp.where(matched, block_lists % local_blocks, 0), axis=2)
    source = (jnp.arange(KV_HEADS, dtype=jnp.int32)[:, None] * local_blocks + within.T).reshape(-1)
    flat_keys = cache_keys.reshape(KV_HEADS * local_blocks, BLK, HEAD_DIM)
    flat_values = cache_values.reshape(KV_HEADS * local_blocks, BLK, HEAD_DIM)
    keys = exchange(flat_keys[source], CHIP)
    values = exchange(flat_values[source], CHIP)
    near_keys = exchange(spread(lax.dynamic_index_in_dim(stretch_keys, group, 0, keepdims=False), 8), COL)
    near_values = exchange(spread(lax.dynamic_index_in_dim(stretch_values, group, 0, keepdims=False), 8), COL)
    my_list = block_lists[col, group]
    place = jnp.stack([core, col]).astype(jnp.int32)
    own, send = attend(
        my_list, place, queries, swap(queries), keys, values,
        near_keys.reshape(8, BLK, HEAD_DIM), near_values.reshape(8, BLK, HEAD_DIM), local_blocks,
    )
    attended = exchange(merge(own, swap(send), 8), COL)

    def halves(x):
        x = x.reshape(8, 2, tokens_here, x.shape[-1])
        mine = lax.dynamic_index_in_dim(x, core, 1, keepdims=False)
        theirs = lax.dynamic_index_in_dim(x, 1 - core, 1, keepdims=False)
        return mine, theirs

    def row_sum(mine, theirs, weight):
        give = mm(theirs, weight).astype(bf16)
        both = mm(mine, weight) + swap(give).astype(f32)
        return jnp.sum(exchange(both.astype(bf16), ZXH).astype(f32), axis=0)

    stream = residual.astype(f32) + row_sum(*halves(attended), out_weight)
    gain = norm_gain.astype(f32)[None, :]
    scaled = (stream * gain).astype(bf16)
    own_rows = exchange(spread(scaled, 8), ZXH)
    other_rows = swap(own_rows)

    def squares(x):
        plain = x.astype(f32) / gain[None]
        return jnp.sum(plain * plain, axis=2)

    parts = jnp.stack([squares(own_rows), squares(other_rows)], axis=1)
    totals = jnp.sum(exchange(parts, COL), axis=0)
    factor = lax.rsqrt(totals.reshape(2, tokens_here) / D + 1e-05)

    def hidden_of(x, factor):
        gate = jnp.sum(exchange(mm(x, gate_weight).astype(bf16), COL).astype(f32), axis=0)
        up = jnp.sum(exchange(mm(x, up_weight).astype(bf16), COL).astype(f32), axis=0)
        gate = gate * factor[:, None]
        hidden = (jax.nn.silu(gate) * (up * factor[:, None])).astype(bf16)
        return exchange(spread(hidden, 8), COL)

    own_hidden = hidden_of(own_rows, factor[0])
    other_hidden = hidden_of(other_rows, factor[1])
    return (stream + row_sum(own_hidden, other_hidden, down_weight)).astype(bf16)


def solution(mesh):
    mesh = Mesh(mesh.devices.reshape(4, 2, 2, 4, 2), AXES)
    in_specs = (
        P(COL, ROW),
        P(None, ROW + COL, None),
        P(None, ROW + COL, None),
        P(None, COL, None),
        P(None, COL, None),
        P(),
        P(ROW, COL),
        P(ROW, COL),
        P(COL),
        P(COL, ROW),
        P(COL, ROW),
        P(ROW, COL),
    )
    return jax.shard_map(local, mesh=mesh, in_specs=in_specs, out_specs=P(ROW, COL), check_vma=False)
```

time: 1110 us -> 396 us (0.36)
  waiting for transfers between devices: 820 us -> 206 us
  blocking collectives: 166 us -> 36.6 us
  starting transfers between devices: 12.1 us -> 65.8 us
  Pallas kernels: 0 us -> 18.5 us
  other arithmetic: 28.8 us -> 11.1 us
  between operations: 13.3 us -> 0.27 us
    psum x1 -> x0, waiting for transfers between devices: 575 us -> none  [local(): summed = lax.psum(partials, 'col')]
    all_to_all x1 -> x13, waiting for transfers between devices: 0.01 us -> 198 us  [exchange(): return lax.all_to_all(x, axes, split_axis=0, concat_axis=0, tiled=True)]
    reduce_scatter x2 -> x0, waiting for transfers between devices: 162 us -> none  [the longest x1 81.9 us: local(): lax.psum_scatter(down_terms, 'row', scatter_dimension=0, tiled=True)]
    all_gather x2 -> x0, blocking collectives: 147 us -> none  [the longest x1 118 us: local(): piece_values = lax.all_gather(own_values, 'col', axis=0, tiled=True)]
    all_gather x2 -> x0, waiting for transfers between devices: 84.1 us -> none  [the longest x1 44.7 us: local(): block_piece = lax.all_gather(normed, 'row', axis=0, tiled=True)]
    all_to_all x1 -> x13, starting transfers between devices: 11.7 us -> 65.7 us  [exchange(): return lax.all_to_all(x, axes, split_axis=0, concat_axis=0, tiled=True)]
    all_to_all x0 -> x2, blocking collectives: none -> 36.6 us  [exchange(): return lax.all_to_all(x, axes, split_axis=0, concat_axis=0, tiled=True)]
    psum x1 -> x0, blocking collectives: 18.8 us -> none  [local(): squares = lax.psum(jnp.sum(stream * stream, axis=1), 'col')]
  transfers between devices with their start and end apart: 6 -> 18, of which waited for: 5 -> 17; matrix products, arithmetic and copies ran while one was open for 0% -> 11% of each run, Pallas kernels for 0% -> 0%
where the time goes in v1:
time: 396 us; the launch traced here: 394 us
  waiting for transfers between devices  206 us (52%)
  starting transfers between devices  65.8 us (17%)
  matrix products  38.6 us (10%)
  blocking collectives  36.6 us (9%)
  Pallas kernels  18.5 us (5%)
  local copies, waits for them, and re-layouts  16.4 us (4%)
  other arithmetic  11.1 us (3%)
    all_to_all x13, waiting for transfers between devices, exchange(): return lax.all_to_all(x, axes, split_axis=0, concat_axis=0, tiled=True)  198 us
    all_to_all x13, starting transfers between devices, exchange(): return lax.all_to_all(x, axes, split_axis=0, concat_axis=0, tiled=True)  65.7 us
    dot_general x8, matrix products, mm(): return jnp.dot(a, b, preferred_element_type=f32)  38.6 us
    all_to_all x2, blocking collectives, exchange(): return lax.all_to_all(x, axes, split_axis=0, concat_axis=0, tiled=True)  36.6 us
    pallas_call x1, Pallas kernels, attend(): pl.pallas_call(functools.partial(attend_kernel, 1.0 / math.sqrt(HEAD_DIM)...  16.2 us
  transfers between devices with their start and end apart: 18, of which 17 were waited for; matrix products, arithmetic and copies ran while one was open for 11% of the time, Pallas kernels for 0%

profile of v1, /device:TPU:0, one launch (start us, length us, event | category | flops | bytes accessed | tf_op | source)
XLA Modules:
  0.0 393.6 jit_solution(1729386164497271474)
XLA Ops:
  1.6 5.5 %all-to-all-start.2 = ((bf16[8,128,128]{2,1,0:T(8,128)(2,1)}), bf16[8,128,128]{2,1,0:T(8,128)(2,1)S(1)}, u32[]{:S(2)}, u32[]{:S(2)}) async-start(bf16[8,128,128]{2,1,0:T(8,128)(2,1)} %broadcast_in_dim.17), calls=%async_computation.2 | async-start | bytes 524288 | tf_op jit(solution)/shard_map/all_to_all | solution.py:178
  9.1 5.3 %all-to-all-done.2.near_keys_ref = bf16[8,128,128]{2,1,0:T(8,128)(2,1)S(1)} async-done(((bf16[8,128,128]{2,1,0:T(8,128)(2,1)}), bf16[8,128,128]{2,1,0:T(8,128)(2,1)S(1)}, u32[]{:S(2)}, u32[]{:S(2)}) %all-to-all-start.2) | async-done | bytes 262176 | tf_op jit(solution)/shard_map/all_to_all | solution.py:178
  20.7 5.1 %all-to-all-done.3.near_values_ref = bf16[8,128,128]{2,1,0:T(8,128)(2,1)S(1)} async-done(((bf16[8,128,128]{2,1,0:T(8,128)(2,1)}), bf16[8,128,128]{2,1,0:T(8,128)(2,1)S(1)}, u32[]{:S(2)}, u32[]{:S(2)}) %all-to-all-start.3) | async-done | bytes 262176 | tf_op jit(solution)/shard_map/all_to_all | solution.py:178
  25.8 9.3 %all-to-all-start = ((bf16[64,128,128]{2,1,0:T(8,128)(2,1)}), bf16[64,128,128]{2,1,0:T(8,128)(2,1)}, u32[]{:S(2)}, u32[]{:S(2)}) async-start(bf16[64,128,128]{2,1,0:T(8,128)(2,1)} %gather_fusion), calls=%async_computation | async-start | bytes 4194304 | tf_op jit(solution)/shard_map/all_to_all | solution.py:178
  38.8 23.1 %all-to-all-done.keys_ref = bf16[64,128,128]{2,1,0:T(8,128)(2,1)} async-done(((bf16[64,128,128]{2,1,0:T(8,128)(2,1)}), bf16[64,128,128]{2,1,0:T(8,128)(2,1)}, u32[]{:S(2)}, u32[]{:S(2)}) %all-to-all-start) | async-done | bytes 2097184 | tf_op jit(solution)/shard_map/all_to_all | solution.py:178
  61.9 5.6 %all-to-all-start.1 = ((bf16[64,128,128]{2,1,0:T(8,128)(2,1)}), bf16[64,128,128]{2,1,0:T(8,128)(2,1)}, u32[]{:S(2)}, u32[]{:S(2)}) async-start(bf16[64,128,128]{2,1,0:T(8,128)(2,1)} %gather_fusion.1), calls=%async_computation.1 | async-start | bytes 4194304 | tf_op jit(solution)/shard_map/all_to_all | solution.py:178
  69.0 24.6 %all-to-all-done.1.values_ref = bf16[64,128,128]{2,1,0:T(8,128)(2,1)} async-done(((bf16[64,128,128]{2,1,0:T(8,128)(2,1)}), bf16[64,128,128]{2,1,0:T(8,128)(2,1)}, u32[]{:S(2)}, u32[]{:S(2)}) %all-to-all-start.1) | async-done | bytes 2097184 | tf_op jit(solution)/shard_map/all_to_all | solution.py:178
  93.6 16.2 %shard_map.118 = (f32[136,512]{1,0:T(8,128)S(1)}, f32[136,512]{1,0:T(8,128)S(1)}) custom-call(s32[64]{0:T(128)S(1)} %fusion.43.list_ref, s32[2]{0:T(128)S(1)} %pad_add_fusion.place_ref, bf16[128,512]{1,0:T(8,128)(2,1)S(1)} %copy-done.2, bf16[128,512]{1,0:T(8,128)(2,1)S(1)} %collective-permute-done.other_q_ref, bf16[64,128,128]{2,1,0:T(8,128)(2,1)} %all-to-all-done.keys_ref, ...), custom_call_target="tpu_custom_call" | custom-call | flops 2684354560 | bytes 4194304 | tf_op jit(solution)/shard_map/pallas_call | solution.py:130
  115.1 6.7 %all-to-all-start.4 = ((bf16[8,128,512]{2,1,0:T(8,128)(2,1)}), bf16[8,128,512]{2,1,0:T(8,128)(2,1)S(1)}, u32[]{:S(2)}, u32[]{:S(2)}) async-start(bf16[8,128,512]{2,1,0:T(8,128)(2,1)} %shard_map.119), calls=%async_computation.4 | async-start | bytes 2097152 | tf_op jit(solution)/shard_map/all_to_all | solution.py:178
  121.8 16.0 %all-to-all-done.4 = bf16[8,128,512]{2,1,0:T(8,128)(2,1)S(1)} async-done(((bf16[8,128,512]{2,1,0:T(8,128)(2,1)}), bf16[8,128,512]{2,1,0:T(8,128)(2,1)S(1)}, u32[]{:S(2)}, u32[]{:S(2)}) %all-to-all-start.4) | async-done | bytes 1048608 | tf_op jit(solution)/shard_map/all_to_all | solution.py:178
  147.1 5.3 %all-to-all-start.5 = ((bf16[8,64,1024]{2,1,0:T(8,128)(2,1)}), bf16[8,64,1024]{2,1,0:T(8,128)(2,1)S(1)}, u32[]{:S(2)}, u32[]{:S(2)}) async-start(bf16[8,64,1024]{2,1,0:T(8,128)(2,1)} %add_convert_fusion.1), calls=%async_computation.5 | async-start | bytes 2097152 | tf_op jit(solution)/shard_map/all_to_all | solution.py:178
  152.4 17.5 %all-to-all-done.5 = bf16[8,64,1024]{2,1,0:T(8,128)(2,1)S(1)} async-done(((bf16[8,64,1024]{2,1,0:T(8,128)(2,1)}), bf16[8,64,1024]{2,1,0:T(8,128)(2,1)S(1)}, u32[]{:S(2)}, u32[]{:S(2)}) %all-to-all-start.5) | async-done | bytes 1048608 | tf_op jit(solution)/shard_map/all_to_all | solution.py:178
  170.3 19.9 %all_to_all.75 = bf16[8,64,1024]{2,1,0:T(8,128)(2,1)S(1)} all-to-all(bf16[8,64,1024]{2,1,0:T(8,128)(2,1)S(1)} %broadcast_in_dim.20), channel_id=1, replica_groups=mesh['z'=4,'xh'=2,'core'=2,'y'=4,'xl'=2] {'z','xh'}, dimensions={0} | all-to-all | bytes 2097152 | tf_op jit(solution)/shard_map/all_to_all | solution.py:178
  198.5 5.3 %fusion.18 = bf16[8,64,1792]{2,1,0:T(8,128)(2,1)} fusion(bf16[8,64,1024]{2,1,0:T(8,128)(2,1)S(1)} %all_to_all.75, bf16[1024,1792]{1,0:T(8,128)(2,1)} %param.22), kind=kOutput, calls=%fused_computation.20 | convolution fusion | flops 1879965696 | bytes 6553600 | tf_op jit(solution)/shard_map/dot_general | solution.py:190
  204.5 5.0 %all-to-all-start.9 = ((bf16[8,64,1792]{2,1,0:T(8,128)(2,1)}), bf16[8,64,1792]{2,1,0:T(8,128)(2,1)}, u32[]{:S(2)}, u32[]{:S(2)}) async-start(bf16[8,64,1792]{2,1,0:T(8,128)(2,1)} %fusion.18), calls=%async_computation.9 | async-start | bytes 3670016 | tf_op jit(solution)/shard_map/all_to_all | solution.py:178
  209.4 5.7 %fusion.21 = bf16[8,64,1792]{2,1,0:T(8,128)(2,1)} fusion(bf16[8,64,1024]{2,1,0:T(8,128)(2,1)} %copy-done.3, bf16[1024,1792]{1,0:T(8,128)(2,1)} %param.22), kind=kOutput, calls=%fused_computation.21 | convolution fusion | flops 1879965696 | bytes 6553600 | tf_op jit(solution)/shard_map/dot_general | solution.py:190
  215.1 18.6 %all-to-all-done.9 = bf16[8,64,1792]{2,1,0:T(8,128)(2,1)} async-done(((bf16[8,64,1792]{2,1,0:T(8,128)(2,1)}), bf16[8,64,1792]{2,1,0:T(8,128)(2,1)}, u32[]{:S(2)}, u32[]{:S(2)}) %all-to-all-start.9) | async-done | bytes 1835040 | tf_op jit(solution)/shard_map/all_to_all | solution.py:178
  233.7 4.3 %all-to-all-start.12 = ((bf16[8,64,1792]{2,1,0:T(8,128)(2,1)}), bf16[8,64,1792]{2,1,0:T(8,128)(2,1)}, u32[]{:S(2)}, u32[]{:S(2)}) async-start(bf16[8,64,1792]{2,1,0:T(8,128)(2,1)} %fusion.21), calls=%async_computation.12 | async-start | bytes 3670016 | tf_op jit(solution)/shard_map/all_to_all | solution.py:178
  238.1 5.7 %fusion.15 = bf16[8,64,1792]{2,1,0:T(8,128)(2,1)} fusion(bf16[8,64,1024]{2,1,0:T(8,128)(2,1)} %copy-done.3, bf16[1024,1792]{1,0:T(8,128)(2,1)} %param.21), kind=kOutput, calls=%fused_computation.19 | convolution fusion | flops 1879965696 | bytes 6553600 | tf_op jit(solution)/shard_map/dot_general | solution.py:190
  243.8 17.6 %all-to-all-done.12 = bf16[8,64,1792]{2,1,0:T(8,128)(2,1)} async-done(((bf16[8,64,1792]{2,1,0:T(8,128)(2,1)}), bf16[8,64,1792]{2,1,0:T(8,128)(2,1)}, u32[]{:S(2)}, u32[]{:S(2)}) %all-to-all-start.12) | async-done | bytes 1835040 | tf_op jit(solution)/shard_map/all_to_all | solution.py:178
  261.4 4.3 %all-to-all-start.11 = ((bf16[8,64,1792]{2,1,0:T(8,128)(2,1)}), bf16[8,64,1792]{2,1,0:T(8,128)(2,1)}, u32[]{:S(2)}, u32[]{:S(2)}) async-start(bf16[8,64,1792]{2,1,0:T(8,128)(2,1)} %fusion.15), calls=%async_computation.11 | async-start | bytes 3670016 | tf_op jit(solution)/shard_map/all_to_all | solution.py:178
  265.7 5.3 %fusion.12 = bf16[8,64,1792]{2,1,0:T(8,128)(2,1)} fusion(bf16[8,64,1024]{2,1,0:T(8,128)(2,1)S(1)} %all_to_all.75, bf16[1024,1792]{1,0:T(8,128)(2,1)} %param.21), kind=kOutput, calls=%fused_computation.18 | convolution fusion | flops 1879965696 | bytes 6553600 | tf_op jit(solution)/shard_map/dot_general | solution.py:190
  271.0 17.4 %all-to-all-done.11 = bf16[8,64,1792]{2,1,0:T(8,128)(2,1)} async-done(((bf16[8,64,1792]{2,1,0:T(8,128)(2,1)}), bf16[8,64,1792]{2,1,0:T(8,128)(2,1)}, u32[]{:S(2)}, u32[]{:S(2)}) %all-to-all-start.11) | async-done | bytes 1835040 | tf_op jit(solution)/shard_map/all_to_all | solution.py:178
  288.4 4.3 %all-to-all-start.7 = ((bf16[8,64,1792]{2,1,0:T(8,128)(2,1)}), bf16[8,64,1792]{2,1,0:T(8,128)(2,1)}, u32[]{:S(2)}, u32[]{:S(2)}) async-start(bf16[8,64,1792]{2,1,0:T(8,128)(2,1)} %fusion.12), calls=%async_computation.7 | async-start | bytes 3670016 | tf_op jit(solution)/shard_map/all_to_all | solution.py:178
  297.9 17.5 %all-to-all-done.7 = bf16[8,64,1792]{2,1,0:T(8,128)(2,1)} async-done(((bf16[8,64,1792]{2,1,0:T(8,128)(2,1)}), bf16[8,64,1792]{2,1,0:T(8,128)(2,1)}, u32[]{:S(2)}, u32[]{:S(2)}) %all-to-all-start.7) | async-done | bytes 1835040 | tf_op jit(solution)/shard_map/all_to_all | solution.py:178
  316.7 4.3 %all-to-all-start.13 = ((bf16[8,64,1792]{2,1,0:T(8,128)(2,1)}), bf16[8,64,1792]{2,1,0:T(8,128)(2,1)}, u32[]{:S(2)}, u32[]{:S(2)}) async-start(bf16[8,64,1792]{2,1,0:T(8,128)(2,1)} %broadcast_in_dim.22), calls=%async_computation.13 | async-start | bytes 3670016 | tf_op jit(solution)/shard_map/all_to_all | solution.py:178
  324.9 18.5 %all-to-all-done.13 = bf16[8,64,1792]{2,1,0:T(8,128)(2,1)} async-done(((bf16[8,64,1792]{2,1,0:T(8,128)(2,1)}), bf16[8,64,1792]{2,1,0:T(8,128)(2,1)}, u32[]{:S(2)}, u32[]{:S(2)}) %all-to-all-start.13) | async-done | bytes 1835040 | tf_op jit(solution)/shard_map/all_to_all | solution.py:178
  344.8 4.3 %all-to-all-start.10 = ((bf16[8,64,1792]{2,1,0:T(8,128)(2,1)}), bf16[8,64,1792]{2,1,0:T(8,128)(2,1)}, u32[]{:S(2)}, u32[]{:S(2)}) async-start(bf16[8,64,1792]{2,1,0:T(8,128)(2,1)} %broadcast_in_dim.21), calls=%async_computation.10 | async-start | bytes 3670016 | tf_op jit(solution)/shard_map/all_to_all | solution.py:178
  349.2 5.6 %fusion.24 = bf16[8,64,1024]{2,1,0:T(8,128)(2,1)} fusion(bf16[8,64,1792]{2,1,0:T(8,128)(2,1)} %all-to-all-done.13, bf16[1792,1024]{1,0:T(8,128)(2,1)} %param.23), kind=kOutput, calls=%fused_computation.29 | convolution fusion | flops 1879572480 | bytes 6553600 | tf_op jit(solution)/shard_map/dot_general | solution.py:190
  354.8 16.5 %all-to-all-done.10 = bf16[8,64,1792]{2,1,0:T(8,128)(2,1)} async-done(((bf16[8,64,1792]{2,1,0:T(8,128)(2,1)}), bf16[8,64,1792]{2,1,0:T(8,128)(2,1)}, u32[]{:S(2)}, u32[]{:S(2)}) %all-to-all-start.10) | async-done | bytes 1835040 | tf_op jit(solution)/shard_map/all_to_all | solution.py:178
  371.4 4.7 %add_convert_fusion = bf16[8,64,1024]{2,1,0:T(8,128)(2,1)S(1)} fusion(bf16[8,64,1024]{2,1,0:T(8,128)(2,1)S(1)} %collective-permute-done.4, bf16[8,64,1792]{2,1,0:T(8,128)(2,1)} %all-to-all-done.10, bf16[1792,1024]{1,0:T(8,128)(2,1)} %param.23), kind=kOutput, calls=%fused_computation.23 | convolution fusion | flops 1880621056 | bytes 7602176 | tf_op jit(solution)/shard_map/dot_general | solution.py:190
  376.0 16.7 %all_to_all.76 = bf16[8,64,1024]{2,1,0:T(8,128)(2,1)S(1)} all-to-all(bf16[8,64,1024]{2,1,0:T(8,128)(2,1)S(1)} %add_convert_fusion), channel_id=1, replica_groups=mesh['z'=4,'xh'=2,'core'=2,'y'=4,'xl'=2] {'z','xh'}, dimensions={0} | all-to-all | bytes 2097152 | tf_op jit(solution)/shard_map/all_to_all | solution.py:178
  (68 shorter events, 51.3 us)
Async XLA Ops:
  0.0 18.6 %copy-start = (bf16[8,1024,128]{2,1,0:T(8,128)(2,1)S(1)}, bf16[8,1024,128]{2,1,0:T(8,128)(2,1)}, u32[]{:S(2)}) copy-start(bf16[8,1024,128]{2,1,0:T(8,128)(2,1)} %param.13) | copy-start | bytes 6291460
  1.6 12.8 %all-to-all-start.2 = ((bf16[8,128,128]{2,1,0:T(8,128)(2,1)}), bf16[8,128,128]{2,1,0:T(8,128)(2,1)S(1)}, u32[]{:S(2)}, u32[]{:S(2)}) async-start(bf16[8,128,128]{2,1,0:T(8,128)(2,1)} %broadcast_in_dim.17), calls=%async_computation.2 | async-start | bytes 524288 | tf_op jit(solution)/shard_map/all_to_all | solution.py:178
  15.1 10.6 %all-to-all-start.3 = ((bf16[8,128,128]{2,1,0:T(8,128)(2,1)}), bf16[8,128,128]{2,1,0:T(8,128)(2,1)S(1)}, u32[]{:S(2)}, u32[]{:S(2)}) async-start(bf16[8,128,128]{2,1,0:T(8,128)(2,1)} %broadcast_in_dim.19), calls=%async_computation.3 | async-start | bytes 524288 | tf_op jit(solution)/shard_map/all_to_all | solution.py:178
  25.8 36.2 %all-to-all-start = ((bf16[64,128,128]{2,1,0:T(8,128)(2,1)}), bf16[64,128,128]{2,1,0:T(8,128)(2,1)}, u32[]{:S(2)}, u32[]{:S(2)}) async-start(bf16[64,128,128]{2,1,0:T(8,128)(2,1)} %gather_fusion), calls=%async_computation | async-start | bytes 4194304 | tf_op jit(solution)/shard_map/all_to_all | solution.py:178
  38.8 28.7 %copy-start.2 = (bf16[128,512]{1,0:T(8,128)(2,1)S(1)}, bf16[128,512]{1,0:T(8,128)(2,1)}, u32[]{:S(2)}) copy-start(bf16[128,512]{1,0:T(8,128)(2,1)} %own_q_ref.1) | copy-start | bytes 393220
  61.9 31.7 %all-to-all-start.1 = ((bf16[64,128,128]{2,1,0:T(8,128)(2,1)}), bf16[64,128,128]{2,1,0:T(8,128)(2,1)}, u32[]{:S(2)}, u32[]{:S(2)}) async-start(bf16[64,128,128]{2,1,0:T(8,128)(2,1)} %gather_fusion.1), calls=%async_computation.1 | async-start | bytes 4194304 | tf_op jit(solution)/shard_map/all_to_all | solution.py:178
  67.5 1.4 collective-permute-start
  109.8 0.7 copy-start.1
  110.6 1.6 collective-permute-start.1
  112.1 0.7 copy-start.5
  115.1 22.8 %all-to-all-start.4 = ((bf16[8,128,512]{2,1,0:T(8,128)(2,1)}), bf16[8,128,512]{2,1,0:T(8,128)(2,1)S(1)}, u32[]{:S(2)}, u32[]{:S(2)}) async-start(bf16[8,128,512]{2,1,0:T(8,128)(2,1)} %shard_map.119), calls=%async_computation.4 | async-start | bytes 2097152 | tf_op jit(solution)/shard_map/all_to_all | solution.py:178
  140.8 3.0 collective-permute-start.2
  140.8 11.6 %copy-start.6 = (bf16[1024]{0:T(1024)(128)(2,1)S(1)}, bf16[1024]{0:T(1024)(128)(2,1)}, u32[]{:S(2)}) copy-start(bf16[1024]{0:T(1024)(128)(2,1)} %param.20) | copy-start | bytes 6148
  147.1 23.1 %copy-start.4 = (bf16[64,1024]{1,0:T(8,128)(2,1)S(1)}, bf16[64,1024]{1,0:T(8,128)(2,1)}, u32[]{:S(2)}) copy-start(bf16[64,1024]{1,0:T(8,128)(2,1)} %param.19) | copy-start | bytes 393220
  147.1 22.9 %all-to-all-start.5 = ((bf16[8,64,1024]{2,1,0:T(8,128)(2,1)}), bf16[8,64,1024]{2,1,0:T(8,128)(2,1)S(1)}, u32[]{:S(2)}, u32[]{:S(2)}) async-start(bf16[8,64,1024]{2,1,0:T(8,128)(2,1)} %add_convert_fusion.1), calls=%async_computation.5 | async-start | bytes 2097152 | tf_op jit(solution)/shard_map/all_to_all | solution.py:178
  190.2 2.7 collective-permute-start.3
  192.9 1.0 copy-start.3
  195.2 9.3 %all-to-all-start.8 = ((f32[8,1,128]{2,1,0:T(1,128)}), f32[8,1,128]{2,1,0:T(1,128)S(1)}, u32[]{:S(2)}, u32[]{:S(2)}) async-start(f32[8,1,128]{2,1,0:T(1,128)} %reshape.148), calls=%async_computation.8 | async-start | bytes 8192 | tf_op jit(solution)/shard_map/all_to_all | solution.py:178
  204.5 29.2 %all-to-all-start.9 = ((bf16[8,64,1792]{2,1,0:T(8,128)(2,1)}), bf16[8,64,1792]{2,1,0:T(8,128)(2,1)}, u32[]{:S(2)}, u32[]{:S(2)}) async-start(bf16[8,64,1792]{2,1,0:T(8,128)(2,1)} %fusion.18), calls=%async_computation.9 | async-start | bytes 3670016 | tf_op jit(solution)/shard_map/all_to_all | solution.py:178
  233.7 27.6 %all-to-all-start.12 = ((bf16[8,64,1792]{2,1,0:T(8,128)(2,1)}), bf16[8,64,1792]{2,1,0:T(8,128)(2,1)}, u32[]{:S(2)}, u32[]{:S(2)}) async-start(bf16[8,64,1792]{2,1,0:T(8,128)(2,1)} %fusion.21), calls=%async_computation.12 | async-start | bytes 3670016 | tf_op jit(solution)/shard_map/all_to_all | solution.py:178
  261.4 27.1 %all-to-all-start.11 = ((bf16[8,64,1792]{2,1,0:T(8,128)(2,1)}), bf16[8,64,1792]{2,1,0:T(8,128)(2,1)}, u32[]{:S(2)}, u32[]{:S(2)}) async-start(bf16[8,64,1792]{2,1,0:T(8,128)(2,1)} %fusion.15), calls=%async_computation.11 | async-start | bytes 3670016 | tf_op jit(solution)/shard_map/all_to_all | solution.py:178
  288.4 26.9 %all-to-all-start.7 = ((bf16[8,64,1792]{2,1,0:T(8,128)(2,1)}), bf16[8,64,1792]{2,1,0:T(8,128)(2,1)}, u32[]{:S(2)}, u32[]{:S(2)}) async-start(bf16[8,64,1792]{2,1,0:T(8,128)(2,1)} %fusion.12), calls=%async_computation.7 | async-start | bytes 3670016 | tf_op jit(solution)/shard_map/all_to_all | solution.py:178
  316.7 26.7 %all-to-all-start.13 = ((bf16[8,64,1792]{2,1,0:T(8,128)(2,1)}), bf16[8,64,1792]{2,1,0:T(8,128)(2,1)}, u32[]{:S(2)}, u32[]{:S(2)}) async-start(bf16[8,64,1792]{2,1,0:T(8,128)(2,1)} %broadcast_in_dim.22), calls=%async_computation.13 | async-start | bytes 3670016 | tf_op jit(solution)/shard_map/all_to_all | solution.py:178
  344.8 26.5 %all-to-all-start.10 = ((bf16[8,64,1792]{2,1,0:T(8,128)(2,1)}), bf16[8,64,1792]{2,1,0:T(8,128)(2,1)}, u32[]{:S(2)}, u32[]{:S(2)}) async-start(bf16[8,64,1792]{2,1,0:T(8,128)(2,1)} %broadcast_in_dim.21), calls=%async_computation.10 | async-start | bytes 3670016 | tf_op jit(solution)/shard_map/all_to_all | solution.py:178
  354.8 16.5 %collective-permute-start.4 = (bf16[8,64,1024]{2,1,0:T(8,128)(2,1)}, bf16[8,64,1024]{2,1,0:T(8,128)(2,1)S(1)}, u32[]{:S(2)}, u32[]{:S(2)}) collective-permute-start(bf16[8,64,1024]{2,1,0:T(8,128)(2,1)} %fusion.24), channel_id=1, source_target_pairs={{0,8},{8,0},{1,9},{9,1},{2,10},{10,2},{3,11},{11,3},{4,12},{12,4},... | collective-permute-start | bytes 3145736 | tf_op jit(solution)/shard_map/ppermute | solution.py:182

commit v2 on v1

--- a/solution.py
+++ b/solution.py
@@ -41,8 +41,6 @@
     other_q_ref,
     keys_ref,
     values_ref,
-    near_keys_ref,
-    near_values_ref,
     own_ref,
     send_ref,
     order_ref,
@@ -79,16 +77,16 @@
             scores = scores + bias
         old = top_ref[half]
         new = jnp.maximum(old, jnp.max(scores, axis=0, keepdims=True))
-        weights = jnp.exp(scores - new)
-        decay = jnp.exp(old - new)
+        weights = jnp.exp2(scores - new)
+        decay = jnp.exp2(old - new)
         top_ref[half] = new
         sum_ref[half] = sum_ref[half] * decay + jnp.sum(weights, axis=0, keepdims=True)
         acc_ref[half] = acc_ref[half] * decay + tn_dot(values, weights.astype(bf16))
 
     def far(step, carry):
         slots = [jnp.minimum(step * per_step + i, count - 1) for i in range(per_step)]
-        keys = jnp.concatenate([keys_ref[order_ref[s]] for s in slots], axis=0)
-        values = jnp.concatenate([values_ref[order_ref[s]] for s in slots], axis=0)
+        keys = jnp.concatenate([keys_ref[order_ref[s], 0:BLK] for s in slots], axis=0)
+        values = jnp.concatenate([values_ref[order_ref[s], 0:BLK] for s in slots], axis=0)
         bias = jnp.concatenate(
             [
                 jnp.full((BLK, 1), jnp.where(step * per_step + i < count, 0.0, NEG), f32)
@@ -108,8 +106,10 @@
         key_pos = lax.broadcasted_iota(jnp.int32, (BLK, rows), 0)
         token = lax.broadcasted_iota(jnp.int32, (BLK, rows), 1) % BLK
         bias = jnp.where(key_pos <= token + shift, 0.0, NEG)
+        keys = jnp.concatenate([keys_ref[i * 8 + which, BLK:] for i in range(8)], axis=0)
+        values = jnp.concatenate([values_ref[i * 8 + which, BLK:] for i in range(8)], axis=0)
         for half in range(2):
-            update(half, near_keys_ref[which], near_values_ref[which], bias)
+            update(half, keys, values, bias)
         return carry
 
     lax.fori_loop(0, (block - core + 2) // 2, near, 0)
@@ -121,16 +121,16 @@
     send_ref[HEAD_DIM + 1 : HEAD_DIM + 2, :] = sum_ref[1]
 
 
-def attend(my_list, place, own_q, other_q, keys, values, near_keys, near_values, local_blocks):
+def attend(my_list, place, own_q, other_q, keys, values, local_blocks):
     heads = own_q.shape[1] // HEAD_DIM
     rows = heads * BLK
     packed = jax.ShapeDtypeStruct((HEAD_DIM + 8, rows), f32)
     smem = pl.BlockSpec(memory_space=pltpu.SMEM)
     vmem = pl.BlockSpec(memory_space=pltpu.VMEM)
     return pl.pallas_call(
-        functools.partial(attend_kernel, 1.0 / math.sqrt(HEAD_DIM), 2, local_blocks),
+        functools.partial(attend_kernel, math.log2(math.e) / math.sqrt(HEAD_DIM), 4, local_blocks),
         out_shape=(packed, packed),
-        in_specs=[smem, smem] + [vmem] * 6,
+        in_specs=[smem, smem] + [vmem] * 4,
         out_specs=(vmem, vmem),
         scratch_shapes=[
             pltpu.SMEM((my_list.shape[0] + 1,), jnp.int32),
@@ -139,21 +139,20 @@
             pltpu.VMEM((2, 1, rows), f32),
             pltpu.VMEM((2, HEAD_DIM, rows), f32),
         ],
-        compiler_params=pltpu.CompilerParams(vmem_limit_bytes=48 * 1024 * 1024),
         cost_estimate=pl.CostEstimate(
             flops=4 * 2 * rows * 40 * BLK * HEAD_DIM,
             bytes_accessed=2 * keys.size * 2,
             transcendentals=2 * rows * 40 * BLK,
         ),
-    )(my_list, place, own_q, other_q, keys, values, near_keys, near_values)
+    )(my_list, place, own_q, other_q, keys, values)
 
 
 def merge_kernel(own_ref, got_ref, out_ref):
     own_top = own_ref[HEAD_DIM : HEAD_DIM + 1, :]
     got_top = got_ref[HEAD_DIM : HEAD_DIM + 1, :]
     top = jnp.maximum(own_top, got_top)
-    own_w = jnp.exp(own_top - top)
-    got_w = jnp.exp(got_top - top)
+    own_w = jnp.exp2(own_top - top)
+    got_w = jnp.exp2(got_top - top)
     total = own_w * own_ref[HEAD_DIM + 1 : HEAD_DIM + 2, :] + got_w * got_ref[HEAD_DIM + 1 : HEAD_DIM + 2, :]
     mixed = (own_ref[0:HEAD_DIM, :] * own_w + got_ref[0:HEAD_DIM, :] * got_w) / total
     heads = mixed.shape[1] // BLK
@@ -174,20 +173,148 @@
     )(own, got)
 
 
+def product_kernel(tiles, pick_ref, x_ref, *refs):
+    weight_refs, add_ref, out_ref = refs[:tiles[0]], refs[tiles[0] : -1], refs[-1]
+    x = x_ref[...].reshape(-1, x_ref.shape[-1])
+    step = pl.program_id(0)
+
+    def put(weight_ref):
+        total = jnp.dot(x, weight_ref[...], preferred_element_type=f32)
+        if add_ref:
+            total = total + add_ref[0][...].reshape(total.shape).astype(f32)
+        out_ref[...] = total.astype(out_ref.dtype).reshape(out_ref.shape)
+
+    for i, weight_ref in enumerate(weight_refs):
+        pl.when(step // tiles[1] == i)(functools.partial(put, weight_ref))
+
+
+def product(x, weights, tile, pick=None, add=None):
+    blocks, pair, tokens, inputs = x.shape
+    width = weights[0].shape[1]
+    count = width // tile
+    taken = pair if pick is None else 1
+    pick = jnp.zeros((1,), jnp.int32) if pick is None else pick.astype(jnp.int32).reshape(1)
+    out_block = (blocks, taken, tokens, tile)
+
+    def weight_spec(i):
+        return pl.BlockSpec((inputs, tile), lambda n, p, i=i: (0, jnp.clip(n - i * count, 0, count - 1)))
+
+    by_column = pl.BlockSpec(out_block, lambda n, p: (0, 0, 0, n))
+    specs = [pl.BlockSpec((blocks, taken, tokens, inputs), lambda n, p: (0, p[0], 0, 0))]
+    specs += [weight_spec(i) for i in range(len(weights))]
+    operands = [x, *weights]
+    if add is not None:
+        specs.append(by_column)
+        operands.append(add)
+    rows = blocks * taken * tokens
+    columns = width * len(weights)
+    return pl.pallas_call(
+        functools.partial(product_kernel, (len(weights), count)),
+        out_shape=jax.ShapeDtypeStruct((blocks, taken, tokens, columns), bf16),
+        grid_spec=pltpu.PrefetchScalarGridSpec(
+            num_scalar_prefetch=1, grid=(count * len(weights),), in_specs=specs, out_specs=by_column
+        ),
+        cost_estimate=pl.CostEstimate(
+            flops=2 * rows * inputs * columns,
+            bytes_accessed=2 * (rows * inputs + inputs * columns + rows * columns),
+            transcendentals=0,
+        ),
+    )(pick, *operands)
+
+
+def split_sum_kernel(side_ref, x_ref, give_ref, keep_ref):
+    side = side_ref[0]
+    give_ref[...] = jnp.sum(x_ref[:, 1 - side].astype(f32), axis=0).astype(bf16)
+    keep_ref[...] = jnp.sum(x_ref[:, side].astype(f32), axis=0)
+
+
+def split_sum(x, side):
+    count, _, tokens, width = x.shape
+    tile = 896
+    by_column = pl.BlockSpec((tokens, tile), lambda n, p: (0, n))
+    return pl.pallas_call(
+        split_sum_kernel,
+        out_shape=(
+            jax.ShapeDtypeStruct((tokens, width), bf16),
+            jax.ShapeDtypeStruct((tokens, width), f32),
+        ),
+        grid_spec=pltpu.PrefetchScalarGridSpec(
+            num_scalar_prefetch=1,
+            grid=(width // tile,),
+            in_specs=[pl.BlockSpec((count, 2, tokens, tile), lambda n, p: (0, 0, 0, n))],
+            out_specs=(by_column, by_column),
+        ),
+        cost_estimate=pl.CostEstimate(flops=x.size, bytes_accessed=x.size * 3, transcendentals=0),
+    )(side.astype(jnp.int32).reshape(1), x)
+
+
+def gated_kernel(gate_refs, up_refs, factor_ref, out_ref):
+    factor = factor_ref[...]
+    gate = sum(jnp.sum(r[...].astype(f32), axis=0) for r in gate_refs) * factor
+    up = sum(jnp.sum(r[...].astype(f32), axis=0) for r in up_refs) * factor
+    out_ref[...] = (gate / (1.0 + jnp.exp(-gate)) * up).astype(bf16)
+
+
+def gated(x, extra, factor):
+    parts = [x] if extra is None else [x, extra]
+    tokens, width = x.shape[1], x.shape[2] // 2
+    tile = 896
+    count = width // tile
+
+    def kernel(*refs):
+        n = len(parts)
+        gated_kernel(refs[:n], refs[n : 2 * n], refs[2 * n], refs[2 * n + 1])
+
+    specs = [
+        pl.BlockSpec((p.shape[0], tokens, tile), lambda n, first=first: (0, 0, n + first))
+        for first in (0, count)
+        for p in parts
+    ]
+    return pl.pallas_call(
+        kernel,
+        grid=(count,),
+        out_shape=jax.ShapeDtypeStruct((tokens, width), bf16),
+        in_specs=specs + [pl.BlockSpec((tokens, 1), lambda n: (0, 0))],
+        out_specs=pl.BlockSpec((tokens, tile), lambda n: (0, n)),
+        cost_estimate=pl.CostEstimate(
+            flops=8 * x.size, bytes_accessed=3 * x.size, transcendentals=tokens * width
+        ),
+    )(*parts, *parts, factor[:, None])
+
+
+def pair_kernel(side_ref, mine_ref, got_ref, out_ref):
+    side = side_ref[0]
+    for i in range(out_ref.shape[0]):
+        out_ref[i, side] = mine_ref[...]
+        out_ref[i, 1 - side] = got_ref[...]
+
+
+def pair_up(mine, got, side):
+    tokens, width = mine.shape
+    vmem = pl.BlockSpec(memory_space=pltpu.VMEM)
+    return pl.pallas_call(
+        pair_kernel,
+        out_shape=jax.ShapeDtypeStruct((4, 2, tokens, width), bf16),
+        in_specs=[pl.BlockSpec(memory_space=pltpu.SMEM), vmem, vmem],
+        out_specs=vmem,
+        cost_estimate=pl.CostEstimate(flops=0, bytes_accessed=mine.size * 20, transcendentals=0),
+    )(side.astype(jnp.int32).reshape(1), mine, got)
+
+
 def exchange(x, axes):
     return lax.all_to_all(x, axes, split_axis=0, concat_axis=0, tiled=True)
 
 
-def swap(x):
-    return lax.ppermute(x, "core", [(0, 1), (1, 0)])
+def swap(x, axis="core"):
+    return lax.ppermute(x, axis, [(0, 1), (1, 0)])
 
 
 def spread(x, copies):
     return jnp.broadcast_to(x[None], (copies,) + x.shape)
 
 
-def mm(a, b):
-    return jnp.dot(a, b, preferred_element_type=f32)
+def take(x, index, axis):
+    return lax.dynamic_index_in_dim(x, index, axis, keepdims=False)
 
 
 def local(
@@ -205,42 +332,37 @@
     down_weight,
 ):
     core = lax.axis_index("core")
+    side = lax.axis_index("xl")
     col = lax.axis_index(COL)
-    row = lax.axis_index(ROW)
     group = lax.axis_index(ZXH)
-    me = row * 8 + col
+    me = lax.axis_index(ROW) * 8 + col
     local_blocks = cache_keys.shape[1] // BLK
     tokens_here = residual.shape[0]
 
     matched = block_lists // local_blocks == me
     within = jnp.sum(jnp.where(matched, block_lists % local_blocks, 0), axis=2)
     source = (jnp.arange(KV_HEADS, dtype=jnp.int32)[:, None] * local_blocks + within.T).reshape(-1)
-    flat_keys = cache_keys.reshape(KV_HEADS * local_blocks, BLK, HEAD_DIM)
-    flat_values = cache_values.reshape(KV_HEADS * local_blocks, BLK, HEAD_DIM)
-    keys = exchange(flat_keys[source], CHIP)
-    values = exchange(flat_values[source], CHIP)
-    near_keys = exchange(spread(lax.dynamic_index_in_dim(stretch_keys, group, 0, keepdims=False), 8), COL)
-    near_values = exchange(spread(lax.dynamic_index_in_dim(stretch_values, group, 0, keepdims=False), 8), COL)
+
+    def fetch(cache, stretch):
+        flat = cache.reshape(KV_HEADS * local_blocks, BLK, HEAD_DIM)
+        part = BLK // 8
+        near = lax.dynamic_slice_in_dim(stretch, group * part, part, 1)
+        near = jnp.broadcast_to(near[:, None], (KV_HEADS, 8, part, HEAD_DIM)).reshape(64, part, HEAD_DIM)
+        return exchange(jnp.concatenate([flat[source], near], axis=1), CHIP)
+
+    keys = fetch(cache_keys, stretch_keys)
+    values = fetch(cache_values, stretch_values)
     my_list = block_lists[col, group]
     place = jnp.stack([core, col]).astype(jnp.int32)
-    own, send = attend(
-        my_list, place, queries, swap(queries), keys, values,
-        near_keys.reshape(8, BLK, HEAD_DIM), near_values.reshape(8, BLK, HEAD_DIM), local_blocks,
-    )
-    attended = exchange(merge(own, swap(send), 8), COL)
-
-    def halves(x):
-        x = x.reshape(8, 2, tokens_here, x.shape[-1])
-        mine = lax.dynamic_index_in_dim(x, core, 1, keepdims=False)
-        theirs = lax.dynamic_index_in_dim(x, 1 - core, 1, keepdims=False)
-        return mine, theirs
-
-    def row_sum(mine, theirs, weight):
-        give = mm(theirs, weight).astype(bf16)
-        both = mm(mine, weight) + swap(give).astype(f32)
-        return jnp.sum(exchange(both.astype(bf16), ZXH).astype(f32), axis=0)
-
-    stream = residual.astype(f32) + row_sum(*halves(attended), out_weight)
+    own, send = attend(my_list, place, queries, swap(queries), keys, values, local_blocks)
+    attended = exchange(merge(own, swap(send), 8), COL).reshape(8, 2, tokens_here, -1)
+
+    def row_sum(give, mine, pick, weight):
+        both = product(mine, (weight,), 256, pick, add=swap(give))
+        return jnp.sum(exchange(both.reshape(8, tokens_here, -1), ZXH).astype(f32), axis=0)
+
+    give = product(attended, (out_weight,), 256, 1 - core)
+    stream = residual.astype(f32) + row_sum(give, attended, core, out_weight)
     gain = norm_gain.astype(f32)[None, :]
     scaled = (stream * gain).astype(bf16)
     own_rows = exchange(spread(scaled, 8), ZXH)
@@ -254,16 +376,23 @@
     totals = jnp.sum(exchange(parts, COL), axis=0)
     factor = lax.rsqrt(totals.reshape(2, tokens_here) / D + 1e-05)
 
-    def hidden_of(x, factor):
-        gate = jnp.sum(exchange(mm(x, gate_weight).astype(bf16), COL).astype(f32), axis=0)
-        up = jnp.sum(exchange(mm(x, up_weight).astype(bf16), COL).astype(f32), axis=0)
-        gate = gate * factor[:, None]
-        hidden = (jax.nn.silu(gate) * (up * factor[:, None])).astype(bf16)
-        return exchange(spread(hidden, 8), COL)
-
-    own_hidden = hidden_of(own_rows, factor[0])
-    other_hidden = hidden_of(other_rows, factor[1])
-    return (stream + row_sum(own_hidden, other_hidden, down_weight)).astype(bf16)
+    both = (gate_weight, up_weight)
+    by_pair = (4, 2, tokens_here, own_rows.shape[-1])
+    own_rows = own_rows.reshape(by_pair)
+    own_give = product(own_rows, both, 896, 1 - side)
+    other_part = exchange(product(other_rows.reshape(by_pair), both, 896), "y")
+    own_part = product(own_rows, both, 896, side, add=swap(own_give, "xl"))
+    other_give, other_keep = split_sum(other_part, side)
+    own_part = exchange(own_part.reshape(4, tokens_here, -1), "y")
+    other_hidden = gated(other_keep[None], swap(other_give, "xl")[None], factor[1])
+    other_pair = pair_up(other_hidden, swap(other_hidden, "xl"), side)
+    own_part, other_pair = lax.optimization_barrier((own_part, other_pair))
+    other_all = exchange(other_pair, "y").reshape(8, 1, tokens_here, -1)
+    own_hidden = gated(own_part, None, factor[0])
+    own_pair = pair_up(own_hidden, swap(own_hidden, "xl"), side)
+    own_all = exchange(own_pair, "y").reshape(8, 1, tokens_here, -1)
+    give = product(other_all, (down_weight,), 256)
+    return (stream + row_sum(give, own_all, None, down_weight)).astype(bf16)
 
 
 def solution(mesh):

time: 396 us -> 374 us (0.944)
  Pallas kernels: 18.5 us -> 76.3 us
  matrix products: 38.6 us -> 0 us
  waiting for transfers between devices: 206 us -> 178 us
  starting transfers between devices: 65.8 us -> 54.2 us
    all_to_all x13 -> x9, waiting for transfers between devices: 198 us -> 113 us  [exchange(): return lax.all_to_all(x, axes, split_axis=0, concat_axis=0, tiled=True)]
    pallas_call x1 -> x13, Pallas kernels: 16.2 us -> 74.1 us  [the longest x7 44.6 us: product(): pl.pallas_call(functools.partial(product_kernel, (len(weights), count)),...]
    ppermute x5 -> x9, waiting for transfers between devices: 7.77 us -> 65.2 us  [swap(): return lax.ppermute(x, axis, [(0, 1), (1, 0)])]
    dot_general x8 -> x0, matrix products: 38.6 us -> none  [mm(): return jnp.dot(a, b, preferred_element_type=f32)]
    all_to_all x13 -> x9, starting transfers between devices: 65.7 us -> 47.9 us  [exchange(): return lax.all_to_all(x, axes, split_axis=0, concat_axis=0, tiled=True)]
    reduce_sum x6 -> x2, other arithmetic: 7.57 us -> 0.34 us  [row_sum(): jnp.sum(exchange(both.reshape(8, tokens_here, -1), ZXH).astype(f32), axis=0)]
    ppermute x5 -> x9, starting transfers between devices: 0.1 us -> 6.22 us  [swap(): return lax.ppermute(x, axis, [(0, 1), (1, 0)])]
    broadcast_in_dim x7 -> x1, local copies, waits for them, and re-layouts: 6.05 us -> 0.12 us  [spread(): return jnp.broadcast_to(x[None], (copies,) + x.shape)]
  transfers between devices with their start and end apart: 18 -> 18, of which waited for: 17 -> 13; matrix products, arithmetic and copies ran while one was open for 11% -> 2% of each run, Pallas kernels for 0% -> 12%
where the time goes in v2:
time: 374 us; the launch traced here: 372 us
  waiting for transfers between devices  178 us (48%)
  Pallas kernels  76.3 us (20%)
  starting transfers between devices  54.2 us (14%)
  blocking collectives  36.5 us (10%)
  local copies, waits for them, and re-layouts  17.6 us (5%)
  other arithmetic  9.03 us (2%)
    all_to_all x9, waiting for transfers between devices, exchange(): return lax.all_to_all(x, axes, split_axis=0, concat_axis=0, tiled=True)  113 us
    ppermute x9, waiting for transfers between devices, swap(): return lax.ppermute(x, axis, [(0, 1), (1, 0)])  65.2 us
    all_to_all x9, starting transfers between devices, exchange(): return lax.all_to_all(x, axes, split_axis=0, concat_axis=0, tiled=True)  47.9 us
    pallas_call x7, Pallas kernels, product(): pl.pallas_call(functools.partial(product_kernel, (len(weights), count)),...  44.6 us
    all_to_all x2, blocking collectives, exchange(): return lax.all_to_all(x, axes, split_axis=0, concat_axis=0, tiled=True)  36.5 us
    pallas_call x1, Pallas kernels, attend(): pl.pallas_call(functools.partial(attend_kernel, math.log2(math.e) / math....  16 us
    unnamed x38, local copies, waits for them, and re-layouts  8.65 us
  transfers between devices with their start and end apart: 18, of which 13 were waited for; matrix products, arithmetic and copies ran while one was open for 2% of the time, Pallas kernels for 12%

profile of v2, /device:TPU:0, one launch (start us, length us, event | category | flops | bytes accessed | tf_op | source)
XLA Modules:
  0.0 372.1 jit_solution(49775553542310781)
XLA Ops:
  4.6 3.2 pad_maximum_fusion
  7.8 11.7 %all-to-all-start = ((bf16[64,144,128]{2,1,0:T(8,128)(2,1)}), bf16[64,144,128]{2,1,0:T(8,128)(2,1)}, u32[]{:S(2)}, u32[]{:S(2)}) async-start(bf16[64,144,128]{2,1,0:T(8,128)(2,1)} %pad_maximum_fusion), calls=%async_computation | async-start | bytes 4718592 | tf_op jit(solution)/shard_map/all_to_all | solution.py:305
  23.8 27.9 %all-to-all-done.keys_ref = bf16[64,144,128]{2,1,0:T(8,128)(2,1)} async-done(((bf16[64,144,128]{2,1,0:T(8,128)(2,1)}), bf16[64,144,128]{2,1,0:T(8,128)(2,1)}, u32[]{:S(2)}, u32[]{:S(2)}) %all-to-all-start) | async-done | bytes 2359328 | tf_op jit(solution)/shard_map/all_to_all | solution.py:305
  51.7 6.0 %all-to-all-start.1 = ((bf16[64,144,128]{2,1,0:T(8,128)(2,1)}), bf16[64,144,128]{2,1,0:T(8,128)(2,1)}, u32[]{:S(2)}, u32[]{:S(2)}) async-start(bf16[64,144,128]{2,1,0:T(8,128)(2,1)} %pad_maximum_fusion.1), calls=%async_computation.1 | async-start | bytes 4718592 | tf_op jit(solution)/shard_map/all_to_all | solution.py:305
  59.7 29.7 %all-to-all-done.1.values_ref = bf16[64,144,128]{2,1,0:T(8,128)(2,1)} async-done(((bf16[64,144,128]{2,1,0:T(8,128)(2,1)}), bf16[64,144,128]{2,1,0:T(8,128)(2,1)}, u32[]{:S(2)}, u32[]{:S(2)}) %all-to-all-start.1) | async-done | bytes 2359328 | tf_op jit(solution)/shard_map/all_to_all | solution.py:305
  89.3 16.0 %shard_map.118 = (f32[136,512]{1,0:T(8,128)}, f32[136,512]{1,0:T(8,128)}) custom-call(s32[64]{0:T(128)} %fusion.5.list_ref, s32[2]{0:T(128)} %pad_add_fusion.place_ref, bf16[128,512]{1,0:T(8,128)(2,1)} %own_q_ref.1, bf16[128,512]{1,0:T(8,128)(2,1)} %copy-done.17, bf16[64,144,128]{2,1,0:T(8,128)(2,1)} %all-to-all-done.keys_ref, ...), custom_call_target="tpu_custom_call" | custom-call | flops 2684354560 | bytes 4718592 | tf_op jit(solution)/shard_map/pallas_call | solution.py:130
  110.0 4.7 %all-to-all-start.2 = ((bf16[8,128,512]{2,1,0:T(8,128)(2,1)}), bf16[8,128,512]{2,1,0:T(8,128)(2,1)S(1)}, u32[]{:S(2)}, u32[]{:S(2)}) async-start(bf16[8,128,512]{2,1,0:T(8,128)(2,1)} %shard_map.119), calls=%async_computation.2 | async-start | bytes 2097152 | tf_op jit(solution)/shard_map/all_to_all | solution.py:305
  114.7 16.0 %all-to-all-done.2 = bf16[8,128,512]{2,1,0:T(8,128)(2,1)S(1)} async-done(((bf16[8,128,512]{2,1,0:T(8,128)(2,1)}), bf16[8,128,512]{2,1,0:T(8,128)(2,1)S(1)}, u32[]{:S(2)}, u32[]{:S(2)}) %all-to-all-start.2) | async-done | bytes 1048608 | tf_op jit(solution)/shard_map/all_to_all | solution.py:305
  131.8 4.2 %shard_map.120 = bf16[8,1,64,1024]{3,2,1,0:T(8,128)(2,1)} custom-call(s32[1]{0:T(128)} %bitcast.10.pick_ref, bf16[8,2,64,512]{3,2,1,0:T(8,128)(2,1)} %bitcast.34, bf16[512,1024]{1,0:T(8,128)(2,1)} %refs_0_.8), custom_call_target="tpu_custom_call" | custom-call | flops 536870912 | bytes 2621440 | tf_op jit(solution)/shard_map/pallas_call | solution.py:211
  136.0 2.9 collective-permute-done.2.refs_1_
  139.8 4.4 %shard_map.121 = bf16[8,1,64,1024]{3,2,1,0:T(8,128)(2,1)} custom-call(s32[1]{0:T(128)} %bitcast.pick_ref, bf16[8,2,64,512]{3,2,1,0:T(8,128)(2,1)} %bitcast.35, bf16[512,1024]{1,0:T(8,128)(2,1)} %refs_0_.8, bf16[8,1,64,1024]{3,2,1,0:T(8,128)(2,1)} %copy-done.8), custom_call_target="tpu_custom_call" | custom-call | flops 536870912 | bytes 2621440 | tf_op jit(solution)/shard_map/pallas_call | solution.py:211
  144.2 4.9 %all-to-all-start.3 = ((bf16[8,64,1024]{2,1,0:T(8,128)(2,1)}), bf16[8,64,1024]{2,1,0:T(8,128)(2,1)S(1)}, u32[]{:S(2)}, u32[]{:S(2)}) async-start(bf16[8,64,1024]{2,1,0:T(8,128)(2,1)} %bitcast.38), calls=%async_computation.3 | async-start | bytes 2097152 | tf_op jit(solution)/shard_map/all_to_all | solution.py:305
  149.1 17.5 %all-to-all-done.3 = bf16[8,64,1024]{2,1,0:T(8,128)(2,1)S(1)} async-done(((bf16[8,64,1024]{2,1,0:T(8,128)(2,1)}), bf16[8,64,1024]{2,1,0:T(8,128)(2,1)S(1)}, u32[]{:S(2)}, u32[]{:S(2)}) %all-to-all-start.3) | async-done | bytes 1048608 | tf_op jit(solution)/shard_map/all_to_all | solution.py:305
  167.0 19.9 %all_to_all.55 = bf16[8,64,1024]{2,1,0:T(8,128)(2,1)S(1)} all-to-all(bf16[8,64,1024]{2,1,0:T(8,128)(2,1)S(1)} %broadcast_in_dim.14), channel_id=1, replica_groups=mesh['z'=4,'xh'=2,'core'=2,'y'=4,'xl'=2] {'z','xh'}, dimensions={0} | all-to-all | bytes 2097152 | tf_op jit(solution)/shard_map/all_to_all | solution.py:305
  190.9 3.3 all-to-all-start.7
  194.2 9.2 %shard_map.124 = bf16[4,2,64,3584]{3,2,1,0:T(8,128)(2,1)} custom-call(s32[1]{0:T(128)} %constant.67.clone.1.pick_ref, bf16[4,2,64,1024]{3,2,1,0:T(8,128)(2,1)} %bitcast.47, bf16[1024,1792]{1,0:T(8,128)(2,1)} %refs_0_.11, bf16[1024,1792]{1,0:T(8,128)(2,1)} %refs_1_.5), custom_call_target="tpu_custom_call" | custom-call | flops 3758096384 | bytes 12058624 | tf_op jit(solution)/shard_map/pallas_call | solution.py:211
  203.4 4.8 %all-to-all-start.6 = ((bf16[4,2,64,3584]{3,2,1,0:T(8,128)(2,1)}), bf16[4,2,64,3584]{3,2,1,0:T(8,128)(2,1)}, u32[]{:S(2)}, u32[]{:S(2)}) async-start(bf16[4,2,64,3584]{3,2,1,0:T(8,128)(2,1)} %shard_map.124), calls=%async_computation.6 | async-start | bytes 7340032 | tf_op jit(solution)/shard_map/all_to_all | solution.py:305
  208.2 7.0 %shard_map.122 = bf16[4,1,64,3584]{3,2,1,0:T(8,128)(2,1)} custom-call(s32[1]{0:T(128)} %bitcast.14.pick_ref, bf16[4,2,64,1024]{3,2,1,0:T(8,128)(2,1)} %bitcast.32, bf16[1024,1792]{1,0:T(8,128)(2,1)} %refs_0_.11, bf16[1024,1792]{1,0:T(8,128)(2,1)} %refs_1_.5), custom_call_target="tpu_custom_call" | custom-call | flops 1879048192 | bytes 9699328 | tf_op jit(solution)/shard_map/pallas_call | solution.py:211
  217.0 40.4 %collective-permute-done.3.refs_2_ = bf16[4,1,64,3584]{3,2,1,0:T(8,128)(2,1)S(1)} collective-permute-done((bf16[4,1,64,3584]{3,2,1,0:T(8,128)(2,1)}, bf16[4,1,64,3584]{3,2,1,0:T(8,128)(2,1)S(1)}, u32[]{:S(2)}, u32[]{:S(2)}) %collective-permute-start.3) | collective-permute-done | bytes 1835040 | tf_op jit(solution)/shard_map/ppermute | solution.py:309
  258.6 7.2 %shard_map.123 = bf16[4,1,64,3584]{3,2,1,0:T(8,128)(2,1)} custom-call(s32[1]{0:T(128)} %bitcast.12.pick_ref.side_ref, bf16[4,2,64,1024]{3,2,1,0:T(8,128)(2,1)} %bitcast.33, bf16[1024,1792]{1,0:T(8,128)(2,1)} %refs_0_.11, bf16[1024,1792]{1,0:T(8,128)(2,1)} %refs_1_.5, bf16[4,1,64,3584]{3,2,1,0:T(8,128)(2,1)} %copy-done.6), custom_call_target="tpu_custom_call" | custom-call | flops 1879048192 | bytes 9699328 | tf_op jit(solution)/shard_map/pallas_call | solution.py:211
  265.8 4.4 %all-to-all-start.5 = ((bf16[4,64,3584]{2,1,0:T(8,128)(2,1)}), bf16[4,64,3584]{2,1,0:T(8,128)(2,1)S(1)}, u32[]{:S(2)}, u32[]{:S(2)}) async-start(bf16[4,64,3584]{2,1,0:T(8,128)(2,1)} %bitcast.36), calls=%async_computation.5 | async-start | bytes 3670016 | tf_op jit(solution)/shard_map/all_to_all | solution.py:305
  270.2 4.1 %shard_map.125 = (bf16[64,3584]{1,0:T(8,128)(2,1)}, f32[64,3584]{1,0:T(8,128)}) custom-call(s32[1]{0:T(128)} %bitcast.12.pick_ref.side_ref, bf16[4,2,64,3584]{3,2,1,0:T(8,128)(2,1)} %all-to-all-done.6.x_ref), custom_call_target="tpu_custom_call" | custom-call | flops 1835008 | bytes 5505024 | tf_op jit(solution)/shard_map/pallas_call | solution.py:235
  278.0 7.7 %collective-permute-done.5 = bf16[64,3584]{1,0:T(8,128)(2,1)S(1)} collective-permute-done((bf16[64,3584]{1,0:T(8,128)(2,1)}, bf16[64,3584]{1,0:T(8,128)(2,1)S(1)}, u32[]{:S(2)}, u32[]{:S(2)}) %collective-permute-start.5) | collective-permute-done | bytes 458784 | tf_op jit(solution)/shard_map/ppermute | solution.py:309
  290.0 4.9 %collective-permute-done.6.got_ref = bf16[64,1792]{1,0:T(8,128)(2,1)S(1)} collective-permute-done((bf16[64,1792]{1,0:T(8,128)(2,1)}, bf16[64,1792]{1,0:T(8,128)(2,1)S(1)}, u32[]{:S(2)}, u32[]{:S(2)}) %collective-permute-start.6) | collective-permute-done | bytes 229408 | tf_op jit(solution)/shard_map/ppermute | solution.py:309
  298.0 4.5 %all-to-all-start.9 = ((bf16[4,2,64,1792]{3,2,1,0:T(8,128)(2,1)}), bf16[4,2,64,1792]{3,2,1,0:T(8,128)(2,1)}, u32[]{:S(2)}, u32[]{:S(2)}) async-start(bf16[4,2,64,1792]{3,2,1,0:T(8,128)(2,1)} %shard_map.127), calls=%async_computation.9 | async-start | bytes 3670016 | tf_op jit(solution)/shard_map/all_to_all | solution.py:305
  306.9 4.9 %collective-permute-done.7.got_ref = bf16[64,1792]{1,0:T(8,128)(2,1)S(1)} collective-permute-done((bf16[64,1792]{1,0:T(8,128)(2,1)}, bf16[64,1792]{1,0:T(8,128)(2,1)S(1)}, u32[]{:S(2)}, u32[]{:S(2)}) %collective-permute-start.7) | collective-permute-done | bytes 229408 | tf_op jit(solution)/shard_map/ppermute | solution.py:309
  315.0 8.4 %all-to-all-done.9 = bf16[4,2,64,1792]{3,2,1,0:T(8,128)(2,1)} async-done(((bf16[4,2,64,1792]{3,2,1,0:T(8,128)(2,1)}), bf16[4,2,64,1792]{3,2,1,0:T(8,128)(2,1)}, u32[]{:S(2)}, u32[]{:S(2)}) %all-to-all-start.9) | async-done | bytes 1835040 | tf_op jit(solution)/shard_map/all_to_all | solution.py:305
  323.4 3.6 all-to-all-start.8
  327.0 6.2 %shard_map.130 = bf16[8,1,64,1024]{3,2,1,0:T(8,128)(2,1)} custom-call(s32[1]{0:T(128)} %constant.67.clone.1.pick_ref, bf16[8,1,64,1792]{3,2,1,0:T(8,128)(2,1)} %bitcast.24.x_ref, bf16[1792,1024]{1,0:T(8,128)(2,1)} %refs_0_.13), custom_call_target="tpu_custom_call" | custom-call | flops 1879048192 | bytes 6553600 | tf_op jit(solution)/shard_map/pallas_call | solution.py:211
  333.2 13.5 %all-to-all-done.8 = bf16[4,2,64,1792]{3,2,1,0:T(8,128)(2,1)S(1)} async-done(((bf16[4,2,64,1792]{3,2,1,0:T(8,128)(2,1)}), bf16[4,2,64,1792]{3,2,1,0:T(8,128)(2,1)S(1)}, u32[]{:S(2)}, u32[]{:S(2)}) %all-to-all-start.8) | async-done | bytes 1835040 | tf_op jit(solution)/shard_map/all_to_all | solution.py:305
  348.3 6.4 %shard_map.131 = bf16[8,1,64,1024]{3,2,1,0:T(8,128)(2,1)} custom-call(s32[1]{0:T(128)} %constant.67.clone.1.pick_ref, bf16[8,1,64,1792]{3,2,1,0:T(8,128)(2,1)} %bitcast.37, bf16[1792,1024]{1,0:T(8,128)(2,1)} %refs_0_.13, bf16[8,1,64,1024]{3,2,1,0:T(8,128)(2,1)} %copy-done.10), custom_call_target="tpu_custom_call" | custom-call | flops 1879048192 | bytes 6553600 | tf_op jit(solution)/shard_map/pallas_call | solution.py:211
  354.7 16.6 %all_to_all.56 = bf16[8,64,1024]{2,1,0:T(8,128)(2,1)S(1)} all-to-all(bf16[8,64,1024]{2,1,0:T(8,128)(2,1)} %bitcast.39), channel_id=1, replica_groups=mesh['z'=4,'xh'=2,'core'=2,'y'=4,'xl'=2] {'z','xh'}, dimensions={0} | all-to-all | bytes 2097152 | tf_op jit(solution)/shard_map/all_to_all | solution.py:305
  (89 shorter events, 45.8 us)
Async XLA Ops:
  0.0 1.6 copy-start
  7.8 43.9 %all-to-all-start = ((bf16[64,144,128]{2,1,0:T(8,128)(2,1)}), bf16[64,144,128]{2,1,0:T(8,128)(2,1)}, u32[]{:S(2)}, u32[]{:S(2)}) async-start(bf16[64,144,128]{2,1,0:T(8,128)(2,1)} %pad_maximum_fusion), calls=%async_computation | async-start | bytes 4718592 | tf_op jit(solution)/shard_map/all_to_all | solution.py:305
  23.8 34.0 %copy-start.16 = (bf16[128,512]{1,0:T(8,128)(2,1)S(1)}, bf16[128,512]{1,0:T(8,128)(2,1)}, u32[]{:S(2)}) copy-start(bf16[128,512]{1,0:T(8,128)(2,1)} %own_q_ref.1) | copy-start | bytes 393220
  51.7 37.6 %all-to-all-start.1 = ((bf16[64,144,128]{2,1,0:T(8,128)(2,1)}), bf16[64,144,128]{2,1,0:T(8,128)(2,1)}, u32[]{:S(2)}, u32[]{:S(2)}) async-start(bf16[64,144,128]{2,1,0:T(8,128)(2,1)} %pad_maximum_fusion.1), calls=%async_computation.1 | async-start | bytes 4718592 | tf_op jit(solution)/shard_map/all_to_all | solution.py:305
  57.7 1.9 collective-permute-start
  59.7 29.7 %copy-start.17 = (bf16[128,512]{1,0:T(8,128)(2,1)}, bf16[128,512]{1,0:T(8,128)(2,1)S(1)}, u32[]{:S(2)}) copy-start(bf16[128,512]{1,0:T(8,128)(2,1)S(1)} %collective-permute-done.other_q_ref) | copy-start | bytes 393220
  105.3 1.8 collective-permute-start.1
  110.0 20.7 %all-to-all-start.2 = ((bf16[8,128,512]{2,1,0:T(8,128)(2,1)}), bf16[8,128,512]{2,1,0:T(8,128)(2,1)S(1)}, u32[]{:S(2)}, u32[]{:S(2)}) async-start(bf16[8,128,512]{2,1,0:T(8,128)(2,1)} %shard_map.119), calls=%async_computation.2 | async-start | bytes 2097152 | tf_op jit(solution)/shard_map/all_to_all | solution.py:305
  130.8 1.0 copy-start.4
  136.0 2.9 collective-permute-start.2
  138.9 1.0 copy-start.8
  144.2 4.9 %copy-start.15 = (bf16[1024]{0:T(1024)(128)(2,1)S(1)}, bf16[1024]{0:T(1024)(128)(2,1)}, u32[]{:S(2)}) copy-start(bf16[1024]{0:T(1024)(128)(2,1)} %param.20) | copy-start | bytes 6148
  144.2 22.6 %copy-start.11 = (bf16[64,1024]{1,0:T(8,128)(2,1)S(1)}, bf16[64,1024]{1,0:T(8,128)(2,1)}, u32[]{:S(2)}) copy-start(bf16[64,1024]{1,0:T(8,128)(2,1)} %param.19) | copy-start | bytes 393220
  144.2 22.4 %all-to-all-start.3 = ((bf16[8,64,1024]{2,1,0:T(8,128)(2,1)}), bf16[8,64,1024]{2,1,0:T(8,128)(2,1)S(1)}, u32[]{:S(2)}, u32[]{:S(2)}) async-start(bf16[8,64,1024]{2,1,0:T(8,128)(2,1)} %bitcast.38), calls=%async_computation.3 | async-start | bytes 2097152 | tf_op jit(solution)/shard_map/all_to_all | solution.py:305
  186.9 16.5 %copy-start.2 = (bf16[8,64,1024]{2,1,0:T(8,128)(2,1)}, bf16[8,64,1024]{2,1,0:T(8,128)(2,1)S(1)}, u32[]{:S(2)}) copy-start(bf16[8,64,1024]{2,1,0:T(8,128)(2,1)S(1)} %all_to_all.55) | copy-start | bytes 3145732
  186.9 2.7 collective-permute-start.4
  189.5 4.6 %copy-start.9 = (bf16[8,64,1024]{2,1,0:T(8,128)(2,1)}, bf16[8,64,1024]{2,1,0:T(8,128)(2,1)S(1)}, u32[]{:S(2)}) copy-start(bf16[8,64,1024]{2,1,0:T(8,128)(2,1)S(1)} %collective-permute-done.4) | copy-start | bytes 3145732
  190.9 12.5 %all-to-all-start.7 = ((f32[8,1,128]{2,1,0:T(1,128)}), f32[8,1,128]{2,1,0:T(1,128)S(1)}, u32[]{:S(2)}, u32[]{:S(2)}) async-start(f32[8,1,128]{2,1,0:T(1,128)} %reshape.125), calls=%async_computation.7 | async-start | bytes 8192 | tf_op jit(solution)/shard_map/all_to_all | solution.py:305
  203.4 62.4 %all-to-all-start.6 = ((bf16[4,2,64,3584]{3,2,1,0:T(8,128)(2,1)}), bf16[4,2,64,3584]{3,2,1,0:T(8,128)(2,1)}, u32[]{:S(2)}, u32[]{:S(2)}) async-start(bf16[4,2,64,3584]{3,2,1,0:T(8,128)(2,1)} %shard_map.124), calls=%async_computation.6 | async-start | bytes 7340032 | tf_op jit(solution)/shard_map/all_to_all | solution.py:305
  215.1 42.3 %collective-permute-start.3 = (bf16[4,1,64,3584]{3,2,1,0:T(8,128)(2,1)}, bf16[4,1,64,3584]{3,2,1,0:T(8,128)(2,1)S(1)}, u32[]{:S(2)}, u32[]{:S(2)}) collective-permute-start(bf16[4,1,64,3584]{3,2,1,0:T(8,128)(2,1)} %shard_map.122), channel_id=1, source_target_pairs={{0,1},{1,0},{2,3},{3,2},{4,5},{5,4},{6,7},{7,6},{8,9},{9,8},{10,11... | collective-permute-start | bytes 5505032 | tf_op jit(solution)/shard_map/ppermute | solution.py:309
  257.4 1.2 copy-start.6
  265.8 32.2 %all-to-all-start.5 = ((bf16[4,64,3584]{2,1,0:T(8,128)(2,1)}), bf16[4,64,3584]{2,1,0:T(8,128)(2,1)S(1)}, u32[]{:S(2)}, u32[]{:S(2)}) async-start(bf16[4,64,3584]{2,1,0:T(8,128)(2,1)} %bitcast.36), calls=%async_computation.5 | async-start | bytes 3670016 | tf_op jit(solution)/shard_map/all_to_all | solution.py:305
  274.3 11.3 %collective-permute-start.5 = (bf16[64,3584]{1,0:T(8,128)(2,1)}, bf16[64,3584]{1,0:T(8,128)(2,1)S(1)}, u32[]{:S(2)}, u32[]{:S(2)}) collective-permute-start(bf16[64,3584]{1,0:T(8,128)(2,1)} %get-tuple-element.14), channel_id=1, source_target_pairs={{0,1},{1,0},{2,3},{3,2},{4,5},{5,4},{6,7},{7,6},{8,9},{9,8},{10,11... | collective-permute-start | bytes 1376264 | tf_op jit(solution)/shard_map/ppermute | solution.py:309
  288.7 6.2 %collective-permute-start.6 = (bf16[64,1792]{1,0:T(8,128)(2,1)}, bf16[64,1792]{1,0:T(8,128)(2,1)S(1)}, u32[]{:S(2)}, u32[]{:S(2)}) collective-permute-start(bf16[64,1792]{1,0:T(8,128)(2,1)} %shard_map.126.mine_ref), channel_id=1, source_target_pairs={{0,1},{1,0},{2,3},{3,2},{4,5},{5,4},{6,7},{7,6},{8,9},{9,8},{10,11... | collective-permute-start | bytes 688136 | tf_op jit(solution)/shard_map/ppermute | solution.py:309
  298.0 5.2 %copy-start.3 = (bf16[4,64,3584]{2,1,0:T(8,128)(2,1)}, bf16[4,64,3584]{2,1,0:T(8,128)(2,1)S(1)}, u32[]{:S(2)}) copy-start(bf16[4,64,3584]{2,1,0:T(8,128)(2,1)S(1)} %all-to-all-done.5.refs_0_.refs_1_) | copy-start | bytes 5505028
  298.0 25.4 %all-to-all-start.9 = ((bf16[4,2,64,1792]{3,2,1,0:T(8,128)(2,1)}), bf16[4,2,64,1792]{3,2,1,0:T(8,128)(2,1)}, u32[]{:S(2)}, u32[]{:S(2)}) async-start(bf16[4,2,64,1792]{3,2,1,0:T(8,128)(2,1)} %shard_map.127), calls=%async_computation.9 | async-start | bytes 3670016 | tf_op jit(solution)/shard_map/all_to_all | solution.py:305
  305.6 6.2 %collective-permute-start.7 = (bf16[64,1792]{1,0:T(8,128)(2,1)}, bf16[64,1792]{1,0:T(8,128)(2,1)S(1)}, u32[]{:S(2)}, u32[]{:S(2)}) collective-permute-start(bf16[64,1792]{1,0:T(8,128)(2,1)} %shard_map.128.mine_ref), channel_id=1, source_target_pairs={{0,1},{1,0},{2,3},{3,2},{4,5},{5,4},{6,7},{7,6},{8,9},{9,8},{10,11... | collective-permute-start | bytes 688136 | tf_op jit(solution)/shard_map/ppermute | solution.py:309
  323.4 23.4 %all-to-all-start.8 = ((bf16[4,2,64,1792]{3,2,1,0:T(8,128)(2,1)}), bf16[4,2,64,1792]{3,2,1,0:T(8,128)(2,1)S(1)}, u32[]{:S(2)}, u32[]{:S(2)}) async-start(bf16[4,2,64,1792]{3,2,1,0:T(8,128)(2,1)} %shard_map.129), calls=%async_computation.8 | async-start | bytes 3670016 | tf_op jit(solution)/shard_map/all_to_all | solution.py:305
  333.2 13.5 %collective-permute-start.8 = (bf16[8,1,64,1024]{3,2,1,0:T(8,128)(2,1)}, bf16[8,1,64,1024]{3,2,1,0:T(8,128)(2,1)S(1)}, u32[]{:S(2)}, u32[]{:S(2)}) collective-permute-start(bf16[8,1,64,1024]{3,2,1,0:T(8,128)(2,1)} %shard_map.130), channel_id=1, source_target_pairs={{0,8},{8,0},{1,9},{9,1},{2,10},{10,2},{3,11},{11,3},{4,12},{12,4},... | collective-permute-start | bytes 3145736 | tf_op jit(solution)/shard_map/ppermute | solution.py:309
  346.7 1.2 copy-start.5
  346.7 1.6 copy-start.10
  354.7 17.5 %copy-start.1 = (bf16[8,1024,128]{2,1,0:T(8,128)(2,1)S(1)}, bf16[8,1024,128]{2,1,0:T(8,128)(2,1)}, u32[]{:S(2)}) copy-start(bf16[8,1024,128]{2,1,0:T(8,128)(2,1)} %param.13) | copy-start | bytes 6291460
  (4 other events, 2.9 us)

commit v3 on v1

--- a/solution.py
+++ b/solution.py
@@ -41,8 +41,6 @@
     other_q_ref,
     keys_ref,
     values_ref,
-    near_keys_ref,
-    near_values_ref,
     own_ref,
     send_ref,
     order_ref,
@@ -79,16 +77,16 @@
             scores = scores + bias
         old = top_ref[half]
         new = jnp.maximum(old, jnp.max(scores, axis=0, keepdims=True))
-        weights = jnp.exp(scores - new)
-        decay = jnp.exp(old - new)
+        weights = jnp.exp2(scores - new)
+        decay = jnp.exp2(old - new)
         top_ref[half] = new
         sum_ref[half] = sum_ref[half] * decay + jnp.sum(weights, axis=0, keepdims=True)
         acc_ref[half] = acc_ref[half] * decay + tn_dot(values, weights.astype(bf16))
 
     def far(step, carry):
         slots = [jnp.minimum(step * per_step + i, count - 1) for i in range(per_step)]
-        keys = jnp.concatenate([keys_ref[order_ref[s]] for s in slots], axis=0)
-        values = jnp.concatenate([values_ref[order_ref[s]] for s in slots], axis=0)
+        keys = jnp.concatenate([keys_ref[order_ref[s], 0:BLK] for s in slots], axis=0)
+        values = jnp.concatenate([values_ref[order_ref[s], 0:BLK] for s in slots], axis=0)
         bias = jnp.concatenate(
             [
                 jnp.full((BLK, 1), jnp.where(step * per_step + i < count, 0.0, NEG), f32)
@@ -108,8 +106,10 @@
         key_pos = lax.broadcasted_iota(jnp.int32, (BLK, rows), 0)
         token = lax.broadcasted_iota(jnp.int32, (BLK, rows), 1) % BLK
         bias = jnp.where(key_pos <= token + shift, 0.0, NEG)
+        keys = jnp.concatenate([keys_ref[i * 8 + which, BLK:] for i in range(8)], axis=0)
+        values = jnp.concatenate([values_ref[i * 8 + which, BLK:] for i in range(8)], axis=0)
         for half in range(2):
-            update(half, near_keys_ref[which], near_values_ref[which], bias)
+            update(half, keys, values, bias)
         return carry
 
     lax.fori_loop(0, (block - core + 2) // 2, near, 0)
@@ -121,16 +121,16 @@
     send_ref[HEAD_DIM + 1 : HEAD_DIM + 2, :] = sum_ref[1]
 
 
-def attend(my_list, place, own_q, other_q, keys, values, near_keys, near_values, local_blocks):
+def attend(my_list, place, own_q, other_q, keys, values, local_blocks):
     heads = own_q.shape[1] // HEAD_DIM
     rows = heads * BLK
     packed = jax.ShapeDtypeStruct((HEAD_DIM + 8, rows), f32)
     smem = pl.BlockSpec(memory_space=pltpu.SMEM)
     vmem = pl.BlockSpec(memory_space=pltpu.VMEM)
     return pl.pallas_call(
-        functools.partial(attend_kernel, 1.0 / math.sqrt(HEAD_DIM), 2, local_blocks),
+        functools.partial(attend_kernel, math.log2(math.e) / math.sqrt(HEAD_DIM), 4, local_blocks),
         out_shape=(packed, packed),
-        in_specs=[smem, smem] + [vmem] * 6,
+        in_specs=[smem, smem] + [vmem] * 4,
         out_specs=(vmem, vmem),
         scratch_shapes=[
             pltpu.SMEM((my_list.shape[0] + 1,), jnp.int32),
@@ -139,21 +139,21 @@
             pltpu.VMEM((2, 1, rows), f32),
             pltpu.VMEM((2, HEAD_DIM, rows), f32),
         ],
-        compiler_params=pltpu.CompilerParams(vmem_limit_bytes=48 * 1024 * 1024),
+        compiler_params=pltpu.CompilerParams(vmem_limit_bytes=20 * 1024 * 1024),
         cost_estimate=pl.CostEstimate(
             flops=4 * 2 * rows * 40 * BLK * HEAD_DIM,
             bytes_accessed=2 * keys.size * 2,
             transcendentals=2 * rows * 40 * BLK,
         ),
-    )(my_list, place, own_q, other_q, keys, values, near_keys, near_values)
+    )(my_list, place, own_q, other_q, keys, values)
 
 
 def merge_kernel(own_ref, got_ref, out_ref):
     own_top = own_ref[HEAD_DIM : HEAD_DIM + 1, :]
     got_top = got_ref[HEAD_DIM : HEAD_DIM + 1, :]
     top = jnp.maximum(own_top, got_top)
-    own_w = jnp.exp(own_top - top)
-    got_w = jnp.exp(got_top - top)
+    own_w = jnp.exp2(own_top - top)
+    got_w = jnp.exp2(got_top - top)
     total = own_w * own_ref[HEAD_DIM + 1 : HEAD_DIM + 2, :] + got_w * got_ref[HEAD_DIM + 1 : HEAD_DIM + 2, :]
     mixed = (own_ref[0:HEAD_DIM, :] * own_w + got_ref[0:HEAD_DIM, :] * got_w) / total
     heads = mixed.shape[1] // BLK
@@ -171,23 +171,254 @@
         out_shape=jax.ShapeDtypeStruct((copies, BLK, heads * HEAD_DIM), bf16),
         in_specs=[vmem, vmem],
         out_specs=vmem,
+        compiler_params=pltpu.CompilerParams(vmem_limit_bytes=12 * 1024 * 1024),
     )(own, got)
+
+
+def product_kernel(tile, weight_count, pick_ref, x_ref, *refs):
+    weight_refs, add_ref, out_ref = refs[:weight_count], refs[weight_count:-1], refs[-1]
+    x = x_ref[:, pick_ref[0]] if x_ref.shape[1] > out_ref.shape[1] else x_ref[...]
+    x = x.reshape(-1, x.shape[-1])
+    width = weight_refs[0].shape[1]
+    block = out_ref.shape[:-1] + (tile,)
+    for i, weight_ref in enumerate(weight_refs):
+        for first in range(0, width, tile):
+            total = jnp.dot(x, weight_ref[:, first : first + tile], preferred_element_type=f32)
+            columns = slice(i * width + first, i * width + first + tile)
+            if add_ref:
+                total = total + add_ref[0][..., columns].reshape(total.shape).astype(f32)
+            out_ref[..., columns] = total.astype(bf16).reshape(block)
+
+
+def product(x, weights, tile, pick=None, add=None):
+    blocks, pair, tokens, inputs = x.shape
+    taken = pair if pick is None else 1
+    pick = jnp.zeros((1,), jnp.int32) if pick is None else pick.astype(jnp.int32).reshape(1)
+    vmem = pl.BlockSpec(memory_space=pltpu.VMEM)
+    operands = [x, *weights] if add is None else [x, *weights, add]
+    rows = blocks * taken * tokens
+    columns = weights[0].shape[1] * len(weights)
+    return pl.pallas_call(
+        functools.partial(product_kernel, tile, len(weights)),
+        out_shape=jax.ShapeDtypeStruct((blocks, taken, tokens, columns), bf16),
+        in_specs=[pl.BlockSpec(memory_space=pltpu.SMEM)] + [vmem] * len(operands),
+        out_specs=vmem,
+        compiler_params=pltpu.CompilerParams(vmem_limit_bytes=20 * 1024 * 1024),
+        cost_estimate=pl.CostEstimate(
+            flops=2 * rows * inputs * columns,
+            bytes_accessed=2 * (rows * inputs + inputs * columns + rows * columns),
+            transcendentals=0,
+        ),
+    )(pick, *operands)
+
+
+VMEM = pl.BlockSpec(memory_space=pltpu.VMEM)
+SMEM = pl.BlockSpec(memory_space=pltpu.SMEM)
+
+
+def small_call(kernel, outs, scalars, arrays, moved):
+    return pl.pallas_call(
+        kernel,
+        out_shape=outs,
+        in_specs=[SMEM] * len(scalars) + [VMEM] * len(arrays),
+        out_specs=jax.tree.map(lambda _: VMEM, outs),
+        compiler_params=pltpu.CompilerParams(vmem_limit_bytes=16 * 1024 * 1024),
+        cost_estimate=pl.CostEstimate(flops=moved, bytes_accessed=moved, transcendentals=0),
+    )(*scalars, *arrays)
+
+
+def spread_kernel(place_ref, mine_ref, theirs_ref, gate_ref, up_ref, *out_refs):
+    y, side = place_ref[0], place_ref[1]
+    give_ref, keep_ref, self_ref, right_ref, left_ref, opposite_ref, far_ref = out_refs
+    order = [(y + i) % 4 for i in range(4)]
+    sides = (side, 1 - side)
+    n = mine_ref.shape[2]
+    x = jnp.concatenate(
+        [mine_ref[i, 1 - side] for i in order]
+        + [theirs_ref[i, s] for i in order for s in sides]
+        + [mine_ref[i, side] for i in order],
+        axis=0,
+    )
+    step = pl.program_id(0)
+
+    def put(weight_ref):
+        total = jnp.dot(x, weight_ref[...], preferred_element_type=f32).astype(bf16)
+        for i in range(4):
+            give_ref[i] = total[i * n : (i + 1) * n]
+            keep_ref[i] = total[(12 + i) * n : (13 + i) * n]
+        for first, ref in ((4, self_ref), (6, right_ref), (10, left_ref)):
+            for j in range(2):
+                ref[j] = total[(first + j) * n : (first + j + 1) * n]
+        opposite_ref[...] = total[8 * n : 9 * n]
+        far_ref[...] = total[9 * n : 10 * n]
+
+    half = pl.num_programs(0) // 2
+    pl.when(step < half)(functools.partial(put, gate_ref))
+    pl.when(step >= half)(functools.partial(put, up_ref))
+
+
+def partial_columns(place, mine, theirs, gate, up):
+    tile = 896
+    inputs, width = gate.shape
+    count = width // tile
+    tokens = mine.shape[2]
+    whole = pl.BlockSpec(mine.shape, lambda n, p: (0, 0, 0, 0))
+
+    def out(*lead):
+        block = pl.BlockSpec((*lead, tokens, tile), lambda n, p: (0,) * (len(lead) + 1) + (n,))
+        return jax.ShapeDtypeStruct((*lead, tokens, 2 * width), bf16), block
+
+    shapes, blocks = zip(*[out(4), out(4), out(2), out(2), out(2), out(), out()])
+    rows = 16 * tokens
+    return pl.pallas_call(
+        spread_kernel,
+        out_shape=shapes,
+        grid_spec=pltpu.PrefetchScalarGridSpec(
+            num_scalar_prefetch=1,
+            grid=(2 * count,),
+            in_specs=[
+                whole,
+                whole,
+                pl.BlockSpec((inputs, tile), lambda n, p: (0, jnp.minimum(n, count - 1))),
+                pl.BlockSpec((inputs, tile), lambda n, p: (0, jnp.maximum(n - count, 0))),
+            ],
+            out_specs=blocks,
+        ),
+        compiler_params=pltpu.CompilerParams(vmem_limit_bytes=40 * 1024 * 1024),
+        cost_estimate=pl.CostEstimate(
+            flops=4 * rows * inputs * width,
+            bytes_accessed=2 * (rows * inputs + 2 * inputs * width + 2 * rows * width),
+            transcendentals=0,
+        ),
+    )(place, mine, theirs, gate, up)
+
+
+def arranged_sum(got, keep):
+    tokens, width = keep.shape[1] // 2, keep.shape[2]
+
+    def kernel(got_ref, keep_ref, self_ref, right_ref, left_ref, opposite_ref, far_ref):
+        def block(i, j):
+            rows = pl.ds(j * tokens, tokens)
+            return (got_ref[i, rows].astype(f32) + keep_ref[i, rows].astype(f32)).astype(bf16)
+
+        for i, ref in ((0, self_ref), (1, right_ref), (3, left_ref)):
+            for j in range(2):
+                ref[j] = block(i, j)
+        opposite_ref[...] = block(2, 0)
+        far_ref[...] = block(2, 1)
+
+    two = jax.ShapeDtypeStruct((2, tokens, width), bf16)
+    one = jax.ShapeDtypeStruct((tokens, width), bf16)
+    return small_call(kernel, (two, two, two, one, one), (), (got, keep), 4 * keep.size)
+
+
+def add_pieces(*pieces):
+    def kernel(*refs):
+        refs[-1][...] = sum(r[...].astype(f32) for r in refs[:-1]).astype(bf16)
+
+    first = pieces[0]
+    return small_call(kernel, jax.ShapeDtypeStruct(first.shape, bf16), (), pieces, 2 * first.size)
+
+
+def gated(groups, factor):
+    counts = [len(g) for g in groups]
+    tokens, width = groups[0][0].shape[0], groups[0][0].shape[1] // 2
+
+    def kernel(*refs):
+        factor_ref, out_ref = refs[-2], refs[-1]
+        at = 0
+        for i, count in enumerate(counts):
+            rows = pl.ds(i * tokens, tokens)
+            mine = refs[at : at + count]
+            at += count
+            scale = factor_ref[rows, :]
+            gate = sum(r[:, 0:width].astype(f32) for r in mine) * scale
+            up = sum(r[:, width:].astype(f32) for r in mine) * scale
+            out_ref[rows, :] = (gate / (1.0 + jnp.exp(-gate)) * up).astype(bf16)
+
+    out = jax.ShapeDtypeStruct((tokens * len(groups), width), bf16)
+    arrays = [p for g in groups for p in g] + [factor[:, None]]
+    return small_call(kernel, out, (), arrays, 8 * tokens * width * len(groups))
+
+
+def down_kernel(tile, place_ref, *refs):
+    y, side = place_ref[0], place_ref[1]
+    pieces, weight_ref, add_ref, out_ref = refs[:8], refs[8], refs[9:-1], refs[-1]
+    n = pieces[0].shape[0]
+    x = jnp.concatenate([p[...] for p in pieces], axis=0)
+    total = jnp.dot(x, weight_ref[...], preferred_element_type=f32)
+    for i in range(4):
+        for j in range(2):
+            at = 2 * ((y + i) % 4) + (side if j == 0 else 1 - side)
+            part = total[(2 * i + j) * n : (2 * i + j + 1) * n]
+            if add_ref:
+                part = part + add_ref[0][at].astype(f32)
+            out_ref[at] = part.astype(bf16)
+
+
+def down_product(place, pieces, weight, add=None):
+    tile = 256
+    tokens, inputs = pieces[0].shape
+    width = weight.shape[1]
+    piece = pl.BlockSpec((tokens, inputs), lambda n, p: (0, 0))
+    by_column = pl.BlockSpec((8, tokens, tile), lambda n, p: (0, 0, n))
+    operands = [*pieces, weight] + ([] if add is None else [add])
+    specs = [piece] * 8 + [pl.BlockSpec((inputs, tile), lambda n, p: (0, n))]
+    specs += [] if add is None else [by_column]
+    return pl.pallas_call(
+        functools.partial(down_kernel, tile),
+        out_shape=jax.ShapeDtypeStruct((8, tokens, width), bf16),
+        grid_spec=pltpu.PrefetchScalarGridSpec(
+            num_scalar_prefetch=1, grid=(width // tile,), in_specs=specs, out_specs=by_column
+        ),
+        compiler_params=pltpu.CompilerParams(vmem_limit_bytes=20 * 1024 * 1024),
+        cost_estimate=pl.CostEstimate(
+            flops=16 * tokens * inputs * width,
+            bytes_accessed=2 * (8 * tokens * inputs + inputs * width + 8 * tokens * width),
+            transcendentals=0,
+        ),
+    )(place, *operands)
+
+
+def to_right(x):
+    return lax.ppermute(x, "y", [(i, (i + 1) % 4) for i in range(4)])
+
+
+def to_left(x):
+    return lax.ppermute(x, "y", [(i, (i + 3) % 4) for i in range(4)])
+
+
+def ring_sum(own, right, left, opposite, far):
+    from_left = to_right(opposite)
+    from_right = to_left(far)
+    second_left = to_right(right[1])
+    second_right = to_left(left[0])
+    third_left = to_right(add_pieces(right[0], from_left))
+    third_right = to_left(add_pieces(left[1], from_right))
+    return (own[0], second_right, third_left), (own[1], second_left, third_right)
+
+
+def ring_gather(mine, got):
+    mine_left, mine_right = to_right(mine), to_left(mine)
+    got_left, got_right = to_right(got), to_left(got)
+    mine_far, got_far = to_right(mine_left), to_left(got_right)
+    return mine, got, mine_right, got_right, mine_far, got_far, mine_left, got_left
 
 
 def exchange(x, axes):
     return lax.all_to_all(x, axes, split_axis=0, concat_axis=0, tiled=True)
 
 
-def swap(x):
-    return lax.ppermute(x, "core", [(0, 1), (1, 0)])
+def swap(x, axis="core"):
+    return lax.ppermute(x, axis, [(0, 1), (1, 0)])
 
 
 def spread(x, copies):
     return jnp.broadcast_to(x[None], (copies,) + x.shape)
 
 
-def mm(a, b):
-    return jnp.dot(a, b, preferred_element_type=f32)
+def take(x, index, axis):
+    return lax.dynamic_index_in_dim(x, index, axis, keepdims=False)
 
 
 def local(
@@ -205,42 +436,38 @@
     down_weight,
 ):
     core = lax.axis_index("core")
+    side = lax.axis_index("xl")
     col = lax.axis_index(COL)
-    row = lax.axis_index(ROW)
     group = lax.axis_index(ZXH)
-    me = row * 8 + col
+    me = lax.axis_index(ROW) * 8 + col
     local_blocks = cache_keys.shape[1] // BLK
     tokens_here = residual.shape[0]
 
     matched = block_lists // local_blocks == me
     within = jnp.sum(jnp.where(matched, block_lists % local_blocks, 0), axis=2)
     source = (jnp.arange(KV_HEADS, dtype=jnp.int32)[:, None] * local_blocks + within.T).reshape(-1)
-    flat_keys = cache_keys.reshape(KV_HEADS * local_blocks, BLK, HEAD_DIM)
-    flat_values = cache_values.reshape(KV_HEADS * local_blocks, BLK, HEAD_DIM)
-    keys = exchange(flat_keys[source], CHIP)
-    values = exchange(flat_values[source], CHIP)
-    near_keys = exchange(spread(lax.dynamic_index_in_dim(stretch_keys, group, 0, keepdims=False), 8), COL)
-    near_values = exchange(spread(lax.dynamic_index_in_dim(stretch_values, group, 0, keepdims=False), 8), COL)
+
+    def fetch(cache, stretch):
+        flat = cache.reshape(KV_HEADS * local_blocks, BLK, HEAD_DIM)
+        part = BLK // 8
+        near = lax.dynamic_slice_in_dim(stretch, group * part, part, 1)
+        near = jnp.broadcast_to(near[:, None], (KV_HEADS, 8, part, HEAD_DIM)).reshape(64, part, HEAD_DIM)
+        return exchange(jnp.concatenate([flat[source], near], axis=1), CHIP)
+
+    keys = fetch(cache_keys, stretch_keys)
+    values = fetch(cache_values, stretch_values)
     my_list = block_lists[col, group]
     place = jnp.stack([core, col]).astype(jnp.int32)
-    own, send = attend(
-        my_list, place, queries, swap(queries), keys, values,
-        near_keys.reshape(8, BLK, HEAD_DIM), near_values.reshape(8, BLK, HEAD_DIM), local_blocks,
-    )
-    attended = exchange(merge(own, swap(send), 8), COL)
-
-    def halves(x):
-        x = x.reshape(8, 2, tokens_here, x.shape[-1])
-        mine = lax.dynamic_index_in_dim(x, core, 1, keepdims=False)
-        theirs = lax.dynamic_index_in_dim(x, 1 - core, 1, keepdims=False)
-        return mine, theirs
-
-    def row_sum(mine, theirs, weight):
-        give = mm(theirs, weight).astype(bf16)
-        both = mm(mine, weight) + swap(give).astype(f32)
-        return jnp.sum(exchange(both.astype(bf16), ZXH).astype(f32), axis=0)
-
-    stream = residual.astype(f32) + row_sum(*halves(attended), out_weight)
+    other_queries = swap(queries)
+    own, send = attend(my_list, place, queries, other_queries, keys, values, local_blocks)
+    attended = exchange(merge(own, swap(send), 8), COL).reshape(8, 2, tokens_here, -1)
+
+    def row_sum(give, mine, pick, weight):
+        both = product(mine, (weight,), 512, pick, add=swap(give))
+        return jnp.sum(exchange(both.reshape(8, tokens_here, -1), ZXH).astype(f32), axis=0)
+
+    give = product(attended, (out_weight,), 512, 1 - core)
+    stream = residual.astype(f32) + row_sum(give, attended, core, out_weight)
     gain = norm_gain.astype(f32)[None, :]
     scaled = (stream * gain).astype(bf16)
     own_rows = exchange(spread(scaled, 8), ZXH)
@@ -254,16 +481,24 @@
     totals = jnp.sum(exchange(parts, COL), axis=0)
     factor = lax.rsqrt(totals.reshape(2, tokens_here) / D + 1e-05)
 
-    def hidden_of(x, factor):
-        gate = jnp.sum(exchange(mm(x, gate_weight).astype(bf16), COL).astype(f32), axis=0)
-        up = jnp.sum(exchange(mm(x, up_weight).astype(bf16), COL).astype(f32), axis=0)
-        gate = gate * factor[:, None]
-        hidden = (jax.nn.silu(gate) * (up * factor[:, None])).astype(bf16)
-        return exchange(spread(hidden, 8), COL)
-
-    own_hidden = hidden_of(own_rows, factor[0])
-    other_hidden = hidden_of(other_rows, factor[1])
-    return (stream + row_sum(own_hidden, other_hidden, down_weight)).astype(bf16)
+    by_pair = (4, 2, tokens_here, own_rows.shape[-1])
+    where = jnp.stack([lax.axis_index("y"), side]).astype(jnp.int32)
+    give, keep, *pieces = partial_columns(
+        where, own_rows.reshape(by_pair), other_rows.reshape(by_pair), gate_weight, up_weight
+    )
+    got = swap(give, "xl")
+    here, there = ring_sum(*pieces)
+    other_give = add_pieces(*there)
+    got, other_give = lax.optimization_barrier((got, other_give))
+    own_here, own_there = ring_sum(*arranged_sum(got, keep))
+    other_hidden = gated([(*here, swap(other_give, "xl"))], factor[1])
+    other_all = ring_gather(other_hidden, swap(other_hidden, "xl"))
+    own_hidden = gated([own_here, own_there], factor[0])
+    own_all = ring_gather(own_hidden, swap(own_hidden, "xl"))
+    given = down_product(where, other_all, down_weight)
+    down = down_product(where, own_all, down_weight, add=swap(given))
+    mlp = jnp.sum(exchange(down, ZXH).astype(f32), axis=0)
+    return (stream + mlp).astype(bf16)
 
 
 def solution(mesh):

time: 396 us -> 332 us (0.84)
  waiting for transfers between devices: 206 us -> 157 us
  matrix products: 38.6 us -> 0 us
  Pallas kernels: 18.5 us -> 41.1 us
  blocking collectives: 36.6 us -> 49.7 us
  starting transfers between devices: 65.8 us -> 60 us
    all_to_all x13 -> x4, waiting for transfers between devices: 198 us -> 89 us  [exchange(): return lax.all_to_all(x, axes, split_axis=0, concat_axis=0, tiled=True)]
    ppermute x5 -> x33, waiting for transfers between devices: 7.77 us -> 67.6 us  [the longest x12 23.9 us: to_left(): return lax.ppermute(x, 'y', [(i, (i + 3) % 4) for i in range(4)])]
    dot_general x8 -> x0, matrix products: 38.6 us -> none  [mm(): return jnp.dot(a, b, preferred_element_type=f32)]
    all_to_all x13 -> x4, starting transfers between devices: 65.7 us -> 27.4 us  [exchange(): return lax.all_to_all(x, axes, split_axis=0, concat_axis=0, tiled=True)]
    ppermute x5 -> x33, starting transfers between devices: 0.1 us -> 32.7 us  [the longest x12 20.7 us: to_left(): return lax.ppermute(x, 'y', [(i, (i + 3) % 4) for i in range(4)])]
    pallas_call x1 -> x14, Pallas kernels: 16.2 us -> 39.9 us  [the longest x1 13.2 us: attend(): pl.pallas_call(functools.partial(attend_kernel, math.log2(math.e) / math....]
    all_to_all x2 -> x3, blocking collectives: 36.6 us -> 49.7 us  [exchange(): return lax.all_to_all(x, axes, split_axis=0, concat_axis=0, tiled=True)]
    reduce_sum x6 -> x2, other arithmetic: 7.57 us -> 0.34 us  [the longest x1 0.17 us: row_sum(): jnp.sum(exchange(both.reshape(8, tokens_here, -1), ZXH).astype(f32), axis=0)]
  transfers between devices with their start and end apart: 18 -> 37, of which waited for: 17 -> 22; matrix products, arithmetic and copies ran while one was open for 11% -> 3% of each run, Pallas kernels for 0% -> 2%
where the time goes in v3:
time: 332 us; the launch traced here: 331 us
  waiting for transfers between devices  157 us (47%)
  starting transfers between devices  60 us (18%)
  blocking collectives  49.7 us (15%)
  Pallas kernels  41.1 us (12%)
  local copies, waits for them, and re-layouts  12.7 us (4%)
  other arithmetic  10.1 us (3%)
    all_to_all x4, waiting for transfers between devices, exchange(): return lax.all_to_all(x, axes, split_axis=0, concat_axis=0, tiled=True)  89 us
    all_to_all x3, blocking collectives, exchange(): return lax.all_to_all(x, axes, split_axis=0, concat_axis=0, tiled=True)  49.7 us
    all_to_all x4, starting transfers between devices, exchange(): return lax.all_to_all(x, axes, split_axis=0, concat_axis=0, tiled=True)  27.4 us
    ppermute x12, waiting for transfers between devices, to_left(): return lax.ppermute(x, 'y', [(i, (i + 3) % 4) for i in range(4)])  23.9 us
    ppermute x9, waiting for transfers between devices, swap(): return lax.ppermute(x, axis, [(0, 1), (1, 0)])  23.7 us
    ppermute x12, starting transfers between devices, to_left(): return lax.ppermute(x, 'y', [(i, (i + 3) % 4) for i in range(4)])  20.7 us
    ppermute x12, waiting for transfers between devices, to_right(): return lax.ppermute(x, 'y', [(i, (i + 1) % 4) for i in range(4)])  20 us
    pallas_call x1, Pallas kernels, attend(): pl.pallas_call(functools.partial(attend_kernel, math.log2(math.e) / math....  13.2 us
  transfers between devices with their start and end apart: 37, of which 22 were waited for; matrix products, arithmetic and copies ran while one was open for 3% of the time, Pallas kernels for 2%

profile of v3, /device:TPU:0, one launch (start us, length us, event | category | flops | bytes accessed | tf_op | source)
XLA Modules:
  0.0 330.7 jit_solution(6379632327578584405)
XLA Ops:
  4.6 3.2 pad_maximum_fusion.1
  7.8 11.5 %all-to-all-start.1 = ((bf16[64,144,128]{2,1,0:T(8,128)(2,1)}), bf16[64,144,128]{2,1,0:T(8,128)(2,1)S(1)}, u32[]{:S(2)}, u32[]{:S(2)}) async-start(bf16[64,144,128]{2,1,0:T(8,128)(2,1)} %pad_maximum_fusion.1), calls=%async_computation.1 | async-start | bytes 4718592 | tf_op jit(solution)/shard_map/all_to_all | solution.py:409
  19.3 3.8 %gather_fusion = bf16[64,128,128]{2,1,0:T(8,128)(2,1)} fusion(bf16[64,128,128]{2,1,0:T(8,128)(2,1)} %bitcast.54, s32[1024]{0:T(1024)S(1)} %pad_clamp_fusion), kind=kCustom, calls=%fused_computation | custom fusion | bytes 4194560 | tf_op jit(solution)/shard_map/gather | solution.py:455
  23.1 3.2 pad_maximum_fusion
  26.3 25.3 %all-to-all-done.1.values_ref = bf16[64,144,128]{2,1,0:T(8,128)(2,1)S(1)} async-done(((bf16[64,144,128]{2,1,0:T(8,128)(2,1)}), bf16[64,144,128]{2,1,0:T(8,128)(2,1)S(1)}, u32[]{:S(2)}, u32[]{:S(2)}) %all-to-all-start.1) | async-done | bytes 2359328 | tf_op jit(solution)/shard_map/all_to_all | solution.py:409
  51.6 6.0 %all-to-all-start = ((bf16[64,144,128]{2,1,0:T(8,128)(2,1)}), bf16[64,144,128]{2,1,0:T(8,128)(2,1)}, u32[]{:S(2)}, u32[]{:S(2)}) async-start(bf16[64,144,128]{2,1,0:T(8,128)(2,1)} %pad_maximum_fusion), calls=%async_computation | async-start | bytes 4718592 | tf_op jit(solution)/shard_map/all_to_all | solution.py:409
  59.1 30.2 %all-to-all-done.keys_ref = bf16[64,144,128]{2,1,0:T(8,128)(2,1)} async-done(((bf16[64,144,128]{2,1,0:T(8,128)(2,1)}), bf16[64,144,128]{2,1,0:T(8,128)(2,1)}, u32[]{:S(2)}, u32[]{:S(2)}) %all-to-all-start) | async-done | bytes 2359328 | tf_op jit(solution)/shard_map/all_to_all | solution.py:409
  89.2 13.2 %shard_map.118 = (f32[136,512]{1,0:T(8,128)S(1)}, f32[136,512]{1,0:T(8,128)S(1)}) custom-call(s32[64]{0:T(128)S(1)} %fusion.5.list_ref, s32[2]{0:T(128)S(1)} %pad_add_fusion.place_ref, bf16[128,512]{1,0:T(8,128)(2,1)S(1)} %copy-done.7, bf16[128,512]{1,0:T(8,128)(2,1)S(1)} %collective-permute-done.other_q_ref, bf16[64,144,128]{2,1,0:T(8,128)(2,1)} %all-to-all-done.keys_ref, ...), custom_call_target="tpu_custom_call" | custom-call | flops 2684354560 | bytes 4718592 | tf_op jit(solution)/shard_map/pallas_call | solution.py:130
  105.3 5.8 %all-to-all-start.2 = ((bf16[8,128,512]{2,1,0:T(8,128)(2,1)}), bf16[8,128,512]{2,1,0:T(8,128)(2,1)S(1)}, u32[]{:S(2)}, u32[]{:S(2)}) async-start(bf16[8,128,512]{2,1,0:T(8,128)(2,1)} %shard_map.119), calls=%async_computation.2 | async-start | bytes 2097152 | tf_op jit(solution)/shard_map/all_to_all | solution.py:409
  111.1 16.0 %all-to-all-done.2 = bf16[8,128,512]{2,1,0:T(8,128)(2,1)S(1)} async-done(((bf16[8,128,512]{2,1,0:T(8,128)(2,1)}), bf16[8,128,512]{2,1,0:T(8,128)(2,1)S(1)}, u32[]{:S(2)}, u32[]{:S(2)}) %all-to-all-start.2) | async-done | bytes 1048608 | tf_op jit(solution)/shard_map/all_to_all | solution.py:409
  127.9 2.6 collective-permute-done.2.refs_1_
  132.3 4.0 %all-to-all-start.3 = ((bf16[8,64,1024]{2,1,0:T(8,128)(2,1)}), bf16[8,64,1024]{2,1,0:T(8,128)(2,1)S(1)}, u32[]{:S(2)}, u32[]{:S(2)}) async-start(bf16[8,64,1024]{2,1,0:T(8,128)(2,1)} %bitcast.11), calls=%async_computation.3 | async-start | bytes 2097152 | tf_op jit(solution)/shard_map/all_to_all | solution.py:409
  136.4 17.5 %all-to-all-done.3 = bf16[8,64,1024]{2,1,0:T(8,128)(2,1)S(1)} async-done(((bf16[8,64,1024]{2,1,0:T(8,128)(2,1)}), bf16[8,64,1024]{2,1,0:T(8,128)(2,1)S(1)}, u32[]{:S(2)}, u32[]{:S(2)}) %all-to-all-start.3) | async-done | bytes 1048608 | tf_op jit(solution)/shard_map/all_to_all | solution.py:409
  154.2 20.1 %all_to_all.35 = bf16[8,64,1024]{2,1,0:T(8,128)(2,1)S(1)} all-to-all(bf16[8,64,1024]{2,1,0:T(8,128)(2,1)S(1)} %broadcast_in_dim.10), channel_id=1, replica_groups=mesh['z'=4,'xh'=2,'core'=2,'y'=4,'xl'=2] {'z','xh'}, dimensions={0} | all-to-all | bytes 2097152 | tf_op jit(solution)/shard_map/all_to_all | solution.py:409
  177.1 12.9 %shard_map.122 = (bf16[4,64,3584]{2,1,0:T(8,128)(2,1)S(1)}, bf16[4,64,3584]{2,1,0:T(8,128)(2,1)S(1)}, bf16[2,64,3584]{2,1,0:T(8,128)(2,1)S(1)}, bf16[2,64,3584]{...) custom-call(s32[2]{0:T(128)S(1)} %pad_add_fusion.1.place_ref, ...), custom_call_target="tpu_custom_call" | custom-call | flops 7516192768 | bytes 16777216 | tf_op jit(solution)/shard_map/pallas_call | solution.py:273
  194.6 2.7 collective-permute-start.21
  197.3 6.1 %collective-permute-done.6.refs_1_ = bf16[64,3584]{1,0:T(8,128)(2,1)S(1)} collective-permute-done((bf16[64,3584]{1,0:T(8,128)(2,1)S(1)}, bf16[64,3584]{1,0:T(8,128)(2,1)S(1)}, u32[]{:S(2)}, u32[]{:S(2)}) %collective-permute-start.6) | collective-permute-done | bytes 458784 | tf_op jit(solution)/shard_map/ppermute | solution.py:388
  207.1 8.2 %collective-permute-done.5.refs_1_ = bf16[64,3584]{1,0:T(8,128)(2,1)S(1)} collective-permute-done((bf16[64,3584]{1,0:T(8,128)(2,1)S(1)}, bf16[64,3584]{1,0:T(8,128)(2,1)S(1)}, u32[]{:S(2)}, u32[]{:S(2)}) %collective-permute-start.5) | collective-permute-done | bytes 458784 | tf_op jit(solution)/shard_map/ppermute | solution.py:384
  215.2 6.9 %collective-permute-done.7.refs_2_ = bf16[64,3584]{1,0:T(8,128)(2,1)S(1)} collective-permute-done((bf16[64,3584]{1,0:T(8,128)(2,1)S(1)}, bf16[64,3584]{1,0:T(8,128)(2,1)S(1)}, u32[]{:S(2)}, u32[]{:S(2)}) %collective-permute-start.7) | collective-permute-done | bytes 458784 | tf_op jit(solution)/shard_map/ppermute | solution.py:388
  222.4 11.3 %collective-permute-done.4.got_ref = bf16[4,64,3584]{2,1,0:T(8,128)(2,1)S(1)} collective-permute-done((bf16[4,64,3584]{2,1,0:T(8,128)(2,1)S(1)}, bf16[4,64,3584]{2,1,0:T(8,128)(2,1)S(1)}, u32[]{:S(2)}, u32[]{:S(2)}) %collective-permute-start.4) | collective-permute-done | bytes 1835040 | tf_op jit(solution)/shard_map/ppermute | solution.py:413
  235.8 11.7 %all_to_all.36 = f32[8,1,128]{2,1,0:T(1,128)S(1)} all-to-all(f32[8,1,128]{2,1,0:T(1,128)S(1)} %reshape.98), channel_id=1, replica_groups=mesh['z'=4,'xh'=2,'core'=2,'y'=4,'xl'=2] {'y','xl'}, dimensions={0} | all-to-all | bytes 8192 | tf_op jit(solution)/shard_map/all_to_all | solution.py:409
  257.1 3.2 collective-permute-start.27
  260.4 2.8 collective-permute-done.12.refs_1_
  263.8 4.7 %collective-permute-done.28.refs_6_ = bf16[64,1792]{1,0:T(8,128)(2,1)S(1)} collective-permute-done((bf16[64,1792]{1,0:T(8,128)(2,1)S(1)}, bf16[64,1792]{1,0:T(8,128)(2,1)S(1)}, u32[]{:S(2)}, u32[]{:S(2)}) %collective-permute-start.28) | collective-permute-done | bytes 229408 | tf_op jit(solution)/shard_map/ppermute | solution.py:384
  268.4 3.3 collective-permute-start.30
  274.0 4.2 %collective-permute-done.29.refs_4_ = bf16[64,1792]{1,0:T(8,128)(2,1)S(1)} collective-permute-done((bf16[64,1792]{1,0:T(8,128)(2,1)S(1)}, bf16[64,1792]{1,0:T(8,128)(2,1)S(1)}, u32[]{:S(2)}, u32[]{:S(2)}) %collective-permute-start.29) | collective-permute-done | bytes 229408 | tf_op jit(solution)/shard_map/ppermute | solution.py:384
  280.3 3.8 %shard_map.131 = bf16[8,64,1024]{2,1,0:T(8,128)(2,1)S(1)} custom-call(s32[2]{0:T(128)S(1)} %pad_add_fusion.1.place_ref, bf16[64,1792]{1,0:T(8,128)(2,1)S(1)} %shard_map.130.refs_0_, bf16[64,1792]{1,0:T(8,128)(2,1)S(1)} %collective-permute-done.25.refs_1_, bf16[64,1792]{1,0:T(8,128)(2,1)S(1)} %collective-permute-done.26.refs_2_, ...), custom_call_target="tpu_custom_call" | custom-call | flops 1879048192 | bytes 6553600 | tf_op jit(solution)/shard_map/pallas_call | solution.py:368
  287.7 5.1 %collective-permute-done.14.refs_1_ = bf16[64,1792]{1,0:T(8,128)(2,1)S(1)} collective-permute-done((bf16[64,1792]{1,0:T(8,128)(2,1)S(1)}, bf16[64,1792]{1,0:T(8,128)(2,1)S(1)}, u32[]{:S(2)}, u32[]{:S(2)}) %collective-permute-start.14) | collective-permute-done | bytes 229408 | tf_op jit(solution)/shard_map/ppermute | solution.py:413
  296.8 4.4 %collective-permute-done.16.refs_3_ = bf16[64,1792]{1,0:T(8,128)(2,1)S(1)} collective-permute-done((bf16[64,1792]{1,0:T(8,128)(2,1)S(1)}, bf16[64,1792]{1,0:T(8,128)(2,1)S(1)}, u32[]{:S(2)}, u32[]{:S(2)}) %collective-permute-start.16) | collective-permute-done | bytes 229408 | tf_op jit(solution)/shard_map/ppermute | solution.py:388
  301.2 3.2 collective-permute-start.19
  308.0 3.9 %shard_map.132 = bf16[8,64,1024]{2,1,0:T(8,128)(2,1)S(1)} custom-call(s32[2]{0:T(128)S(1)} %pad_add_fusion.1.place_ref, bf16[64,1792]{1,0:T(8,128)(2,1)S(1)} %shard_map.128.refs_0_, bf16[64,1792]{1,0:T(8,128)(2,1)S(1)} %collective-permute-done.14.refs_1_, bf16[64,1792]{1,0:T(8,128)(2,1)S(1)} %collective-permute-done.15.refs_2_, ...), custom_call_target="tpu_custom_call" | custom-call | flops 1879048192 | bytes 6553600 | tf_op jit(solution)/shard_map/pallas_call | solution.py:368
  311.9 17.9 %all_to_all.37 = bf16[8,64,1024]{2,1,0:T(8,128)(2,1)S(1)} all-to-all(bf16[8,64,1024]{2,1,0:T(8,128)(2,1)S(1)} %shard_map.132), channel_id=1, replica_groups=mesh['z'=4,'xh'=2,'core'=2,'y'=4,'xl'=2] {'z','xh'}, dimensions={0} | all-to-all | bytes 2097152 | tf_op jit(solution)/shard_map/all_to_all | solution.py:409
  (122 shorter events, 51.7 us)
Async XLA Ops:
  7.8 43.8 %all-to-all-start.1 = ((bf16[64,144,128]{2,1,0:T(8,128)(2,1)}), bf16[64,144,128]{2,1,0:T(8,128)(2,1)S(1)}, u32[]{:S(2)}, u32[]{:S(2)}) async-start(bf16[64,144,128]{2,1,0:T(8,128)(2,1)} %pad_maximum_fusion.1), calls=%async_computation.1 | async-start | bytes 4718592 | tf_op jit(solution)/shard_map/all_to_all | solution.py:409
  51.6 37.6 %all-to-all-start = ((bf16[64,144,128]{2,1,0:T(8,128)(2,1)}), bf16[64,144,128]{2,1,0:T(8,128)(2,1)}, u32[]{:S(2)}, u32[]{:S(2)}) async-start(bf16[64,144,128]{2,1,0:T(8,128)(2,1)} %pad_maximum_fusion), calls=%async_computation | async-start | bytes 4718592 | tf_op jit(solution)/shard_map/all_to_all | solution.py:409
  105.3 21.8 %all-to-all-start.2 = ((bf16[8,128,512]{2,1,0:T(8,128)(2,1)}), bf16[8,128,512]{2,1,0:T(8,128)(2,1)S(1)}, u32[]{:S(2)}, u32[]{:S(2)}) async-start(bf16[8,128,512]{2,1,0:T(8,128)(2,1)} %shard_map.119), calls=%async_computation.2 | async-start | bytes 2097152 | tf_op jit(solution)/shard_map/all_to_all | solution.py:409
  132.3 21.6 %all-to-all-start.3 = ((bf16[8,64,1024]{2,1,0:T(8,128)(2,1)}), bf16[8,64,1024]{2,1,0:T(8,128)(2,1)S(1)}, u32[]{:S(2)}, u32[]{:S(2)}) async-start(bf16[8,64,1024]{2,1,0:T(8,128)(2,1)} %bitcast.11), calls=%async_computation.3 | async-start | bytes 2097152 | tf_op jit(solution)/shard_map/all_to_all | solution.py:409
  189.9 13.4 %collective-permute-start.6 = (bf16[64,3584]{1,0:T(8,128)(2,1)S(1)}, bf16[64,3584]{1,0:T(8,128)(2,1)S(1)}, u32[]{:S(2)}, u32[]{:S(2)}) collective-permute-start(bf16[64,3584]{1,0:T(8,128)(2,1)S(1)} %get-tuple-element.27), channel_id=1, source_target_pairs={{0,6},{2,0},{4,2},{6,4},{1,7},{3,1},{5,3},{7,5},{8,14},{10,8},{12,... | collective-permute-start | bytes 1376264 | tf_op jit(solution)/shard_map/ppermute | solution.py:388
  190.8 15.4 %collective-permute-start.22 = (bf16[64,3584]{1,0:T(8,128)(2,1)S(1)}, bf16[64,3584]{1,0:T(8,128)(2,1)S(1)}, u32[]{:S(2)}, u32[]{:S(2)}) collective-permute-start(bf16[64,3584]{1,0:T(8,128)(2,1)S(1)} %get-tuple-element.35), channel_id=1, source_target_pairs={{0,2},{2,4},{4,6},{6,0},{1,3},{3,5},{5,7},{7,1},{8,10},{10,12},{12... | collective-permute-start | bytes 1376264 | tf_op jit(solution)/shard_map/ppermute | solution.py:384
  192.1 41.6 %collective-permute-start.4 = (bf16[4,64,3584]{2,1,0:T(8,128)(2,1)S(1)}, bf16[4,64,3584]{2,1,0:T(8,128)(2,1)S(1)}, u32[]{:S(2)}, u32[]{:S(2)}) collective-permute-start(bf16[4,64,3584]{2,1,0:T(8,128)(2,1)S(1)} %get-tuple-element.23), channel_id=1, source_target_pairs={{0,1},{1,0},{2,3},{3,2},{4,5},{5,4},{6,7},{7,6},{8,9},{9,8},{10,11... | collective-permute-start | bytes 5505032 | tf_op jit(solution)/shard_map/ppermute | solution.py:413
  193.0 22.3 %collective-permute-start.5 = (bf16[64,3584]{1,0:T(8,128)(2,1)S(1)}, bf16[64,3584]{1,0:T(8,128)(2,1)S(1)}, u32[]{:S(2)}, u32[]{:S(2)}) collective-permute-start(bf16[64,3584]{1,0:T(8,128)(2,1)S(1)} %get-tuple-element.40), channel_id=1, source_target_pairs={{0,2},{2,4},{4,6},{6,0},{1,3},{3,5},{5,7},{7,1},{8,10},{10,12},{12... | collective-permute-start | bytes 1376264 | tf_op jit(solution)/shard_map/ppermute | solution.py:384
  194.6 54.2 %collective-permute-start.21 = (bf16[64,3584]{1,0:T(8,128)(2,1)}, bf16[64,3584]{1,0:T(8,128)(2,1)S(1)}, u32[]{:S(2)}, u32[]{:S(2)}) collective-permute-start(bf16[64,3584]{1,0:T(8,128)(2,1)} %get-tuple-element.41), channel_id=1, source_target_pairs={{0,6},{2,0},{4,2},{6,4},{1,7},{3,1},{5,3},{7,5},{8,14},{10,8},{12,... | collective-permute-start | bytes 1376264 | tf_op jit(solution)/shard_map/ppermute | solution.py:388
  203.5 18.7 %collective-permute-start.7 = (bf16[64,3584]{1,0:T(8,128)(2,1)S(1)}, bf16[64,3584]{1,0:T(8,128)(2,1)S(1)}, u32[]{:S(2)}, u32[]{:S(2)}) collective-permute-start(bf16[64,3584]{1,0:T(8,128)(2,1)S(1)} %shard_map.123), channel_id=1, source_target_pairs={{0,6},{2,0},{4,2},{6,4},{1,7},{3,1},{5,3},{7,5},{8,14},{10,8},{12,... | collective-permute-start | bytes 1376264 | tf_op jit(solution)/shard_map/ppermute | solution.py:388
  207.1 41.8 %collective-permute-start.23 = (bf16[64,3584]{1,0:T(8,128)(2,1)}, bf16[64,3584]{1,0:T(8,128)(2,1)}, u32[]{:S(2)}, u32[]{:S(2)}) collective-permute-start(bf16[64,3584]{1,0:T(8,128)(2,1)} %shard_map.129), channel_id=1, source_target_pairs={{0,2},{2,4},{4,6},{6,0},{1,3},{3,5},{5,7},{7,1},{8,10},{10,12},{12... | collective-permute-start | bytes 1376264 | tf_op jit(solution)/shard_map/ppermute | solution.py:384
  234.9 14.0 %collective-permute-start.24 = (bf16[64,3584]{1,0:T(8,128)(2,1)S(1)}, bf16[64,3584]{1,0:T(8,128)(2,1)}, u32[]{:S(2)}, u32[]{:S(2)}) collective-permute-start(bf16[64,3584]{1,0:T(8,128)(2,1)S(1)} %shard_map.124), channel_id=1, source_target_pairs={{0,1},{1,0},{2,3},{3,2},{4,5},{5,4},{6,7},{7,6},{8,9},{9,8},{10,11... | collective-permute-start | bytes 1376264 | tf_op jit(solution)/shard_map/ppermute | solution.py:413
  250.5 6.5 %collective-permute-start.25 = (bf16[64,1792]{1,0:T(8,128)(2,1)S(1)}, bf16[64,1792]{1,0:T(8,128)(2,1)S(1)}, u32[]{:S(2)}, u32[]{:S(2)}) collective-permute-start(bf16[64,1792]{1,0:T(8,128)(2,1)S(1)} %shard_map.130.refs_0_), channel_id=1, source_target_pairs={{0,1},{1,0},{2,3},{3,2},{4,5},{5,4},{6,7},{7,6},{8,9},{9,8},{10,11... | collective-permute-start | bytes 688136 | tf_op jit(solution)/shard_map/ppermute | solution.py:413
  253.7 18.1 %collective-permute-start.9 = (bf16[32,3584]{1,0:T(8,128)(2,1)S(1)}, bf16[32,3584]{1,0:T(8,128)(2,1)S(1)}, u32[]{:S(2)}, u32[]{:S(2)}) collective-permute-start(bf16[32,3584]{1,0:T(8,128)(2,1)S(1)} %get-tuple-element.33), channel_id=1, source_target_pairs={{0,2},{2,4},{4,6},{6,0},{1,3},{3,5},{5,7},{7,1},{8,10},{10,12},{12... | collective-permute-start | bytes 688136 | tf_op jit(solution)/shard_map/ppermute | solution.py:384
  254.7 8.5 %collective-permute-start.12 = (bf16[32,3584]{1,0:T(8,128)(2,1)S(1)}, bf16[32,3584]{1,0:T(8,128)(2,1)S(1)}, u32[]{:S(2)}, u32[]{:S(2)}) collective-permute-start(bf16[32,3584]{1,0:T(8,128)(2,1)S(1)} %get-tuple-element.34), channel_id=1, source_target_pairs={{0,6},{2,0},{4,2},{6,4},{1,7},{3,1},{5,3},{7,5},{8,14},{10,8},{12,... | collective-permute-start | bytes 688136 | tf_op jit(solution)/shard_map/ppermute | solution.py:388
  257.0 11.4 %collective-permute-start.28 = (bf16[64,1792]{1,0:T(8,128)(2,1)S(1)}, bf16[64,1792]{1,0:T(8,128)(2,1)S(1)}, u32[]{:S(2)}, u32[]{:S(2)}) collective-permute-start(bf16[64,1792]{1,0:T(8,128)(2,1)S(1)} %shard_map.130.refs_0_), channel_id=1, source_target_pairs={{0,2},{2,4},{4,6},{6,0},{1,3},{3,5},{5,7},{7,1},{8,10},{10,12},{12... | collective-permute-start | bytes 688136 | tf_op jit(solution)/shard_map/ppermute | solution.py:384
  257.1 11.4 %collective-permute-start.27 = (bf16[64,1792]{1,0:T(8,128)(2,1)S(1)}, bf16[64,1792]{1,0:T(8,128)(2,1)S(1)}, u32[]{:S(2)}, u32[]{:S(2)}) collective-permute-start(bf16[64,1792]{1,0:T(8,128)(2,1)S(1)} %collective-permute-done.25.refs_1_), channel_id=1, source_target_pairs={{0,6},{2,0},{4,2},{6,4},{1,7},{3,1},{5,3},{7,5},{8,14},{10,8},{12,... | collective-permute-start | bytes 688136 | tf_op jit(solution)/shard_map/ppermute | solution.py:388
  260.3 12.7 %collective-permute-start.26 = (bf16[64,1792]{1,0:T(8,128)(2,1)S(1)}, bf16[64,1792]{1,0:T(8,128)(2,1)S(1)}, u32[]{:S(2)}, u32[]{:S(2)}) collective-permute-start(bf16[64,1792]{1,0:T(8,128)(2,1)S(1)} %shard_map.130.refs_0_), channel_id=1, source_target_pairs={{0,6},{2,0},{4,2},{6,4},{1,7},{3,1},{5,3},{7,5},{8,14},{10,8},{12,... | collective-permute-start | bytes 688136 | tf_op jit(solution)/shard_map/ppermute | solution.py:388
  263.2 15.8 %collective-permute-start.31 = (bf16[64,1792]{1,0:T(8,128)(2,1)S(1)}, bf16[64,1792]{1,0:T(8,128)(2,1)S(1)}, u32[]{:S(2)}, u32[]{:S(2)}) collective-permute-start(bf16[64,1792]{1,0:T(8,128)(2,1)S(1)} %collective-permute-done.25.refs_1_), channel_id=1, source_target_pairs={{0,2},{2,4},{4,6},{6,0},{1,3},{3,5},{5,7},{7,1},{8,10},{10,12},{12... | collective-permute-start | bytes 688136 | tf_op jit(solution)/shard_map/ppermute | solution.py:384
  268.4 9.8 %collective-permute-start.29 = (bf16[64,1792]{1,0:T(8,128)(2,1)S(1)}, bf16[64,1792]{1,0:T(8,128)(2,1)S(1)}, u32[]{:S(2)}, u32[]{:S(2)}) collective-permute-start(bf16[64,1792]{1,0:T(8,128)(2,1)S(1)} %collective-permute-done.28.refs_6_), channel_id=1, source_target_pairs={{0,2},{2,4},{4,6},{6,0},{1,3},{3,5},{5,7},{7,1},{8,10},{10,12},{12... | collective-permute-start | bytes 688136 | tf_op jit(solution)/shard_map/ppermute | solution.py:384
  268.4 11.9 %collective-permute-start.30 = (bf16[64,1792]{1,0:T(8,128)(2,1)S(1)}, bf16[64,1792]{1,0:T(8,128)(2,1)S(1)}, u32[]{:S(2)}, u32[]{:S(2)}) collective-permute-start(bf16[64,1792]{1,0:T(8,128)(2,1)S(1)} %collective-permute-done.27.refs_3_), channel_id=1, source_target_pairs={{0,6},{2,0},{4,2},{6,4},{1,7},{3,1},{5,3},{7,5},{8,14},{10,8},{12,... | collective-permute-start | bytes 688136 | tf_op jit(solution)/shard_map/ppermute | solution.py:388
  271.8 12.4 %collective-permute-start.8 = (bf16[32,3584]{1,0:T(8,128)(2,1)S(1)}, bf16[32,3584]{1,0:T(8,128)(2,1)S(1)}, u32[]{:S(2)}, u32[]{:S(2)}) collective-permute-start(bf16[32,3584]{1,0:T(8,128)(2,1)S(1)} %get-tuple-element.46), channel_id=1, source_target_pairs={{0,6},{2,0},{4,2},{6,4},{1,7},{3,1},{5,3},{7,5},{8,14},{10,8},{12,... | collective-permute-start | bytes 688136 | tf_op jit(solution)/shard_map/ppermute | solution.py:388
  273.0 11.2 %collective-permute-start.11 = (bf16[32,3584]{1,0:T(8,128)(2,1)S(1)}, bf16[32,3584]{1,0:T(8,128)(2,1)S(1)}, u32[]{:S(2)}, u32[]{:S(2)}) collective-permute-start(bf16[32,3584]{1,0:T(8,128)(2,1)S(1)} %get-tuple-element.47), channel_id=1, source_target_pairs={{0,2},{2,4},{4,6},{6,0},{1,3},{3,5},{5,7},{7,1},{8,10},{10,12},{12... | collective-permute-start | bytes 688136 | tf_op jit(solution)/shard_map/ppermute | solution.py:384
  279.0 7.2 %collective-permute-start.10 = (bf16[32,3584]{1,0:T(8,128)(2,1)S(1)}, bf16[32,3584]{1,0:T(8,128)(2,1)S(1)}, u32[]{:S(2)}, u32[]{:S(2)}) collective-permute-start(bf16[32,3584]{1,0:T(8,128)(2,1)S(1)} %shard_map.126), channel_id=1, source_target_pairs={{0,2},{2,4},{4,6},{6,0},{1,3},{3,5},{5,7},{7,1},{8,10},{10,12},{12... | collective-permute-start | bytes 688136 | tf_op jit(solution)/shard_map/ppermute | solution.py:384
  284.1 23.9 %collective-permute-start.32 = (bf16[8,64,1024]{2,1,0:T(8,128)(2,1)S(1)}, bf16[8,64,1024]{2,1,0:T(8,128)(2,1)S(1)}, u32[]{:S(2)}, u32[]{:S(2)}) collective-permute-start(bf16[8,64,1024]{2,1,0:T(8,128)(2,1)S(1)} %shard_map.131), channel_id=1, source_target_pairs={{0,8},{8,0},{1,9},{9,1},{2,10},{10,2},{3,11},{11,3},{4,12},{12,4},... | collective-permute-start | bytes 3145736 | tf_op jit(solution)/shard_map/ppermute | solution.py:413
  286.6 6.1 %collective-permute-start.14 = (bf16[64,1792]{1,0:T(8,128)(2,1)S(1)}, bf16[64,1792]{1,0:T(8,128)(2,1)S(1)}, u32[]{:S(2)}, u32[]{:S(2)}) collective-permute-start(bf16[64,1792]{1,0:T(8,128)(2,1)S(1)} %shard_map.128.refs_0_), channel_id=1, source_target_pairs={{0,1},{1,0},{2,3},{3,2},{4,5},{5,4},{6,7},{7,6},{8,9},{9,8},{10,11... | collective-permute-start | bytes 688136 | tf_op jit(solution)/shard_map/ppermute | solution.py:413
  287.6 9.1 %collective-permute-start.17 = (bf16[64,1792]{1,0:T(8,128)(2,1)S(1)}, bf16[64,1792]{1,0:T(8,128)(2,1)S(1)}, u32[]{:S(2)}, u32[]{:S(2)}) collective-permute-start(bf16[64,1792]{1,0:T(8,128)(2,1)S(1)} %shard_map.128.refs_0_), channel_id=1, source_target_pairs={{0,2},{2,4},{4,6},{6,0},{1,3},{3,5},{5,7},{7,1},{8,10},{10,12},{12... | collective-permute-start | bytes 688136 | tf_op jit(solution)/shard_map/ppermute | solution.py:384
  292.7 8.5 %collective-permute-start.16 = (bf16[64,1792]{1,0:T(8,128)(2,1)S(1)}, bf16[64,1792]{1,0:T(8,128)(2,1)S(1)}, u32[]{:S(2)}, u32[]{:S(2)}) collective-permute-start(bf16[64,1792]{1,0:T(8,128)(2,1)S(1)} %collective-permute-done.14.refs_1_), channel_id=1, source_target_pairs={{0,6},{2,0},{4,2},{6,4},{1,7},{3,1},{5,3},{7,5},{8,14},{10,8},{12,... | collective-permute-start | bytes 688136 | tf_op jit(solution)/shard_map/ppermute | solution.py:388
  294.7 10.8 %collective-permute-start.15 = (bf16[64,1792]{1,0:T(8,128)(2,1)S(1)}, bf16[64,1792]{1,0:T(8,128)(2,1)S(1)}, u32[]{:S(2)}, u32[]{:S(2)}) collective-permute-start(bf16[64,1792]{1,0:T(8,128)(2,1)S(1)} %shard_map.128.refs_0_), channel_id=1, source_target_pairs={{0,6},{2,0},{4,2},{6,4},{1,7},{3,1},{5,3},{7,5},{8,14},{10,8},{12,... | collective-permute-start | bytes 688136 | tf_op jit(solution)/shard_map/ppermute | solution.py:388
  294.7 11.7 %collective-permute-start.20 = (bf16[64,1792]{1,0:T(8,128)(2,1)S(1)}, bf16[64,1792]{1,0:T(8,128)(2,1)S(1)}, u32[]{:S(2)}, u32[]{:S(2)}) collective-permute-start(bf16[64,1792]{1,0:T(8,128)(2,1)S(1)} %collective-permute-done.14.refs_1_), channel_id=1, source_target_pairs={{0,2},{2,4},{4,6},{6,0},{1,3},{3,5},{5,7},{7,1},{8,10},{10,12},{12... | collective-permute-start | bytes 688136 | tf_op jit(solution)/shard_map/ppermute | solution.py:384
  296.7 9.7 %collective-permute-start.18 = (bf16[64,1792]{1,0:T(8,128)(2,1)S(1)}, bf16[64,1792]{1,0:T(8,128)(2,1)S(1)}, u32[]{:S(2)}, u32[]{:S(2)}) collective-permute-start(bf16[64,1792]{1,0:T(8,128)(2,1)S(1)} %collective-permute-done.17.refs_6_), channel_id=1, source_target_pairs={{0,2},{2,4},{4,6},{6,0},{1,3},{3,5},{5,7},{7,1},{8,10},{10,12},{12... | collective-permute-start | bytes 688136 | tf_op jit(solution)/shard_map/ppermute | solution.py:384
  301.2 6.8 %collective-permute-start.19 = (bf16[64,1792]{1,0:T(8,128)(2,1)S(1)}, bf16[64,1792]{1,0:T(8,128)(2,1)S(1)}, u32[]{:S(2)}, u32[]{:S(2)}) collective-permute-start(bf16[64,1792]{1,0:T(8,128)(2,1)S(1)} %collective-permute-done.16.refs_3_), channel_id=1, source_target_pairs={{0,6},{2,0},{4,2},{6,4},{1,7},{3,1},{5,3},{7,5},{8,14},{10,8},{12,... | collective-permute-start | bytes 688136 | tf_op jit(solution)/shard_map/ppermute | solution.py:388
  (16 other events, 191.5 us)

commit v4 on v3

v4 whole, which is shorter than its diff:
```python
import functools
import math

import jax
import jax.numpy as jnp
from jax import lax
from jax.experimental import pallas as pl
from jax.experimental.pallas import tpu as pltpu
from jax.sharding import Mesh, PartitionSpec as P

D = 8192
KV_HEADS = 8
HEAD_DIM = 128
BLK = 128
GROUP = 8
MOVED = 16
AXES = ("z", "xh", "core", "y", "xl")
ROW = ("z", "xh", "core")
ZXH = ("z", "xh")
COL = ("y", "xl")
CHIP = ("z", "xh", "y", "xl")
NEG = -1e30
bf16 = jnp.bfloat16
f32 = jnp.float32


def nt_dot(a, b):
    return lax.dot_general(a, b, (((1,), (1,)), ((), ())), preferred_element_type=f32)


def tn_dot(a, b):
    return lax.dot_general(a, b, (((0,), (0,)), ((), ())), preferred_element_type=f32)


def attend_kernel(scale, local_blocks, last, list_ref, place_ref, own_q_ref, other_q_ref, *refs):
    per_step = 8
    half_blk = BLK // 2
    if last:
        first_ref, chunk_ref, own_in_ref, send_in_ref = refs[:4]
    else:
        chunk_ref = refs[0]
    own_ref, send_ref, order_ref, q_ref, top_ref, sum_ref, acc_ref = refs[-7:]
    core = place_ref[0]
    block = place_ref[1]
    length = list_ref.shape[0]
    heads = own_q_ref.shape[1] // HEAD_DIM
    rows = heads * BLK
    for h in range(heads):
        cols = pl.ds(h * HEAD_DIM, HEAD_DIM)
        q_ref[pl.ds(h * BLK, BLK), :] = own_q_ref[:, cols]
        q_ref[pl.ds(rows + h * BLK, BLK), :] = other_q_ref[:, cols]
    if last:
        for half, ref in ((0, own_in_ref), (1, send_in_ref)):
            acc_ref[half] = ref[0:HEAD_DIM, :]
            top_ref[half] = ref[HEAD_DIM : HEAD_DIM + 1, :]
            sum_ref[half] = ref[HEAD_DIM + 1 : HEAD_DIM + 2, :]
    else:
        top_ref[...] = jnp.full_like(top_ref, NEG)
        sum_ref[...] = jnp.zeros_like(sum_ref)
        acc_ref[...] = jnp.zeros_like(acc_ref)

    def collect(i, count):
        device = list_ref[i] // local_blocks
        row = device // 8
        order_ref[count] = (row // 2) * 8 + device % 8
        return count + jnp.where(row % 2 == core, 1, 0)

    count = lax.fori_loop(0, length, collect, jnp.int32(0))

    def update(half, keys, values, bias):
        part = pl.ds(half * rows, rows)
        scores = nt_dot(keys, q_ref[part, :]) * scale + bias
        old = top_ref[half]
        new = jnp.maximum(old, jnp.max(scores, axis=0, keepdims=True))
        weights = jnp.exp2(scores - new)
        decay = jnp.exp2(old - new)
        top_ref[half] = new
        sum_ref[half] = sum_ref[half] * decay + jnp.sum(weights, axis=0, keepdims=True)
        acc_ref[half] = acc_ref[half] * decay + tn_dot(values, weights.astype(bf16))

    def far(step, carry):
        slots = [order_ref[jnp.minimum(step * per_step + i, count - 1)] for i in range(per_step)]
        keys = jnp.concatenate([chunk_ref[s, 0:half_blk] for s in slots], axis=0)
        values = jnp.concatenate([chunk_ref[s, half_blk : 2 * half_blk] for s in slots], axis=0)
        bias = jnp.concatenate(
            [
                jnp.full((half_blk, 1), jnp.where(step * per_step + i < count, 0.0, NEG), f32)
                for i in range(per_step)
            ],
            axis=0,
        )
        for half in range(2):
            update(half, keys, values, bias)
        return carry

    lax.fori_loop(0, (count + per_step - 1) // per_step, far, 0)

    def near(j, carry):
        which = core + 2 * j
        shift = (block - which) * BLK
        key_pos = lax.broadcasted_iota(jnp.int32, (BLK, rows), 0)
        token = lax.broadcasted_iota(jnp.int32, (BLK, rows), 1) % BLK
        bias = jnp.where(key_pos <= token + shift, 0.0, NEG)
        keys = jnp.concatenate([first_ref[i * 8 + which, BLK:] for i in range(8)], axis=0)
        values = jnp.concatenate([chunk_ref[i * 8 + which, BLK:] for i in range(8)], axis=0)
        for half in range(2):
            update(half, keys, values, bias)
        return carry

    if last:
        lax.fori_loop(0, (block - core + 2) // 2, near, 0)
    for half, ref in ((0, own_ref), (1, send_ref)):
        ref[0:HEAD_DIM, :] = acc_ref[half]
        ref[HEAD_DIM : HEAD_DIM + 1, :] = top_ref[half]
        ref[HEAD_DIM + 1 : HEAD_DIM + 2, :] = sum_ref[half]


def attend(my_list, place, own_q, other_q, chunks, state, local_blocks):
    heads = own_q.shape[1] // HEAD_DIM
    rows = heads * BLK
    packed = jax.ShapeDtypeStruct((HEAD_DIM + 8, rows), f32)
    smem = pl.BlockSpec(memory_space=pltpu.SMEM)
    vmem = pl.BlockSpec(memory_space=pltpu.VMEM)
    scale = math.log2(math.e) / math.sqrt(HEAD_DIM)
    arrays = [own_q, other_q, *chunks, *state]
    return pl.pallas_call(
        functools.partial(attend_kernel, scale, local_blocks, len(state) > 0),
        out_shape=(packed, packed),
        in_specs=[smem, smem] + [vmem] * len(arrays),
        out_specs=(vmem, vmem),
        scratch_shapes=[
            pltpu.SMEM((my_list.shape[0] + 1,), jnp.int32),
            pltpu.VMEM((2 * rows, HEAD_DIM), bf16),
            pltpu.VMEM((2, 1, rows), f32),
            pltpu.VMEM((2, 1, rows), f32),
            pltpu.VMEM((2, HEAD_DIM, rows), f32),
        ],
        compiler_params=pltpu.CompilerParams(vmem_limit_bytes=24 * 1024 * 1024),
        cost_estimate=pl.CostEstimate(
            flops=4 * 2 * rows * 20 * BLK * HEAD_DIM,
            bytes_accessed=2 * chunks[-1].size * 2,
            transcendentals=2 * rows * 20 * BLK,
        ),
    )(my_list, place, *arrays)


def merge_kernel(own_ref, got_ref, out_ref):
    own_top = own_ref[HEAD_DIM : HEAD_DIM + 1, :]
    got_top = got_ref[HEAD_DIM : HEAD_DIM + 1, :]
    top = jnp.maximum(own_top, got_top)
    own_w = jnp.exp2(own_top - top)
    got_w = jnp.exp2(got_top - top)
    total = own_w * own_ref[HEAD_DIM + 1 : HEAD_DIM + 2, :] + got_w * got_ref[HEAD_DIM + 1 : HEAD_DIM + 2, :]
    mixed = (own_ref[0:HEAD_DIM, :] * own_w + got_ref[0:HEAD_DIM, :] * got_w) / total
    heads = mixed.shape[1] // BLK
    for h in range(heads):
        piece = mixed[:, h * BLK : (h + 1) * BLK].T.astype(bf16)
        for i in range(out_ref.shape[0]):
            out_ref[i, :, pl.ds(h * HEAD_DIM, HEAD_DIM)] = piece


def merge(own, got, copies):
    heads = own.shape[1] // BLK
    vmem = pl.BlockSpec(memory_space=pltpu.VMEM)
    return pl.pallas_call(
        merge_kernel,
        out_shape=jax.ShapeDtypeStruct((copies, BLK, heads * HEAD_DIM), bf16),
        in_specs=[vmem, vmem],
        out_specs=vmem,
        compiler_params=pltpu.CompilerParams(vmem_limit_bytes=12 * 1024 * 1024),
    )(own, got)


def product_kernel(tile, weight_count, pick_ref, x_ref, *refs):
    weight_refs, add_ref, out_ref = refs[:weight_count], refs[weight_count:-1], refs[-1]
    x = x_ref[:, pick_ref[0]] if x_ref.shape[1] > out_ref.shape[1] else x_ref[...]
    x = x.reshape(-1, x.shape[-1])
    width = weight_refs[0].shape[1]
    block = out_ref.shape[:-1] + (tile,)
    for i, weight_ref in enumerate(weight_refs):
        for first in range(0, width, tile):
            total = jnp.dot(x, weight_ref[:, first : first + tile], preferred_element_type=f32)
            columns = slice(i * width + first, i * width + first + tile)
            if add_ref:
                total = total + add_ref[0][..., columns].reshape(total.shape).astype(f32)
            out_ref[..., columns] = total.astype(bf16).reshape(block)


def product(x, weights, tile, pick=None, add=None):
    blocks, pair, tokens, inputs = x.shape
    taken = pair if pick is None else 1
    pick = jnp.zeros((1,), jnp.int32) if pick is None else pick.astype(jnp.int32).reshape(1)
    vmem = pl.BlockSpec(memory_space=pltpu.VMEM)
    operands = [x, *weights] if add is None else [x, *weights, add]
    rows = blocks * taken * tokens
    columns = weights[0].shape[1] * len(weights)
    return pl.pallas_call(
        functools.partial(product_kernel, tile, len(weights)),
        out_shape=jax.ShapeDtypeStruct((blocks, taken, tokens, columns), bf16),
        in_specs=[pl.BlockSpec(memory_space=pltpu.SMEM)] + [vmem] * len(operands),
        out_specs=vmem,
        compiler_params=pltpu.CompilerParams(vmem_limit_bytes=20 * 1024 * 1024),
        cost_estimate=pl.CostEstimate(
            flops=2 * rows * inputs * columns,
            bytes_accessed=2 * (rows * inputs + inputs * columns + rows * columns),
            transcendentals=0,
        ),
    )(pick, *operands)


VMEM = pl.BlockSpec(memory_space=pltpu.VMEM)
SMEM = pl.BlockSpec(memory_space=pltpu.SMEM)


def small_call(kernel, outs, scalars, arrays, moved):
    return pl.pallas_call(
        kernel,
        out_shape=outs,
        in_specs=[SMEM] * len(scalars) + [VMEM] * len(arrays),
        out_specs=jax.tree.map(lambda _: VMEM, outs),
        compiler_params=pltpu.CompilerParams(vmem_limit_bytes=16 * 1024 * 1024),
        cost_estimate=pl.CostEstimate(flops=moved, bytes_accessed=moved, transcendentals=0),
    )(*scalars, *arrays)


def spread_kernel(place_ref, mine_ref, theirs_ref, gain_ref, gate_ref, up_ref, *out_refs):
    y, side = place_ref[0], place_ref[1]
    give_ref, keep_ref, self_ref, right_ref, left_ref, opposite_ref, far_ref, squares_ref = out_refs
    order = [(y + i) % 4 for i in range(4)]
    sides = (side, 1 - side)
    n = mine_ref.shape[2]
    kept = n - MOVED
    joint = n + MOVED
    rows = [mine_ref[i, 1 - side, MOVED:] for i in order]
    for i in order:
        for s in sides:
            rows += [theirs_ref[i, s], mine_ref[i, s, :MOVED]]
    rows += [mine_ref[i, side, MOVED:] for i in order]
    x = jnp.concatenate(rows, axis=0)
    base = 4 * kept
    end = base + 8 * joint
    step = pl.program_id(0)

    @pl.when(step == pl.num_programs(0) - 1)
    def _():
        ones = jnp.ones((8, x.shape[1]), f32)
        plain = x.astype(f32) / gain_ref[...]
        sums = lax.dot_general(
            ones, plain * plain, (((1,), (1,)), ((), ())),
            precision=lax.Precision.HIGHEST, preferred_element_type=f32,
        )
        for i in range(4):
            for j, (first, k) in enumerate(((0, 1), (end, 0))):
                at = base + (2 * i + k) * joint
                squares_ref[j, i, :, 0:joint] = sums[:, at : at + joint]
                squares_ref[j, i, :, joint:] = sums[:, first + i * kept : first + (i + 1) * kept]

    def put(weight_ref):
        total = jnp.dot(x, weight_ref[...], preferred_element_type=f32).astype(bf16)
        for i in range(4):
            give_ref[i] = total[i * kept : (i + 1) * kept]
            keep_ref[i] = total[end + i * kept : end + (i + 1) * kept]
        for first, ref in ((0, self_ref), (2, right_ref), (6, left_ref)):
            for j in range(2):
                at = base + (first + j) * joint
                ref[j] = total[at : at + joint]
        opposite_ref[...] = total[base + 4 * joint : base + 5 * joint]
        far_ref[...] = total[base + 5 * joint : base + 6 * joint]

    half = pl.num_programs(0) // 2
    pl.when(step < half)(functools.partial(put, gate_ref))
    pl.when(step >= half)(functools.partial(put, up_ref))


def partial_columns(place, mine, theirs, gain, gate, up):
    tile = 896
    inputs, width = gate.shape
    count = width // tile
    tokens = mine.shape[2]
    whole = pl.BlockSpec(mine.shape, lambda n, p: (0, 0, 0, 0))

    def out(*lead):
        block = pl.BlockSpec((*lead, tile), lambda n, p: (0,) * len(lead) + (n,))
        return jax.ShapeDtypeStruct((*lead, 2 * width), bf16), block

    kept, joint = tokens - MOVED, tokens + MOVED
    shapes, blocks = zip(*[out(4, kept)] * 2, *[out(2, joint)] * 3, *[out(joint)] * 2)
    shapes += (jax.ShapeDtypeStruct((2, 4, 8, 2 * tokens), f32),)
    blocks += (pl.BlockSpec((2, 4, 8, 2 * tokens), lambda n, p: (0, 0, 0, 0)),)
    rows = 16 * tokens
    return pl.pallas_call(
        spread_kernel,
        out_shape=shapes,
        grid_spec=pltpu.PrefetchScalarGridSpec(
            num_scalar_prefetch=1,
            grid=(2 * count,),
            in_specs=[
                whole,
                whole,
                pl.BlockSpec((1, inputs), lambda n, p: (0, 0)),
                pl.BlockSpec((inputs, tile), lambda n, p: (0, jnp.minimum(n, count - 1))),
                pl.BlockSpec((inputs, tile), lambda n, p: (0, jnp.maximum(n - count, 0))),
            ],
            out_specs=blocks,
        ),
        compiler_params=pltpu.CompilerParams(vmem_limit_bytes=40 * 1024 * 1024),
        cost_estimate=pl.CostEstimate(
            flops=4 * rows * inputs * width,
            bytes_accessed=2 * (rows * inputs + 2 * inputs * width + 2 * rows * width),
            transcendentals=0,
        ),
    )(place, mine, theirs, gain, gate, up)


def arranged_sum(got, keep):
    tokens, width = keep.shape[1], keep.shape[2] // 2

    def kernel(got_ref, keep_ref, self_ref, right_ref, left_ref, opposite_ref, far_ref):
        def block(i, j):
            columns = pl.ds(j * width, width)
            return (got_ref[i, :, columns].astype(f32) + keep_ref[i, :, columns].astype(f32)).astype(bf16)

        for i, ref in ((0, self_ref), (1, right_ref), (3, left_ref)):
            for j in range(2):
                ref[j] = block(i, j)
        opposite_ref[...] = block(2, 0)
        far_ref[...] = block(2, 1)

    two = jax.ShapeDtypeStruct((2, tokens, width), bf16)
    one = jax.ShapeDtypeStruct((tokens, width), bf16)
    return small_call(kernel, (two, two, two, one, one), (), (got, keep), 4 * keep.size)


def add_pieces(*pieces):
    def kernel(*refs):
        refs[-1][...] = sum(r[...].astype(f32) for r in refs[:-1]).astype(bf16)

    first = pieces[0]
    return small_call(kernel, jax.ShapeDtypeStruct(first.shape, bf16), (), pieces, 2 * first.size)


def gated(gates, ups, factor):
    pieces = list(gates) + ([] if ups is None else list(ups))
    tokens = pieces[0].shape[0]
    width = pieces[0].shape[1] // (2 if ups is None else 1)

    def kernel(*refs):
        scale = refs[-2][...]
        if ups is None:
            gate = sum(r[:, 0:width].astype(f32) for r in refs[:-2]) * scale
            up = sum(r[:, width:].astype(f32) for r in refs[:-2]) * scale
        else:
            gate = sum(r[...].astype(f32) for r in refs[: len(gates)]) * scale
            up = sum(r[...].astype(f32) for r in refs[len(gates) : -2]) * scale
        refs[-1][...] = (gate / (1.0 + jnp.exp(-gate)) * up).astype(bf16)

    out = jax.ShapeDtypeStruct((tokens, width), bf16)
    return small_call(kernel, out, (), [*pieces, factor[:, None]], 8 * tokens * width)


def down_product(place, pieces, weight, rest=()):
    tile = 256
    n, inputs = pieces[0].shape
    width = weight.shape[1]
    tokens = n - MOVED if not rest else n + MOVED

    def kernel(place_ref, *refs):
        y, side = place_ref[0], place_ref[1]
        x = jnp.concatenate([p[...] for p in refs[:8]], axis=0)
        total = jnp.dot(x, refs[8][...], preferred_element_type=f32)
        for i in range(4):
            for j in range(2):
                at = 2 * ((y + i) % 4) + (side if j == 0 else 1 - side)
                part = total[(2 * i + j) * n : (2 * i + j + 1) * n]
                if rest:
                    before_ref, add_ref, out_ref = refs[9:]
                    add = add_ref[at].astype(f32)
                    out_ref[at, :MOVED] = (before_ref[at] + add[:MOVED]).astype(bf16)
                    out_ref[at, MOVED:] = (part + add[MOVED:]).astype(bf16)
                else:
                    give_ref, first_ref = refs[9:]
                    give_ref[at] = part[:tokens].astype(bf16)
                    first_ref[at] = part[tokens:]

    def by_column(rows):
        return pl.BlockSpec((8, rows, tile), lambda c, p: (0, 0, c))

    specs = [pl.BlockSpec((n, inputs), lambda c, p: (0, 0))] * 8
    specs += [pl.BlockSpec((inputs, tile), lambda c, p: (0, c))]
    specs += [by_column(MOVED), by_column(tokens)] if rest else []
    whole = jax.ShapeDtypeStruct((8, tokens, width), bf16)
    first = jax.ShapeDtypeStruct((8, MOVED, width), f32)
    return pl.pallas_call(
        kernel,
        out_shape=whole if rest else (whole, first),
        grid_spec=pltpu.PrefetchScalarGridSpec(
            num_scalar_prefetch=1,
            grid=(width // tile,),
            in_specs=specs,
            out_specs=by_column(tokens) if rest else (by_column(tokens), by_column(MOVED)),
        ),
        compiler_params=pltpu.CompilerParams(vmem_limit_bytes=20 * 1024 * 1024),
        cost_estimate=pl.CostEstimate(
            flops=16 * n * inputs * width,
            bytes_accessed=2 * (8 * n * inputs + inputs * width + 8 * n * width),
            transcendentals=0,
        ),
    )(place, *pieces, weight, *rest)


def to_right(x):
    return lax.ppermute(x, "y", [(i, (i + 1) % 4) for i in range(4)])


def to_left(x):
    return lax.ppermute(x, "y", [(i, (i + 3) % 4) for i in range(4)])


def ring_start(pieces):
    _, right, left, opposite, far = pieces
    return to_right(opposite), to_left(far), to_right(right[1]), to_left(left[0])


def ring_middle(pieces, from_left, from_right):
    return add_pieces(pieces[1][0], from_left), add_pieces(pieces[2][1], from_right)


def ring_end(pieces, arrived, sums):
    third_left, third_right = to_right(sums[0]), to_left(sums[1])
    own = pieces[0]
    return (own[0], arrived[3], third_left), (own[1], arrived[2], third_right)


def ring_gather(mine, got):
    mine_left, mine_right = to_right(mine), to_left(mine)
    got_left, got_right = to_right(got), to_left(got)
    mine_far, got_far = to_right(mine_left), to_left(got_right)
    return mine, got, mine_right, got_right, mine_far, got_far, mine_left, got_left


def exchange(x, axes):
    return lax.all_to_all(x, axes, split_axis=0, concat_axis=0, tiled=True)


def swap(x, axis="core"):
    return lax.ppermute(x, axis, [(0, 1), (1, 0)])


def spread(x, copies):
    return jnp.broadcast_to(x[None], (copies,) + x.shape)


def take(x, index, axis):
    return lax.dynamic_index_in_dim(x, index, axis, keepdims=False)


def local(
    queries,
    cache_keys,
    cache_values,
    stretch_keys,
    stretch_values,
    block_lists,
    out_weight,
    residual,
    norm_gain,
    gate_weight,
    up_weight,
    down_weight,
):
    core = lax.axis_index("core")
    side = lax.axis_index("xl")
    col = lax.axis_index(COL)
    group = lax.axis_index(ZXH)
    me = lax.axis_index(ROW) * 8 + col
    local_blocks = cache_keys.shape[1] // BLK
    tokens_here = residual.shape[0]

    matched = block_lists // local_blocks == me
    within = jnp.sum(jnp.where(matched, block_lists % local_blocks, 0), axis=2)
    source = (jnp.arange(KV_HEADS, dtype=jnp.int32)[:, None] * local_blocks + within.T).reshape(-1)

    flat_keys = cache_keys.reshape(2 * KV_HEADS * local_blocks, BLK // 2, HEAD_DIM)
    flat_values = cache_values.reshape(2 * KV_HEADS * local_blocks, BLK // 2, HEAD_DIM)

    def fetch(half, stretch):
        part = BLK // 8
        near = lax.dynamic_slice_in_dim(stretch, group * part, part, 1)
        near = jnp.broadcast_to(near[:, None], (KV_HEADS, 8, part, HEAD_DIM)).reshape(64, part, HEAD_DIM)
        picked = 2 * source + half
        return exchange(jnp.concatenate([flat_keys[picked], flat_values[picked], near], axis=1), CHIP)

    first = fetch(0, stretch_keys)
    second = fetch(1, stretch_values)
    my_list = block_lists[col, group]
    place = jnp.stack([core, col]).astype(jnp.int32)
    other_queries = swap(queries)
    state = attend(my_list, place, queries, other_queries, (first,), (), local_blocks)
    own, send = attend(my_list, place, queries, other_queries, (first, second), state, local_blocks)
    attended = exchange(merge(own, swap(send), 8), COL).reshape(8, 2, tokens_here, -1)

    def row_sum(give, mine, pick, weight):
        both = product(mine, (weight,), 512, pick, add=swap(give))
        return jnp.sum(exchange(both.reshape(8, tokens_here, -1), ZXH).astype(f32), axis=0)

    give = product(attended, (out_weight,), 512, 1 - core)
    stream = residual.astype(f32) + row_sum(give, attended, core, out_weight)
    gain = norm_gain.astype(f32)[None, :]
    scaled = (stream * gain).astype(bf16)
    own_rows = exchange(spread(scaled, 8), ZXH)
    other_rows = swap(own_rows)

    by_pair = (4, 2, tokens_here, own_rows.shape[-1])
    where = jnp.stack([lax.axis_index("y"), side]).astype(jnp.int32)
    give, keep, *pieces, squares = partial_columns(
        where, own_rows.reshape(by_pair), other_rows.reshape(by_pair), gain, gate_weight, up_weight
    )
    got = swap(give, "xl")
    arrived = ring_start(pieces)
    here, there = ring_end(pieces, arrived, ring_middle(pieces, *arrived[:2]))
    squares = squares[1] + swap(squares[0], "xl")
    across = lax.ppermute(squares[2], "y", [(i, (i + 2) % 4) for i in range(4)])
    totals = squares[0] + across + to_right(squares[1]) + to_left(squares[3])
    factor = lax.rsqrt(totals[0] / D + 1e-05)
    joint = tokens_here + MOVED
    other_give = add_pieces(*there)
    got, other_give, factor = lax.optimization_barrier((got, other_give, factor))
    pieces = arranged_sum(got, keep)
    arrived = ring_start(pieces)
    near_sums, other_got = lax.optimization_barrier((arrived[:2], swap(other_give, "xl")))
    sums = ring_middle(pieces, *near_sums)
    other_hidden = gated((*here, other_got), None, factor[:joint])
    other_pair = (other_hidden, swap(other_hidden, "xl"))
    gates, ups, other_pair = lax.optimization_barrier((*ring_end(pieces, arrived, sums), other_pair))
    own_hidden = gated(gates, ups, factor[joint:])
    other_all = ring_gather(*other_pair)
    own_all = ring_gather(own_hidden, swap(own_hidden, "xl"))
    given, before = down_product(where, other_all, down_weight)
    down = down_product(where, own_all, down_weight, (before, swap(given)))
    mlp = jnp.sum(exchange(down, ZXH).astype(f32), axis=0)
    return (stream + mlp).astype(bf16)


def solution(mesh):
    mesh = Mesh(mesh.devices.reshape(4, 2, 2, 4, 2), AXES)
    in_specs = (
        P(COL, ROW),
        P(None, ROW + COL, None),
        P(None, ROW + COL, None),
        P(None, COL, None),
        P(None, COL, None),
        P(),
        P(ROW, COL),
        P(ROW, COL),
        P(COL),
        P(COL, ROW),
        P(COL, ROW),
        P(ROW, COL),
    )
    return jax.shard_map(local, mesh=mesh, in_specs=in_specs, out_specs=P(ROW, COL), check_vma=False)
```

time: 332 us -> 342 us (1.030)
  blocking collectives: 49.7 us -> 38.3 us
  starting transfers between devices: 60 us -> 70.2 us
  local copies, waits for them, and re-layouts: 12.7 us -> 22.1 us
  Pallas kernels: 41.1 us -> 50.2 us
  waiting for transfers between devices: 157 us -> 152 us
    ppermute x0 -> x1, waiting for transfers between devices: none -> 11.6 us  [local(): across = lax.ppermute(squares[2], 'y', [(i, (i + 2) % 4) for i in range(4)])]
    all_to_all x3 -> x2, blocking collectives: 49.7 us -> 38.3 us  [exchange(): return lax.all_to_all(x, axes, split_axis=0, concat_axis=0, tiled=True)]
    all_to_all x4, waiting for transfers between devices: 89 us -> 83.3 us  [exchange(): return lax.all_to_all(x, axes, split_axis=0, concat_axis=0, tiled=True)]
    ppermute x9 -> x10, waiting for transfers between devices: 23.7 us -> 18.2 us  [swap(): return lax.ppermute(x, axis, [(0, 1), (1, 0)])]
    unnamed x24 -> x54, local copies, waits for them, and re-layouts: 3.24 us -> 8.63 us
    ppermute x12 -> x13, waiting for transfers between devices: 20 us -> 15.6 us  [to_right(): return lax.ppermute(x, 'y', [(i, (i + 1) % 4) for i in range(4)])]
    pallas_call x3 -> x4, Pallas kernels: 20.9 us -> 25.1 us  [the longest x2 16.6 us: attend(): pl.pallas_call(functools.partial(attend_kernel, scale, local_blocks, len(...]
    pallas_call x1, Pallas kernels: 12.9 us -> 16.4 us  [partial_columns(): pl.pallas_call(spread_kernel, out_shape=shapes, grid_spec=pltpu.PrefetchS...]
  transfers between devices with their start and end apart: 37 -> 41, of which waited for: 22 -> 25; matrix products, arithmetic and copies ran while one was open for 3% -> 3% of each run, Pallas kernels for 2% -> 4%
where the time goes in v4:
time: 342 us; the launch traced here: 340 us
  waiting for transfers between devices  152 us (44%)
  starting transfers between devices  70.2 us (21%)
  Pallas kernels  50.2 us (15%)
  blocking collectives  38.3 us (11%)
  local copies, waits for them, and re-layouts  22.1 us (6%)
  other arithmetic  6.79 us (2%)
    all_to_all x4, waiting for transfers between devices, exchange(): return lax.all_to_all(x, axes, split_axis=0, concat_axis=0, tiled=True)  83.3 us
    all_to_all x2, blocking collectives, exchange(): return lax.all_to_all(x, axes, split_axis=0, concat_axis=0, tiled=True)  38.3 us
    all_to_all x4, starting transfers between devices, exchange(): return lax.all_to_all(x, axes, split_axis=0, concat_axis=0, tiled=True)  27.3 us
    ppermute x13, starting transfers between devices, to_left(): return lax.ppermute(x, 'y', [(i, (i + 3) % 4) for i in range(4)])  24.1 us
    ppermute x13, waiting for transfers between devices, to_left(): return lax.ppermute(x, 'y', [(i, (i + 3) % 4) for i in range(4)])  23.7 us
    ppermute x10, waiting for transfers between devices, swap(): return lax.ppermute(x, axis, [(0, 1), (1, 0)])  18.2 us
    pallas_call x2, Pallas kernels, attend(): pl.pallas_call(functools.partial(attend_kernel, scale, local_blocks, len(...  16.6 us
    pallas_call x1, Pallas kernels, partial_columns(): pl.pallas_call(spread_kernel, out_shape=shapes, grid_spec=pltpu.PrefetchS...  16.4 us
  transfers between devices with their start and end apart: 41, of which 25 were waited for; matrix products, arithmetic and copies ran while one was open for 3% of the time, Pallas kernels for 4%

profile of v4, /device:TPU:0, one launch (start us, length us, event | category | flops | bytes accessed | tf_op | source)
XLA Modules:
  0.0 340.5 jit_solution(11609451986692051210)
XLA Ops:
  2.4 3.3 gather_fusion
  6.5 2.8 pad_maximum_fusion
  9.3 11.7 %all-to-all-start = ((bf16[64,144,128]{2,1,0:T(8,128)(2,1)}), bf16[64,144,128]{2,1,0:T(8,128)(2,1)}, u32[]{:S(2)}, u32[]{:S(2)}) async-start(bf16[64,144,128]{2,1,0:T(8,128)(2,1)} %pad_maximum_fusion), calls=%async_computation | async-start | bytes 4718592 | tf_op jit(solution)/shard_map/all_to_all | solution.py:442
  25.7 27.4 %all-to-all-done.refs_0_ = bf16[64,144,128]{2,1,0:T(8,128)(2,1)} async-done(((bf16[64,144,128]{2,1,0:T(8,128)(2,1)}), bf16[64,144,128]{2,1,0:T(8,128)(2,1)}, u32[]{:S(2)}, u32[]{:S(2)}) %all-to-all-start) | async-done | bytes 2359328 | tf_op jit(solution)/shard_map/all_to_all | solution.py:442
  53.1 5.8 %all-to-all-start.1 = ((bf16[64,144,128]{2,1,0:T(8,128)(2,1)}), bf16[64,144,128]{2,1,0:T(8,128)(2,1)S(1)}, u32[]{:S(2)}, u32[]{:S(2)}) async-start(bf16[64,144,128]{2,1,0:T(8,128)(2,1)} %pad_maximum_fusion.1), calls=%async_computation.1 | async-start | bytes 4718592 | tf_op jit(solution)/shard_map/all_to_all | solution.py:442
  60.4 7.9 %shard_map.118 = (f32[136,512]{1,0:T(8,128)S(1)}, f32[136,512]{1,0:T(8,128)S(1)}) custom-call(s32[64]{0:T(128)S(1)} %fusion.8.list_ref, s32[2]{0:T(128)S(1)} %pad_add_fusion.place_ref, bf16[128,512]{1,0:T(8,128)(2,1)S(1)} %copy-done.16, bf16[128,512]{1,0:T(8,128)(2,1)S(1)} %collective-permute-done.other_q_ref, bf16[64,144,128]{2,1,0:T(8,128)(2,1)} %all-to-all-done.refs_0_), custom_call_target="tpu_custom_call" | custom-call | flops 1342177280 | bytes 4718592 | tf_op jit(solution)/shard_map/pallas_call | solution.py:126
  68.3 22.3 %all-to-all-done.1.refs_1_ = bf16[64,144,128]{2,1,0:T(8,128)(2,1)S(1)} async-done(((bf16[64,144,128]{2,1,0:T(8,128)(2,1)}), bf16[64,144,128]{2,1,0:T(8,128)(2,1)S(1)}, u32[]{:S(2)}, u32[]{:S(2)}) %all-to-all-start.1) | async-done | bytes 2359328 | tf_op jit(solution)/shard_map/all_to_all | solution.py:442
  90.7 8.6 %shard_map.119 = (f32[136,512]{1,0:T(8,128)S(1)}, f32[136,512]{1,0:T(8,128)S(1)}) custom-call(s32[64]{0:T(128)S(1)} %fusion.8.list_ref, s32[2]{0:T(128)S(1)} %pad_add_fusion.place_ref, bf16[128,512]{1,0:T(8,128)(2,1)S(1)} %copy-done.16, bf16[128,512]{1,0:T(8,128)(2,1)S(1)} %collective-permute-done.other_q_ref, bf16[64,144,128]{2,1,0:T(8,128)(2,1)} %all-to-all-done.refs_0_, ...), custom_call_target="tpu_custom_call" | custom-call | flops 1342177280 | bytes 4718592 | tf_op jit(solution)/shard_map/pallas_call | solution.py:126
  102.2 5.8 %all-to-all-start.2 = ((bf16[8,128,512]{2,1,0:T(8,128)(2,1)}), bf16[8,128,512]{2,1,0:T(8,128)(2,1)S(1)}, u32[]{:S(2)}, u32[]{:S(2)}) async-start(bf16[8,128,512]{2,1,0:T(8,128)(2,1)} %shard_map.120), calls=%async_computation.2 | async-start | bytes 2097152 | tf_op jit(solution)/shard_map/all_to_all | solution.py:442
  108.0 16.0 %all-to-all-done.2 = bf16[8,128,512]{2,1,0:T(8,128)(2,1)S(1)} async-done(((bf16[8,128,512]{2,1,0:T(8,128)(2,1)}), bf16[8,128,512]{2,1,0:T(8,128)(2,1)S(1)}, u32[]{:S(2)}, u32[]{:S(2)}) %all-to-all-start.2) | async-done | bytes 1048608 | tf_op jit(solution)/shard_map/all_to_all | solution.py:442
  124.8 2.6 collective-permute-done.2.refs_1_
  129.2 4.0 %all-to-all-start.3 = ((bf16[8,64,1024]{2,1,0:T(8,128)(2,1)}), bf16[8,64,1024]{2,1,0:T(8,128)(2,1)S(1)}, u32[]{:S(2)}, u32[]{:S(2)}) async-start(bf16[8,64,1024]{2,1,0:T(8,128)(2,1)} %bitcast.12), calls=%async_computation.3 | async-start | bytes 2097152 | tf_op jit(solution)/shard_map/all_to_all | solution.py:442
  133.2 17.5 %all-to-all-done.3 = bf16[8,64,1024]{2,1,0:T(8,128)(2,1)S(1)} async-done(((bf16[8,64,1024]{2,1,0:T(8,128)(2,1)}), bf16[8,64,1024]{2,1,0:T(8,128)(2,1)S(1)}, u32[]{:S(2)}, u32[]{:S(2)}) %all-to-all-start.3) | async-done | bytes 1048608 | tf_op jit(solution)/shard_map/all_to_all | solution.py:442
  151.8 20.0 %all_to_all.30 = bf16[8,64,1024]{2,1,0:T(8,128)(2,1)S(1)} all-to-all(bf16[8,64,1024]{2,1,0:T(8,128)(2,1)S(1)} %broadcast_in_dim.16), channel_id=1, replica_groups=mesh['z'=4,'xh'=2,'core'=2,'y'=4,'xl'=2] {'z','xh'}, dimensions={0} | all-to-all | bytes 2097152 | tf_op jit(solution)/shard_map/all_to_all | solution.py:442
  174.5 16.4 %shard_map.123 = (bf16[4,48,3584]{2,1,0:T(8,128)(2,1)S(1)}, bf16[4,48,3584]{2,1,0:T(8,128)(2,1)S(1)}, bf16[2,80,3584]{2,1,0:T(8,128)(2,1)S(1)}, bf16[2,80,3584]{...) custom-call(s32[2]{0:T(128)S(1)} %pad_add_fusion.1.place_ref, ...), custom_call_target="tpu_custom_call" | custom-call | flops 7516192768 | bytes 16777216 | tf_op jit(solution)/shard_map/pallas_call | solution.py:291
  194.8 3.1 collective-permute-start.9
  198.8 7.8 %collective-permute-done.6.refs_1_ = bf16[80,3584]{1,0:T(8,128)(2,1)S(1)} collective-permute-done((bf16[80,3584]{1,0:T(8,128)(2,1)S(1)}, bf16[80,3584]{1,0:T(8,128)(2,1)S(1)}, u32[]{:S(2)}, u32[]{:S(2)}) %collective-permute-start.6) | collective-permute-done | bytes 573472 | tf_op jit(solution)/shard_map/ppermute | solution.py:416
  208.0 11.6 %collective-permute-done.9 = f32[8,128]{1,0:T(8,128)S(1)} collective-permute-done((f32[8,128]{1,0:T(8,128)S(1)}, f32[8,128]{1,0:T(8,128)S(1)}, u32[]{:S(2)}, u32[]{:S(2)}) %collective-permute-start.9) | collective-permute-done | bytes 4128 | tf_op jit(solution)/shard_map/ppermute | solution.py:522
  219.6 3.2 collective-permute-start.7
  227.5 8.8 %collective-permute-done.7.refs_2_ = bf16[80,3584]{1,0:T(8,128)(2,1)S(1)} collective-permute-done((bf16[80,3584]{1,0:T(8,128)(2,1)S(1)}, bf16[80,3584]{1,0:T(8,128)(2,1)S(1)}, u32[]{:S(2)}, u32[]{:S(2)}) %collective-permute-start.7) | collective-permute-done | bytes 573472 | tf_op jit(solution)/shard_map/ppermute | solution.py:416
  247.7 3.6 %collective-permute-done.14.refs_1_ = bf16[48,1792]{1,0:T(8,128)(2,1)} collective-permute-done((bf16[48,1792]{1,0:T(8,128)(2,1)}, bf16[48,1792]{1,0:T(8,128)(2,1)}, u32[]{:S(2)}, u32[]{:S(2)}) %collective-permute-start.14) | collective-permute-done | bytes 172064 | tf_op jit(solution)/shard_map/ppermute | solution.py:416
  267.2 3.2 collective-permute-start.31
  272.4 5.7 %collective-permute-done.32.refs_6_ = bf16[80,1792]{1,0:T(8,128)(2,1)S(1)} collective-permute-done((bf16[80,1792]{1,0:T(8,128)(2,1)S(1)}, bf16[80,1792]{1,0:T(8,128)(2,1)S(1)}, u32[]{:S(2)}, u32[]{:S(2)}) %collective-permute-start.32) | collective-permute-done | bytes 286752 | tf_op jit(solution)/shard_map/ppermute | solution.py:412
  278.1 3.2 collective-permute-start.34
  281.7 4.3 %collective-permute-done.33.refs_4_ = bf16[80,1792]{1,0:T(8,128)(2,1)S(1)} collective-permute-done((bf16[80,1792]{1,0:T(8,128)(2,1)S(1)}, bf16[80,1792]{1,0:T(8,128)(2,1)S(1)}, u32[]{:S(2)}, u32[]{:S(2)}) %collective-permute-start.33) | collective-permute-done | bytes 286752 | tf_op jit(solution)/shard_map/ppermute | solution.py:412
  286.0 5.0 %shard_map.132 = (bf16[8,64,1024]{2,1,0:T(8,128)(2,1)}, f32[8,16,1024]{2,1,0:T(8,128)S(1)}) custom-call(s32[2]{0:T(128)S(1)} %copy-done.18, bf16[80,1792]{1,0:T(8,128)(2,1)S(1)} %shard_map.130.refs_0_, bf16[80,1792]{1,0:T(8,128)(2,1)S(1)} %collective-permute-done.22.refs_1_, bf16[80,1792]{1,0:T(8,128)(2,1)S(1)} %collective-permute-done.30.refs_2_, ...), custom_call_target="tpu_custom_call" | custom-call | flops 2348810240 | bytes 7274496 | tf_op jit(solution)/shard_map/pallas_call | solution.py:393
  294.0 6.0 %collective-permute-done.23.refs_1_ = bf16[48,1792]{1,0:T(8,128)(2,1)S(1)} collective-permute-done((bf16[48,1792]{1,0:T(8,128)(2,1)S(1)}, bf16[48,1792]{1,0:T(8,128)(2,1)S(1)}, u32[]{:S(2)}, u32[]{:S(2)}) %collective-permute-start.23) | collective-permute-done | bytes 172064 | tf_op jit(solution)/shard_map/ppermute | solution.py:446
  300.0 3.2 collective-permute-start.25
  305.3 2.7 collective-permute-done.25.refs_3_
  308.0 3.7 %collective-permute-start.28 = (bf16[48,1792]{1,0:T(8,128)(2,1)S(1)}, bf16[48,1792]{1,0:T(8,128)(2,1)S(1)}, u32[]{:S(2)}, u32[]{:S(2)}) collective-permute-start(bf16[48,1792]{1,0:T(8,128)(2,1)S(1)} %collective-permute-done.25.refs_3_), channel_id=1, source_target_pairs={{0,6},{2,0},{4,2},{6,4},{1,7},{3,1},{5,3},{7,5},{8,14},{10,8},{12,... | collective-permute-start | bytes 516104 | tf_op jit(solution)/shard_map/ppermute | solution.py:416
  317.7 3.5 %shard_map.133 = bf16[8,64,1024]{2,1,0:T(8,128)(2,1)S(1)} custom-call(s32[2]{0:T(128)S(1)} %copy-done.18, bf16[48,1792]{1,0:T(8,128)(2,1)S(1)} %shard_map.131.refs_0_, bf16[48,1792]{1,0:T(8,128)(2,1)S(1)} %collective-permute-done.23.refs_1_, bf16[48,1792]{1,0:T(8,128)(2,1)S(1)} %collective-permute-done.24.refs_2_, ...), custom_call_target="tpu_custom_call" | custom-call | flops 1409286144 | bytes 5832704 | tf_op jit(solution)/shard_map/pallas_call | solution.py:393
  321.3 18.3 %all_to_all.31 = bf16[8,64,1024]{2,1,0:T(8,128)(2,1)S(1)} all-to-all(bf16[8,64,1024]{2,1,0:T(8,128)(2,1)S(1)} %shard_map.133), channel_id=1, replica_groups=mesh['z'=4,'xh'=2,'core'=2,'y'=4,'xl'=2] {'z','xh'}, dimensions={0} | all-to-all | bytes 2097152 | tf_op jit(solution)/shard_map/all_to_all | solution.py:442
  (162 shorter events, 70.6 us)
Async XLA Ops:
  9.3 43.9 %all-to-all-start = ((bf16[64,144,128]{2,1,0:T(8,128)(2,1)}), bf16[64,144,128]{2,1,0:T(8,128)(2,1)}, u32[]{:S(2)}, u32[]{:S(2)}) async-start(bf16[64,144,128]{2,1,0:T(8,128)(2,1)} %pad_maximum_fusion), calls=%async_computation | async-start | bytes 4718592 | tf_op jit(solution)/shard_map/all_to_all | solution.py:442
  53.1 37.5 %all-to-all-start.1 = ((bf16[64,144,128]{2,1,0:T(8,128)(2,1)}), bf16[64,144,128]{2,1,0:T(8,128)(2,1)S(1)}, u32[]{:S(2)}, u32[]{:S(2)}) async-start(bf16[64,144,128]{2,1,0:T(8,128)(2,1)} %pad_maximum_fusion.1), calls=%async_computation.1 | async-start | bytes 4718592 | tf_op jit(solution)/shard_map/all_to_all | solution.py:442
  102.2 21.8 %all-to-all-start.2 = ((bf16[8,128,512]{2,1,0:T(8,128)(2,1)}), bf16[8,128,512]{2,1,0:T(8,128)(2,1)S(1)}, u32[]{:S(2)}, u32[]{:S(2)}) async-start(bf16[8,128,512]{2,1,0:T(8,128)(2,1)} %shard_map.120), calls=%async_computation.2 | async-start | bytes 2097152 | tf_op jit(solution)/shard_map/all_to_all | solution.py:442
  129.2 21.6 %all-to-all-start.3 = ((bf16[8,64,1024]{2,1,0:T(8,128)(2,1)}), bf16[8,64,1024]{2,1,0:T(8,128)(2,1)S(1)}, u32[]{:S(2)}, u32[]{:S(2)}) async-start(bf16[8,64,1024]{2,1,0:T(8,128)(2,1)} %bitcast.12), calls=%async_computation.3 | async-start | bytes 2097152 | tf_op jit(solution)/shard_map/all_to_all | solution.py:442
  191.8 14.8 %collective-permute-start.6 = (bf16[80,3584]{1,0:T(8,128)(2,1)S(1)}, bf16[80,3584]{1,0:T(8,128)(2,1)S(1)}, u32[]{:S(2)}, u32[]{:S(2)}) collective-permute-start(bf16[80,3584]{1,0:T(8,128)(2,1)S(1)} %get-tuple-element.46), channel_id=1, source_target_pairs={{0,6},{2,0},{4,2},{6,4},{1,7},{3,1},{5,3},{7,5},{8,14},{10,8},{12,... | collective-permute-start | bytes 1720328 | tf_op jit(solution)/shard_map/ppermute | solution.py:416
  193.0 31.5 %collective-permute-start.20 = (bf16[80,3584]{1,0:T(8,128)(2,1)S(1)}, bf16[80,3584]{1,0:T(8,128)(2,1)S(1)}, u32[]{:S(2)}, u32[]{:S(2)}) collective-permute-start(bf16[80,3584]{1,0:T(8,128)(2,1)S(1)} %get-tuple-element.58), channel_id=1, source_target_pairs={{0,2},{2,4},{4,6},{6,0},{1,3},{3,5},{5,7},{7,1},{8,10},{10,12},{12... | collective-permute-start | bytes 1720328 | tf_op jit(solution)/shard_map/ppermute | solution.py:412
  193.9 33.6 %collective-permute-start.5 = (bf16[80,3584]{1,0:T(8,128)(2,1)S(1)}, bf16[80,3584]{1,0:T(8,128)(2,1)S(1)}, u32[]{:S(2)}, u32[]{:S(2)}) collective-permute-start(bf16[80,3584]{1,0:T(8,128)(2,1)S(1)} %get-tuple-element.72), channel_id=1, source_target_pairs={{0,2},{2,4},{4,6},{6,0},{1,3},{3,5},{5,7},{7,1},{8,10},{10,12},{12... | collective-permute-start | bytes 1720328 | tf_op jit(solution)/shard_map/ppermute | solution.py:412
  194.8 24.8 %collective-permute-start.9 = (f32[8,128]{1,0:T(8,128)S(1)}, f32[8,128]{1,0:T(8,128)S(1)}, u32[]{:S(2)}, u32[]{:S(2)}) collective-permute-start(f32[8,128]{1,0:T(8,128)S(1)} %get-tuple-element.83), channel_id=1, source_target_pairs={{0,4},{2,6},{4,0},{6,2},{1,5},{3,7},{5,1},{7,3},{8,12},{10,14},{12... | collective-permute-start | bytes 12296 | tf_op jit(solution)/shard_map/ppermute | solution.py:522
  197.9 21.7 %collective-permute-start.11 = (f32[8,128]{1,0:T(8,128)S(1)}, f32[8,128]{1,0:T(8,128)S(1)}, u32[]{:S(2)}, u32[]{:S(2)}) collective-permute-start(f32[8,128]{1,0:T(8,128)S(1)} %get-tuple-element.84), channel_id=1, source_target_pairs={{0,6},{2,0},{4,2},{6,4},{1,7},{3,1},{5,3},{7,5},{8,14},{10,8},{12,... | collective-permute-start | bytes 12296 | tf_op jit(solution)/shard_map/ppermute | solution.py:416
  206.6 31.0 %collective-permute-start.4 = (bf16[4,48,3584]{2,1,0:T(8,128)(2,1)S(1)}, bf16[4,48,3584]{2,1,0:T(8,128)(2,1)S(1)}, u32[]{:S(2)}, u32[]{:S(2)}) collective-permute-start(bf16[4,48,3584]{2,1,0:T(8,128)(2,1)S(1)} %get-tuple-element.42), channel_id=1, source_target_pairs={{0,1},{1,0},{2,3},{3,2},{4,5},{5,4},{6,7},{7,6},{8,9},{9,8},{10,11... | collective-permute-start | bytes 4128776 | tf_op jit(solution)/shard_map/ppermute | solution.py:446
  219.6 16.7 %collective-permute-start.7 = (bf16[80,3584]{1,0:T(8,128)(2,1)S(1)}, bf16[80,3584]{1,0:T(8,128)(2,1)S(1)}, u32[]{:S(2)}, u32[]{:S(2)}) collective-permute-start(bf16[80,3584]{1,0:T(8,128)(2,1)S(1)} %shard_map.124), channel_id=1, source_target_pairs={{0,6},{2,0},{4,2},{6,4},{1,7},{3,1},{5,3},{7,5},{8,14},{10,8},{12,... | collective-permute-start | bytes 1720328 | tf_op jit(solution)/shard_map/ppermute | solution.py:416
  224.4 33.5 %collective-permute-start.19 = (bf16[80,3584]{1,0:T(8,128)(2,1)}, bf16[80,3584]{1,0:T(8,128)(2,1)S(1)}, u32[]{:S(2)}, u32[]{:S(2)}) collective-permute-start(bf16[80,3584]{1,0:T(8,128)(2,1)} %get-tuple-element.73), channel_id=1, source_target_pairs={{0,6},{2,0},{4,2},{6,4},{1,7},{3,1},{5,3},{7,5},{8,14},{10,8},{12,... | collective-permute-start | bytes 1720328 | tf_op jit(solution)/shard_map/ppermute | solution.py:416
  225.5 33.5 %collective-permute-start.21 = (bf16[80,3584]{1,0:T(8,128)(2,1)}, bf16[80,3584]{1,0:T(8,128)(2,1)S(1)}, u32[]{:S(2)}, u32[]{:S(2)}) collective-permute-start(bf16[80,3584]{1,0:T(8,128)(2,1)} %shard_map.129), channel_id=1, source_target_pairs={{0,2},{2,4},{4,6},{6,0},{1,3},{3,5},{5,7},{7,1},{8,10},{10,12},{12... | collective-permute-start | bytes 1720328 | tf_op jit(solution)/shard_map/ppermute | solution.py:412
  238.6 7.8 %collective-permute-start.13 = (bf16[48,1792]{1,0:T(8,128)(2,1)}, bf16[48,1792]{1,0:T(8,128)(2,1)}, u32[]{:S(2)}, u32[]{:S(2)}) collective-permute-start(bf16[48,1792]{1,0:T(8,128)(2,1)} %get-tuple-element.53), channel_id=1, source_target_pairs={{0,2},{2,4},{4,6},{6,0},{1,3},{3,5},{5,7},{7,1},{8,10},{10,12},{12... | collective-permute-start | bytes 516104 | tf_op jit(solution)/shard_map/ppermute | solution.py:412
  239.2 12.1 %collective-permute-start.14 = (bf16[48,1792]{1,0:T(8,128)(2,1)}, bf16[48,1792]{1,0:T(8,128)(2,1)}, u32[]{:S(2)}, u32[]{:S(2)}) collective-permute-start(bf16[48,1792]{1,0:T(8,128)(2,1)} %get-tuple-element.54), channel_id=1, source_target_pairs={{0,6},{2,0},{4,2},{6,4},{1,7},{3,1},{5,3},{7,5},{8,14},{10,8},{12,... | collective-permute-start | bytes 516104 | tf_op jit(solution)/shard_map/ppermute | solution.py:416
  242.5 12.3 %collective-permute-start.15 = (bf16[80,3584]{1,0:T(8,128)(2,1)S(1)}, bf16[80,3584]{1,0:T(8,128)(2,1)S(1)}, u32[]{:S(2)}, u32[]{:S(2)}) collective-permute-start(bf16[80,3584]{1,0:T(8,128)(2,1)S(1)} %shard_map.125), channel_id=1, source_target_pairs={{0,1},{1,0},{2,3},{3,2},{4,5},{5,4},{6,7},{7,6},{8,9},{9,8},{10,11... | collective-permute-start | bytes 1720328 | tf_op jit(solution)/shard_map/ppermute | solution.py:446
  246.3 15.4 %collective-permute-start.12 = (bf16[48,1792]{1,0:T(8,128)(2,1)}, bf16[48,1792]{1,0:T(8,128)(2,1)S(1)}, u32[]{:S(2)}, u32[]{:S(2)}) collective-permute-start(bf16[48,1792]{1,0:T(8,128)(2,1)} %get-tuple-element.78), channel_id=1, source_target_pairs={{0,6},{2,0},{4,2},{6,4},{1,7},{3,1},{5,3},{7,5},{8,14},{10,8},{12,... | collective-permute-start | bytes 516104 | tf_op jit(solution)/shard_map/ppermute | solution.py:416
  251.3 11.1 %collective-permute-start.17 = (bf16[48,1792]{1,0:T(8,128)(2,1)}, bf16[48,1792]{1,0:T(8,128)(2,1)S(1)}, u32[]{:S(2)}, u32[]{:S(2)}) collective-permute-start(bf16[48,1792]{1,0:T(8,128)(2,1)} %get-tuple-element.79), channel_id=1, source_target_pairs={{0,2},{2,4},{4,6},{6,0},{1,3},{3,5},{5,7},{7,1},{8,10},{10,12},{12... | collective-permute-start | bytes 516104 | tf_op jit(solution)/shard_map/ppermute | solution.py:412
  255.8 7.3 %collective-permute-start.18 = (bf16[48,1792]{1,0:T(8,128)(2,1)S(1)}, bf16[48,1792]{1,0:T(8,128)(2,1)S(1)}, u32[]{:S(2)}, u32[]{:S(2)}) collective-permute-start(bf16[48,1792]{1,0:T(8,128)(2,1)S(1)} %shard_map.128), channel_id=1, source_target_pairs={{0,6},{2,0},{4,2},{6,4},{1,7},{3,1},{5,3},{7,5},{8,14},{10,8},{12,... | collective-permute-start | bytes 516104 | tf_op jit(solution)/shard_map/ppermute | solution.py:416
  267.1 11.1 %collective-permute-start.32 = (bf16[80,1792]{1,0:T(8,128)(2,1)S(1)}, bf16[80,1792]{1,0:T(8,128)(2,1)S(1)}, u32[]{:S(2)}, u32[]{:S(2)}) collective-permute-start(bf16[80,1792]{1,0:T(8,128)(2,1)S(1)} %shard_map.130.refs_0_), channel_id=1, source_target_pairs={{0,2},{2,4},{4,6},{6,0},{1,3},{3,5},{5,7},{7,1},{8,10},{10,12},{12... | collective-permute-start | bytes 860168 | tf_op jit(solution)/shard_map/ppermute | solution.py:412
  267.2 11.0 %collective-permute-start.31 = (bf16[80,1792]{1,0:T(8,128)(2,1)S(1)}, bf16[80,1792]{1,0:T(8,128)(2,1)S(1)}, u32[]{:S(2)}, u32[]{:S(2)}) collective-permute-start(bf16[80,1792]{1,0:T(8,128)(2,1)S(1)} %collective-permute-done.22.refs_1_), channel_id=1, source_target_pairs={{0,6},{2,0},{4,2},{6,4},{1,7},{3,1},{5,3},{7,5},{8,14},{10,8},{12,... | collective-permute-start | bytes 860168 | tf_op jit(solution)/shard_map/ppermute | solution.py:416
  270.4 11.0 %collective-permute-start.30 = (bf16[80,1792]{1,0:T(8,128)(2,1)S(1)}, bf16[80,1792]{1,0:T(8,128)(2,1)S(1)}, u32[]{:S(2)}, u32[]{:S(2)}) collective-permute-start(bf16[80,1792]{1,0:T(8,128)(2,1)S(1)} %shard_map.130.refs_0_), channel_id=1, source_target_pairs={{0,6},{2,0},{4,2},{6,4},{1,7},{3,1},{5,3},{7,5},{8,14},{10,8},{12,... | collective-permute-start | bytes 860168 | tf_op jit(solution)/shard_map/ppermute | solution.py:416
  271.5 10.1 %collective-permute-start.35 = (bf16[80,1792]{1,0:T(8,128)(2,1)S(1)}, bf16[80,1792]{1,0:T(8,128)(2,1)S(1)}, u32[]{:S(2)}, u32[]{:S(2)}) collective-permute-start(bf16[80,1792]{1,0:T(8,128)(2,1)S(1)} %collective-permute-done.22.refs_1_), channel_id=1, source_target_pairs={{0,2},{2,4},{4,6},{6,0},{1,3},{3,5},{5,7},{7,1},{8,10},{10,12},{12... | collective-permute-start | bytes 860168 | tf_op jit(solution)/shard_map/ppermute | solution.py:412
  278.1 7.8 %collective-permute-start.33 = (bf16[80,1792]{1,0:T(8,128)(2,1)S(1)}, bf16[80,1792]{1,0:T(8,128)(2,1)S(1)}, u32[]{:S(2)}, u32[]{:S(2)}) collective-permute-start(bf16[80,1792]{1,0:T(8,128)(2,1)S(1)} %collective-permute-done.32.refs_6_), channel_id=1, source_target_pairs={{0,2},{2,4},{4,6},{6,0},{1,3},{3,5},{5,7},{7,1},{8,10},{10,12},{12... | collective-permute-start | bytes 860168 | tf_op jit(solution)/shard_map/ppermute | solution.py:412
  278.1 7.8 %collective-permute-start.34 = (bf16[80,1792]{1,0:T(8,128)(2,1)S(1)}, bf16[80,1792]{1,0:T(8,128)(2,1)S(1)}, u32[]{:S(2)}, u32[]{:S(2)}) collective-permute-start(bf16[80,1792]{1,0:T(8,128)(2,1)S(1)} %collective-permute-done.31.refs_3_), channel_id=1, source_target_pairs={{0,6},{2,0},{4,2},{6,4},{1,7},{3,1},{5,3},{7,5},{8,14},{10,8},{12,... | collective-permute-start | bytes 860168 | tf_op jit(solution)/shard_map/ppermute | solution.py:416
  291.8 22.9 %collective-permute-start.36 = (bf16[8,64,1024]{2,1,0:T(8,128)(2,1)}, bf16[8,64,1024]{2,1,0:T(8,128)(2,1)S(1)}, u32[]{:S(2)}, u32[]{:S(2)}) collective-permute-start(bf16[8,64,1024]{2,1,0:T(8,128)(2,1)} %get-tuple-element.70), channel_id=1, source_target_pairs={{0,8},{8,0},{1,9},{9,1},{2,10},{10,2},{3,11},{11,3},{4,12},{12,4},... | collective-permute-start | bytes 3145736 | tf_op jit(solution)/shard_map/ppermute | solution.py:446
  293.1 6.9 %collective-permute-start.23 = (bf16[48,1792]{1,0:T(8,128)(2,1)S(1)}, bf16[48,1792]{1,0:T(8,128)(2,1)S(1)}, u32[]{:S(2)}, u32[]{:S(2)}) collective-permute-start(bf16[48,1792]{1,0:T(8,128)(2,1)S(1)} %shard_map.131.refs_0_), channel_id=1, source_target_pairs={{0,1},{1,0},{2,3},{3,2},{4,5},{5,4},{6,7},{7,6},{8,9},{9,8},{10,11... | collective-permute-start | bytes 516104 | tf_op jit(solution)/shard_map/ppermute | solution.py:446
  294.0 11.3 %collective-permute-start.26 = (bf16[48,1792]{1,0:T(8,128)(2,1)S(1)}, bf16[48,1792]{1,0:T(8,128)(2,1)S(1)}, u32[]{:S(2)}, u32[]{:S(2)}) collective-permute-start(bf16[48,1792]{1,0:T(8,128)(2,1)S(1)} %shard_map.131.refs_0_), channel_id=1, source_target_pairs={{0,2},{2,4},{4,6},{6,0},{1,3},{3,5},{5,7},{7,1},{8,10},{10,12},{12... | collective-permute-start | bytes 516104 | tf_op jit(solution)/shard_map/ppermute | solution.py:412
  300.0 8.0 %collective-permute-start.25 = (bf16[48,1792]{1,0:T(8,128)(2,1)S(1)}, bf16[48,1792]{1,0:T(8,128)(2,1)S(1)}, u32[]{:S(2)}, u32[]{:S(2)}) collective-permute-start(bf16[48,1792]{1,0:T(8,128)(2,1)S(1)} %collective-permute-done.23.refs_1_), channel_id=1, source_target_pairs={{0,6},{2,0},{4,2},{6,4},{1,7},{3,1},{5,3},{7,5},{8,14},{10,8},{12,... | collective-permute-start | bytes 516104 | tf_op jit(solution)/shard_map/ppermute | solution.py:416
  303.2 8.5 %collective-permute-start.24 = (bf16[48,1792]{1,0:T(8,128)(2,1)S(1)}, bf16[48,1792]{1,0:T(8,128)(2,1)S(1)}, u32[]{:S(2)}, u32[]{:S(2)}) collective-permute-start(bf16[48,1792]{1,0:T(8,128)(2,1)S(1)} %shard_map.131.refs_0_), channel_id=1, source_target_pairs={{0,6},{2,0},{4,2},{6,4},{1,7},{3,1},{5,3},{7,5},{8,14},{10,8},{12,... | collective-permute-start | bytes 516104 | tf_op jit(solution)/shard_map/ppermute | solution.py:416
  303.3 10.6 %collective-permute-start.29 = (bf16[48,1792]{1,0:T(8,128)(2,1)S(1)}, bf16[48,1792]{1,0:T(8,128)(2,1)S(1)}, u32[]{:S(2)}, u32[]{:S(2)}) collective-permute-start(bf16[48,1792]{1,0:T(8,128)(2,1)S(1)} %collective-permute-done.23.refs_1_), channel_id=1, source_target_pairs={{0,2},{2,4},{4,6},{6,0},{1,3},{3,5},{5,7},{7,1},{8,10},{10,12},{12... | collective-permute-start | bytes 516104 | tf_op jit(solution)/shard_map/ppermute | solution.py:412
  305.3 8.6 %collective-permute-start.27 = (bf16[48,1792]{1,0:T(8,128)(2,1)S(1)}, bf16[48,1792]{1,0:T(8,128)(2,1)S(1)}, u32[]{:S(2)}, u32[]{:S(2)}) collective-permute-start(bf16[48,1792]{1,0:T(8,128)(2,1)S(1)} %collective-permute-done.26.refs_6_), channel_id=1, source_target_pairs={{0,2},{2,4},{4,6},{6,0},{1,3},{3,5},{5,7},{7,1},{8,10},{10,12},{12... | collective-permute-start | bytes 516104 | tf_op jit(solution)/shard_map/ppermute | solution.py:412
  (36 other events, 451.6 us)

commit v5 on v3

--- a/solution.py
+++ b/solution.py
@@ -31,50 +31,47 @@
     return lax.dot_general(a, b, (((0,), (0,)), ((), ())), preferred_element_type=f32)
 
 
-def attend_kernel(
-    scale,
-    per_step,
-    local_blocks,
-    list_ref,
-    place_ref,
-    own_q_ref,
-    other_q_ref,
-    keys_ref,
-    values_ref,
-    own_ref,
-    send_ref,
-    order_ref,
-    q_ref,
-    top_ref,
-    sum_ref,
-    acc_ref,
-):
-    core = place_ref[0]
-    block = place_ref[1]
-    length = list_ref.shape[0]
+def attend_kernel(scale, per_step, local_blocks, last, *refs):
+    if last:
+        order_ref, own_q_ref, other_q_ref, chunk_ref, own_in_ref, send_in_ref = refs[:6]
+    else:
+        list_ref, place_ref, own_q_ref, other_q_ref, chunk_ref = refs[:5]
+        order_ref = refs[7]
+    own_ref, send_ref = refs[6:8] if last else refs[5:7]
+    q_ref, top_ref, sum_ref, acc_ref = refs[-4:]
+    length = order_ref.shape[0] - 1
+    part_rows = (chunk_ref.shape[1] - (0 if last else BLK // 4)) // 2
     heads = own_q_ref.shape[1] // HEAD_DIM
     rows = heads * BLK
     for h in range(heads):
         cols = pl.ds(h * HEAD_DIM, HEAD_DIM)
         q_ref[pl.ds(h * BLK, BLK), :] = own_q_ref[:, cols]
         q_ref[pl.ds(rows + h * BLK, BLK), :] = other_q_ref[:, cols]
-    top_ref[...] = jnp.full_like(top_ref, NEG)
-    sum_ref[...] = jnp.zeros_like(sum_ref)
-    acc_ref[...] = jnp.zeros_like(acc_ref)
-
-    def collect(i, count):
-        device = list_ref[i] // local_blocks
-        row = device // 8
-        order_ref[count] = (row // 2) * 8 + device % 8
-        return count + jnp.where(row % 2 == core, 1, 0)
-
-    count = lax.fori_loop(0, length, collect, jnp.int32(0))
+    if last:
+        for half, ref in ((0, own_in_ref), (1, send_in_ref)):
+            acc_ref[half] = ref[0:HEAD_DIM, :]
+            top_ref[half] = ref[HEAD_DIM : HEAD_DIM + 1, :]
+            sum_ref[half] = ref[HEAD_DIM + 1 : HEAD_DIM + 2, :]
+        count = order_ref[length]
+    else:
+        core = place_ref[0]
+        block = place_ref[1]
+        top_ref[...] = jnp.full_like(top_ref, NEG)
+        sum_ref[...] = jnp.zeros_like(sum_ref)
+        acc_ref[...] = jnp.zeros_like(acc_ref)
+
+        def collect(i, count):
+            device = list_ref[i] // local_blocks
+            row = device // 8
+            order_ref[count] = (row // 2) * 8 + device % 8
+            return count + jnp.where(row % 2 == core, 1, 0)
+
+        count = lax.fori_loop(0, length, collect, jnp.int32(0))
+        order_ref[length] = count
 
     def update(half, keys, values, bias):
         part = pl.ds(half * rows, rows)
-        scores = nt_dot(keys, q_ref[part, :]) * scale
-        if bias is not None:
-            scores = scores + bias
+        scores = nt_dot(keys, q_ref[part, :]) * scale + bias
         old = top_ref[half]
         new = jnp.maximum(old, jnp.max(scores, axis=0, keepdims=True))
         weights = jnp.exp2(scores - new)
@@ -84,12 +81,12 @@
         acc_ref[half] = acc_ref[half] * decay + tn_dot(values, weights.astype(bf16))
 
     def far(step, carry):
-        slots = [jnp.minimum(step * per_step + i, count - 1) for i in range(per_step)]
-        keys = jnp.concatenate([keys_ref[order_ref[s], 0:BLK] for s in slots], axis=0)
-        values = jnp.concatenate([values_ref[order_ref[s], 0:BLK] for s in slots], axis=0)
+        slots = [order_ref[jnp.minimum(step * per_step + i, count - 1)] for i in range(per_step)]
+        keys = jnp.concatenate([chunk_ref[s, 0:part_rows] for s in slots], axis=0)
+        values = jnp.concatenate([chunk_ref[s, part_rows : 2 * part_rows] for s in slots], axis=0)
         bias = jnp.concatenate(
             [
-                jnp.full((BLK, 1), jnp.where(step * per_step + i < count, 0.0, NEG), f32)
+                jnp.full((part_rows, 1), jnp.where(step * per_step + i < count, 0.0, NEG), f32)
                 for i in range(per_step)
             ],
             axis=0,
@@ -106,46 +103,52 @@
         key_pos = lax.broadcasted_iota(jnp.int32, (BLK, rows), 0)
         token = lax.broadcasted_iota(jnp.int32, (BLK, rows), 1) % BLK
         bias = jnp.where(key_pos <= token + shift, 0.0, NEG)
-        keys = jnp.concatenate([keys_ref[i * 8 + which, BLK:] for i in range(8)], axis=0)
-        values = jnp.concatenate([values_ref[i * 8 + which, BLK:] for i in range(8)], axis=0)
+        at = 2 * part_rows
+        eighth = BLK // 8
+        keys = jnp.concatenate([chunk_ref[i * 8 + which, at : at + eighth] for i in range(8)], axis=0)
+        values = jnp.concatenate([chunk_ref[i * 8 + which, at + eighth :] for i in range(8)], axis=0)
         for half in range(2):
             update(half, keys, values, bias)
         return carry
 
-    lax.fori_loop(0, (block - core + 2) // 2, near, 0)
-    own_ref[0:HEAD_DIM, :] = acc_ref[0]
-    own_ref[HEAD_DIM : HEAD_DIM + 1, :] = top_ref[0]
-    own_ref[HEAD_DIM + 1 : HEAD_DIM + 2, :] = sum_ref[0]
-    send_ref[0:HEAD_DIM, :] = acc_ref[1]
-    send_ref[HEAD_DIM : HEAD_DIM + 1, :] = top_ref[1]
-    send_ref[HEAD_DIM + 1 : HEAD_DIM + 2, :] = sum_ref[1]
-
-
-def attend(my_list, place, own_q, other_q, keys, values, local_blocks):
+    if not last:
+        lax.fori_loop(0, (block - core + 2) // 2, near, 0)
+    for half, ref in ((0, own_ref), (1, send_ref)):
+        ref[0:HEAD_DIM, :] = acc_ref[half]
+        ref[HEAD_DIM : HEAD_DIM + 1, :] = top_ref[half]
+        ref[HEAD_DIM + 1 : HEAD_DIM + 2, :] = sum_ref[half]
+
+
+def attend(scalars, own_q, other_q, chunk, state, local_blocks, per_step):
     heads = own_q.shape[1] // HEAD_DIM
     rows = heads * BLK
+    length = scalars[0].shape[0] - len(state) // 2
     packed = jax.ShapeDtypeStruct((HEAD_DIM + 8, rows), f32)
     smem = pl.BlockSpec(memory_space=pltpu.SMEM)
     vmem = pl.BlockSpec(memory_space=pltpu.VMEM)
+    scale = math.log2(math.e) / math.sqrt(HEAD_DIM)
+    arrays = [own_q, other_q, chunk, *state]
+    outs = [packed, packed]
+    if not state:
+        outs.append(jax.ShapeDtypeStruct((length + 1,), jnp.int32))
     return pl.pallas_call(
-        functools.partial(attend_kernel, math.log2(math.e) / math.sqrt(HEAD_DIM), 4, local_blocks),
-        out_shape=(packed, packed),
-        in_specs=[smem, smem] + [vmem] * 4,
-        out_specs=(vmem, vmem),
+        functools.partial(attend_kernel, scale, per_step, local_blocks, len(state) > 0),
+        out_shape=outs,
+        in_specs=[smem] * len(scalars) + [vmem] * len(arrays),
+        out_specs=[vmem, vmem, smem][: len(outs)],
         scratch_shapes=[
-            pltpu.SMEM((my_list.shape[0] + 1,), jnp.int32),
             pltpu.VMEM((2 * rows, HEAD_DIM), bf16),
             pltpu.VMEM((2, 1, rows), f32),
             pltpu.VMEM((2, 1, rows), f32),
             pltpu.VMEM((2, HEAD_DIM, rows), f32),
         ],
-        compiler_params=pltpu.CompilerParams(vmem_limit_bytes=20 * 1024 * 1024),
+        compiler_params=pltpu.CompilerParams(vmem_limit_bytes=24 * 1024 * 1024),
         cost_estimate=pl.CostEstimate(
-            flops=4 * 2 * rows * 40 * BLK * HEAD_DIM,
-            bytes_accessed=2 * keys.size * 2,
-            transcendentals=2 * rows * 40 * BLK,
+            flops=2 * rows * 40 * chunk.shape[1] * HEAD_DIM,
+            bytes_accessed=2 * chunk.size,
+            transcendentals=rows * 40 * chunk.shape[1],
         ),
-    )(my_list, place, own_q, other_q, keys, values)
+    )(*scalars, *arrays)
 
 
 def merge_kernel(own_ref, got_ref, out_ref):
@@ -320,24 +323,22 @@
     return small_call(kernel, jax.ShapeDtypeStruct(first.shape, bf16), (), pieces, 2 * first.size)
 
 
-def gated(groups, factor):
+def gated(groups):
     counts = [len(g) for g in groups]
     tokens, width = groups[0][0].shape[0], groups[0][0].shape[1] // 2
 
     def kernel(*refs):
-        factor_ref, out_ref = refs[-2], refs[-1]
+        out_ref = refs[-1]
         at = 0
         for i, count in enumerate(counts):
-            rows = pl.ds(i * tokens, tokens)
             mine = refs[at : at + count]
             at += count
-            scale = factor_ref[rows, :]
-            gate = sum(r[:, 0:width].astype(f32) for r in mine) * scale
-            up = sum(r[:, width:].astype(f32) for r in mine) * scale
-            out_ref[rows, :] = (gate / (1.0 + jnp.exp(-gate)) * up).astype(bf16)
+            gate = sum(r[:, 0:width].astype(f32) for r in mine)
+            up = sum(r[:, width:].astype(f32) for r in mine)
+            out_ref[i * tokens : (i + 1) * tokens, :] = (gate / (1.0 + jnp.exp(-gate)) * up).astype(bf16)
 
     out = jax.ShapeDtypeStruct((tokens * len(groups), width), bf16)
-    arrays = [p for g in groups for p in g] + [factor[:, None]]
+    arrays = [p for g in groups for p in g]
     return small_call(kernel, out, (), arrays, 8 * tokens * width * len(groups))
 
 
@@ -388,21 +389,31 @@
     return lax.ppermute(x, "y", [(i, (i + 3) % 4) for i in range(4)])
 
 
-def ring_sum(own, right, left, opposite, far):
-    from_left = to_right(opposite)
-    from_right = to_left(far)
-    second_left = to_right(right[1])
-    second_right = to_left(left[0])
-    third_left = to_right(add_pieces(right[0], from_left))
-    third_right = to_left(add_pieces(left[1], from_right))
-    return (own[0], second_right, third_left), (own[1], second_left, third_right)
-
-
-def ring_gather(mine, got):
-    mine_left, mine_right = to_right(mine), to_left(mine)
-    got_left, got_right = to_right(got), to_left(got)
-    mine_far, got_far = to_right(mine_left), to_left(got_right)
-    return mine, got, mine_right, got_right, mine_far, got_far, mine_left, got_left
+def ring_start(pieces):
+    _, right, left, opposite, far = pieces
+    return to_right(opposite), to_left(far), to_right(right[1]), to_left(left[0])
+
+
+def ring_middle(pieces, from_left, from_right):
+    return add_pieces(pieces[1][0], from_left), add_pieces(pieces[2][1], from_right)
+
+
+def ring_end(pieces, arrived, sums):
+    third_left, third_right = to_right(sums[0]), to_left(sums[1])
+    own = pieces[0]
+    return (own[0], arrived[3], third_left), (own[1], arrived[2], third_right)
+
+
+def gather_start(mine):
+    return to_right(mine), to_left(mine)
+
+
+def gather_middle(got, mine_left):
+    return to_right(got), to_left(got), to_right(mine_left)
+
+
+def gather_end(mine, got, mine_left, mine_right, got_left, got_right, mine_far):
+    return mine, got, mine_right, got_right, mine_far, to_left(got_right), mine_left, got_left
 
 
 def exchange(x, axes):
@@ -447,19 +458,28 @@
     within = jnp.sum(jnp.where(matched, block_lists % local_blocks, 0), axis=2)
     source = (jnp.arange(KV_HEADS, dtype=jnp.int32)[:, None] * local_blocks + within.T).reshape(-1)
 
-    def fetch(cache, stretch):
-        flat = cache.reshape(KV_HEADS * local_blocks, BLK, HEAD_DIM)
+    piece = BLK // 4
+    flat_keys = cache_keys.reshape(4 * KV_HEADS * local_blocks, piece, HEAD_DIM)
+    flat_values = cache_values.reshape(4 * KV_HEADS * local_blocks, piece, HEAD_DIM)
+
+    def pick(flat, first, count):
+        index = 4 * source[:, None] + jnp.arange(first, first + count, dtype=jnp.int32)[None, :]
+        return flat[index].reshape(64, count * piece, HEAD_DIM)
+
+    def near(stretch):
         part = BLK // 8
-        near = lax.dynamic_slice_in_dim(stretch, group * part, part, 1)
-        near = jnp.broadcast_to(near[:, None], (KV_HEADS, 8, part, HEAD_DIM)).reshape(64, part, HEAD_DIM)
-        return exchange(jnp.concatenate([flat[source], near], axis=1), CHIP)
-
-    keys = fetch(cache_keys, stretch_keys)
-    values = fetch(cache_values, stretch_values)
+        rows = lax.dynamic_slice_in_dim(stretch, group * part, part, 1)
+        return jnp.broadcast_to(rows[:, None], (KV_HEADS, 8, part, HEAD_DIM)).reshape(64, part, HEAD_DIM)
+
+    first = [pick(flat_keys, 0, 3), pick(flat_values, 0, 3), near(stretch_keys), near(stretch_values)]
+    first = exchange(jnp.concatenate(first, axis=1), CHIP)
+    second = [pick(flat_keys, 3, 1), pick(flat_values, 3, 1)]
+    second = exchange(jnp.concatenate(second, axis=1), CHIP)
     my_list = block_lists[col, group]
     place = jnp.stack([core, col]).astype(jnp.int32)
     other_queries = swap(queries)
-    own, send = attend(my_list, place, queries, other_queries, keys, values, local_blocks)
+    own, send, order = attend((my_list, place), queries, other_queries, first, (), local_blocks, 5)
+    own, send = attend((order,), queries, other_queries, second, (own, send), local_blocks, 16)
     attended = exchange(merge(own, swap(send), 8), COL).reshape(8, 2, tokens_here, -1)
 
     def row_sum(give, mine, pick, weight):
@@ -468,18 +488,13 @@
 
     give = product(attended, (out_weight,), 512, 1 - core)
     stream = residual.astype(f32) + row_sum(give, attended, core, out_weight)
-    gain = norm_gain.astype(f32)[None, :]
-    scaled = (stream * gain).astype(bf16)
-    own_rows = exchange(spread(scaled, 8), ZXH)
+    squares = jnp.broadcast_to(jnp.sum(stream * stream, axis=1)[None], (8, tokens_here))
+    squares = squares + swap(squares, "xl")
+    across = lax.ppermute(squares, "y", [(i, (i + 2) % 4) for i in range(4)])
+    squares = squares + across + to_right(squares) + to_left(squares)
+    normed = stream * lax.rsqrt(squares[0] / D + 1e-05)[:, None] * norm_gain.astype(f32)[None, :]
+    own_rows = exchange(spread(normed.astype(bf16), 8), ZXH)
     other_rows = swap(own_rows)
-
-    def squares(x):
-        plain = x.astype(f32) / gain[None]
-        return jnp.sum(plain * plain, axis=2)
-
-    parts = jnp.stack([squares(own_rows), squares(other_rows)], axis=1)
-    totals = jnp.sum(exchange(parts, COL), axis=0)
-    factor = lax.rsqrt(totals.reshape(2, tokens_here) / D + 1e-05)
 
     by_pair = (4, 2, tokens_here, own_rows.shape[-1])
     where = jnp.stack([lax.axis_index("y"), side]).astype(jnp.int32)
@@ -487,14 +502,24 @@
         where, own_rows.reshape(by_pair), other_rows.reshape(by_pair), gate_weight, up_weight
     )
     got = swap(give, "xl")
-    here, there = ring_sum(*pieces)
+    arrived = ring_start(pieces)
+    here, there = ring_end(pieces, arrived, ring_middle(pieces, *arrived[:2]))
     other_give = add_pieces(*there)
     got, other_give = lax.optimization_barrier((got, other_give))
-    own_here, own_there = ring_sum(*arranged_sum(got, keep))
-    other_hidden = gated([(*here, swap(other_give, "xl"))], factor[1])
-    other_all = ring_gather(other_hidden, swap(other_hidden, "xl"))
-    own_hidden = gated([own_here, own_there], factor[0])
-    own_all = ring_gather(own_hidden, swap(own_hidden, "xl"))
+    pieces = arranged_sum(got, keep)
+    arrived, other_got = lax.optimization_barrier((ring_start(pieces), swap(other_give, "xl")))
+    sums = ring_middle(pieces, *arrived[:2])
+    other_hidden = gated([(*here, other_got)])
+    own_sums = ring_end(pieces, arrived, sums)
+    own_sums, other_first = lax.optimization_barrier((own_sums, gather_start(other_hidden)))
+    own_hidden = gated(own_sums)
+    other_got = swap(other_hidden, "xl")
+    other_second, own_first, own_got = lax.optimization_barrier(
+        (gather_middle(other_got, other_first[0]), gather_start(own_hidden), swap(own_hidden, "xl"))
+    )
+    other_all = gather_end(other_hidden, other_got, *other_first, *other_second)
+    own_second = gather_middle(own_got, own_first[0])
+    own_all = gather_end(own_hidden, own_got, *own_first, *own_second)
     given = down_product(where, other_all, down_weight)
     down = down_product(where, own_all, down_weight, add=swap(given))
     mlp = jnp.sum(exchange(down, ZXH).astype(f32), axis=0)

time: 332 us -> 336 us (1.012)
  blocking collectives: 49.7 us -> 59.9 us
    all_to_all x4 -> x3, waiting for transfers between devices: 89 us -> 61.9 us  [exchange(): return lax.all_to_all(x, axes, split_axis=0, concat_axis=0, tiled=True)]
    ppermute x12 -> x13, waiting for transfers between devices: 20 us -> 37.3 us  [to_right(): return lax.ppermute(x, 'y', [(i, (i + 1) % 4) for i in range(4)])]
    all_to_all x3, blocking collectives: 49.7 us -> 59.9 us  [exchange(): return lax.all_to_all(x, axes, split_axis=0, concat_axis=0, tiled=True)]
    ppermute x12 -> x13, starting transfers between devices: 20.7 us -> 27.5 us  [to_left(): return lax.ppermute(x, 'y', [(i, (i + 3) % 4) for i in range(4)])]
    all_to_all x4 -> x3, starting transfers between devices: 27.4 us -> 22.2 us  [exchange(): return lax.all_to_all(x, axes, split_axis=0, concat_axis=0, tiled=True)]
    ppermute x9 -> x10, waiting for transfers between devices: 23.7 us -> 28.1 us  [swap(): return lax.ppermute(x, axis, [(0, 1), (1, 0)])]
    pallas_call x1 -> x2, Pallas kernels: 13.2 us -> 16.7 us  [attend(): pl.pallas_call(functools.partial(attend_kernel, scale, per_step, local_bl...]
    ppermute x0 -> x1, waiting for transfers between devices: none -> 3.53 us  [local(): across = lax.ppermute(squares, 'y', [(i, (i + 2) % 4) for i in range(4)])]
  transfers between devices with their start and end apart: 37 -> 40, of which waited for: 22 -> 26; matrix products, arithmetic and copies ran while one was open for 3% -> 2% of each run, Pallas kernels for 2% -> 4%
where the time goes in v5:
time: 336 us; the launch traced here: 335 us
  waiting for transfers between devices  155 us (46%)
  starting transfers between devices  59.9 us (18%)
  blocking collectives  59.9 us (18%)
  Pallas kernels  41.5 us (12%)
  local copies, waits for them, and re-layouts  11.2 us (3%)
  other arithmetic  7.17 us (2%)
    all_to_all x3, waiting for transfers between devices, exchange(): return lax.all_to_all(x, axes, split_axis=0, concat_axis=0, tiled=True)  61.9 us
    all_to_all x3, blocking collectives, exchange(): return lax.all_to_all(x, axes, split_axis=0, concat_axis=0, tiled=True)  59.9 us
    ppermute x13, waiting for transfers between devices, to_right(): return lax.ppermute(x, 'y', [(i, (i + 1) % 4) for i in range(4)])  37.3 us
    ppermute x10, waiting for transfers between devices, swap(): return lax.ppermute(x, axis, [(0, 1), (1, 0)])  28.1 us
    ppermute x13, starting transfers between devices, to_left(): return lax.ppermute(x, 'y', [(i, (i + 3) % 4) for i in range(4)])  27.5 us
    ppermute x13, waiting for transfers between devices, to_left(): return lax.ppermute(x, 'y', [(i, (i + 3) % 4) for i in range(4)])  24.2 us
    all_to_all x3, starting transfers between devices, exchange(): return lax.all_to_all(x, axes, split_axis=0, concat_axis=0, tiled=True)  22.2 us
    pallas_call x2, Pallas kernels, attend(): pl.pallas_call(functools.partial(attend_kernel, scale, per_step, local_bl...  16.7 us
  transfers between devices with their start and end apart: 40, of which 26 were waited for; matrix products, arithmetic and copies ran while one was open for 2% of the time, Pallas kernels for 4%

profile of v5, /device:TPU:0, one launch (start us, length us, event | category | flops | bytes accessed | tf_op | source)
XLA Modules:
  0.0 335.2 jit_solution(2037806292176397559)
XLA Ops:
  3.7 3.6 %gather_fusion = bf16[192,32,128]{2,1,0:T(8,128)(2,1)} fusion(bf16[256,32,128]{2,1,0:T(8,128)(2,1)} %bitcast.62, s32[1024]{0:T(1024)S(1)} %pad_clamp_fusion.1), kind=kCustom, calls=%fused_computation | custom fusion | bytes 3146496 | tf_op jit(solution)/shard_map/gather | solution.py:467
  8.1 3.3 pad_maximum_fusion
  11.5 11.7 %all-to-all-start = ((bf16[64,224,128]{2,1,0:T(8,128)(2,1)}), bf16[64,224,128]{2,1,0:T(8,128)(2,1)}, u32[]{:S(2)}, u32[]{:S(2)}) async-start(bf16[64,224,128]{2,1,0:T(8,128)(2,1)} %pad_maximum_fusion), calls=%async_computation | async-start | bytes 7340032 | tf_op jit(solution)/shard_map/all_to_all | solution.py:420
  27.6 41.9 %all-to-all-done.refs_4_ = bf16[64,224,128]{2,1,0:T(8,128)(2,1)} async-done(((bf16[64,224,128]{2,1,0:T(8,128)(2,1)}), bf16[64,224,128]{2,1,0:T(8,128)(2,1)}, u32[]{:S(2)}, u32[]{:S(2)}) %all-to-all-start) | async-done | bytes 3670048 | tf_op jit(solution)/shard_map/all_to_all | solution.py:420
  69.6 6.9 %all-to-all-start.1 = ((bf16[64,64,128]{2,1,0:T(8,128)(2,1)}), bf16[64,64,128]{2,1,0:T(8,128)(2,1)S(1)}, u32[]{:S(2)}, u32[]{:S(2)}) async-start(bf16[64,64,128]{2,1,0:T(8,128)(2,1)} %pad_maximum_fusion.1), calls=%async_computation.1 | async-start | bytes 2097152 | tf_op jit(solution)/shard_map/all_to_all | solution.py:420
  78.0 12.7 %shard_map.118 = (f32[136,512]{1,0:T(8,128)S(1)}, f32[136,512]{1,0:T(8,128)S(1)}, s32[65]{0:T(128)S(1)}) custom-call(s32[64]{0:T(128)S(1)} %fusion.6.refs_0_, s32[2]{0:T(128)S(1)} %pad_add_fusion.refs_1_, bf16[128,512]{1,0:T(8,128)(2,1)S(1)} %copy-done.5, bf16[128,512]{1,0:T(8,128)(2,1)S(1)} %collective-permute-done.refs_3_.refs_2_, ...), custom_call_target="tpu_custom_call" | custom-call | flops 1174405120 | bytes 3670016 | tf_op jit(solution)/shard_map/pallas_call | solution.py:134
  90.7 3.7 %all-to-all-done.1.refs_3_ = bf16[64,64,128]{2,1,0:T(8,128)(2,1)S(1)} async-done(((bf16[64,64,128]{2,1,0:T(8,128)(2,1)}), bf16[64,64,128]{2,1,0:T(8,128)(2,1)S(1)}, u32[]{:S(2)}, u32[]{:S(2)}) %all-to-all-start.1) | async-done | bytes 1048608 | tf_op jit(solution)/shard_map/all_to_all | solution.py:420
  94.4 4.0 %shard_map.119 = (f32[136,512]{1,0:T(8,128)S(1)}, f32[136,512]{1,0:T(8,128)S(1)}) custom-call(s32[65]{0:T(128)S(1)} %get-tuple-element.43.refs_0_, bf16[128,512]{1,0:T(8,128)(2,1)S(1)} %copy-done.5, bf16[128,512]{1,0:T(8,128)(2,1)S(1)} %collective-permute-done.refs_3_.refs_2_, bf16[64,64,128]{2,1,0:T(8,128)(2,1)S(1)} %all-to-all-done.1.refs_3_, ...), custom_call_target="tpu_custom_call" | custom-call | flops 335544320 | bytes 1048576 | tf_op jit(solution)/shard_map/pallas_call | solution.py:134
  101.3 3.6 %all-to-all-start.2 = ((bf16[8,128,512]{2,1,0:T(8,128)(2,1)}), bf16[8,128,512]{2,1,0:T(8,128)(2,1)S(1)}, u32[]{:S(2)}, u32[]{:S(2)}) async-start(bf16[8,128,512]{2,1,0:T(8,128)(2,1)} %shard_map.120), calls=%async_computation.2 | async-start | bytes 2097152 | tf_op jit(solution)/shard_map/all_to_all | solution.py:420
  104.9 16.3 %all-to-all-done.2 = bf16[8,128,512]{2,1,0:T(8,128)(2,1)S(1)} async-done(((bf16[8,128,512]{2,1,0:T(8,128)(2,1)}), bf16[8,128,512]{2,1,0:T(8,128)(2,1)S(1)}, u32[]{:S(2)}, u32[]{:S(2)}) %all-to-all-start.2) | async-done | bytes 1048608 | tf_op jit(solution)/shard_map/all_to_all | solution.py:420
  125.3 24.2 %all_to_all.30 = bf16[8,64,1024]{2,1,0:T(8,128)(2,1)S(1)} all-to-all(bf16[8,64,1024]{2,1,0:T(8,128)(2,1)S(1)} %bitcast.57), channel_id=1, replica_groups=mesh['z'=4,'xh'=2,'core'=2,'y'=4,'xl'=2] {'z','xh'}, dimensions={0} | all-to-all | bytes 2097152 | tf_op jit(solution)/shard_map/all_to_all | solution.py:420
  150.2 3.4 %collective-permute-done.3 = f32[8,64]{1,0:T(8,128)S(1)} collective-permute-done((f32[8,64]{1,0:T(8,128)S(1)}, f32[8,64]{1,0:T(8,128)S(1)}, u32[]{:S(2)}, u32[]{:S(2)}) %collective-permute-start.3) | collective-permute-done | bytes 2080 | tf_op jit(solution)/shard_map/ppermute | solution.py:424
  153.6 3.2 collective-permute-start.6
  158.4 3.5 %collective-permute-done.4 = f32[8,64]{1,0:T(8,128)S(1)} collective-permute-done((f32[8,64]{1,0:T(8,128)S(1)}, f32[8,64]{1,0:T(8,128)S(1)}, u32[]{:S(2)}, u32[]{:S(2)}) %collective-permute-start.4) | collective-permute-done | bytes 2080 | tf_op jit(solution)/shard_map/ppermute | solution.py:493
  162.2 16.4 %all_to_all.31 = bf16[8,64,1024]{2,1,0:T(8,128)(2,1)S(1)} all-to-all(bf16[8,64,1024]{2,1,0:T(8,128)(2,1)S(1)} %broadcast_in_dim.13), channel_id=1, replica_groups=mesh['z'=4,'xh'=2,'core'=2,'y'=4,'xl'=2] {'z','xh'}, dimensions={0} | all-to-all | bytes 2097152 | tf_op jit(solution)/shard_map/all_to_all | solution.py:420
  181.2 12.8 %shard_map.123 = (bf16[4,64,3584]{2,1,0:T(8,128)(2,1)S(1)}, bf16[4,64,3584]{2,1,0:T(8,128)(2,1)S(1)}, bf16[2,64,3584]{2,1,0:T(8,128)(2,1)S(1)}, bf16[2,64,3584]{...) custom-call(s32[2]{0:T(128)S(1)} %pad_add_fusion.1.place_ref, ...), custom_call_target="tpu_custom_call" | custom-call | flops 7516192768 | bytes 16777216 | tf_op jit(solution)/shard_map/pallas_call | solution.py:276
  196.6 10.0 %collective-permute-done.10.refs_1_ = bf16[64,3584]{1,0:T(8,128)(2,1)S(1)} collective-permute-done((bf16[64,3584]{1,0:T(8,128)(2,1)S(1)}, bf16[64,3584]{1,0:T(8,128)(2,1)S(1)}, u32[]{:S(2)}, u32[]{:S(2)}) %collective-permute-start.10) | collective-permute-done | bytes 458784 | tf_op jit(solution)/shard_map/ppermute | solution.py:389
  210.7 8.1 %collective-permute-done.9.refs_1_ = bf16[64,3584]{1,0:T(8,128)(2,1)S(1)} collective-permute-done((bf16[64,3584]{1,0:T(8,128)(2,1)S(1)}, bf16[64,3584]{1,0:T(8,128)(2,1)S(1)}, u32[]{:S(2)}, u32[]{:S(2)}) %collective-permute-start.9) | collective-permute-done | bytes 458784 | tf_op jit(solution)/shard_map/ppermute | solution.py:385
  220.5 17.4 %collective-permute-done.8.got_ref = bf16[4,64,3584]{2,1,0:T(8,128)(2,1)S(1)} collective-permute-done((bf16[4,64,3584]{2,1,0:T(8,128)(2,1)S(1)}, bf16[4,64,3584]{2,1,0:T(8,128)(2,1)S(1)}, u32[]{:S(2)}, u32[]{:S(2)}) %collective-permute-start.8) | collective-permute-done | bytes 1835040 | tf_op jit(solution)/shard_map/ppermute | solution.py:424
  242.1 3.7 %collective-permute-done.12.refs_1_ = bf16[32,3584]{1,0:T(8,128)(2,1)S(1)} collective-permute-done((bf16[32,3584]{1,0:T(8,128)(2,1)S(1)}, bf16[32,3584]{1,0:T(8,128)(2,1)S(1)}, u32[]{:S(2)}, u32[]{:S(2)}) %collective-permute-start.12) | collective-permute-done | bytes 229408 | tf_op jit(solution)/shard_map/ppermute | solution.py:385
  245.8 3.2 collective-permute-start.15
  249.0 4.0 %collective-permute-done.14.refs_4_ = bf16[32,3584]{1,0:T(8,128)(2,1)S(1)} collective-permute-done((bf16[32,3584]{1,0:T(8,128)(2,1)S(1)}, bf16[32,3584]{1,0:T(8,128)(2,1)S(1)}, u32[]{:S(2)}, u32[]{:S(2)}) %collective-permute-start.14) | collective-permute-done | bytes 229408 | tf_op jit(solution)/shard_map/ppermute | solution.py:385
  257.3 3.3 collective-permute-start.18
  262.8 4.0 %collective-permute-done.17.refs_2_ = bf16[32,3584]{1,0:T(8,128)(2,1)S(1)} collective-permute-done((bf16[32,3584]{1,0:T(8,128)(2,1)S(1)}, bf16[32,3584]{1,0:T(8,128)(2,1)S(1)}, u32[]{:S(2)}, u32[]{:S(2)}) %collective-permute-start.17) | collective-permute-done | bytes 229408 | tf_op jit(solution)/shard_map/ppermute | solution.py:385
  270.1 3.7 %collective-permute-start.29 = (bf16[64,1792]{1,0:T(8,128)(2,1)S(1)}, bf16[64,1792]{1,0:T(8,128)(2,1)S(1)}, u32[]{:S(2)}, u32[]{:S(2)}) collective-permute-start(bf16[64,1792]{1,0:T(8,128)(2,1)S(1)} %shard_map.131.refs_0_), channel_id=1, source_target_pairs={{0,6},{2,0},{4,2},{6,4},{1,7},{3,1},{5,3},{7,5},{8,14},{10,8},{12,... | collective-permute-start | bytes 688136 | tf_op jit(solution)/shard_map/ppermute | solution.py:389
  275.2 5.8 %collective-permute-done.25.refs_7_ = bf16[64,1792]{1,0:T(8,128)(2,1)S(1)} collective-permute-done((bf16[64,1792]{1,0:T(8,128)(2,1)S(1)}, bf16[64,1792]{1,0:T(8,128)(2,1)S(1)}, u32[]{:S(2)}, u32[]{:S(2)}) %collective-permute-start.25) | collective-permute-done | bytes 229408 | tf_op jit(solution)/shard_map/ppermute | solution.py:385
  285.9 6.0 %collective-permute-done.35.refs_5_ = bf16[64,1792]{1,0:T(8,128)(2,1)S(1)} collective-permute-done((bf16[64,1792]{1,0:T(8,128)(2,1)S(1)}, bf16[64,1792]{1,0:T(8,128)(2,1)S(1)}, u32[]{:S(2)}, u32[]{:S(2)}) %collective-permute-start.35) | collective-permute-done | bytes 229408 | tf_op jit(solution)/shard_map/ppermute | solution.py:389
  291.9 3.8 %shard_map.132 = bf16[8,64,1024]{2,1,0:T(8,128)(2,1)S(1)} custom-call(s32[2]{0:T(128)S(1)} %pad_add_fusion.1.place_ref, bf16[64,1792]{1,0:T(8,128)(2,1)S(1)} %shard_map.130.refs_0_, bf16[64,1792]{1,0:T(8,128)(2,1)S(1)} %collective-permute-done.24.refs_1_, bf16[64,1792]{1,0:T(8,128)(2,1)S(1)} %collective-permute-done.23.refs_2_, ...), custom_call_target="tpu_custom_call" | custom-call | flops 1879048192 | bytes 6553600 | tf_op jit(solution)/shard_map/pallas_call | solution.py:369
  298.0 5.9 %collective-permute-done.31.refs_3_ = bf16[64,1792]{1,0:T(8,128)(2,1)S(1)} collective-permute-done((bf16[64,1792]{1,0:T(8,128)(2,1)S(1)}, bf16[64,1792]{1,0:T(8,128)(2,1)S(1)}, u32[]{:S(2)}, u32[]{:S(2)}) %collective-permute-start.31) | collective-permute-done | bytes 229408 | tf_op jit(solution)/shard_map/ppermute | solution.py:389
  306.3 4.6 %collective-permute-done.32.refs_4_ = bf16[64,1792]{1,0:T(8,128)(2,1)S(1)} collective-permute-done((bf16[64,1792]{1,0:T(8,128)(2,1)S(1)}, bf16[64,1792]{1,0:T(8,128)(2,1)S(1)}, u32[]{:S(2)}, u32[]{:S(2)}) %collective-permute-start.32) | collective-permute-done | bytes 229408 | tf_op jit(solution)/shard_map/ppermute | solution.py:385
  311.0 3.9 %shard_map.133 = bf16[8,64,1024]{2,1,0:T(8,128)(2,1)S(1)} custom-call(s32[2]{0:T(128)S(1)} %pad_add_fusion.1.place_ref, bf16[64,1792]{1,0:T(8,128)(2,1)S(1)} %shard_map.131.refs_0_, bf16[64,1792]{1,0:T(8,128)(2,1)S(1)} %collective-permute-done.30.refs_1_, bf16[64,1792]{1,0:T(8,128)(2,1)S(1)} %collective-permute-done.29.refs_2_, ...), custom_call_target="tpu_custom_call" | custom-call | flops 1879048192 | bytes 6553600 | tf_op jit(solution)/shard_map/pallas_call | solution.py:369
  314.9 19.3 %all_to_all.32 = bf16[8,64,1024]{2,1,0:T(8,128)(2,1)S(1)} all-to-all(bf16[8,64,1024]{2,1,0:T(8,128)(2,1)S(1)} %shard_map.133), channel_id=1, replica_groups=mesh['z'=4,'xh'=2,'core'=2,'y'=4,'xl'=2] {'z','xh'}, dimensions={0} | all-to-all | bytes 2097152 | tf_op jit(solution)/shard_map/all_to_all | solution.py:420
  (126 shorter events, 56.5 us)
Async XLA Ops:
  11.5 58.1 %all-to-all-start = ((bf16[64,224,128]{2,1,0:T(8,128)(2,1)}), bf16[64,224,128]{2,1,0:T(8,128)(2,1)}, u32[]{:S(2)}, u32[]{:S(2)}) async-start(bf16[64,224,128]{2,1,0:T(8,128)(2,1)} %pad_maximum_fusion), calls=%async_computation | async-start | bytes 7340032 | tf_op jit(solution)/shard_map/all_to_all | solution.py:420
  69.6 24.8 %all-to-all-start.1 = ((bf16[64,64,128]{2,1,0:T(8,128)(2,1)}), bf16[64,64,128]{2,1,0:T(8,128)(2,1)S(1)}, u32[]{:S(2)}, u32[]{:S(2)}) async-start(bf16[64,64,128]{2,1,0:T(8,128)(2,1)} %pad_maximum_fusion.1), calls=%async_computation.1 | async-start | bytes 2097152 | tf_op jit(solution)/shard_map/all_to_all | solution.py:420
  101.3 19.8 %all-to-all-start.2 = ((bf16[8,128,512]{2,1,0:T(8,128)(2,1)}), bf16[8,128,512]{2,1,0:T(8,128)(2,1)S(1)}, u32[]{:S(2)}, u32[]{:S(2)}) async-start(bf16[8,128,512]{2,1,0:T(8,128)(2,1)} %shard_map.120), calls=%async_computation.2 | async-start | bytes 2097152 | tf_op jit(solution)/shard_map/all_to_all | solution.py:420
  194.1 12.6 %collective-permute-start.10 = (bf16[64,3584]{1,0:T(8,128)(2,1)S(1)}, bf16[64,3584]{1,0:T(8,128)(2,1)S(1)}, u32[]{:S(2)}, u32[]{:S(2)}) collective-permute-start(bf16[64,3584]{1,0:T(8,128)(2,1)S(1)} %get-tuple-element.52), channel_id=1, source_target_pairs={{0,6},{2,0},{4,2},{6,4},{1,7},{3,1},{5,3},{7,5},{8,14},{10,8},{12,... | collective-permute-start | bytes 1376264 | tf_op jit(solution)/shard_map/ppermute | solution.py:389
  194.4 14.6 %collective-permute-start.20 = (bf16[64,3584]{1,0:T(8,128)(2,1)S(1)}, bf16[64,3584]{1,0:T(8,128)(2,1)S(1)}, u32[]{:S(2)}, u32[]{:S(2)}) collective-permute-start(bf16[64,3584]{1,0:T(8,128)(2,1)S(1)} %get-tuple-element.65), channel_id=1, source_target_pairs={{0,2},{2,4},{4,6},{6,0},{1,3},{3,5},{5,7},{7,1},{8,10},{10,12},{12... | collective-permute-start | bytes 1376264 | tf_op jit(solution)/shard_map/ppermute | solution.py:385
  196.2 22.6 %collective-permute-start.9 = (bf16[64,3584]{1,0:T(8,128)(2,1)S(1)}, bf16[64,3584]{1,0:T(8,128)(2,1)S(1)}, u32[]{:S(2)}, u32[]{:S(2)}) collective-permute-start(bf16[64,3584]{1,0:T(8,128)(2,1)S(1)} %get-tuple-element.82), channel_id=1, source_target_pairs={{0,2},{2,4},{4,6},{6,0},{1,3},{3,5},{5,7},{7,1},{8,10},{10,12},{12... | collective-permute-start | bytes 1376264 | tf_op jit(solution)/shard_map/ppermute | solution.py:385
  196.3 41.6 %collective-permute-start.8 = (bf16[4,64,3584]{2,1,0:T(8,128)(2,1)S(1)}, bf16[4,64,3584]{2,1,0:T(8,128)(2,1)S(1)}, u32[]{:S(2)}, u32[]{:S(2)}) collective-permute-start(bf16[4,64,3584]{2,1,0:T(8,128)(2,1)S(1)} %get-tuple-element.48), channel_id=1, source_target_pairs={{0,1},{1,0},{2,3},{3,2},{4,5},{5,4},{6,7},{7,6},{8,9},{9,8},{10,11... | collective-permute-start | bytes 5505032 | tf_op jit(solution)/shard_map/ppermute | solution.py:424
  206.8 13.5 %collective-permute-start.11 = (bf16[64,3584]{1,0:T(8,128)(2,1)S(1)}, bf16[64,3584]{1,0:T(8,128)(2,1)S(1)}, u32[]{:S(2)}, u32[]{:S(2)}) collective-permute-start(bf16[64,3584]{1,0:T(8,128)(2,1)S(1)} %shard_map.124), channel_id=1, source_target_pairs={{0,6},{2,0},{4,2},{6,4},{1,7},{3,1},{5,3},{7,5},{8,14},{10,8},{12,... | collective-permute-start | bytes 1376264 | tf_op jit(solution)/shard_map/ppermute | solution.py:389
  208.4 44.6 %collective-permute-start.19 = (bf16[64,3584]{1,0:T(8,128)(2,1)S(1)}, bf16[64,3584]{1,0:T(8,128)(2,1)S(1)}, u32[]{:S(2)}, u32[]{:S(2)}) collective-permute-start(bf16[64,3584]{1,0:T(8,128)(2,1)S(1)} %get-tuple-element.83), channel_id=1, source_target_pairs={{0,6},{2,0},{4,2},{6,4},{1,7},{3,1},{5,3},{7,5},{8,14},{10,8},{12,... | collective-permute-start | bytes 1376264 | tf_op jit(solution)/shard_map/ppermute | solution.py:389
  209.1 43.9 %collective-permute-start.21 = (bf16[64,3584]{1,0:T(8,128)(2,1)S(1)}, bf16[64,3584]{1,0:T(8,128)(2,1)S(1)}, u32[]{:S(2)}, u32[]{:S(2)}) collective-permute-start(bf16[64,3584]{1,0:T(8,128)(2,1)S(1)} %shard_map.129), channel_id=1, source_target_pairs={{0,2},{2,4},{4,6},{6,0},{1,3},{3,5},{5,7},{7,1},{8,10},{10,12},{12... | collective-permute-start | bytes 1376264 | tf_op jit(solution)/shard_map/ppermute | solution.py:385
  238.3 7.5 %collective-permute-start.12 = (bf16[32,3584]{1,0:T(8,128)(2,1)S(1)}, bf16[32,3584]{1,0:T(8,128)(2,1)S(1)}, u32[]{:S(2)}, u32[]{:S(2)}) collective-permute-start(bf16[32,3584]{1,0:T(8,128)(2,1)S(1)} %get-tuple-element.56), channel_id=1, source_target_pairs={{0,2},{2,4},{4,6},{6,0},{1,3},{3,5},{5,7},{7,1},{8,10},{10,12},{12... | collective-permute-start | bytes 688136 | tf_op jit(solution)/shard_map/ppermute | solution.py:385
  238.7 7.1 %collective-permute-start.13 = (bf16[32,3584]{1,0:T(8,128)(2,1)S(1)}, bf16[32,3584]{1,0:T(8,128)(2,1)S(1)}, u32[]{:S(2)}, u32[]{:S(2)}) collective-permute-start(bf16[32,3584]{1,0:T(8,128)(2,1)S(1)} %get-tuple-element.57), channel_id=1, source_target_pairs={{0,6},{2,0},{4,2},{6,4},{1,7},{3,1},{5,3},{7,5},{8,14},{10,8},{12,... | collective-permute-start | bytes 688136 | tf_op jit(solution)/shard_map/ppermute | solution.py:389
  241.7 11.4 %collective-permute-start.16 = (bf16[64,3584]{1,0:T(8,128)(2,1)S(1)}, bf16[64,3584]{1,0:T(8,128)(2,1)S(1)}, u32[]{:S(2)}, u32[]{:S(2)}) collective-permute-start(bf16[64,3584]{1,0:T(8,128)(2,1)S(1)} %shard_map.125), channel_id=1, source_target_pairs={{0,1},{1,0},{2,3},{3,2},{4,5},{5,4},{6,7},{7,6},{8,9},{9,8},{10,11... | collective-permute-start | bytes 1376264 | tf_op jit(solution)/shard_map/ppermute | solution.py:424
  245.8 7.2 %collective-permute-start.14 = (bf16[32,3584]{1,0:T(8,128)(2,1)S(1)}, bf16[32,3584]{1,0:T(8,128)(2,1)S(1)}, u32[]{:S(2)}, u32[]{:S(2)}) collective-permute-start(bf16[32,3584]{1,0:T(8,128)(2,1)S(1)} %get-tuple-element.92), channel_id=1, source_target_pairs={{0,2},{2,4},{4,6},{6,0},{1,3},{3,5},{5,7},{7,1},{8,10},{10,12},{12... | collective-permute-start | bytes 688136 | tf_op jit(solution)/shard_map/ppermute | solution.py:385
  245.8 7.2 %collective-permute-start.15 = (bf16[32,3584]{1,0:T(8,128)(2,1)S(1)}, bf16[32,3584]{1,0:T(8,128)(2,1)S(1)}, u32[]{:S(2)}, u32[]{:S(2)}) collective-permute-start(bf16[32,3584]{1,0:T(8,128)(2,1)S(1)} %get-tuple-element.88), channel_id=1, source_target_pairs={{0,6},{2,0},{4,2},{6,4},{1,7},{3,1},{5,3},{7,5},{8,14},{10,8},{12,... | collective-permute-start | bytes 688136 | tf_op jit(solution)/shard_map/ppermute | solution.py:389
  253.4 7.2 %collective-permute-start.24 = (bf16[64,1792]{1,0:T(8,128)(2,1)S(1)}, bf16[64,1792]{1,0:T(8,128)(2,1)S(1)}, u32[]{:S(2)}, u32[]{:S(2)}) collective-permute-start(bf16[64,1792]{1,0:T(8,128)(2,1)S(1)} %shard_map.130.refs_0_), channel_id=1, source_target_pairs={{0,1},{1,0},{2,3},{3,2},{4,5},{5,4},{6,7},{7,6},{8,9},{9,8},{10,11... | collective-permute-start | bytes 688136 | tf_op jit(solution)/shard_map/ppermute | solution.py:424
  253.9 13.6 %collective-permute-start.23 = (bf16[64,1792]{1,0:T(8,128)(2,1)S(1)}, bf16[64,1792]{1,0:T(8,128)(2,1)S(1)}, u32[]{:S(2)}, u32[]{:S(2)}) collective-permute-start(bf16[64,1792]{1,0:T(8,128)(2,1)S(1)} %shard_map.130.refs_0_), channel_id=1, source_target_pairs={{0,6},{2,0},{4,2},{6,4},{1,7},{3,1},{5,3},{7,5},{8,14},{10,8},{12,... | collective-permute-start | bytes 688136 | tf_op jit(solution)/shard_map/ppermute | solution.py:389
  257.1 10.4 %collective-permute-start.22 = (bf16[64,1792]{1,0:T(8,128)(2,1)S(1)}, bf16[64,1792]{1,0:T(8,128)(2,1)S(1)}, u32[]{:S(2)}, u32[]{:S(2)}) collective-permute-start(bf16[64,1792]{1,0:T(8,128)(2,1)S(1)} %shard_map.130.refs_0_), channel_id=1, source_target_pairs={{0,2},{2,4},{4,6},{6,0},{1,3},{3,5},{5,7},{7,1},{8,10},{10,12},{12... | collective-permute-start | bytes 688136 | tf_op jit(solution)/shard_map/ppermute | solution.py:385
  257.2 9.6 %collective-permute-start.17 = (bf16[32,3584]{1,0:T(8,128)(2,1)S(1)}, bf16[32,3584]{1,0:T(8,128)(2,1)S(1)}, u32[]{:S(2)}, u32[]{:S(2)}) collective-permute-start(bf16[32,3584]{1,0:T(8,128)(2,1)S(1)} %shard_map.127), channel_id=1, source_target_pairs={{0,2},{2,4},{4,6},{6,0},{1,3},{3,5},{5,7},{7,1},{8,10},{10,12},{12... | collective-permute-start | bytes 688136 | tf_op jit(solution)/shard_map/ppermute | solution.py:385
  257.3 10.1 %collective-permute-start.18 = (bf16[32,3584]{1,0:T(8,128)(2,1)S(1)}, bf16[32,3584]{1,0:T(8,128)(2,1)S(1)}, u32[]{:S(2)}, u32[]{:S(2)}) collective-permute-start(bf16[32,3584]{1,0:T(8,128)(2,1)S(1)} %shard_map.128), channel_id=1, source_target_pairs={{0,6},{2,0},{4,2},{6,4},{1,7},{3,1},{5,3},{7,5},{8,14},{10,8},{12,... | collective-permute-start | bytes 688136 | tf_op jit(solution)/shard_map/ppermute | solution.py:389
  260.6 13.2 %collective-permute-start.26 = (bf16[64,1792]{1,0:T(8,128)(2,1)S(1)}, bf16[64,1792]{1,0:T(8,128)(2,1)S(1)}, u32[]{:S(2)}, u32[]{:S(2)}) collective-permute-start(bf16[64,1792]{1,0:T(8,128)(2,1)S(1)} %collective-permute-done.24.refs_1_), channel_id=1, source_target_pairs={{0,6},{2,0},{4,2},{6,4},{1,7},{3,1},{5,3},{7,5},{8,14},{10,8},{12,... | collective-permute-start | bytes 688136 | tf_op jit(solution)/shard_map/ppermute | solution.py:389
  267.7 13.3 %collective-permute-start.30 = (bf16[64,1792]{1,0:T(8,128)(2,1)S(1)}, bf16[64,1792]{1,0:T(8,128)(2,1)S(1)}, u32[]{:S(2)}, u32[]{:S(2)}) collective-permute-start(bf16[64,1792]{1,0:T(8,128)(2,1)S(1)} %shard_map.131.refs_0_), channel_id=1, source_target_pairs={{0,1},{1,0},{2,3},{3,2},{4,5},{5,4},{6,7},{7,6},{8,9},{9,8},{10,11... | collective-permute-start | bytes 688136 | tf_op jit(solution)/shard_map/ppermute | solution.py:424
  270.1 10.9 %collective-permute-start.29 = (bf16[64,1792]{1,0:T(8,128)(2,1)S(1)}, bf16[64,1792]{1,0:T(8,128)(2,1)S(1)}, u32[]{:S(2)}, u32[]{:S(2)}) collective-permute-start(bf16[64,1792]{1,0:T(8,128)(2,1)S(1)} %shard_map.131.refs_0_), channel_id=1, source_target_pairs={{0,6},{2,0},{4,2},{6,4},{1,7},{3,1},{5,3},{7,5},{8,14},{10,8},{12,... | collective-permute-start | bytes 688136 | tf_op jit(solution)/shard_map/ppermute | solution.py:389
  273.8 7.2 %collective-permute-start.25 = (bf16[64,1792]{1,0:T(8,128)(2,1)S(1)}, bf16[64,1792]{1,0:T(8,128)(2,1)S(1)}, u32[]{:S(2)}, u32[]{:S(2)}) collective-permute-start(bf16[64,1792]{1,0:T(8,128)(2,1)S(1)} %collective-permute-done.24.refs_1_), channel_id=1, source_target_pairs={{0,2},{2,4},{4,6},{6,0},{1,3},{3,5},{5,7},{7,1},{8,10},{10,12},{12... | collective-permute-start | bytes 688136 | tf_op jit(solution)/shard_map/ppermute | solution.py:385
  273.8 9.7 %collective-permute-start.28 = (bf16[64,1792]{1,0:T(8,128)(2,1)S(1)}, bf16[64,1792]{1,0:T(8,128)(2,1)S(1)}, u32[]{:S(2)}, u32[]{:S(2)}) collective-permute-start(bf16[64,1792]{1,0:T(8,128)(2,1)S(1)} %shard_map.131.refs_0_), channel_id=1, source_target_pairs={{0,2},{2,4},{4,6},{6,0},{1,3},{3,5},{5,7},{7,1},{8,10},{10,12},{12... | collective-permute-start | bytes 688136 | tf_op jit(solution)/shard_map/ppermute | solution.py:385
  273.8 12.1 %collective-permute-start.27 = (bf16[64,1792]{1,0:T(8,128)(2,1)S(1)}, bf16[64,1792]{1,0:T(8,128)(2,1)S(1)}, u32[]{:S(2)}, u32[]{:S(2)}) collective-permute-start(bf16[64,1792]{1,0:T(8,128)(2,1)S(1)} %collective-permute-done.22.refs_6_), channel_id=1, source_target_pairs={{0,2},{2,4},{4,6},{6,0},{1,3},{3,5},{5,7},{7,1},{8,10},{10,12},{12... | collective-permute-start | bytes 688136 | tf_op jit(solution)/shard_map/ppermute | solution.py:385
  285.9 6.0 %collective-permute-start.35 = (bf16[64,1792]{1,0:T(8,128)(2,1)S(1)}, bf16[64,1792]{1,0:T(8,128)(2,1)S(1)}, u32[]{:S(2)}, u32[]{:S(2)}) collective-permute-start(bf16[64,1792]{1,0:T(8,128)(2,1)S(1)} %collective-permute-done.26.refs_3_), channel_id=1, source_target_pairs={{0,6},{2,0},{4,2},{6,4},{1,7},{3,1},{5,3},{7,5},{8,14},{10,8},{12,... | collective-permute-start | bytes 688136 | tf_op jit(solution)/shard_map/ppermute | solution.py:389
  295.7 15.3 %collective-permute-start.36 = (bf16[8,64,1024]{2,1,0:T(8,128)(2,1)S(1)}, bf16[8,64,1024]{2,1,0:T(8,128)(2,1)S(1)}, u32[]{:S(2)}, u32[]{:S(2)}) collective-permute-start(bf16[8,64,1024]{2,1,0:T(8,128)(2,1)S(1)} %shard_map.132), channel_id=1, source_target_pairs={{0,8},{8,0},{1,9},{9,1},{2,10},{10,2},{3,11},{11,3},{4,12},{12,4},... | collective-permute-start | bytes 3145736 | tf_op jit(solution)/shard_map/ppermute | solution.py:424
  295.8 8.0 %collective-permute-start.31 = (bf16[64,1792]{1,0:T(8,128)(2,1)S(1)}, bf16[64,1792]{1,0:T(8,128)(2,1)S(1)}, u32[]{:S(2)}, u32[]{:S(2)}) collective-permute-start(bf16[64,1792]{1,0:T(8,128)(2,1)S(1)} %collective-permute-done.30.refs_1_), channel_id=1, source_target_pairs={{0,6},{2,0},{4,2},{6,4},{1,7},{3,1},{5,3},{7,5},{8,14},{10,8},{12,... | collective-permute-start | bytes 688136 | tf_op jit(solution)/shard_map/ppermute | solution.py:389
  297.1 13.8 %collective-permute-start.34 = (bf16[64,1792]{1,0:T(8,128)(2,1)S(1)}, bf16[64,1792]{1,0:T(8,128)(2,1)S(1)}, u32[]{:S(2)}, u32[]{:S(2)}) collective-permute-start(bf16[64,1792]{1,0:T(8,128)(2,1)S(1)} %collective-permute-done.30.refs_1_), channel_id=1, source_target_pairs={{0,2},{2,4},{4,6},{6,0},{1,3},{3,5},{5,7},{7,1},{8,10},{10,12},{12... | collective-permute-start | bytes 688136 | tf_op jit(solution)/shard_map/ppermute | solution.py:385
  297.9 13.0 %collective-permute-start.32 = (bf16[64,1792]{1,0:T(8,128)(2,1)S(1)}, bf16[64,1792]{1,0:T(8,128)(2,1)S(1)}, u32[]{:S(2)}, u32[]{:S(2)}) collective-permute-start(bf16[64,1792]{1,0:T(8,128)(2,1)S(1)} %collective-permute-done.28.refs_6_), channel_id=1, source_target_pairs={{0,2},{2,4},{4,6},{6,0},{1,3},{3,5},{5,7},{7,1},{8,10},{10,12},{12... | collective-permute-start | bytes 688136 | tf_op jit(solution)/shard_map/ppermute | solution.py:385
  303.8 7.2 %collective-permute-start.33 = (bf16[64,1792]{1,0:T(8,128)(2,1)S(1)}, bf16[64,1792]{1,0:T(8,128)(2,1)S(1)}, u32[]{:S(2)}, u32[]{:S(2)}) collective-permute-start(bf16[64,1792]{1,0:T(8,128)(2,1)S(1)} %collective-permute-done.31.refs_3_), channel_id=1, source_target_pairs={{0,6},{2,0},{4,2},{6,4},{1,7},{3,1},{5,3},{7,5},{8,14},{10,8},{12,... | collective-permute-start | bytes 688136 | tf_op jit(solution)/shard_map/ppermute | solution.py:389
  (16 other events, 251.4 us)

commit v6 on v5

--- a/solution.py
+++ b/solution.py
@@ -237,9 +237,9 @@
     sides = (side, 1 - side)
     n = mine_ref.shape[2]
     x = jnp.concatenate(
-        [mine_ref[i, 1 - side] for i in order]
+        [mine_ref[i, 1 - side] for i in range(4)]
         + [theirs_ref[i, s] for i in order for s in sides]
-        + [mine_ref[i, side] for i in order],
+        + [mine_ref[i, side] for i in range(4)],
         axis=0,
     )
     step = pl.program_id(0)
@@ -287,7 +287,7 @@
             ],
             out_specs=blocks,
         ),
-        compiler_params=pltpu.CompilerParams(vmem_limit_bytes=40 * 1024 * 1024),
+        compiler_params=pltpu.CompilerParams(vmem_limit_bytes=60 * 1024 * 1024),
         cost_estimate=pl.CostEstimate(
             flops=4 * rows * inputs * width,
             bytes_accessed=2 * (rows * inputs + 2 * inputs * width + 2 * rows * width),
@@ -296,25 +296,6 @@
     )(place, mine, theirs, gate, up)
 
 
-def arranged_sum(got, keep):
-    tokens, width = keep.shape[1] // 2, keep.shape[2]
-
-    def kernel(got_ref, keep_ref, self_ref, right_ref, left_ref, opposite_ref, far_ref):
-        def block(i, j):
-            rows = pl.ds(j * tokens, tokens)
-            return (got_ref[i, rows].astype(f32) + keep_ref[i, rows].astype(f32)).astype(bf16)
-
-        for i, ref in ((0, self_ref), (1, right_ref), (3, left_ref)):
-            for j in range(2):
-                ref[j] = block(i, j)
-        opposite_ref[...] = block(2, 0)
-        far_ref[...] = block(2, 1)
-
-    two = jax.ShapeDtypeStruct((2, tokens, width), bf16)
-    one = jax.ShapeDtypeStruct((tokens, width), bf16)
-    return small_call(kernel, (two, two, two, one, one), (), (got, keep), 4 * keep.size)
-
-
 def add_pieces(*pieces):
     def kernel(*refs):
         refs[-1][...] = sum(r[...].astype(f32) for r in refs[:-1]).astype(bf16)
@@ -323,23 +304,21 @@
     return small_call(kernel, jax.ShapeDtypeStruct(first.shape, bf16), (), pieces, 2 * first.size)
 
 
-def gated(groups):
-    counts = [len(g) for g in groups]
-    tokens, width = groups[0][0].shape[0], groups[0][0].shape[1] // 2
+def gated(pieces, factor):
+    tokens, width = pieces[0].shape[-2], pieces[0].shape[-1] // 2
 
     def kernel(*refs):
-        out_ref = refs[-1]
-        at = 0
-        for i, count in enumerate(counts):
-            mine = refs[at : at + count]
-            at += count
-            gate = sum(r[:, 0:width].astype(f32) for r in mine)
-            up = sum(r[:, width:].astype(f32) for r in mine)
-            out_ref[i * tokens : (i + 1) * tokens, :] = (gate / (1.0 + jnp.exp(-gate)) * up).astype(bf16)
-
-    out = jax.ShapeDtypeStruct((tokens * len(groups), width), bf16)
-    arrays = [p for g in groups for p in g]
-    return small_call(kernel, out, (), arrays, 8 * tokens * width * len(groups))
+        scale = refs[-2][...]
+
+        def total(columns):
+            parts = [r[..., columns].astype(f32) for r in refs[:-2]]
+            return sum(jnp.sum(v, axis=0) if v.ndim == 3 else v for v in parts) * scale
+
+        gate = total(slice(0, width))
+        refs[-1][...] = (gate / (1.0 + jnp.exp(-gate)) * total(slice(width, 2 * width))).astype(bf16)
+
+    out = jax.ShapeDtypeStruct((tokens, width), bf16)
+    return small_call(kernel, out, (), [*pieces, factor[:, None]], 8 * tokens * width)
 
 
 def down_kernel(tile, place_ref, *refs):
@@ -488,38 +467,42 @@
 
     give = product(attended, (out_weight,), 512, 1 - core)
     stream = residual.astype(f32) + row_sum(give, attended, core, out_weight)
-    squares = jnp.broadcast_to(jnp.sum(stream * stream, axis=1)[None], (8, tokens_here))
-    squares = squares + swap(squares, "xl")
-    across = lax.ppermute(squares, "y", [(i, (i + 2) % 4) for i in range(4)])
-    squares = squares + across + to_right(squares) + to_left(squares)
-    normed = stream * lax.rsqrt(squares[0] / D + 1e-05)[:, None] * norm_gain.astype(f32)[None, :]
-    own_rows = exchange(spread(normed.astype(bf16), 8), ZXH)
+    gain = norm_gain.astype(f32)[None, :]
+    own_rows = exchange(spread((stream * gain).astype(bf16), 8), ZXH)
     other_rows = swap(own_rows)
+
+    def squares(x):
+        plain = x.astype(f32) / gain[None]
+        return jnp.sum(plain * plain, axis=2)
+
+    squares = jnp.stack([squares(own_rows), squares(other_rows)], axis=1)
 
     by_pair = (4, 2, tokens_here, own_rows.shape[-1])
     where = jnp.stack([lax.axis_index("y"), side]).astype(jnp.int32)
-    give, keep, *pieces = partial_columns(
+    columns = partial_columns(
         where, own_rows.reshape(by_pair), other_rows.reshape(by_pair), gate_weight, up_weight
     )
+    (give, keep, *pieces), squares = lax.optimization_barrier((columns, squares))
+    squares = exchange(squares, COL)
     got = swap(give, "xl")
     arrived = ring_start(pieces)
-    here, there = ring_end(pieces, arrived, ring_middle(pieces, *arrived[:2]))
+    steps, squares = lax.optimization_barrier((arrived[:2], squares))
+    factor = lax.rsqrt(jnp.sum(squares, axis=0).reshape(2, tokens_here) / D + 1e-05)
+    here, there = ring_end(pieces, arrived, ring_middle(pieces, *steps))
     other_give = add_pieces(*there)
-    got, other_give = lax.optimization_barrier((got, other_give))
-    pieces = arranged_sum(got, keep)
-    arrived, other_got = lax.optimization_barrier((ring_start(pieces), swap(other_give, "xl")))
-    sums = ring_middle(pieces, *arrived[:2])
-    other_hidden = gated([(*here, other_got)])
-    own_sums = ring_end(pieces, arrived, sums)
-    own_sums, other_first = lax.optimization_barrier((own_sums, gather_start(other_hidden)))
-    own_hidden = gated(own_sums)
+    got, other_give, here, factor = lax.optimization_barrier((got, other_give, here, factor))
+    own_part = exchange((got.astype(f32) + keep.astype(f32)).astype(bf16), "y")
+    other_hidden = gated((*here, swap(other_give, "xl")), factor[1])
     other_got = swap(other_hidden, "xl")
-    other_second, own_first, own_got = lax.optimization_barrier(
-        (gather_middle(other_got, other_first[0]), gather_start(own_hidden), swap(own_hidden, "xl"))
-    )
-    other_all = gather_end(other_hidden, other_got, *other_first, *other_second)
-    own_second = gather_middle(own_got, own_first[0])
-    own_all = gather_end(own_hidden, own_got, *own_first, *own_second)
+    first = gather_start(other_hidden)
+    other_all = gather_end(other_hidden, other_got, *first, *gather_middle(other_got, first[0]))
+    own_part, other_all = lax.optimization_barrier((own_part, other_all))
+    own_hidden = gated((own_part,), factor[0])
+    own_got = swap(own_hidden, "xl")
+    first = gather_start(own_hidden)
+    second = gather_middle(own_got, first[0])
+    first, second, other_all = lax.optimization_barrier((first, second, other_all))
+    own_all = gather_end(own_hidden, own_got, *first, *second)
     given = down_product(where, other_all, down_weight)
     down = down_product(where, own_all, down_weight, add=swap(given))
     mlp = jnp.sum(exchange(down, ZXH).astype(f32), axis=0)

time: 336 us -> 350 us (1.042)
  blocking collectives: 59.9 us -> 39.7 us
  local copies, waits for them, and re-layouts: 11.2 us -> 23.2 us
  starting transfers between devices: 59.9 us -> 71.3 us
  Pallas kernels: 41.5 us -> 48.6 us
  other arithmetic: 7.17 us -> 12.1 us
    all_to_all x3 -> x2, blocking collectives: 59.9 us -> 39.7 us  [exchange(): return lax.all_to_all(x, axes, split_axis=0, concat_axis=0, tiled=True)]
    all_to_all x3 -> x6, waiting for transfers between devices: 61.9 us -> 78.3 us  [exchange(): return lax.all_to_all(x, axes, split_axis=0, concat_axis=0, tiled=True)]
    all_to_all x3 -> x6, starting transfers between devices: 22.2 us -> 37.3 us  [exchange(): return lax.all_to_all(x, axes, split_axis=0, concat_axis=0, tiled=True)]
    ppermute x13 -> x9, waiting for transfers between devices: 37.3 us -> 23.2 us  [to_right(): return lax.ppermute(x, 'y', [(i, (i + 1) % 4) for i in range(4)])]
    ppermute x13 -> x9, waiting for transfers between devices: 24.2 us -> 15.3 us  [to_left(): return lax.ppermute(x, 'y', [(i, (i + 3) % 4) for i in range(4)])]
    ppermute x10 -> x9, waiting for transfers between devices: 28.1 us -> 36.9 us  [swap(): return lax.ppermute(x, axis, [(0, 1), (1, 0)])]
    unnamed x16 -> x55, local copies, waits for them, and re-layouts: 0.11 us -> 8.66 us
    ppermute x13 -> x9, starting transfers between devices: 27.5 us -> 20.9 us  [to_left(): return lax.ppermute(x, 'y', [(i, (i + 3) % 4) for i in range(4)])]
  transfers between devices with their start and end apart: 40 -> 33, of which waited for: 26 -> 19; matrix products, arithmetic and copies ran while one was open for 2% -> 3% of each run, Pallas kernels for 4% -> 5%
where the time goes in v6:
time: 350 us; the launch traced here: 349 us
  waiting for transfers between devices  154 us (44%)
  starting transfers between devices  71.3 us (20%)
  Pallas kernels  48.6 us (14%)
  blocking collectives  39.7 us (11%)
  local copies, waits for them, and re-layouts  23.2 us (7%)
  other arithmetic  12.1 us (3%)
    all_to_all x6, waiting for transfers between devices, exchange(): return lax.all_to_all(x, axes, split_axis=0, concat_axis=0, tiled=True)  78.3 us
    all_to_all x2, blocking collectives, exchange(): return lax.all_to_all(x, axes, split_axis=0, concat_axis=0, tiled=True)  39.7 us
    all_to_all x6, starting transfers between devices, exchange(): return lax.all_to_all(x, axes, split_axis=0, concat_axis=0, tiled=True)  37.3 us
    ppermute x9, waiting for transfers between devices, swap(): return lax.ppermute(x, axis, [(0, 1), (1, 0)])  36.9 us
    ppermute x9, waiting for transfers between devices, to_right(): return lax.ppermute(x, 'y', [(i, (i + 1) % 4) for i in range(4)])  23.2 us
    ppermute x9, starting transfers between devices, to_left(): return lax.ppermute(x, 'y', [(i, (i + 3) % 4) for i in range(4)])  20.9 us
    pallas_call x2, Pallas kernels, attend(): pl.pallas_call(functools.partial(attend_kernel, scale, per_step, local_bl...  17.8 us
    ppermute x9, waiting for transfers between devices, to_left(): return lax.ppermute(x, 'y', [(i, (i + 3) % 4) for i in range(4)])  15.3 us
  transfers between devices with their start and end apart: 33, of which 19 were waited for; matrix products, arithmetic and copies ran while one was open for 3% of the time, Pallas kernels for 5%

profile of v6, /device:TPU:0, one launch (start us, length us, event | category | flops | bytes accessed | tf_op | source)
XLA Modules:
  0.0 349.1 jit_solution(6137862969189926259)
XLA Ops:
  3.6 3.6 %gather_fusion.1 = bf16[192,32,128]{2,1,0:T(8,128)(2,1)} fusion(bf16[256,32,128]{2,1,0:T(8,128)(2,1)} %bitcast.52, s32[1024]{0:T(1024)S(1)} %pad_clamp_fusion.1), kind=kCustom, calls=%fused_computation.1 | custom fusion | bytes 3146496 | tf_op jit(solution)/shard_map/gather | solution.py:446
  8.1 3.3 pad_maximum_fusion
  11.4 11.7 %all-to-all-start = ((bf16[64,224,128]{2,1,0:T(8,128)(2,1)}), bf16[64,224,128]{2,1,0:T(8,128)(2,1)}, u32[]{:S(2)}, u32[]{:S(2)}) async-start(bf16[64,224,128]{2,1,0:T(8,128)(2,1)} %pad_maximum_fusion), calls=%async_computation | async-start | bytes 7340032 | tf_op jit(solution)/shard_map/all_to_all | solution.py:399
  27.6 41.9 %all-to-all-done.refs_4_ = bf16[64,224,128]{2,1,0:T(8,128)(2,1)} async-done(((bf16[64,224,128]{2,1,0:T(8,128)(2,1)}), bf16[64,224,128]{2,1,0:T(8,128)(2,1)}, u32[]{:S(2)}, u32[]{:S(2)}) %all-to-all-start) | async-done | bytes 3670048 | tf_op jit(solution)/shard_map/all_to_all | solution.py:399
  69.5 6.9 %all-to-all-start.1 = ((bf16[64,64,128]{2,1,0:T(8,128)(2,1)}), bf16[64,64,128]{2,1,0:T(8,128)(2,1)S(1)}, u32[]{:S(2)}, u32[]{:S(2)}) async-start(bf16[64,64,128]{2,1,0:T(8,128)(2,1)} %pad_maximum_fusion.1), calls=%async_computation.1 | async-start | bytes 2097152 | tf_op jit(solution)/shard_map/all_to_all | solution.py:399
  77.9 13.8 %shard_map.118 = (f32[136,512]{1,0:T(8,128)S(1)}, f32[136,512]{1,0:T(8,128)S(1)}, s32[65]{0:T(128)S(1)}) custom-call(s32[64]{0:T(128)S(1)} %fusion.6.refs_0_, s32[2]{0:T(128)S(1)} %pad_add_fusion.refs_1_, bf16[128,512]{1,0:T(8,128)(2,1)S(1)} %copy-done.16, bf16[128,512]{1,0:T(8,128)(2,1)S(1)} %collective-permute-done.refs_3_.refs_2_, ...), custom_call_target="tpu_custom_call" | custom-call | flops 1174405120 | bytes 3670016 | tf_op jit(solution)/shard_map/pallas_call | solution.py:134
  94.4 4.0 %shard_map.119 = (f32[136,512]{1,0:T(8,128)S(1)}, f32[136,512]{1,0:T(8,128)S(1)}) custom-call(s32[65]{0:T(128)S(1)} %get-tuple-element.56.refs_0_, bf16[128,512]{1,0:T(8,128)(2,1)S(1)} %copy-done.16, bf16[128,512]{1,0:T(8,128)(2,1)S(1)} %collective-permute-done.refs_3_.refs_2_, bf16[64,64,128]{2,1,0:T(8,128)(2,1)S(1)} %all-to-all-done.1.refs_3_, ...), custom_call_target="tpu_custom_call" | custom-call | flops 335544320 | bytes 1048576 | tf_op jit(solution)/shard_map/pallas_call | solution.py:134
  101.3 3.6 %all-to-all-start.2 = ((bf16[8,128,512]{2,1,0:T(8,128)(2,1)}), bf16[8,128,512]{2,1,0:T(8,128)(2,1)S(1)}, u32[]{:S(2)}, u32[]{:S(2)}) async-start(bf16[8,128,512]{2,1,0:T(8,128)(2,1)} %shard_map.120), calls=%async_computation.2 | async-start | bytes 2097152 | tf_op jit(solution)/shard_map/all_to_all | solution.py:399
  104.8 16.3 %all-to-all-done.2 = bf16[8,128,512]{2,1,0:T(8,128)(2,1)S(1)} async-done(((bf16[8,128,512]{2,1,0:T(8,128)(2,1)}), bf16[8,128,512]{2,1,0:T(8,128)(2,1)S(1)}, u32[]{:S(2)}, u32[]{:S(2)}) %all-to-all-start.2) | async-done | bytes 1048608 | tf_op jit(solution)/shard_map/all_to_all | solution.py:399
  126.3 7.3 %all-to-all-start.3 = ((bf16[8,64,1024]{2,1,0:T(8,128)(2,1)}), bf16[8,64,1024]{2,1,0:T(8,128)(2,1)S(1)}, u32[]{:S(2)}, u32[]{:S(2)}) async-start(bf16[8,64,1024]{2,1,0:T(8,128)(2,1)} %bitcast.15), calls=%async_computation.3 | async-start | bytes 2097152 | tf_op jit(solution)/shard_map/all_to_all | solution.py:399
  133.6 17.5 %all-to-all-done.3 = bf16[8,64,1024]{2,1,0:T(8,128)(2,1)S(1)} async-done(((bf16[8,64,1024]{2,1,0:T(8,128)(2,1)}), bf16[8,64,1024]{2,1,0:T(8,128)(2,1)S(1)}, u32[]{:S(2)}, u32[]{:S(2)}) %all-to-all-start.3) | async-done | bytes 1048608 | tf_op jit(solution)/shard_map/all_to_all | solution.py:399
  152.1 19.9 %all_to_all.40 = bf16[8,64,1024]{2,1,0:T(8,128)(2,1)S(1)} all-to-all(bf16[8,64,1024]{2,1,0:T(8,128)(2,1)S(1)} %broadcast_in_dim.10), channel_id=1, replica_groups=mesh['z'=4,'xh'=2,'core'=2,'y'=4,'xl'=2] {'z','xh'}, dimensions={0} | all-to-all | bytes 2097152 | tf_op jit(solution)/shard_map/all_to_all | solution.py:399
  175.7 14.8 %shard_map.123 = (bf16[4,64,3584]{2,1,0:T(8,128)(2,1)}, bf16[4,64,3584]{2,1,0:T(8,128)(2,1)}, bf16[2,64,3584]{2,1,0:T(8,128)(2,1)}, bf16[2,64,3584]{2,1,0:T(8,12...) custom-call(s32[2]{0:T(128)} %pad_add_fusion.1.place_ref, ...), custom_call_target="tpu_custom_call" | custom-call | flops 7516192768 | bytes 16777216 | tf_op jit(solution)/shard_map/pallas_call | solution.py:276
  190.5 3.2 collective-permute-start.7
  194.4 3.3 all-to-all-start.5
  208.3 3.0 collective-permute-start.8
  211.5 5.9 %collective-permute-done.5.refs_1_ = bf16[64,3584]{1,0:T(8,128)(2,1)S(1)} collective-permute-done((bf16[64,3584]{1,0:T(8,128)(2,1)}, bf16[64,3584]{1,0:T(8,128)(2,1)S(1)}, u32[]{:S(2)}, u32[]{:S(2)}) %collective-permute-start.5) | collective-permute-done | bytes 458784 | tf_op jit(solution)/shard_map/ppermute | solution.py:364
  217.4 7.8 %collective-permute-done.8.refs_2_ = bf16[64,3584]{1,0:T(8,128)(2,1)S(1)} collective-permute-done((bf16[64,3584]{1,0:T(8,128)(2,1)S(1)}, bf16[64,3584]{1,0:T(8,128)(2,1)S(1)}, u32[]{:S(2)}, u32[]{:S(2)}) %collective-permute-start.8) | collective-permute-done | bytes 458784 | tf_op jit(solution)/shard_map/ppermute | solution.py:368
  225.4 16.2 %collective-permute-done.4 = bf16[4,64,3584]{2,1,0:T(8,128)(2,1)} collective-permute-done((bf16[4,64,3584]{2,1,0:T(8,128)(2,1)}, bf16[4,64,3584]{2,1,0:T(8,128)(2,1)}, u32[]{:S(2)}, u32[]{:S(2)}) %collective-permute-start.4) | collective-permute-done | bytes 1835040 | tf_op jit(solution)/shard_map/ppermute | solution.py:403
  241.6 3.2 add_convert_fusion
  244.8 4.4 %all-to-all-start.6 = ((bf16[4,64,3584]{2,1,0:T(8,128)(2,1)}), bf16[4,64,3584]{2,1,0:T(8,128)(2,1)S(1)}, u32[]{:S(2)}, u32[]{:S(2)}) async-start(bf16[4,64,3584]{2,1,0:T(8,128)(2,1)} %add_convert_fusion), calls=%async_computation.6 | async-start | bytes 3670016 | tf_op jit(solution)/shard_map/all_to_all | solution.py:399
  250.8 9.1 %collective-permute-done.11.refs_3_ = bf16[64,3584]{1,0:T(8,128)(2,1)} collective-permute-done((bf16[64,3584]{1,0:T(8,128)(2,1)S(1)}, bf16[64,3584]{1,0:T(8,128)(2,1)}, u32[]{:S(2)}, u32[]{:S(2)}) %collective-permute-start.11) | collective-permute-done | bytes 458784 | tf_op jit(solution)/shard_map/ppermute | solution.py:403
  268.6 3.0 collective-permute-start.14
  273.6 2.9 collective-permute-done.15.refs_6_
  277.5 2.9 collective-permute-start.17
  280.5 5.6 %collective-permute-done.16.refs_4_ = bf16[64,1792]{1,0:T(8,128)(2,1)} collective-permute-done((bf16[64,1792]{1,0:T(8,128)(2,1)S(1)}, bf16[64,1792]{1,0:T(8,128)(2,1)}, u32[]{:S(2)}, u32[]{:S(2)}) %collective-permute-start.16) | collective-permute-done | bytes 229408 | tf_op jit(solution)/shard_map/ppermute | solution.py:364
  293.4 3.2 collective-permute-start.23
  296.6 6.3 %collective-permute-done.22.refs_7_ = bf16[64,1792]{1,0:T(8,128)(2,1)S(1)} collective-permute-done((bf16[64,1792]{1,0:T(8,128)(2,1)S(1)}, bf16[64,1792]{1,0:T(8,128)(2,1)S(1)}, u32[]{:S(2)}, u32[]{:S(2)}) %collective-permute-start.22) | collective-permute-done | bytes 229408 | tf_op jit(solution)/shard_map/ppermute | solution.py:364
  311.2 5.1 %shard_map.129 = bf16[8,64,1024]{2,1,0:T(8,128)(2,1)S(1)} custom-call(s32[2]{0:T(128)S(1)} %copy-done.7, bf16[64,1792]{1,0:T(8,128)(2,1)S(1)} %shard_map.127.refs_0_, bf16[64,1792]{1,0:T(8,128)(2,1)S(1)} %collective-permute-done.12.refs_1_, bf16[64,1792]{1,0:T(8,128)(2,1)S(1)} %copy-done.13, bf16[64,1792]{1,0:T(8,128)(2,1)S(1)} %copy-done.11, ...), custom_call_target="tpu_custom_call" | custom-call | flops 1879048192 | bytes 6553600 | tf_op jit(solution)/shard_map/pallas_call | solution.py:348
  316.9 7.5 %collective-permute-done.25.refs_5_ = bf16[64,1792]{1,0:T(8,128)(2,1)S(1)} collective-permute-done((bf16[64,1792]{1,0:T(8,128)(2,1)S(1)}, bf16[64,1792]{1,0:T(8,128)(2,1)S(1)}, u32[]{:S(2)}, u32[]{:S(2)}) %collective-permute-start.25) | collective-permute-done | bytes 229408 | tf_op jit(solution)/shard_map/ppermute | solution.py:368
  324.4 3.9 %shard_map.130 = bf16[8,64,1024]{2,1,0:T(8,128)(2,1)S(1)} custom-call(s32[2]{0:T(128)S(1)} %copy-done.7, bf16[64,1792]{1,0:T(8,128)(2,1)S(1)} %shard_map.128.refs_0_, bf16[64,1792]{1,0:T(8,128)(2,1)S(1)} %collective-permute-done.19.refs_1_, bf16[64,1792]{1,0:T(8,128)(2,1)S(1)} %collective-permute-done.21.refs_2_, ...), custom_call_target="tpu_custom_call" | custom-call | flops 1879048192 | bytes 6553600 | tf_op jit(solution)/shard_map/pallas_call | solution.py:348
  328.4 19.9 %all_to_all.41 = bf16[8,64,1024]{2,1,0:T(8,128)(2,1)S(1)} all-to-all(bf16[8,64,1024]{2,1,0:T(8,128)(2,1)S(1)} %shard_map.130), channel_id=1, replica_groups=mesh['z'=4,'xh'=2,'core'=2,'y'=4,'xl'=2] {'z','xh'}, dimensions={0} | all-to-all | bytes 2097152 | tf_op jit(solution)/shard_map/all_to_all | solution.py:399
  (150 shorter events, 67.6 us)
Async XLA Ops:
  11.4 58.1 %all-to-all-start = ((bf16[64,224,128]{2,1,0:T(8,128)(2,1)}), bf16[64,224,128]{2,1,0:T(8,128)(2,1)}, u32[]{:S(2)}, u32[]{:S(2)}) async-start(bf16[64,224,128]{2,1,0:T(8,128)(2,1)} %pad_maximum_fusion), calls=%async_computation | async-start | bytes 7340032 | tf_op jit(solution)/shard_map/all_to_all | solution.py:399
  69.5 24.8 %all-to-all-start.1 = ((bf16[64,64,128]{2,1,0:T(8,128)(2,1)}), bf16[64,64,128]{2,1,0:T(8,128)(2,1)S(1)}, u32[]{:S(2)}, u32[]{:S(2)}) async-start(bf16[64,64,128]{2,1,0:T(8,128)(2,1)} %pad_maximum_fusion.1), calls=%async_computation.1 | async-start | bytes 2097152 | tf_op jit(solution)/shard_map/all_to_all | solution.py:399
  98.4 1.6 collective-permute-start.1
  101.3 19.8 %all-to-all-start.2 = ((bf16[8,128,512]{2,1,0:T(8,128)(2,1)}), bf16[8,128,512]{2,1,0:T(8,128)(2,1)S(1)}, u32[]{:S(2)}, u32[]{:S(2)}) async-start(bf16[8,128,512]{2,1,0:T(8,128)(2,1)} %shard_map.120), calls=%async_computation.2 | async-start | bytes 2097152 | tf_op jit(solution)/shard_map/all_to_all | solution.py:399
  121.8 2.7 collective-permute-start.2
  126.3 24.8 %all-to-all-start.3 = ((bf16[8,64,1024]{2,1,0:T(8,128)(2,1)}), bf16[8,64,1024]{2,1,0:T(8,128)(2,1)S(1)}, u32[]{:S(2)}, u32[]{:S(2)}) async-start(bf16[8,64,1024]{2,1,0:T(8,128)(2,1)} %bitcast.15), calls=%async_computation.3 | async-start | bytes 2097152 | tf_op jit(solution)/shard_map/all_to_all | solution.py:399
  172.0 2.7 collective-permute-start.3
  190.4 16.6 %collective-permute-start.6 = (bf16[64,3584]{1,0:T(8,128)(2,1)}, bf16[64,3584]{1,0:T(8,128)(2,1)S(1)}, u32[]{:S(2)}, u32[]{:S(2)}) collective-permute-start(bf16[64,3584]{1,0:T(8,128)(2,1)} %get-tuple-element.72), channel_id=1, source_target_pairs={{0,2},{2,4},{4,6},{6,0},{1,3},{3,5},{5,7},{7,1},{8,10},{10,12},{12... | collective-permute-start | bytes 1376264 | tf_op jit(solution)/shard_map/ppermute | solution.py:364
  190.5 16.5 %collective-permute-start.7 = (bf16[64,3584]{1,0:T(8,128)(2,1)}, bf16[64,3584]{1,0:T(8,128)(2,1)S(1)}, u32[]{:S(2)}, u32[]{:S(2)}) collective-permute-start(bf16[64,3584]{1,0:T(8,128)(2,1)} %get-tuple-element.73), channel_id=1, source_target_pairs={{0,6},{2,0},{4,2},{6,4},{1,7},{3,1},{5,3},{7,5},{8,14},{10,8},{12,... | collective-permute-start | bytes 1376264 | tf_op jit(solution)/shard_map/ppermute | solution.py:368
  194.4 11.3 %all-to-all-start.5 = ((f32[8,1,128]{2,1,0:T(1,128)}), f32[8,1,128]{2,1,0:T(1,128)S(1)}, u32[]{:S(2)}, u32[]{:S(2)}) async-start(f32[8,1,128]{2,1,0:T(1,128)} %reshape.185), calls=%async_computation.5 | async-start | bytes 8192 | tf_op jit(solution)/shard_map/all_to_all | solution.py:399
  199.7 41.8 %collective-permute-start.4 = (bf16[4,64,3584]{2,1,0:T(8,128)(2,1)}, bf16[4,64,3584]{2,1,0:T(8,128)(2,1)}, u32[]{:S(2)}, u32[]{:S(2)}) collective-permute-start(bf16[4,64,3584]{2,1,0:T(8,128)(2,1)} %get-tuple-element.68), channel_id=1, source_target_pairs={{0,1},{1,0},{2,3},{3,2},{4,5},{5,4},{6,7},{7,6},{8,9},{9,8},{10,11... | collective-permute-start | bytes 5505032 | tf_op jit(solution)/shard_map/ppermute | solution.py:403
  202.5 14.9 %collective-permute-start.5 = (bf16[64,3584]{1,0:T(8,128)(2,1)}, bf16[64,3584]{1,0:T(8,128)(2,1)S(1)}, u32[]{:S(2)}, u32[]{:S(2)}) collective-permute-start(bf16[64,3584]{1,0:T(8,128)(2,1)} %get-tuple-element.110), channel_id=1, source_target_pairs={{0,2},{2,4},{4,6},{6,0},{1,3},{3,5},{5,7},{7,1},{8,10},{10,12},{12... | collective-permute-start | bytes 1376264 | tf_op jit(solution)/shard_map/ppermute | solution.py:364
  204.0 21.4 %collective-permute-start.9 = (bf16[64,3584]{1,0:T(8,128)(2,1)}, bf16[64,3584]{1,0:T(8,128)(2,1)S(1)}, u32[]{:S(2)}, u32[]{:S(2)}) collective-permute-start(bf16[64,3584]{1,0:T(8,128)(2,1)} %get-tuple-element.111), channel_id=1, source_target_pairs={{0,6},{2,0},{4,2},{6,4},{1,7},{3,1},{5,3},{7,5},{8,14},{10,8},{12,... | collective-permute-start | bytes 1376264 | tf_op jit(solution)/shard_map/ppermute | solution.py:368
  207.9 17.4 %collective-permute-start.10 = (bf16[64,3584]{1,0:T(8,128)(2,1)}, bf16[64,3584]{1,0:T(8,128)(2,1)S(1)}, u32[]{:S(2)}, u32[]{:S(2)}) collective-permute-start(bf16[64,3584]{1,0:T(8,128)(2,1)} %shard_map.126), channel_id=1, source_target_pairs={{0,2},{2,4},{4,6},{6,0},{1,3},{3,5},{5,7},{7,1},{8,10},{10,12},{12... | collective-permute-start | bytes 1376264 | tf_op jit(solution)/shard_map/ppermute | solution.py:364
  208.3 16.9 %collective-permute-start.8 = (bf16[64,3584]{1,0:T(8,128)(2,1)S(1)}, bf16[64,3584]{1,0:T(8,128)(2,1)S(1)}, u32[]{:S(2)}, u32[]{:S(2)}) collective-permute-start(bf16[64,3584]{1,0:T(8,128)(2,1)S(1)} %shard_map.124), channel_id=1, source_target_pairs={{0,6},{2,0},{4,2},{6,4},{1,7},{3,1},{5,3},{7,5},{8,14},{10,8},{12,... | collective-permute-start | bytes 1376264 | tf_op jit(solution)/shard_map/ppermute | solution.py:368
  244.8 41.4 %all-to-all-start.6 = ((bf16[4,64,3584]{2,1,0:T(8,128)(2,1)}), bf16[4,64,3584]{2,1,0:T(8,128)(2,1)S(1)}, u32[]{:S(2)}, u32[]{:S(2)}) async-start(bf16[4,64,3584]{2,1,0:T(8,128)(2,1)} %add_convert_fusion), calls=%async_computation.6 | async-start | bytes 3670016 | tf_op jit(solution)/shard_map/all_to_all | solution.py:399
  249.2 10.6 %collective-permute-start.11 = (bf16[64,3584]{1,0:T(8,128)(2,1)S(1)}, bf16[64,3584]{1,0:T(8,128)(2,1)}, u32[]{:S(2)}, u32[]{:S(2)}) collective-permute-start(bf16[64,3584]{1,0:T(8,128)(2,1)S(1)} %shard_map.125), channel_id=1, source_target_pairs={{0,1},{1,0},{2,3},{3,2},{4,5},{5,4},{6,7},{7,6},{8,9},{9,8},{10,11... | collective-permute-start | bytes 1376264 | tf_op jit(solution)/shard_map/ppermute | solution.py:403
  262.5 6.1 %collective-permute-start.12 = (bf16[64,1792]{1,0:T(8,128)(2,1)S(1)}, bf16[64,1792]{1,0:T(8,128)(2,1)S(1)}, u32[]{:S(2)}, u32[]{:S(2)}) collective-permute-start(bf16[64,1792]{1,0:T(8,128)(2,1)S(1)} %shard_map.127.refs_0_), channel_id=1, source_target_pairs={{0,1},{1,0},{2,3},{3,2},{4,5},{5,4},{6,7},{7,6},{8,9},{9,8},{10,11... | collective-permute-start | bytes 688136 | tf_op jit(solution)/shard_map/ppermute | solution.py:403
  264.0 12.4 %collective-permute-start.15 = (bf16[64,1792]{1,0:T(8,128)(2,1)S(1)}, bf16[64,1792]{1,0:T(8,128)(2,1)S(1)}, u32[]{:S(2)}, u32[]{:S(2)}) collective-permute-start(bf16[64,1792]{1,0:T(8,128)(2,1)S(1)} %shard_map.127.refs_0_), channel_id=1, source_target_pairs={{0,2},{2,4},{4,6},{6,0},{1,3},{3,5},{5,7},{7,1},{8,10},{10,12},{12... | collective-permute-start | bytes 688136 | tf_op jit(solution)/shard_map/ppermute | solution.py:364
  268.6 8.9 %collective-permute-start.14 = (bf16[64,1792]{1,0:T(8,128)(2,1)S(1)}, bf16[64,1792]{1,0:T(8,128)(2,1)S(1)}, u32[]{:S(2)}, u32[]{:S(2)}) collective-permute-start(bf16[64,1792]{1,0:T(8,128)(2,1)S(1)} %collective-permute-done.12.refs_1_), channel_id=1, source_target_pairs={{0,6},{2,0},{4,2},{6,4},{1,7},{3,1},{5,3},{7,5},{8,14},{10,8},{12,... | collective-permute-start | bytes 688136 | tf_op jit(solution)/shard_map/ppermute | solution.py:368
  271.5 9.0 %collective-permute-start.13 = (bf16[64,1792]{1,0:T(8,128)(2,1)S(1)}, bf16[64,1792]{1,0:T(8,128)(2,1)S(1)}, u32[]{:S(2)}, u32[]{:S(2)}) collective-permute-start(bf16[64,1792]{1,0:T(8,128)(2,1)S(1)} %shard_map.127.refs_0_), channel_id=1, source_target_pairs={{0,6},{2,0},{4,2},{6,4},{1,7},{3,1},{5,3},{7,5},{8,14},{10,8},{12,... | collective-permute-start | bytes 688136 | tf_op jit(solution)/shard_map/ppermute | solution.py:368
  272.4 13.7 %collective-permute-start.18 = (bf16[64,1792]{1,0:T(8,128)(2,1)S(1)}, bf16[64,1792]{1,0:T(8,128)(2,1)S(1)}, u32[]{:S(2)}, u32[]{:S(2)}) collective-permute-start(bf16[64,1792]{1,0:T(8,128)(2,1)S(1)} %collective-permute-done.12.refs_1_), channel_id=1, source_target_pairs={{0,2},{2,4},{4,6},{6,0},{1,3},{3,5},{5,7},{7,1},{8,10},{10,12},{12... | collective-permute-start | bytes 688136 | tf_op jit(solution)/shard_map/ppermute | solution.py:364
  276.5 9.7 %collective-permute-start.16 = (bf16[64,1792]{1,0:T(8,128)(2,1)S(1)}, bf16[64,1792]{1,0:T(8,128)(2,1)}, u32[]{:S(2)}, u32[]{:S(2)}) collective-permute-start(bf16[64,1792]{1,0:T(8,128)(2,1)S(1)} %collective-permute-done.15.refs_6_), channel_id=1, source_target_pairs={{0,2},{2,4},{4,6},{6,0},{1,3},{3,5},{5,7},{7,1},{8,10},{10,12},{12... | collective-permute-start | bytes 688136 | tf_op jit(solution)/shard_map/ppermute | solution.py:364
  277.5 8.7 %collective-permute-start.17 = (bf16[64,1792]{1,0:T(8,128)(2,1)S(1)}, bf16[64,1792]{1,0:T(8,128)(2,1)}, u32[]{:S(2)}, u32[]{:S(2)}) collective-permute-start(bf16[64,1792]{1,0:T(8,128)(2,1)S(1)} %collective-permute-done.14.refs_3_), channel_id=1, source_target_pairs={{0,6},{2,0},{4,2},{6,4},{1,7},{3,1},{5,3},{7,5},{8,14},{10,8},{12,... | collective-permute-start | bytes 688136 | tf_op jit(solution)/shard_map/ppermute | solution.py:368
  286.7 6.7 %collective-permute-start.19 = (bf16[64,1792]{1,0:T(8,128)(2,1)S(1)}, bf16[64,1792]{1,0:T(8,128)(2,1)S(1)}, u32[]{:S(2)}, u32[]{:S(2)}) collective-permute-start(bf16[64,1792]{1,0:T(8,128)(2,1)S(1)} %shard_map.128.refs_0_), channel_id=1, source_target_pairs={{0,1},{1,0},{2,3},{3,2},{4,5},{5,4},{6,7},{7,6},{8,9},{9,8},{10,11... | collective-permute-start | bytes 688136 | tf_op jit(solution)/shard_map/ppermute | solution.py:403
  288.0 8.7 %collective-permute-start.20 = (bf16[64,1792]{1,0:T(8,128)(2,1)S(1)}, bf16[64,1792]{1,0:T(8,128)(2,1)S(1)}, u32[]{:S(2)}, u32[]{:S(2)}) collective-permute-start(bf16[64,1792]{1,0:T(8,128)(2,1)S(1)} %shard_map.128.refs_0_), channel_id=1, source_target_pairs={{0,2},{2,4},{4,6},{6,0},{1,3},{3,5},{5,7},{7,1},{8,10},{10,12},{12... | collective-permute-start | bytes 688136 | tf_op jit(solution)/shard_map/ppermute | solution.py:364
  288.8 7.8 %collective-permute-start.21 = (bf16[64,1792]{1,0:T(8,128)(2,1)S(1)}, bf16[64,1792]{1,0:T(8,128)(2,1)S(1)}, u32[]{:S(2)}, u32[]{:S(2)}) collective-permute-start(bf16[64,1792]{1,0:T(8,128)(2,1)S(1)} %shard_map.128.refs_0_), channel_id=1, source_target_pairs={{0,6},{2,0},{4,2},{6,4},{1,7},{3,1},{5,3},{7,5},{8,14},{10,8},{12,... | collective-permute-start | bytes 688136 | tf_op jit(solution)/shard_map/ppermute | solution.py:368
  293.4 9.6 %collective-permute-start.22 = (bf16[64,1792]{1,0:T(8,128)(2,1)S(1)}, bf16[64,1792]{1,0:T(8,128)(2,1)S(1)}, u32[]{:S(2)}, u32[]{:S(2)}) collective-permute-start(bf16[64,1792]{1,0:T(8,128)(2,1)S(1)} %collective-permute-done.19.refs_1_), channel_id=1, source_target_pairs={{0,2},{2,4},{4,6},{6,0},{1,3},{3,5},{5,7},{7,1},{8,10},{10,12},{12... | collective-permute-start | bytes 688136 | tf_op jit(solution)/shard_map/ppermute | solution.py:364
  293.4 9.6 %collective-permute-start.23 = (bf16[64,1792]{1,0:T(8,128)(2,1)S(1)}, bf16[64,1792]{1,0:T(8,128)(2,1)S(1)}, u32[]{:S(2)}, u32[]{:S(2)}) collective-permute-start(bf16[64,1792]{1,0:T(8,128)(2,1)S(1)} %collective-permute-done.19.refs_1_), channel_id=1, source_target_pairs={{0,6},{2,0},{4,2},{6,4},{1,7},{3,1},{5,3},{7,5},{8,14},{10,8},{12,... | collective-permute-start | bytes 688136 | tf_op jit(solution)/shard_map/ppermute | solution.py:368
  296.6 8.8 %collective-permute-start.24 = (bf16[64,1792]{1,0:T(8,128)(2,1)S(1)}, bf16[64,1792]{1,0:T(8,128)(2,1)S(1)}, u32[]{:S(2)}, u32[]{:S(2)}) collective-permute-start(bf16[64,1792]{1,0:T(8,128)(2,1)S(1)} %collective-permute-done.20.refs_6_), channel_id=1, source_target_pairs={{0,2},{2,4},{4,6},{6,0},{1,3},{3,5},{5,7},{7,1},{8,10},{10,12},{12... | collective-permute-start | bytes 688136 | tf_op jit(solution)/shard_map/ppermute | solution.py:364
  316.3 8.1 %collective-permute-start.26 = (bf16[8,64,1024]{2,1,0:T(8,128)(2,1)S(1)}, bf16[8,64,1024]{2,1,0:T(8,128)(2,1)S(1)}, u32[]{:S(2)}, u32[]{:S(2)}) collective-permute-start(bf16[8,64,1024]{2,1,0:T(8,128)(2,1)S(1)} %shard_map.129), channel_id=1, source_target_pairs={{0,8},{8,0},{1,9},{9,1},{2,10},{10,2},{3,11},{11,3},{4,12},{12,4},... | collective-permute-start | bytes 3145736 | tf_op jit(solution)/shard_map/ppermute | solution.py:403
  316.4 8.0 %collective-permute-start.25 = (bf16[64,1792]{1,0:T(8,128)(2,1)S(1)}, bf16[64,1792]{1,0:T(8,128)(2,1)S(1)}, u32[]{:S(2)}, u32[]{:S(2)}) collective-permute-start(bf16[64,1792]{1,0:T(8,128)(2,1)S(1)} %collective-permute-done.23.refs_3_), channel_id=1, source_target_pairs={{0,6},{2,0},{4,2},{6,4},{1,7},{3,1},{5,3},{7,5},{8,14},{10,8},{12,... | collective-permute-start | bytes 688136 | tf_op jit(solution)/shard_map/ppermute | solution.py:368
  (28 other events, 347.0 us)

commit v7 on v6

--- a/solution.py
+++ b/solution.py
@@ -230,30 +230,19 @@
     )(*scalars, *arrays)
 
 
-def spread_kernel(place_ref, mine_ref, theirs_ref, gate_ref, up_ref, *out_refs):
+def columns_kernel(place_ref, mine_ref, theirs_ref, gate_ref, up_ref, *out_refs):
     y, side = place_ref[0], place_ref[1]
-    give_ref, keep_ref, self_ref, right_ref, left_ref, opposite_ref, far_ref = out_refs
-    order = [(y + i) % 4 for i in range(4)]
-    sides = (side, 1 - side)
     n = mine_ref.shape[2]
     x = jnp.concatenate(
-        [mine_ref[i, 1 - side] for i in range(4)]
-        + [theirs_ref[i, s] for i in order for s in sides]
-        + [mine_ref[i, side] for i in range(4)],
+        [ref[(y + i) % 4, s] for s in (1 - side, side) for i in range(4) for ref in (mine_ref, theirs_ref)],
         axis=0,
     )
     step = pl.program_id(0)
 
     def put(weight_ref):
         total = jnp.dot(x, weight_ref[...], preferred_element_type=f32).astype(bf16)
-        for i in range(4):
-            give_ref[i] = total[i * n : (i + 1) * n]
-            keep_ref[i] = total[(12 + i) * n : (13 + i) * n]
-        for first, ref in ((4, self_ref), (6, right_ref), (10, left_ref)):
-            for j in range(2):
-                ref[j] = total[(first + j) * n : (first + j + 1) * n]
-        opposite_ref[...] = total[8 * n : 9 * n]
-        far_ref[...] = total[9 * n : 10 * n]
+        for i, ref in enumerate(out_refs):
+            ref[...] = total[i * n : (i + 1) * n]
 
     half = pl.num_programs(0) // 2
     pl.when(step < half)(functools.partial(put, gate_ref))
@@ -266,16 +255,10 @@
     count = width // tile
     tokens = mine.shape[2]
     whole = pl.BlockSpec(mine.shape, lambda n, p: (0, 0, 0, 0))
-
-    def out(*lead):
-        block = pl.BlockSpec((*lead, tokens, tile), lambda n, p: (0,) * (len(lead) + 1) + (n,))
-        return jax.ShapeDtypeStruct((*lead, tokens, 2 * width), bf16), block
-
-    shapes, blocks = zip(*[out(4), out(4), out(2), out(2), out(2), out(), out()])
     rows = 16 * tokens
     return pl.pallas_call(
-        spread_kernel,
-        out_shape=shapes,
+        columns_kernel,
+        out_shape=(jax.ShapeDtypeStruct((tokens, 2 * width), bf16),) * 16,
         grid_spec=pltpu.PrefetchScalarGridSpec(
             num_scalar_prefetch=1,
             grid=(2 * count,),
@@ -285,7 +268,7 @@
                 pl.BlockSpec((inputs, tile), lambda n, p: (0, jnp.minimum(n, count - 1))),
                 pl.BlockSpec((inputs, tile), lambda n, p: (0, jnp.maximum(n - count, 0))),
             ],
-            out_specs=blocks,
+            out_specs=(pl.BlockSpec((tokens, tile), lambda n, p: (0, n)),) * 16,
         ),
         compiler_params=pltpu.CompilerParams(vmem_limit_bytes=60 * 1024 * 1024),
         cost_estimate=pl.CostEstimate(
@@ -304,21 +287,41 @@
     return small_call(kernel, jax.ShapeDtypeStruct(first.shape, bf16), (), pieces, 2 * first.size)
 
 
-def gated(pieces, factor):
-    tokens, width = pieces[0].shape[-2], pieces[0].shape[-1] // 2
+def add_halves(*halves):
+    count = len(halves[0])
 
     def kernel(*refs):
-        scale = refs[-2][...]
-
-        def total(columns):
-            parts = [r[..., columns].astype(f32) for r in refs[:-2]]
-            return sum(jnp.sum(v, axis=0) if v.ndim == 3 else v for v in parts) * scale
-
-        gate = total(slice(0, width))
-        refs[-1][...] = (gate / (1.0 + jnp.exp(-gate)) * total(slice(width, 2 * width))).astype(bf16)
-
-    out = jax.ShapeDtypeStruct((tokens, width), bf16)
-    return small_call(kernel, out, (), [*pieces, factor[:, None]], 8 * tokens * width)
+        for i in range(len(halves)):
+            mine = refs[i * count : (i + 1) * count]
+            refs[-1][i] = sum(r[...].astype(f32) for r in mine).astype(bf16)
+
+    first = halves[0][0]
+    out = jax.ShapeDtypeStruct((len(halves), *first.shape), bf16)
+    return small_call(kernel, out, (), [p for h in halves for p in h], 8 * first.size)
+
+
+def gated(halves, got, factor):
+    count = len(halves[0])
+    tokens, width = halves[0][0].shape[0], halves[0][0].shape[1] // 2
+
+    def kernel(*refs):
+        got_ref, factor_ref, out_ref = refs[-3:]
+        for i in range(len(halves)):
+            rows = pl.ds(i * tokens, tokens)
+            mine = refs[i * count : (i + 1) * count]
+            scale = factor_ref[rows, :]
+
+            def total(columns):
+                parts = sum(r[:, columns].astype(f32) for r in mine)
+                return (parts + got_ref[i, :, columns].astype(f32)) * scale
+
+            gate = total(slice(0, width))
+            up = total(slice(width, 2 * width))
+            out_ref[rows, :] = (gate / (1.0 + jnp.exp(-gate)) * up).astype(bf16)
+
+    out = jax.ShapeDtypeStruct((tokens * len(halves), width), bf16)
+    arrays = [p for h in halves for p in h] + [got, factor[:, None]]
+    return small_call(kernel, out, (), arrays, 16 * tokens * width)
 
 
 def down_kernel(tile, place_ref, *refs):
@@ -336,11 +339,11 @@
             out_ref[at] = part.astype(bf16)
 
 
-def down_product(place, pieces, weight, add=None):
+def down_product(place, pieces, half, weight, add=None):
     tile = 256
-    tokens, inputs = pieces[0].shape
+    tokens, inputs = pieces[0].shape[0] // 2, pieces[0].shape[1]
     width = weight.shape[1]
-    piece = pl.BlockSpec((tokens, inputs), lambda n, p: (0, 0))
+    piece = pl.BlockSpec((tokens, inputs), lambda n, p: (half, 0))
     by_column = pl.BlockSpec((8, tokens, tile), lambda n, p: (0, 0, n))
     operands = [*pieces, weight] + ([] if add is None else [add])
     specs = [piece] * 8 + [pl.BlockSpec((inputs, tile), lambda n, p: (0, n))]
@@ -369,18 +372,17 @@
 
 
 def ring_start(pieces):
-    _, right, left, opposite, far = pieces
-    return to_right(opposite), to_left(far), to_right(right[1]), to_left(left[0])
+    right, left, opposite = pieces[2:4], pieces[6:8], pieces[4:6]
+    return to_right(opposite[0]), to_left(opposite[1]), to_right(right[1]), to_left(left[0])
 
 
 def ring_middle(pieces, from_left, from_right):
-    return add_pieces(pieces[1][0], from_left), add_pieces(pieces[2][1], from_right)
+    return add_pieces(pieces[2], from_left), add_pieces(pieces[7], from_right)
 
 
 def ring_end(pieces, arrived, sums):
     third_left, third_right = to_right(sums[0]), to_left(sums[1])
-    own = pieces[0]
-    return (own[0], arrived[3], third_left), (own[1], arrived[2], third_right)
+    return (pieces[0], arrived[3], third_left), (pieces[1], arrived[2], third_right)
 
 
 def gather_start(mine):
@@ -482,29 +484,23 @@
     columns = partial_columns(
         where, own_rows.reshape(by_pair), other_rows.reshape(by_pair), gate_weight, up_weight
     )
-    (give, keep, *pieces), squares = lax.optimization_barrier((columns, squares))
+    theirs, mine = columns[:8], columns[8:]
+    arrived = ring_start(theirs)
+    sums = ring_middle(theirs, *arrived[:2])
+    sums, mine, squares = lax.optimization_barrier((sums, mine, squares))
     squares = exchange(squares, COL)
-    got = swap(give, "xl")
-    arrived = ring_start(pieces)
-    steps, squares = lax.optimization_barrier((arrived[:2], squares))
-    factor = lax.rsqrt(jnp.sum(squares, axis=0).reshape(2, tokens_here) / D + 1e-05)
-    here, there = ring_end(pieces, arrived, ring_middle(pieces, *steps))
-    other_give = add_pieces(*there)
-    got, other_give, here, factor = lax.optimization_barrier((got, other_give, here, factor))
-    own_part = exchange((got.astype(f32) + keep.astype(f32)).astype(bf16), "y")
-    other_hidden = gated((*here, swap(other_give, "xl")), factor[1])
-    other_got = swap(other_hidden, "xl")
-    first = gather_start(other_hidden)
-    other_all = gather_end(other_hidden, other_got, *first, *gather_middle(other_got, first[0]))
-    own_part, other_all = lax.optimization_barrier((own_part, other_all))
-    own_hidden = gated((own_part,), factor[0])
-    own_got = swap(own_hidden, "xl")
-    first = gather_start(own_hidden)
-    second = gather_middle(own_got, first[0])
-    first, second, other_all = lax.optimization_barrier((first, second, other_all))
-    own_all = gather_end(own_hidden, own_got, *first, *second)
-    given = down_product(where, other_all, down_weight)
-    down = down_product(where, own_all, down_weight, add=swap(given))
+    halves = ring_end(theirs, arrived, sums)
+    mine_arrived = ring_start(mine)
+    halves, squares = lax.optimization_barrier((halves, squares))
+    got = swap(add_halves(*halves), "xl")
+    factor = lax.rsqrt(jnp.sum(squares, axis=0).reshape(-1) / D + 1e-05)
+    halves = ring_end(mine, mine_arrived, ring_middle(mine, *mine_arrived[:2]))
+    hidden = gated(halves, got, factor)
+    hidden_got = swap(hidden, "xl")
+    first = gather_start(hidden)
+    pieces = gather_end(hidden, hidden_got, *first, *gather_middle(hidden_got, first[0]))
+    given = down_product(where, pieces, 1, down_weight)
+    down = down_product(where, pieces, 0, down_weight, add=swap(given))
     mlp = jnp.sum(exchange(down, ZXH).astype(f32), axis=0)
     return (stream + mlp).astype(bf16)
 

time: 350 us -> 333 us (0.951)
  starting transfers between devices: 71.3 us -> 54.8 us
  local copies, waits for them, and re-layouts: 23.2 us -> 16.1 us
  waiting for transfers between devices: 154 us -> 161 us
    ppermute x9, waiting for transfers between devices: 15.3 us -> 34.8 us  [to_left(): return lax.ppermute(x, 'y', [(i, (i + 3) % 4) for i in range(4)])]
    ppermute x9 -> x7, waiting for transfers between devices: 36.9 us -> 19.9 us  [swap(): return lax.ppermute(x, axis, [(0, 1), (1, 0)])]
    all_to_all x6 -> x5, waiting for transfers between devices: 78.3 us -> 86.7 us  [exchange(): return lax.all_to_all(x, axes, split_axis=0, concat_axis=0, tiled=True)]
    ppermute x9 -> x7, starting transfers between devices: 6.54 us -> 0.85 us  [swap(): return lax.ppermute(x, axis, [(0, 1), (1, 0)])]
    all_to_all x6 -> x5, starting transfers between devices: 37.3 us -> 32.5 us  [exchange(): return lax.all_to_all(x, axes, split_axis=0, concat_axis=0, tiled=True)]
    ppermute x9, starting transfers between devices: 20.9 us -> 16.6 us  [to_left(): return lax.ppermute(x, 'y', [(i, (i + 3) % 4) for i in range(4)])]
    ppermute x9, waiting for transfers between devices: 23.2 us -> 19.1 us  [to_right(): return lax.ppermute(x, 'y', [(i, (i + 1) % 4) for i in range(4)])]
    unnamed x55 -> x41, local copies, waits for them, and re-layouts: 8.66 us -> 4.6 us
  transfers between devices with their start and end apart: 33 -> 30, of which waited for: 19 -> 22; matrix products, arithmetic and copies ran while one was open for 3% -> 3% of each run, Pallas kernels for 5% -> 5%
where the time goes in v7:
time: 333 us; the launch traced here: 332 us
  waiting for transfers between devices  161 us (48%)
  starting transfers between devices  54.8 us (16%)
  Pallas kernels  49.3 us (15%)
  blocking collectives  40.3 us (12%)
  local copies, waits for them, and re-layouts  16.1 us (5%)
  other arithmetic  10.4 us (3%)
    all_to_all x5, waiting for transfers between devices, exchange(): return lax.all_to_all(x, axes, split_axis=0, concat_axis=0, tiled=True)  86.7 us
    all_to_all x2, blocking collectives, exchange(): return lax.all_to_all(x, axes, split_axis=0, concat_axis=0, tiled=True)  40.3 us
    ppermute x9, waiting for transfers between devices, to_left(): return lax.ppermute(x, 'y', [(i, (i + 3) % 4) for i in range(4)])  34.8 us
    all_to_all x5, starting transfers between devices, exchange(): return lax.all_to_all(x, axes, split_axis=0, concat_axis=0, tiled=True)  32.5 us
    ppermute x7, waiting for transfers between devices, swap(): return lax.ppermute(x, axis, [(0, 1), (1, 0)])  19.9 us
    ppermute x9, waiting for transfers between devices, to_right(): return lax.ppermute(x, 'y', [(i, (i + 1) % 4) for i in range(4)])  19.1 us
    pallas_call x2, Pallas kernels, attend(): pl.pallas_call(functools.partial(attend_kernel, scale, per_step, local_bl...  16.7 us
    ppermute x9, starting transfers between devices, to_left(): return lax.ppermute(x, 'y', [(i, (i + 3) % 4) for i in range(4)])  16.6 us
  transfers between devices with their start and end apart: 30, of which 22 were waited for; matrix products, arithmetic and copies ran while one was open for 3% of the time, Pallas kernels for 5%

profile of v7, /device:TPU:0, one launch (start us, length us, event | category | flops | bytes accessed | tf_op | source)
XLA Modules:
  0.0 331.9 jit_solution(14254908353109473359)
XLA Ops:
  3.6 3.6 %gather_fusion.1 = bf16[192,32,128]{2,1,0:T(8,128)(2,1)} fusion(bf16[256,32,128]{2,1,0:T(8,128)(2,1)} %bitcast.35, s32[1024]{0:T(1024)S(1)} %pad_clamp_fusion.1), kind=kCustom, calls=%fused_computation.1 | custom fusion | bytes 3146496 | tf_op jit(solution)/shard_map/gather | solution.py:448
  8.1 3.3 pad_maximum_fusion
  11.4 11.7 %all-to-all-start = ((bf16[64,224,128]{2,1,0:T(8,128)(2,1)}), bf16[64,224,128]{2,1,0:T(8,128)(2,1)}, u32[]{:S(2)}, u32[]{:S(2)}) async-start(bf16[64,224,128]{2,1,0:T(8,128)(2,1)} %pad_maximum_fusion), calls=%async_computation | async-start | bytes 7340032 | tf_op jit(solution)/shard_map/all_to_all | solution.py:401
  27.6 41.9 %all-to-all-done.refs_4_ = bf16[64,224,128]{2,1,0:T(8,128)(2,1)} async-done(((bf16[64,224,128]{2,1,0:T(8,128)(2,1)}), bf16[64,224,128]{2,1,0:T(8,128)(2,1)}, u32[]{:S(2)}, u32[]{:S(2)}) %all-to-all-start) | async-done | bytes 3670048 | tf_op jit(solution)/shard_map/all_to_all | solution.py:401
  69.5 6.9 %all-to-all-start.1 = ((bf16[64,64,128]{2,1,0:T(8,128)(2,1)}), bf16[64,64,128]{2,1,0:T(8,128)(2,1)S(1)}, u32[]{:S(2)}, u32[]{:S(2)}) async-start(bf16[64,64,128]{2,1,0:T(8,128)(2,1)} %pad_maximum_fusion.1), calls=%async_computation.1 | async-start | bytes 2097152 | tf_op jit(solution)/shard_map/all_to_all | solution.py:401
  77.9 12.7 %shard_map.118 = (f32[136,512]{1,0:T(8,128)S(1)}, f32[136,512]{1,0:T(8,128)S(1)}, s32[65]{0:T(128)S(1)}) custom-call(s32[64]{0:T(128)S(1)} %fusion.6.refs_0_, s32[2]{0:T(128)S(1)} %pad_add_fusion.refs_1_, bf16[128,512]{1,0:T(8,128)(2,1)S(1)} %copy-done.15, bf16[128,512]{1,0:T(8,128)(2,1)S(1)} %collective-permute-done.refs_3_.refs_2_, ...), custom_call_target="tpu_custom_call" | custom-call | flops 1174405120 | bytes 3670016 | tf_op jit(solution)/shard_map/pallas_call | solution.py:134
  90.7 3.7 %all-to-all-done.1.refs_3_ = bf16[64,64,128]{2,1,0:T(8,128)(2,1)S(1)} async-done(((bf16[64,64,128]{2,1,0:T(8,128)(2,1)}), bf16[64,64,128]{2,1,0:T(8,128)(2,1)S(1)}, u32[]{:S(2)}, u32[]{:S(2)}) %all-to-all-start.1) | async-done | bytes 1048608 | tf_op jit(solution)/shard_map/all_to_all | solution.py:401
  94.4 4.0 %shard_map.119 = (f32[136,512]{1,0:T(8,128)S(1)}, f32[136,512]{1,0:T(8,128)S(1)}) custom-call(s32[65]{0:T(128)S(1)} %get-tuple-element.44.refs_0_, bf16[128,512]{1,0:T(8,128)(2,1)S(1)} %copy-done.15, bf16[128,512]{1,0:T(8,128)(2,1)S(1)} %collective-permute-done.refs_3_.refs_2_, bf16[64,64,128]{2,1,0:T(8,128)(2,1)S(1)} %all-to-all-done.1.refs_3_, ...), custom_call_target="tpu_custom_call" | custom-call | flops 335544320 | bytes 1048576 | tf_op jit(solution)/shard_map/pallas_call | solution.py:134
  101.2 3.6 %all-to-all-start.2 = ((bf16[8,128,512]{2,1,0:T(8,128)(2,1)}), bf16[8,128,512]{2,1,0:T(8,128)(2,1)S(1)}, u32[]{:S(2)}, u32[]{:S(2)}) async-start(bf16[8,128,512]{2,1,0:T(8,128)(2,1)} %shard_map.120), calls=%async_computation.2 | async-start | bytes 2097152 | tf_op jit(solution)/shard_map/all_to_all | solution.py:401
  104.8 16.3 %all-to-all-done.2 = bf16[8,128,512]{2,1,0:T(8,128)(2,1)S(1)} async-done(((bf16[8,128,512]{2,1,0:T(8,128)(2,1)}), bf16[8,128,512]{2,1,0:T(8,128)(2,1)S(1)}, u32[]{:S(2)}, u32[]{:S(2)}) %all-to-all-start.2) | async-done | bytes 1048608 | tf_op jit(solution)/shard_map/all_to_all | solution.py:401
  121.9 2.6 collective-permute-done.2.refs_1_
  126.2 6.9 %all-to-all-start.3 = ((bf16[8,64,1024]{2,1,0:T(8,128)(2,1)}), bf16[8,64,1024]{2,1,0:T(8,128)(2,1)S(1)}, u32[]{:S(2)}, u32[]{:S(2)}) async-start(bf16[8,64,1024]{2,1,0:T(8,128)(2,1)} %bitcast.15), calls=%async_computation.3 | async-start | bytes 2097152 | tf_op jit(solution)/shard_map/all_to_all | solution.py:401
  133.1 17.5 %all-to-all-done.3 = bf16[8,64,1024]{2,1,0:T(8,128)(2,1)S(1)} async-done(((bf16[8,64,1024]{2,1,0:T(8,128)(2,1)}), bf16[8,64,1024]{2,1,0:T(8,128)(2,1)S(1)}, u32[]{:S(2)}, u32[]{:S(2)}) %all-to-all-start.3) | async-done | bytes 1048608 | tf_op jit(solution)/shard_map/all_to_all | solution.py:401
  151.0 20.0 %all_to_all.35 = bf16[8,64,1024]{2,1,0:T(8,128)(2,1)} all-to-all(bf16[8,64,1024]{2,1,0:T(8,128)(2,1)S(1)} %broadcast_in_dim.10), channel_id=1, replica_groups=mesh['z'=4,'xh'=2,'core'=2,'y'=4,'xl'=2] {'z','xh'}, dimensions={0} | all-to-all | bytes 2097152 | tf_op jit(solution)/shard_map/all_to_all | solution.py:401
  174.8 14.8 %shard_map.123 = (bf16[64,3584]{1,0:T(8,128)(2,1)}, bf16[64,3584]{1,0:T(8,128)(2,1)}, bf16[64,3584]{1,0:T(8,128)(2,1)}, bf16[64,3584]{1,0:T(8,128)(2,1)}, bf16[6...) custom-call(s32[2]{0:T(128)} %pad_add_fusion.1.place_ref, ...), custom_call_target="tpu_custom_call" | custom-call | flops 7516192768 | bytes 16777216 | tf_op jit(solution)/shard_map/pallas_call | solution.py:259
  196.4 6.9 %collective-permute-done.5.refs_1_ = bf16[64,3584]{1,0:T(8,128)(2,1)S(1)} collective-permute-done((bf16[64,3584]{1,0:T(8,128)(2,1)}, bf16[64,3584]{1,0:T(8,128)(2,1)S(1)}, u32[]{:S(2)}, u32[]{:S(2)}) %collective-permute-start.5) | collective-permute-done | bytes 458784 | tf_op jit(solution)/shard_map/ppermute | solution.py:371
  206.7 3.2 collective-permute-start.15
  210.6 3.3 all-to-all-start.5
  213.9 3.2 collective-permute-start.10
  217.1 7.4 %all-to-all-done.5 = f32[8,1,128]{2,1,0:T(1,128)S(1)} async-done(((f32[8,1,128]{2,1,0:T(1,128)}), f32[8,1,128]{2,1,0:T(1,128)S(1)}, u32[]{:S(2)}, u32[]{:S(2)}) %all-to-all-start.5) | async-done | bytes 4128 | tf_op jit(solution)/shard_map/all_to_all | solution.py:401
  228.1 3.2 collective-permute-start.6
  238.0 2.6 collective-permute-done.7.refs_1_
  242.7 7.8 %collective-permute-done.9.refs_4_ = bf16[64,3584]{1,0:T(8,128)(2,1)} collective-permute-done((bf16[64,3584]{1,0:T(8,128)(2,1)}, bf16[64,3584]{1,0:T(8,128)(2,1)}, u32[]{:S(2)}, u32[]{:S(2)}) %collective-permute-start.9) | collective-permute-done | bytes 458784 | tf_op jit(solution)/shard_map/ppermute | solution.py:367
  251.8 6.4 %collective-permute-done.8.refs_2_ = bf16[64,3584]{1,0:T(8,128)(2,1)} collective-permute-done((bf16[64,3584]{1,0:T(8,128)(2,1)}, bf16[64,3584]{1,0:T(8,128)(2,1)}, u32[]{:S(2)}, u32[]{:S(2)}) %collective-permute-start.8) | collective-permute-done | bytes 458784 | tf_op jit(solution)/shard_map/ppermute | solution.py:367
  260.8 10.2 %collective-permute-done.17.refs_1_ = bf16[128,1792]{1,0:T(8,128)(2,1)S(1)} collective-permute-done((bf16[128,1792]{1,0:T(8,128)(2,1)S(1)}, bf16[128,1792]{1,0:T(8,128)(2,1)S(1)}, u32[]{:S(2)}, u32[]{:S(2)}) %collective-permute-start.17) | collective-permute-done | bytes 458784 | tf_op jit(solution)/shard_map/ppermute | solution.py:405
  275.1 9.4 %collective-permute-done.19.refs_3_ = bf16[128,1792]{1,0:T(8,128)(2,1)S(1)} collective-permute-done((bf16[128,1792]{1,0:T(8,128)(2,1)S(1)}, bf16[128,1792]{1,0:T(8,128)(2,1)S(1)}, u32[]{:S(2)}, u32[]{:S(2)}) %collective-permute-start.19) | collective-permute-done | bytes 458784 | tf_op jit(solution)/shard_map/ppermute | solution.py:371
  285.7 8.6 %collective-permute-done.18.refs_2_ = bf16[128,1792]{1,0:T(8,128)(2,1)S(1)} collective-permute-done((bf16[128,1792]{1,0:T(8,128)(2,1)S(1)}, bf16[128,1792]{1,0:T(8,128)(2,1)S(1)}, u32[]{:S(2)}, u32[]{:S(2)}) %collective-permute-start.18) | collective-permute-done | bytes 458784 | tf_op jit(solution)/shard_map/ppermute | solution.py:371
  294.3 5.9 %collective-permute-done.22.refs_5_ = bf16[128,1792]{1,0:T(8,128)(2,1)S(1)} collective-permute-done((bf16[128,1792]{1,0:T(8,128)(2,1)S(1)}, bf16[128,1792]{1,0:T(8,128)(2,1)S(1)}, u32[]{:S(2)}, u32[]{:S(2)}) %collective-permute-start.22) | collective-permute-done | bytes 458784 | tf_op jit(solution)/shard_map/ppermute | solution.py:371
  300.2 3.8 %shard_map.130 = bf16[8,64,1024]{2,1,0:T(8,128)(2,1)S(1)} custom-call(s32[2]{0:T(128)S(1)} %copy-done.14, bf16[128,1792]{1,0:T(8,128)(2,1)S(1)} %shard_map.129.refs_0_, bf16[128,1792]{1,0:T(8,128)(2,1)S(1)} %collective-permute-done.17.refs_1_, bf16[128,1792]{1,0:T(8,128)(2,1)S(1)} %collective-permute-done.18.refs_2_, ...), custom_call_target="tpu_custom_call" | custom-call | flops 1879048192 | bytes 6553600 | tf_op jit(solution)/shard_map/pallas_call | solution.py:351
  304.1 2.6 collective-permute-done.24.refs_9_
  306.8 3.9 %shard_map.131 = bf16[8,64,1024]{2,1,0:T(8,128)(2,1)S(1)} custom-call(s32[2]{0:T(128)S(1)} %copy-done.14, bf16[128,1792]{1,0:T(8,128)(2,1)S(1)} %shard_map.129.refs_0_, bf16[128,1792]{1,0:T(8,128)(2,1)S(1)} %collective-permute-done.17.refs_1_, bf16[128,1792]{1,0:T(8,128)(2,1)S(1)} %collective-permute-done.18.refs_2_, ...), custom_call_target="tpu_custom_call" | custom-call | flops 1879048192 | bytes 6553600 | tf_op jit(solution)/shard_map/pallas_call | solution.py:351
  310.7 20.3 %all_to_all.36 = bf16[8,64,1024]{2,1,0:T(8,128)(2,1)S(1)} all-to-all(bf16[8,64,1024]{2,1,0:T(8,128)(2,1)S(1)} %shard_map.131), channel_id=1, replica_groups=mesh['z'=4,'xh'=2,'core'=2,'y'=4,'xl'=2] {'z','xh'}, dimensions={0} | all-to-all | bytes 2097152 | tf_op jit(solution)/shard_map/all_to_all | solution.py:401
  (125 shorter events, 53.2 us)
Async XLA Ops:
  11.4 58.1 %all-to-all-start = ((bf16[64,224,128]{2,1,0:T(8,128)(2,1)}), bf16[64,224,128]{2,1,0:T(8,128)(2,1)}, u32[]{:S(2)}, u32[]{:S(2)}) async-start(bf16[64,224,128]{2,1,0:T(8,128)(2,1)} %pad_maximum_fusion), calls=%async_computation | async-start | bytes 7340032 | tf_op jit(solution)/shard_map/all_to_all | solution.py:401
  69.5 24.8 %all-to-all-start.1 = ((bf16[64,64,128]{2,1,0:T(8,128)(2,1)}), bf16[64,64,128]{2,1,0:T(8,128)(2,1)S(1)}, u32[]{:S(2)}, u32[]{:S(2)}) async-start(bf16[64,64,128]{2,1,0:T(8,128)(2,1)} %pad_maximum_fusion.1), calls=%async_computation.1 | async-start | bytes 2097152 | tf_op jit(solution)/shard_map/all_to_all | solution.py:401
  76.5 1.4 collective-permute-start
  98.4 1.6 collective-permute-start.1
  101.2 19.8 %all-to-all-start.2 = ((bf16[8,128,512]{2,1,0:T(8,128)(2,1)}), bf16[8,128,512]{2,1,0:T(8,128)(2,1)S(1)}, u32[]{:S(2)}, u32[]{:S(2)}) async-start(bf16[8,128,512]{2,1,0:T(8,128)(2,1)} %shard_map.120), calls=%async_computation.2 | async-start | bytes 2097152 | tf_op jit(solution)/shard_map/all_to_all | solution.py:401
  121.8 2.7 collective-permute-start.2
  126.2 24.5 %all-to-all-start.3 = ((bf16[8,64,1024]{2,1,0:T(8,128)(2,1)}), bf16[8,64,1024]{2,1,0:T(8,128)(2,1)S(1)}, u32[]{:S(2)}, u32[]{:S(2)}) async-start(bf16[8,64,1024]{2,1,0:T(8,128)(2,1)} %bitcast.15), calls=%async_computation.3 | async-start | bytes 2097152 | tf_op jit(solution)/shard_map/all_to_all | solution.py:401
  171.0 2.9 collective-permute-start.3
  189.7 13.6 %collective-permute-start.5 = (bf16[64,3584]{1,0:T(8,128)(2,1)}, bf16[64,3584]{1,0:T(8,128)(2,1)S(1)}, u32[]{:S(2)}, u32[]{:S(2)}) collective-permute-start(bf16[64,3584]{1,0:T(8,128)(2,1)} %get-tuple-element.52), channel_id=1, source_target_pairs={{0,6},{2,0},{4,2},{6,4},{1,7},{3,1},{5,3},{7,5},{8,14},{10,8},{12,... | collective-permute-start | bytes 1376264 | tf_op jit(solution)/shard_map/ppermute | solution.py:371
  190.9 14.8 %collective-permute-start.4 = (bf16[64,3584]{1,0:T(8,128)(2,1)}, bf16[64,3584]{1,0:T(8,128)(2,1)S(1)}, u32[]{:S(2)}, u32[]{:S(2)}) collective-permute-start(bf16[64,3584]{1,0:T(8,128)(2,1)} %get-tuple-element.50), channel_id=1, source_target_pairs={{0,2},{2,4},{4,6},{6,0},{1,3},{3,5},{5,7},{7,1},{8,10},{10,12},{12... | collective-permute-start | bytes 1376264 | tf_op jit(solution)/shard_map/ppermute | solution.py:367
  191.8 33.9 %collective-permute-start.12 = (bf16[64,3584]{1,0:T(8,128)(2,1)}, bf16[64,3584]{1,0:T(8,128)(2,1)S(1)}, u32[]{:S(2)}, u32[]{:S(2)}) collective-permute-start(bf16[64,3584]{1,0:T(8,128)(2,1)} %get-tuple-element.70), channel_id=1, source_target_pairs={{0,6},{2,0},{4,2},{6,4},{1,7},{3,1},{5,3},{7,5},{8,14},{10,8},{12,... | collective-permute-start | bytes 1376264 | tf_op jit(solution)/shard_map/ppermute | solution.py:371
  194.2 31.5 %collective-permute-start.14 = (bf16[64,3584]{1,0:T(8,128)(2,1)}, bf16[64,3584]{1,0:T(8,128)(2,1)S(1)}, u32[]{:S(2)}, u32[]{:S(2)}) collective-permute-start(bf16[64,3584]{1,0:T(8,128)(2,1)} %get-tuple-element.73), channel_id=1, source_target_pairs={{0,2},{2,4},{4,6},{6,0},{1,3},{3,5},{5,7},{7,1},{8,10},{10,12},{12... | collective-permute-start | bytes 1376264 | tf_op jit(solution)/shard_map/ppermute | solution.py:367
  206.7 19.0 %collective-permute-start.13 = (bf16[64,3584]{1,0:T(8,128)(2,1)}, bf16[64,3584]{1,0:T(8,128)(2,1)S(1)}, u32[]{:S(2)}, u32[]{:S(2)}) collective-permute-start(bf16[64,3584]{1,0:T(8,128)(2,1)} %shard_map.124), channel_id=1, source_target_pairs={{0,2},{2,4},{4,6},{6,0},{1,3},{3,5},{5,7},{7,1},{8,10},{10,12},{12... | collective-permute-start | bytes 1376264 | tf_op jit(solution)/shard_map/ppermute | solution.py:367
  206.7 19.1 %collective-permute-start.15 = (bf16[64,3584]{1,0:T(8,128)(2,1)S(1)}, bf16[64,3584]{1,0:T(8,128)(2,1)S(1)}, u32[]{:S(2)}, u32[]{:S(2)}) collective-permute-start(bf16[64,3584]{1,0:T(8,128)(2,1)S(1)} %shard_map.125), channel_id=1, source_target_pairs={{0,6},{2,0},{4,2},{6,4},{1,7},{3,1},{5,3},{7,5},{8,14},{10,8},{12,... | collective-permute-start | bytes 1376264 | tf_op jit(solution)/shard_map/ppermute | solution.py:371
  210.6 13.8 %all-to-all-start.5 = ((f32[8,1,128]{2,1,0:T(1,128)}), f32[8,1,128]{2,1,0:T(1,128)S(1)}, u32[]{:S(2)}, u32[]{:S(2)}) async-start(f32[8,1,128]{2,1,0:T(1,128)} %reshape.207), calls=%async_computation.5 | async-start | bytes 8192 | tf_op jit(solution)/shard_map/all_to_all | solution.py:401
  213.9 19.1 %collective-permute-start.10 = (bf16[64,3584]{1,0:T(8,128)(2,1)}, bf16[64,3584]{1,0:T(8,128)(2,1)}, u32[]{:S(2)}, u32[]{:S(2)}) collective-permute-start(bf16[64,3584]{1,0:T(8,128)(2,1)} %get-tuple-element.68), channel_id=1, source_target_pairs={{0,6},{2,0},{4,2},{6,4},{1,7},{3,1},{5,3},{7,5},{8,14},{10,8},{12,... | collective-permute-start | bytes 1376264 | tf_op jit(solution)/shard_map/ppermute | solution.py:371
  225.7 14.9 %collective-permute-start.7 = (bf16[64,3584]{1,0:T(8,128)(2,1)}, bf16[64,3584]{1,0:T(8,128)(2,1)S(1)}, u32[]{:S(2)}, u32[]{:S(2)}) collective-permute-start(bf16[64,3584]{1,0:T(8,128)(2,1)} %get-tuple-element.64), channel_id=1, source_target_pairs={{0,2},{2,4},{4,6},{6,0},{1,3},{3,5},{5,7},{7,1},{8,10},{10,12},{12... | collective-permute-start | bytes 1376264 | tf_op jit(solution)/shard_map/ppermute | solution.py:367
  227.9 30.3 %collective-permute-start.16 = (bf16[2,64,3584]{2,1,0:T(8,128)(2,1)S(1)}, bf16[2,64,3584]{2,1,0:T(8,128)(2,1)S(1)}, u32[]{:S(2)}, u32[]{:S(2)}) collective-permute-start(bf16[2,64,3584]{2,1,0:T(8,128)(2,1)S(1)} %shard_map.128), channel_id=1, source_target_pairs={{0,1},{1,0},{2,3},{3,2},{4,5},{5,4},{6,7},{7,6},{8,9},{9,8},{10,11... | collective-permute-start | bytes 2752520 | tf_op jit(solution)/shard_map/ppermute | solution.py:405
  228.1 14.5 %collective-permute-start.6 = (bf16[64,3584]{1,0:T(8,128)(2,1)}, bf16[64,3584]{1,0:T(8,128)(2,1)S(1)}, u32[]{:S(2)}, u32[]{:S(2)}) collective-permute-start(bf16[64,3584]{1,0:T(8,128)(2,1)} %get-tuple-element.62), channel_id=1, source_target_pairs={{0,6},{2,0},{4,2},{6,4},{1,7},{3,1},{5,3},{7,5},{8,14},{10,8},{12,... | collective-permute-start | bytes 1376264 | tf_op jit(solution)/shard_map/ppermute | solution.py:371
  231.4 19.1 %collective-permute-start.9 = (bf16[64,3584]{1,0:T(8,128)(2,1)}, bf16[64,3584]{1,0:T(8,128)(2,1)}, u32[]{:S(2)}, u32[]{:S(2)}) collective-permute-start(bf16[64,3584]{1,0:T(8,128)(2,1)} %get-tuple-element.66), channel_id=1, source_target_pairs={{0,2},{2,4},{4,6},{6,0},{1,3},{3,5},{5,7},{7,1},{8,10},{10,12},{12... | collective-permute-start | bytes 1376264 | tf_op jit(solution)/shard_map/ppermute | solution.py:367
  235.9 15.9 %collective-permute-start.11 = (bf16[64,3584]{1,0:T(8,128)(2,1)}, bf16[64,3584]{1,0:T(8,128)(2,1)}, u32[]{:S(2)}, u32[]{:S(2)}) collective-permute-start(bf16[64,3584]{1,0:T(8,128)(2,1)} %shard_map.127), channel_id=1, source_target_pairs={{0,6},{2,0},{4,2},{6,4},{1,7},{3,1},{5,3},{7,5},{8,14},{10,8},{12,... | collective-permute-start | bytes 1376264 | tf_op jit(solution)/shard_map/ppermute | solution.py:371
  241.5 16.8 %collective-permute-start.8 = (bf16[64,3584]{1,0:T(8,128)(2,1)}, bf16[64,3584]{1,0:T(8,128)(2,1)}, u32[]{:S(2)}, u32[]{:S(2)}) collective-permute-start(bf16[64,3584]{1,0:T(8,128)(2,1)} %shard_map.126), channel_id=1, source_target_pairs={{0,2},{2,4},{4,6},{6,0},{1,3},{3,5},{5,7},{7,1},{8,10},{10,12},{12... | collective-permute-start | bytes 1376264 | tf_op jit(solution)/shard_map/ppermute | solution.py:367
  241.6 58.6 %copy-start.2 = (bf16[1792,1024]{1,0:T(8,128)(2,1)S(1)}, bf16[1792,1024]{1,0:T(8,128)(2,1)}, u32[]{:S(2)}) copy-start(bf16[1792,1024]{1,0:T(8,128)(2,1)} %refs_8_.3) | copy-start | bytes 11010052
  241.6 58.6 %copy-start.14 = (s32[2]{0:T(128)S(1)}, s32[2]{0:T(128)}, u32[]{:S(2)}) copy-start(s32[2]{0:T(128)} %pad_add_fusion.1.place_ref) | copy-start | bytes 28
  260.5 10.5 %collective-permute-start.17 = (bf16[128,1792]{1,0:T(8,128)(2,1)S(1)}, bf16[128,1792]{1,0:T(8,128)(2,1)S(1)}, u32[]{:S(2)}, u32[]{:S(2)}) collective-permute-start(bf16[128,1792]{1,0:T(8,128)(2,1)S(1)} %shard_map.129.refs_0_), channel_id=1, source_target_pairs={{0,1},{1,0},{2,3},{3,2},{4,5},{5,4},{6,7},{7,6},{8,9},{9,8},{10,11... | collective-permute-start | bytes 1376264 | tf_op jit(solution)/shard_map/ppermute | solution.py:405
  260.8 12.3 %collective-permute-start.20 = (bf16[128,1792]{1,0:T(8,128)(2,1)S(1)}, bf16[128,1792]{1,0:T(8,128)(2,1)S(1)}, u32[]{:S(2)}, u32[]{:S(2)}) collective-permute-start(bf16[128,1792]{1,0:T(8,128)(2,1)S(1)} %shard_map.129.refs_0_), channel_id=1, source_target_pairs={{0,2},{2,4},{4,6},{6,0},{1,3},{3,5},{5,7},{7,1},{8,10},{10,12},{12... | collective-permute-start | bytes 1376264 | tf_op jit(solution)/shard_map/ppermute | solution.py:367
  271.0 13.5 %collective-permute-start.19 = (bf16[128,1792]{1,0:T(8,128)(2,1)S(1)}, bf16[128,1792]{1,0:T(8,128)(2,1)S(1)}, u32[]{:S(2)}, u32[]{:S(2)}) collective-permute-start(bf16[128,1792]{1,0:T(8,128)(2,1)S(1)} %collective-permute-done.17.refs_1_), channel_id=1, source_target_pairs={{0,6},{2,0},{4,2},{6,4},{1,7},{3,1},{5,3},{7,5},{8,14},{10,8},{12,... | collective-permute-start | bytes 1376264 | tf_op jit(solution)/shard_map/ppermute | solution.py:371
  271.0 23.3 %collective-permute-start.18 = (bf16[128,1792]{1,0:T(8,128)(2,1)S(1)}, bf16[128,1792]{1,0:T(8,128)(2,1)S(1)}, u32[]{:S(2)}, u32[]{:S(2)}) collective-permute-start(bf16[128,1792]{1,0:T(8,128)(2,1)S(1)} %shard_map.129.refs_0_), channel_id=1, source_target_pairs={{0,6},{2,0},{4,2},{6,4},{1,7},{3,1},{5,3},{7,5},{8,14},{10,8},{12,... | collective-permute-start | bytes 1376264 | tf_op jit(solution)/shard_map/ppermute | solution.py:371
  271.1 23.3 %collective-permute-start.23 = (bf16[128,1792]{1,0:T(8,128)(2,1)S(1)}, bf16[128,1792]{1,0:T(8,128)(2,1)S(1)}, u32[]{:S(2)}, u32[]{:S(2)}) collective-permute-start(bf16[128,1792]{1,0:T(8,128)(2,1)S(1)} %collective-permute-done.17.refs_1_), channel_id=1, source_target_pairs={{0,2},{2,4},{4,6},{6,0},{1,3},{3,5},{5,7},{7,1},{8,10},{10,12},{12... | collective-permute-start | bytes 1376264 | tf_op jit(solution)/shard_map/ppermute | solution.py:367
  273.1 21.2 %collective-permute-start.21 = (bf16[128,1792]{1,0:T(8,128)(2,1)S(1)}, bf16[128,1792]{1,0:T(8,128)(2,1)S(1)}, u32[]{:S(2)}, u32[]{:S(2)}) collective-permute-start(bf16[128,1792]{1,0:T(8,128)(2,1)S(1)} %collective-permute-done.20.refs_6_), channel_id=1, source_target_pairs={{0,2},{2,4},{4,6},{6,0},{1,3},{3,5},{5,7},{7,1},{8,10},{10,12},{12... | collective-permute-start | bytes 1376264 | tf_op jit(solution)/shard_map/ppermute | solution.py:367
  284.5 15.7 %collective-permute-start.22 = (bf16[128,1792]{1,0:T(8,128)(2,1)S(1)}, bf16[128,1792]{1,0:T(8,128)(2,1)S(1)}, u32[]{:S(2)}, u32[]{:S(2)}) collective-permute-start(bf16[128,1792]{1,0:T(8,128)(2,1)S(1)} %collective-permute-done.19.refs_3_), channel_id=1, source_target_pairs={{0,6},{2,0},{4,2},{6,4},{1,7},{3,1},{5,3},{7,5},{8,14},{10,8},{12,... | collective-permute-start | bytes 1376264 | tf_op jit(solution)/shard_map/ppermute | solution.py:371
  304.0 2.7 collective-permute-start.24
  (18 other events, 323.6 us)

commit v8 on v7

--- a/solution.py
+++ b/solution.py
@@ -324,43 +324,57 @@
     return small_call(kernel, out, (), arrays, 16 * tokens * width)
 
 
-def down_kernel(tile, place_ref, *refs):
-    y, side = place_ref[0], place_ref[1]
-    pieces, weight_ref, add_ref, out_ref = refs[:8], refs[8], refs[9:-1], refs[-1]
-    n = pieces[0].shape[0]
-    x = jnp.concatenate([p[...] for p in pieces], axis=0)
-    total = jnp.dot(x, weight_ref[...], preferred_element_type=f32)
-    for i in range(4):
-        for j in range(2):
-            at = 2 * ((y + i) % 4) + (side if j == 0 else 1 - side)
-            part = total[(2 * i + j) * n : (2 * i + j + 1) * n]
-            if add_ref:
-                part = part + add_ref[0][at].astype(f32)
-            out_ref[at] = part.astype(bf16)
-
-
-def down_product(place, pieces, half, weight, add=None):
-    tile = 256
-    tokens, inputs = pieces[0].shape[0] // 2, pieces[0].shape[1]
+def down_product(pieces, weight):
+    tile = 512
+    count, tokens, inputs = len(pieces), pieces[0].shape[0] // 2, pieces[0].shape[1]
     width = weight.shape[1]
-    piece = pl.BlockSpec((tokens, inputs), lambda n, p: (half, 0))
-    by_column = pl.BlockSpec((8, tokens, tile), lambda n, p: (0, 0, n))
-    operands = [*pieces, weight] + ([] if add is None else [add])
-    specs = [piece] * 8 + [pl.BlockSpec((inputs, tile), lambda n, p: (0, n))]
-    specs += [] if add is None else [by_column]
-    return pl.pallas_call(
-        functools.partial(down_kernel, tile),
-        out_shape=jax.ShapeDtypeStruct((8, tokens, width), bf16),
-        grid_spec=pltpu.PrefetchScalarGridSpec(
-            num_scalar_prefetch=1, grid=(width // tile,), in_specs=specs, out_specs=by_column
-        ),
-        compiler_params=pltpu.CompilerParams(vmem_limit_bytes=20 * 1024 * 1024),
+
+    def kernel(*refs):
+        weight_ref, keep_ref, give_ref = refs[count:]
+        x = jnp.concatenate([p[...] for p in refs[:count]], axis=0)
+        total = jnp.dot(x, weight_ref[...], preferred_element_type=f32)
+        for i in range(count):
+            at = 2 * i * tokens
+            keep_ref[i] = total[at : at + tokens]
+            give_ref[i] = total[at + tokens : at + 2 * tokens].astype(bf16)
+
+    by_column = pl.BlockSpec((count, tokens, tile), lambda n: (0, 0, n))
+    specs = [pl.BlockSpec((2 * tokens, inputs), lambda n: (0, 0))] * count
+    return pl.pallas_call(
+        kernel,
+        grid=(width // tile,),
+        out_shape=(
+            jax.ShapeDtypeStruct((count, tokens, width), f32),
+            jax.ShapeDtypeStruct((count, tokens, width), bf16),
+        ),
+        in_specs=specs + [pl.BlockSpec((inputs, tile), lambda n: (0, n))],
+        out_specs=(by_column, by_column),
+        compiler_params=pltpu.CompilerParams(vmem_limit_bytes=24 * 1024 * 1024),
         cost_estimate=pl.CostEstimate(
-            flops=16 * tokens * inputs * width,
-            bytes_accessed=2 * (8 * tokens * inputs + inputs * width + 8 * tokens * width),
+            flops=4 * count * tokens * inputs * width,
+            bytes_accessed=2 * (2 * count * tokens * inputs + inputs * width + 3 * count * tokens * width),
             transcendentals=0,
         ),
-    )(place, *operands)
+    )(*pieces, weight)
+
+
+def join_blocks(place, near, far):
+    def kernel(place_ref, near_ref, near_got_ref, far_ref, far_got_ref, out_ref):
+        y, side = place_ref[0], place_ref[1]
+        for i, (kept_ref, got_ref, first) in enumerate(
+            (
+                (near_ref, near_got_ref, 0),
+                (near_ref, near_got_ref, 2),
+                (far_ref, far_got_ref, 0),
+                (near_ref, near_got_ref, 4),
+            )
+        ):
+            for j in range(2):
+                at = 2 * ((y + i) % 4) + (side if j == 0 else 1 - side)
+                out_ref[at] = (kept_ref[first + j] + got_ref[first + j].astype(f32)).astype(bf16)
+
+    out = jax.ShapeDtypeStruct((8, *near[0].shape[1:]), bf16)
+    return small_call(kernel, out, (place,), (*near, *far), 4 * near[0].size)
 
 
 def to_right(x):
@@ -389,12 +403,37 @@
     return to_right(mine), to_left(mine)
 
 
-def gather_middle(got, mine_left):
-    return to_right(got), to_left(got), to_right(mine_left)
-
-
-def gather_end(mine, got, mine_left, mine_right, got_left, got_right, mine_far):
-    return mine, got, mine_right, got_right, mine_far, to_left(got_right), mine_left, got_left
+def pack_kernel(within_ref, group_ref, keys_ref, values_ref, near_keys_ref, near_values_ref, out_ref):
+    eighth = BLK // 8
+    rows = (out_ref.shape[1] - 2 * eighth) // 2
+    goal = pl.program_id(0)
+    near = pl.ds(pl.multiple_of(group_ref[0] * eighth, eighth), eighth)
+    for i in range(out_ref.shape[0]):
+        at = within_ref[goal, i]
+        out_ref[i, 0:rows] = keys_ref[at, 0:rows]
+        out_ref[i, rows : 2 * rows] = values_ref[at, 0:rows]
+        out_ref[i, 2 * rows : 2 * rows + eighth] = near_keys_ref[0, near]
+        out_ref[i, 2 * rows + eighth :] = near_values_ref[0, near]
+
+
+def pack(within, group, keys, values, near_keys, near_values, rows):
+    def of_group(x):
+        return pl.BlockSpec((x.shape[0] // KV_HEADS, *x.shape[1:]), lambda n, s, g: (n, 0, 0))
+
+    arrays = (keys, values, near_keys, near_values)
+    height = 2 * rows + BLK // 4
+    return pl.pallas_call(
+        pack_kernel,
+        out_shape=jax.ShapeDtypeStruct((64, height, HEAD_DIM), bf16),
+        grid_spec=pltpu.PrefetchScalarGridSpec(
+            num_scalar_prefetch=2,
+            grid=(8,),
+            in_specs=[of_group(x) for x in arrays],
+            out_specs=pl.BlockSpec((8, height, HEAD_DIM), lambda n, s, g: (n, 0, 0)),
+        ),
+        compiler_params=pltpu.CompilerParams(vmem_limit_bytes=60 * 1024 * 1024),
+        cost_estimate=pl.CostEstimate(flops=0, bytes_accessed=64 * height * 512, transcendentals=0),
+    )(within, group.astype(jnp.int32).reshape(1), *arrays)
 
 
 def exchange(x, axes):
@@ -447,13 +486,12 @@
         index = 4 * source[:, None] + jnp.arange(first, first + count, dtype=jnp.int32)[None, :]
         return flat[index].reshape(64, count * piece, HEAD_DIM)
 
-    def near(stretch):
-        part = BLK // 8
-        rows = lax.dynamic_slice_in_dim(stretch, group * part, part, 1)
-        return jnp.broadcast_to(rows[:, None], (KV_HEADS, 8, part, HEAD_DIM)).reshape(64, part, HEAD_DIM)
-
-    first = [pick(flat_keys, 0, 3), pick(flat_values, 0, 3), near(stretch_keys), near(stretch_values)]
-    first = exchange(jnp.concatenate(first, axis=1), CHIP)
+    blocked = (KV_HEADS * local_blocks, BLK, HEAD_DIM)
+    first = pack(
+        within.T, group, cache_keys.reshape(blocked), cache_values.reshape(blocked),
+        stretch_keys, stretch_values, 3 * piece,
+    )
+    first = exchange(first, CHIP)
     second = [pick(flat_keys, 3, 1), pick(flat_values, 3, 1)]
     second = exchange(jnp.concatenate(second, axis=1), CHIP)
     my_list = block_lists[col, group]
@@ -496,11 +534,15 @@
     factor = lax.rsqrt(jnp.sum(squares, axis=0).reshape(-1) / D + 1e-05)
     halves = ring_end(mine, mine_arrived, ring_middle(mine, *mine_arrived[:2]))
     hidden = gated(halves, got, factor)
-    hidden_got = swap(hidden, "xl")
-    first = gather_start(hidden)
-    pieces = gather_end(hidden, hidden_got, *first, *gather_middle(hidden_got, first[0]))
-    given = down_product(where, pieces, 1, down_weight)
-    down = down_product(where, pieces, 0, down_weight, add=swap(given))
+    first, hidden_got = lax.optimization_barrier((gather_start(hidden), swap(hidden, "xl")))
+    got_left, got_right = to_right(hidden_got), to_left(hidden_got)
+    mine_far = to_right(first[0])
+    got_left, got_right, mine_far = lax.optimization_barrier((got_left, got_right, mine_far))
+    got_far = to_left(got_right)
+    near = (hidden, hidden_got, first[1], got_right, first[0], got_left)
+    kept, give = down_product(near, down_weight)
+    far_kept, far_give = down_product((mine_far, got_far), down_weight)
+    down = join_blocks(where, (kept, swap(give)), (far_kept, swap(far_give)))
     mlp = jnp.sum(exchange(down, ZXH).astype(f32), axis=0)
     return (stream + mlp).astype(bf16)
 

time: 333 us -> 325 us (0.976)
  waiting for transfers between devices: 161 us -> 155 us
  local copies, waits for them, and re-layouts: 16.1 us -> 10.4 us
  other arithmetic: 10.4 us -> 6.98 us
    ppermute x9, waiting for transfers between devices: 19.1 us -> 43.3 us  [to_right(): return lax.ppermute(x, 'y', [(i, (i + 1) % 4) for i in range(4)])]
    ppermute x9, waiting for transfers between devices: 34.8 us -> 15.7 us  [to_left(): return lax.ppermute(x, 'y', [(i, (i + 3) % 4) for i in range(4)])]
    ppermute x7 -> x8, waiting for transfers between devices: 19.9 us -> 10.2 us  [swap(): return lax.ppermute(x, axis, [(0, 1), (1, 0)])]
    ppermute x9, starting transfers between devices: 16.6 us -> 21.8 us  [to_left(): return lax.ppermute(x, 'y', [(i, (i + 3) % 4) for i in range(4)])]
    pallas_call x2 -> x3, Pallas kernels: 7.73 us -> 12.4 us  [the longest x1 7.19 us: pack(): pl.pallas_call(pack_kernel, out_shape=jax.ShapeDtypeStruct((64, height, H...]
    gather x4 -> x2, local copies, waits for them, and re-layouts: 8.54 us -> 4.5 us  [pick(): return flat[index].reshape(64, count * piece, HEAD_DIM)]
    ppermute x9, starting transfers between devices: 4.91 us -> 1.12 us  [to_right(): return lax.ppermute(x, 'y', [(i, (i + 1) % 4) for i in range(4)])]
    pallas_call x6 -> x7, Pallas kernels: 6.42 us -> 7.13 us  [small_call(): pl.pallas_call(kernel, out_shape=outs, in_specs=[SMEM] * len(scalars) + [...]
  transfers between devices with their start and end apart: 30 -> 31, of which waited for: 22 -> 23; matrix products, arithmetic and copies ran while one was open for 3% -> 4% of each run, Pallas kernels for 5% -> 6%
where the time goes in v8:
time: 325 us; the launch traced here: 324 us
  waiting for transfers between devices  155 us (48%)
  starting transfers between devices  58.1 us (18%)
  Pallas kernels  52.4 us (16%)
  blocking collectives  40.3 us (12%)
  local copies, waits for them, and re-layouts  10.4 us (3%)
  other arithmetic  6.98 us (2%)
    all_to_all x5, waiting for transfers between devices, exchange(): return lax.all_to_all(x, axes, split_axis=0, concat_axis=0, tiled=True)  86.1 us
    ppermute x9, waiting for transfers between devices, to_right(): return lax.ppermute(x, 'y', [(i, (i + 1) % 4) for i in range(4)])  43.3 us
    all_to_all x2, blocking collectives, exchange(): return lax.all_to_all(x, axes, split_axis=0, concat_axis=0, tiled=True)  40.3 us
    all_to_all x5, starting transfers between devices, exchange(): return lax.all_to_all(x, axes, split_axis=0, concat_axis=0, tiled=True)  33.9 us
    ppermute x9, starting transfers between devices, to_left(): return lax.ppermute(x, 'y', [(i, (i + 3) % 4) for i in range(4)])  21.8 us
    ppermute x9, waiting for transfers between devices, to_left(): return lax.ppermute(x, 'y', [(i, (i + 3) % 4) for i in range(4)])  15.7 us
    pallas_call x1, Pallas kernels, partial_columns(): pl.pallas_call(columns_kernel, out_shape=(jax.ShapeDtypeStruct((tokens, 2...  14.8 us
    pallas_call x2, Pallas kernels, attend(): pl.pallas_call(functools.partial(attend_kernel, scale, per_step, local_bl...  14.5 us
  transfers between devices with their start and end apart: 31, of which 23 were waited for; matrix products, arithmetic and copies ran while one was open for 4% of the time, Pallas kernels for 6%

profile of v8, /device:TPU:0, one launch (start us, length us, event | category | flops | bytes accessed | tf_op | source)
XLA Modules:
  0.0 323.9 jit_solution(15325334589499631634)
XLA Ops:
  1.6 7.2 %shard_map.118 = bf16[64,224,128]{2,1,0:T(8,128)(2,1)} custom-call(s32[8,8]{1,0:T(8,128)} %bitcast.29, s32[1]{0:T(128)} %bitcast.4.group_ref, bf16[64,128,128]{2,1,0:T(8,128)(2,1)} %bitcast.25, bf16[64,128,128]{2,1,0:T(8,128)(2,1)} %bitcast.27, bf16[8,128,128]{2,1,0:T(8,128)(2,1)} %near_keys_ref.1, bf16[8,128,128]{2,1,0:T(8,128)(2,1)} %near_values_ref.1), custom_call_target="tpu_custom_call" | custom-call | bytes 7340032 | tf_op jit(solution)/shard_map/pallas_call | solution.py:425
  8.8 11.9 %all-to-all-start = ((bf16[64,224,128]{2,1,0:T(8,128)(2,1)}), bf16[64,224,128]{2,1,0:T(8,128)(2,1)}, u32[]{:S(2)}, u32[]{:S(2)}) async-start(bf16[64,224,128]{2,1,0:T(8,128)(2,1)} %shard_map.118), calls=%async_computation | async-start | bytes 7340032 | tf_op jit(solution)/shard_map/all_to_all | solution.py:440
  26.7 40.3 %all-to-all-done.refs_4_ = bf16[64,224,128]{2,1,0:T(8,128)(2,1)} async-done(((bf16[64,224,128]{2,1,0:T(8,128)(2,1)}), bf16[64,224,128]{2,1,0:T(8,128)(2,1)}, u32[]{:S(2)}, u32[]{:S(2)}) %all-to-all-start) | async-done | bytes 3670048 | tf_op jit(solution)/shard_map/all_to_all | solution.py:440
  67.1 6.9 %all-to-all-start.1 = ((bf16[64,64,128]{2,1,0:T(8,128)(2,1)}), bf16[64,64,128]{2,1,0:T(8,128)(2,1)S(1)}, u32[]{:S(2)}, u32[]{:S(2)}) async-start(bf16[64,64,128]{2,1,0:T(8,128)(2,1)} %pad_maximum_fusion), calls=%async_computation.1 | async-start | bytes 2097152 | tf_op jit(solution)/shard_map/all_to_all | solution.py:440
  75.5 11.6 %shard_map.119 = (f32[136,512]{1,0:T(8,128)S(1)}, f32[136,512]{1,0:T(8,128)S(1)}, s32[65]{0:T(128)S(1)}) custom-call(s32[64]{0:T(128)S(1)} %dynamic-slice_bitcast_fusion.refs_0_, s32[2]{0:T(128)S(1)} %pad_add_fusion.refs_1_, bf16[128,512]{1,0:T(8,128)(2,1)S(1)} %copy-done.13, bf16[128,512]{1,0:T(8,128)(2,1)S(1)} %collective-permute-done.refs_3_.refs_2_, ...), custom_call_target="tpu_custom_call" | custom-call | flops 1174405120 | bytes 3670016 | tf_op jit(solution)/shard_map/pallas_call | solution.py:134
  87.1 4.8 %all-to-all-done.1.refs_3_ = bf16[64,64,128]{2,1,0:T(8,128)(2,1)S(1)} async-done(((bf16[64,64,128]{2,1,0:T(8,128)(2,1)}), bf16[64,64,128]{2,1,0:T(8,128)(2,1)S(1)}, u32[]{:S(2)}, u32[]{:S(2)}) %all-to-all-start.1) | async-done | bytes 1048608 | tf_op jit(solution)/shard_map/all_to_all | solution.py:440
  91.9 2.9 shard_map.120
  97.7 4.0 %all-to-all-start.2 = ((bf16[8,128,512]{2,1,0:T(8,128)(2,1)}), bf16[8,128,512]{2,1,0:T(8,128)(2,1)S(1)}, u32[]{:S(2)}, u32[]{:S(2)}) async-start(bf16[8,128,512]{2,1,0:T(8,128)(2,1)} %shard_map.121), calls=%async_computation.2 | async-start | bytes 2097152 | tf_op jit(solution)/shard_map/all_to_all | solution.py:440
  101.7 16.0 %all-to-all-done.2 = bf16[8,128,512]{2,1,0:T(8,128)(2,1)S(1)} async-done(((bf16[8,128,512]{2,1,0:T(8,128)(2,1)}), bf16[8,128,512]{2,1,0:T(8,128)(2,1)S(1)}, u32[]{:S(2)}, u32[]{:S(2)}) %all-to-all-start.2) | async-done | bytes 1048608 | tf_op jit(solution)/shard_map/all_to_all | solution.py:440
  118.6 2.6 collective-permute-done.2.refs_1_
  122.9 7.8 %all-to-all-start.3 = ((bf16[8,64,1024]{2,1,0:T(8,128)(2,1)}), bf16[8,64,1024]{2,1,0:T(8,128)(2,1)S(1)}, u32[]{:S(2)}, u32[]{:S(2)}) async-start(bf16[8,64,1024]{2,1,0:T(8,128)(2,1)} %bitcast.12), calls=%async_computation.3 | async-start | bytes 2097152 | tf_op jit(solution)/shard_map/all_to_all | solution.py:440
  130.7 17.5 %all-to-all-done.3 = bf16[8,64,1024]{2,1,0:T(8,128)(2,1)S(1)} async-done(((bf16[8,64,1024]{2,1,0:T(8,128)(2,1)}), bf16[8,64,1024]{2,1,0:T(8,128)(2,1)S(1)}, u32[]{:S(2)}, u32[]{:S(2)}) %all-to-all-start.3) | async-done | bytes 1048608 | tf_op jit(solution)/shard_map/all_to_all | solution.py:440
  148.6 20.0 %all_to_all.35 = bf16[8,64,1024]{2,1,0:T(8,128)(2,1)} all-to-all(bf16[8,64,1024]{2,1,0:T(8,128)(2,1)S(1)} %broadcast_in_dim.4), channel_id=1, replica_groups=mesh['z'=4,'xh'=2,'core'=2,'y'=4,'xl'=2] {'z','xh'}, dimensions={0} | all-to-all | bytes 2097152 | tf_op jit(solution)/shard_map/all_to_all | solution.py:440
  169.2 2.4 collective-permute-done.3
  171.6 14.8 %shard_map.124 = (bf16[64,3584]{1,0:T(8,128)(2,1)}, bf16[64,3584]{1,0:T(8,128)(2,1)}, bf16[64,3584]{1,0:T(8,128)(2,1)}, bf16[64,3584]{1,0:T(8,128)(2,1)}, bf16[6...) custom-call(s32[2]{0:T(128)} %pad_add_fusion.1.place_ref, ...), custom_call_target="tpu_custom_call" | custom-call | flops 7516192768 | bytes 16777216 | tf_op jit(solution)/shard_map/pallas_call | solution.py:259
  193.0 7.1 %collective-permute-done.5.refs_1_ = bf16[64,3584]{1,0:T(8,128)(2,1)S(1)} collective-permute-done((bf16[64,3584]{1,0:T(8,128)(2,1)}, bf16[64,3584]{1,0:T(8,128)(2,1)S(1)}, u32[]{:S(2)}, u32[]{:S(2)}) %collective-permute-start.5) | collective-permute-done | bytes 458784 | tf_op jit(solution)/shard_map/ppermute | solution.py:385
  203.2 3.2 collective-permute-start.15
  207.1 3.3 %all-to-all-start.5 = ((f32[8,1,128]{2,1,0:T(1,128)}), f32[8,1,128]{2,1,0:T(1,128)S(1)}, u32[]{:S(2)}, u32[]{:S(2)}) async-start(f32[8,1,128]{2,1,0:T(1,128)} %reshape.135), calls=%async_computation.5 | async-start | bytes 8192 | tf_op jit(solution)/shard_map/all_to_all | solution.py:440
  210.4 3.2 collective-permute-start.10
  213.6 7.3 %all-to-all-done.5 = f32[8,1,128]{2,1,0:T(1,128)S(1)} async-done(((f32[8,1,128]{2,1,0:T(1,128)}), f32[8,1,128]{2,1,0:T(1,128)S(1)}, u32[]{:S(2)}, u32[]{:S(2)}) %all-to-all-start.5) | async-done | bytes 4128 | tf_op jit(solution)/shard_map/all_to_all | solution.py:440
  224.9 3.2 collective-permute-start.6
  234.5 2.6 collective-permute-done.7.refs_1_
  239.4 7.6 %collective-permute-done.9.refs_4_ = bf16[64,3584]{1,0:T(8,128)(2,1)} collective-permute-done((bf16[64,3584]{1,0:T(8,128)(2,1)}, bf16[64,3584]{1,0:T(8,128)(2,1)}, u32[]{:S(2)}, u32[]{:S(2)}) %collective-permute-start.9) | collective-permute-done | bytes 458784 | tf_op jit(solution)/shard_map/ppermute | solution.py:381
  248.6 6.2 %collective-permute-done.8.refs_2_ = bf16[64,3584]{1,0:T(8,128)(2,1)} collective-permute-done((bf16[64,3584]{1,0:T(8,128)(2,1)}, bf16[64,3584]{1,0:T(8,128)(2,1)}, u32[]{:S(2)}, u32[]{:S(2)}) %collective-permute-start.8) | collective-permute-done | bytes 458784 | tf_op jit(solution)/shard_map/ppermute | solution.py:381
  257.1 3.2 collective-permute-start.18
  260.8 8.0 %collective-permute-done.17.refs_4_ = bf16[128,1792]{1,0:T(8,128)(2,1)S(1)} collective-permute-done((bf16[128,1792]{1,0:T(8,128)(2,1)S(1)}, bf16[128,1792]{1,0:T(8,128)(2,1)S(1)}, u32[]{:S(2)}, u32[]{:S(2)}) %collective-permute-start.17) | collective-permute-done | bytes 458784 | tf_op jit(solution)/shard_map/ppermute | solution.py:381
  270.2 3.2 collective-permute-start.21
  273.5 11.4 %collective-permute-done.20.refs_5_ = bf16[128,1792]{1,0:T(8,128)(2,1)S(1)} collective-permute-done((bf16[128,1792]{1,0:T(8,128)(2,1)S(1)}, bf16[128,1792]{1,0:T(8,128)(2,1)S(1)}, u32[]{:S(2)}, u32[]{:S(2)}) %collective-permute-start.20) | collective-permute-done | bytes 458784 | tf_op jit(solution)/shard_map/ppermute | solution.py:381
  284.9 5.3 %collective-permute-done.22.refs_0_ = bf16[128,1792]{1,0:T(8,128)(2,1)S(1)} collective-permute-done((bf16[128,1792]{1,0:T(8,128)(2,1)S(1)}, bf16[128,1792]{1,0:T(8,128)(2,1)S(1)}, u32[]{:S(2)}, u32[]{:S(2)}) %collective-permute-start.22) | collective-permute-done | bytes 458784 | tf_op jit(solution)/shard_map/ppermute | solution.py:381
  290.8 3.6 %shard_map.131 = (f32[6,64,1024]{2,1,0:T(8,128)S(1)}, bf16[6,64,1024]{2,1,0:T(8,128)(2,1)S(1)}) custom-call(bf16[128,1792]{1,0:T(8,128)(2,1)S(1)} %shard_map.130.refs_0_, bf16[128,1792]{1,0:T(8,128)(2,1)S(1)} %collective-permute-done.19.refs_1_, bf16[128,1792]{1,0:T(8,128)(2,1)S(1)} %collective-permute-done.18.refs_2_, ...), custom_call_target="tpu_custom_call" | custom-call | flops 2818572288 | bytes 8781824 | tf_op jit(solution)/shard_map/pallas_call | solution.py:343
  294.5 4.2 %collective-permute-done.24.refs_1_ = bf16[128,1792]{1,0:T(8,128)(2,1)S(1)} collective-permute-done((bf16[128,1792]{1,0:T(8,128)(2,1)S(1)}, bf16[128,1792]{1,0:T(8,128)(2,1)S(1)}, u32[]{:S(2)}, u32[]{:S(2)}) %collective-permute-start.24) | collective-permute-done | bytes 458784 | tf_op jit(solution)/shard_map/ppermute | solution.py:385
  302.6 20.3 %all_to_all.36 = bf16[8,64,1024]{2,1,0:T(8,128)(2,1)S(1)} all-to-all(bf16[8,64,1024]{2,1,0:T(8,128)(2,1)S(1)} %shard_map.133), channel_id=1, replica_groups=mesh['z'=4,'xh'=2,'core'=2,'y'=4,'xl'=2] {'z','xh'}, dimensions={0} | all-to-all | bytes 2097152 | tf_op jit(solution)/shard_map/all_to_all | solution.py:440
  (113 shorter events, 49.5 us)
Async XLA Ops:
  8.8 58.2 %all-to-all-start = ((bf16[64,224,128]{2,1,0:T(8,128)(2,1)}), bf16[64,224,128]{2,1,0:T(8,128)(2,1)}, u32[]{:S(2)}, u32[]{:S(2)}) async-start(bf16[64,224,128]{2,1,0:T(8,128)(2,1)} %shard_map.118), calls=%async_computation | async-start | bytes 7340032 | tf_op jit(solution)/shard_map/all_to_all | solution.py:440
  67.1 24.8 %all-to-all-start.1 = ((bf16[64,64,128]{2,1,0:T(8,128)(2,1)}), bf16[64,64,128]{2,1,0:T(8,128)(2,1)S(1)}, u32[]{:S(2)}, u32[]{:S(2)}) async-start(bf16[64,64,128]{2,1,0:T(8,128)(2,1)} %pad_maximum_fusion), calls=%async_computation.1 | async-start | bytes 2097152 | tf_op jit(solution)/shard_map/all_to_all | solution.py:440
  74.1 1.4 collective-permute-start
  94.8 1.6 collective-permute-start.1
  97.7 20.1 %all-to-all-start.2 = ((bf16[8,128,512]{2,1,0:T(8,128)(2,1)}), bf16[8,128,512]{2,1,0:T(8,128)(2,1)S(1)}, u32[]{:S(2)}, u32[]{:S(2)}) async-start(bf16[8,128,512]{2,1,0:T(8,128)(2,1)} %shard_map.121), calls=%async_computation.2 | async-start | bytes 2097152 | tf_op jit(solution)/shard_map/all_to_all | solution.py:440
  118.5 2.7 collective-permute-start.2
  122.9 25.3 %all-to-all-start.3 = ((bf16[8,64,1024]{2,1,0:T(8,128)(2,1)}), bf16[8,64,1024]{2,1,0:T(8,128)(2,1)S(1)}, u32[]{:S(2)}, u32[]{:S(2)}) async-start(bf16[8,64,1024]{2,1,0:T(8,128)(2,1)} %bitcast.12), calls=%async_computation.3 | async-start | bytes 2097152 | tf_op jit(solution)/shard_map/all_to_all | solution.py:440
  168.6 3.0 collective-permute-start.3
  186.4 13.6 %collective-permute-start.5 = (bf16[64,3584]{1,0:T(8,128)(2,1)}, bf16[64,3584]{1,0:T(8,128)(2,1)S(1)}, u32[]{:S(2)}, u32[]{:S(2)}) collective-permute-start(bf16[64,3584]{1,0:T(8,128)(2,1)} %get-tuple-element.62), channel_id=1, source_target_pairs={{0,6},{2,0},{4,2},{6,4},{1,7},{3,1},{5,3},{7,5},{8,14},{10,8},{12,... | collective-permute-start | bytes 1376264 | tf_op jit(solution)/shard_map/ppermute | solution.py:385
  187.5 14.8 %collective-permute-start.4 = (bf16[64,3584]{1,0:T(8,128)(2,1)}, bf16[64,3584]{1,0:T(8,128)(2,1)S(1)}, u32[]{:S(2)}, u32[]{:S(2)}) collective-permute-start(bf16[64,3584]{1,0:T(8,128)(2,1)} %get-tuple-element.60), channel_id=1, source_target_pairs={{0,2},{2,4},{4,6},{6,0},{1,3},{3,5},{5,7},{7,1},{8,10},{10,12},{12... | collective-permute-start | bytes 1376264 | tf_op jit(solution)/shard_map/ppermute | solution.py:381
  188.5 33.7 %collective-permute-start.12 = (bf16[64,3584]{1,0:T(8,128)(2,1)}, bf16[64,3584]{1,0:T(8,128)(2,1)S(1)}, u32[]{:S(2)}, u32[]{:S(2)}) collective-permute-start(bf16[64,3584]{1,0:T(8,128)(2,1)} %get-tuple-element.80), channel_id=1, source_target_pairs={{0,6},{2,0},{4,2},{6,4},{1,7},{3,1},{5,3},{7,5},{8,14},{10,8},{12,... | collective-permute-start | bytes 1376264 | tf_op jit(solution)/shard_map/ppermute | solution.py:385
  190.7 31.5 %collective-permute-start.14 = (bf16[64,3584]{1,0:T(8,128)(2,1)}, bf16[64,3584]{1,0:T(8,128)(2,1)S(1)}, u32[]{:S(2)}, u32[]{:S(2)}) collective-permute-start(bf16[64,3584]{1,0:T(8,128)(2,1)} %get-tuple-element.83), channel_id=1, source_target_pairs={{0,2},{2,4},{4,6},{6,0},{1,3},{3,5},{5,7},{7,1},{8,10},{10,12},{12... | collective-permute-start | bytes 1376264 | tf_op jit(solution)/shard_map/ppermute | solution.py:381
  203.2 19.0 %collective-permute-start.13 = (bf16[64,3584]{1,0:T(8,128)(2,1)}, bf16[64,3584]{1,0:T(8,128)(2,1)S(1)}, u32[]{:S(2)}, u32[]{:S(2)}) collective-permute-start(bf16[64,3584]{1,0:T(8,128)(2,1)} %shard_map.125), channel_id=1, source_target_pairs={{0,2},{2,4},{4,6},{6,0},{1,3},{3,5},{5,7},{7,1},{8,10},{10,12},{12... | collective-permute-start | bytes 1376264 | tf_op jit(solution)/shard_map/ppermute | solution.py:381
  203.2 19.0 %collective-permute-start.15 = (bf16[64,3584]{1,0:T(8,128)(2,1)S(1)}, bf16[64,3584]{1,0:T(8,128)(2,1)S(1)}, u32[]{:S(2)}, u32[]{:S(2)}) collective-permute-start(bf16[64,3584]{1,0:T(8,128)(2,1)S(1)} %shard_map.126), channel_id=1, source_target_pairs={{0,6},{2,0},{4,2},{6,4},{1,7},{3,1},{5,3},{7,5},{8,14},{10,8},{12,... | collective-permute-start | bytes 1376264 | tf_op jit(solution)/shard_map/ppermute | solution.py:385
  207.1 13.8 %all-to-all-start.5 = ((f32[8,1,128]{2,1,0:T(1,128)}), f32[8,1,128]{2,1,0:T(1,128)S(1)}, u32[]{:S(2)}, u32[]{:S(2)}) async-start(f32[8,1,128]{2,1,0:T(1,128)} %reshape.135), calls=%async_computation.5 | async-start | bytes 8192 | tf_op jit(solution)/shard_map/all_to_all | solution.py:440
  210.4 19.3 %collective-permute-start.10 = (bf16[64,3584]{1,0:T(8,128)(2,1)}, bf16[64,3584]{1,0:T(8,128)(2,1)}, u32[]{:S(2)}, u32[]{:S(2)}) collective-permute-start(bf16[64,3584]{1,0:T(8,128)(2,1)} %get-tuple-element.78), channel_id=1, source_target_pairs={{0,6},{2,0},{4,2},{6,4},{1,7},{3,1},{5,3},{7,5},{8,14},{10,8},{12,... | collective-permute-start | bytes 1376264 | tf_op jit(solution)/shard_map/ppermute | solution.py:385
  222.2 14.9 %collective-permute-start.7 = (bf16[64,3584]{1,0:T(8,128)(2,1)}, bf16[64,3584]{1,0:T(8,128)(2,1)S(1)}, u32[]{:S(2)}, u32[]{:S(2)}) collective-permute-start(bf16[64,3584]{1,0:T(8,128)(2,1)} %get-tuple-element.74), channel_id=1, source_target_pairs={{0,2},{2,4},{4,6},{6,0},{1,3},{3,5},{5,7},{7,1},{8,10},{10,12},{12... | collective-permute-start | bytes 1376264 | tf_op jit(solution)/shard_map/ppermute | solution.py:381
  224.4 30.3 %collective-permute-start.16 = (bf16[2,64,3584]{2,1,0:T(8,128)(2,1)S(1)}, bf16[2,64,3584]{2,1,0:T(8,128)(2,1)S(1)}, u32[]{:S(2)}, u32[]{:S(2)}) collective-permute-start(bf16[2,64,3584]{2,1,0:T(8,128)(2,1)S(1)} %shard_map.129), channel_id=1, source_target_pairs={{0,1},{1,0},{2,3},{3,2},{4,5},{5,4},{6,7},{7,6},{8,9},{9,8},{10,11... | collective-permute-start | bytes 2752520 | tf_op jit(solution)/shard_map/ppermute | solution.py:444
  224.9 14.5 %collective-permute-start.6 = (bf16[64,3584]{1,0:T(8,128)(2,1)}, bf16[64,3584]{1,0:T(8,128)(2,1)S(1)}, u32[]{:S(2)}, u32[]{:S(2)}) collective-permute-start(bf16[64,3584]{1,0:T(8,128)(2,1)} %get-tuple-element.72), channel_id=1, source_target_pairs={{0,6},{2,0},{4,2},{6,4},{1,7},{3,1},{5,3},{7,5},{8,14},{10,8},{12,... | collective-permute-start | bytes 1376264 | tf_op jit(solution)/shard_map/ppermute | solution.py:385
  228.1 19.0 %collective-permute-start.9 = (bf16[64,3584]{1,0:T(8,128)(2,1)}, bf16[64,3584]{1,0:T(8,128)(2,1)}, u32[]{:S(2)}, u32[]{:S(2)}) collective-permute-start(bf16[64,3584]{1,0:T(8,128)(2,1)} %get-tuple-element.76), channel_id=1, source_target_pairs={{0,2},{2,4},{4,6},{6,0},{1,3},{3,5},{5,7},{7,1},{8,10},{10,12},{12... | collective-permute-start | bytes 1376264 | tf_op jit(solution)/shard_map/ppermute | solution.py:381
  232.6 15.9 %collective-permute-start.11 = (bf16[64,3584]{1,0:T(8,128)(2,1)}, bf16[64,3584]{1,0:T(8,128)(2,1)}, u32[]{:S(2)}, u32[]{:S(2)}) collective-permute-start(bf16[64,3584]{1,0:T(8,128)(2,1)} %shard_map.128), channel_id=1, source_target_pairs={{0,6},{2,0},{4,2},{6,4},{1,7},{3,1},{5,3},{7,5},{8,14},{10,8},{12,... | collective-permute-start | bytes 1376264 | tf_op jit(solution)/shard_map/ppermute | solution.py:385
  238.0 16.8 %collective-permute-start.8 = (bf16[64,3584]{1,0:T(8,128)(2,1)}, bf16[64,3584]{1,0:T(8,128)(2,1)}, u32[]{:S(2)}, u32[]{:S(2)}) collective-permute-start(bf16[64,3584]{1,0:T(8,128)(2,1)} %shard_map.127), channel_id=1, source_target_pairs={{0,2},{2,4},{4,6},{6,0},{1,3},{3,5},{5,7},{7,1},{8,10},{10,12},{12... | collective-permute-start | bytes 1376264 | tf_op jit(solution)/shard_map/ppermute | solution.py:381
  238.2 52.6 %copy-start.1 = (bf16[1792,1024]{1,0:T(8,128)(2,1)S(1)}, bf16[1792,1024]{1,0:T(8,128)(2,1)}, u32[]{:S(2)}) copy-start(bf16[1792,1024]{1,0:T(8,128)(2,1)} %refs_2_.3) | copy-start | bytes 11010052
  257.1 11.7 %collective-permute-start.17 = (bf16[128,1792]{1,0:T(8,128)(2,1)S(1)}, bf16[128,1792]{1,0:T(8,128)(2,1)S(1)}, u32[]{:S(2)}, u32[]{:S(2)}) collective-permute-start(bf16[128,1792]{1,0:T(8,128)(2,1)S(1)} %shard_map.130.refs_0_), channel_id=1, source_target_pairs={{0,2},{2,4},{4,6},{6,0},{1,3},{3,5},{5,7},{7,1},{8,10},{10,12},{12... | collective-permute-start | bytes 1376264 | tf_op jit(solution)/shard_map/ppermute | solution.py:381
  257.1 11.6 %collective-permute-start.18 = (bf16[128,1792]{1,0:T(8,128)(2,1)S(1)}, bf16[128,1792]{1,0:T(8,128)(2,1)S(1)}, u32[]{:S(2)}, u32[]{:S(2)}) collective-permute-start(bf16[128,1792]{1,0:T(8,128)(2,1)S(1)} %shard_map.130.refs_0_), channel_id=1, source_target_pairs={{0,6},{2,0},{4,2},{6,4},{1,7},{3,1},{5,3},{7,5},{8,14},{10,8},{12,... | collective-permute-start | bytes 1376264 | tf_op jit(solution)/shard_map/ppermute | solution.py:385
  260.4 9.9 %collective-permute-start.19 = (bf16[128,1792]{1,0:T(8,128)(2,1)S(1)}, bf16[128,1792]{1,0:T(8,128)(2,1)S(1)}, u32[]{:S(2)}, u32[]{:S(2)}) collective-permute-start(bf16[128,1792]{1,0:T(8,128)(2,1)S(1)} %shard_map.130.refs_0_), channel_id=1, source_target_pairs={{0,1},{1,0},{2,3},{3,2},{4,5},{5,4},{6,7},{7,6},{8,9},{9,8},{10,11... | collective-permute-start | bytes 1376264 | tf_op jit(solution)/shard_map/ppermute | solution.py:444
  270.2 14.7 %collective-permute-start.20 = (bf16[128,1792]{1,0:T(8,128)(2,1)S(1)}, bf16[128,1792]{1,0:T(8,128)(2,1)S(1)}, u32[]{:S(2)}, u32[]{:S(2)}) collective-permute-start(bf16[128,1792]{1,0:T(8,128)(2,1)S(1)} %collective-permute-done.19.refs_1_), channel_id=1, source_target_pairs={{0,2},{2,4},{4,6},{6,0},{1,3},{3,5},{5,7},{7,1},{8,10},{10,12},{12... | collective-permute-start | bytes 1376264 | tf_op jit(solution)/shard_map/ppermute | solution.py:381
  270.2 14.7 %collective-permute-start.21 = (bf16[128,1792]{1,0:T(8,128)(2,1)S(1)}, bf16[128,1792]{1,0:T(8,128)(2,1)S(1)}, u32[]{:S(2)}, u32[]{:S(2)}) collective-permute-start(bf16[128,1792]{1,0:T(8,128)(2,1)S(1)} %collective-permute-done.19.refs_1_), channel_id=1, source_target_pairs={{0,6},{2,0},{4,2},{6,4},{1,7},{3,1},{5,3},{7,5},{8,14},{10,8},{12,... | collective-permute-start | bytes 1376264 | tf_op jit(solution)/shard_map/ppermute | solution.py:385
  273.5 16.7 %collective-permute-start.22 = (bf16[128,1792]{1,0:T(8,128)(2,1)S(1)}, bf16[128,1792]{1,0:T(8,128)(2,1)S(1)}, u32[]{:S(2)}, u32[]{:S(2)}) collective-permute-start(bf16[128,1792]{1,0:T(8,128)(2,1)S(1)} %collective-permute-done.17.refs_4_), channel_id=1, source_target_pairs={{0,2},{2,4},{4,6},{6,0},{1,3},{3,5},{5,7},{7,1},{8,10},{10,12},{12... | collective-permute-start | bytes 1376264 | tf_op jit(solution)/shard_map/ppermute | solution.py:381
  290.2 8.5 %collective-permute-start.24 = (bf16[128,1792]{1,0:T(8,128)(2,1)S(1)}, bf16[128,1792]{1,0:T(8,128)(2,1)S(1)}, u32[]{:S(2)}, u32[]{:S(2)}) collective-permute-start(bf16[128,1792]{1,0:T(8,128)(2,1)S(1)} %collective-permute-done.21.refs_3_), channel_id=1, source_target_pairs={{0,6},{2,0},{4,2},{6,4},{1,7},{3,1},{5,3},{7,5},{8,14},{10,8},{12,... | collective-permute-start | bytes 1376264 | tf_op jit(solution)/shard_map/ppermute | solution.py:385
  294.4 7.5 %collective-permute-start.23 = (bf16[6,64,1024]{2,1,0:T(8,128)(2,1)S(1)}, bf16[6,64,1024]{2,1,0:T(8,128)(2,1)S(1)}, u32[]{:S(2)}, u32[]{:S(2)}) collective-permute-start(bf16[6,64,1024]{2,1,0:T(8,128)(2,1)S(1)} %get-tuple-element.99), channel_id=1, source_target_pairs={{0,8},{8,0},{1,9},{9,1},{2,10},{10,2},{3,11},{11,3},{4,12},{12,4},... | collective-permute-start | bytes 2359304 | tf_op jit(solution)/shard_map/ppermute | solution.py:444
  300.3 1.6 collective-permute-start.25
  (17 other events, 315.5 us)

commit v9 on v8

--- a/solution.py
+++ b/solution.py
@@ -241,8 +241,12 @@
 
     def put(weight_ref):
         total = jnp.dot(x, weight_ref[...], preferred_element_type=f32).astype(bf16)
-        for i, ref in enumerate(out_refs):
-            ref[...] = total[i * n : (i + 1) * n]
+        for i, ref in enumerate(out_refs[:12]):
+            at = (0, 1, 2, 3, 4, 5, 6, 7, 8, 9, 10, 15)[i]
+            ref[...] = total[at * n : (at + 1) * n]
+        for ref, pair in ((out_refs[12], (12, 11)), (out_refs[13], (13, 14))):
+            for j, at in enumerate(pair):
+                ref[j] = total[at * n : (at + 1) * n]
 
     half = pl.num_programs(0) // 2
     pl.when(step < half)(functools.partial(put, gate_ref))
@@ -258,7 +262,8 @@
     rows = 16 * tokens
     return pl.pallas_call(
         columns_kernel,
-        out_shape=(jax.ShapeDtypeStruct((tokens, 2 * width), bf16),) * 16,
+        out_shape=(jax.ShapeDtypeStruct((tokens, 2 * width), bf16),) * 12
+        + (jax.ShapeDtypeStruct((2, tokens, 2 * width), bf16),) * 2,
         grid_spec=pltpu.PrefetchScalarGridSpec(
             num_scalar_prefetch=1,
             grid=(2 * count,),
@@ -268,7 +273,8 @@
                 pl.BlockSpec((inputs, tile), lambda n, p: (0, jnp.minimum(n, count - 1))),
                 pl.BlockSpec((inputs, tile), lambda n, p: (0, jnp.maximum(n - count, 0))),
             ],
-            out_specs=(pl.BlockSpec((tokens, tile), lambda n, p: (0, n)),) * 16,
+            out_specs=(pl.BlockSpec((tokens, tile), lambda n, p: (0, n)),) * 12
+            + (pl.BlockSpec((2, tokens, tile), lambda n, p: (0, 0, n)),) * 2,
         ),
         compiler_params=pltpu.CompilerParams(vmem_limit_bytes=60 * 1024 * 1024),
         cost_estimate=pl.CostEstimate(
@@ -279,12 +285,13 @@
     )(place, mine, theirs, gate, up)
 
 
-def add_pieces(*pieces):
-    def kernel(*refs):
-        refs[-1][...] = sum(r[...].astype(f32) for r in refs[:-1]).astype(bf16)
-
-    first = pieces[0]
-    return small_call(kernel, jax.ShapeDtypeStruct(first.shape, bf16), (), pieces, 2 * first.size)
+def add_pieces(piece, other):
+    def kernel(a_ref, b_ref, out_ref):
+        b = b_ref[...] if other.ndim == 2 else b_ref[0]
+        out_ref[...] = (a_ref[...].astype(f32) + b.astype(f32)).astype(bf16)
+
+    out = jax.ShapeDtypeStruct(piece.shape, bf16)
+    return small_call(kernel, out, (), (piece, other), 2 * piece.size)
 
 
 def add_halves(*halves):
@@ -312,7 +319,7 @@
             scale = factor_ref[rows, :]
 
             def total(columns):
-                parts = sum(r[:, columns].astype(f32) for r in mine)
+                parts = sum((r[:, columns] if len(r.shape) == 2 else r[1, :, columns]).astype(f32) for r in mine)
                 return (parts + got_ref[i, :, columns].astype(f32)) * scale
 
             gate = total(slice(0, width))
@@ -417,10 +424,10 @@
 
 
 def pack(within, group, keys, values, near_keys, near_values, rows):
-    def of_group(x):
-        return pl.BlockSpec((x.shape[0] // KV_HEADS, *x.shape[1:]), lambda n, s, g: (n, 0, 0))
-
-    arrays = (keys, values, near_keys, near_values)
+    def of_group(x, height):
+        return pl.BlockSpec((x.shape[0] // KV_HEADS, height, HEAD_DIM), lambda n, s, g: (n, 0, 0))
+
+    arrays = ((keys, rows), (values, rows), (near_keys, BLK), (near_values, BLK))
     height = 2 * rows + BLK // 4
     return pl.pallas_call(
         pack_kernel,
@@ -428,12 +435,12 @@
         grid_spec=pltpu.PrefetchScalarGridSpec(
             num_scalar_prefetch=2,
             grid=(8,),
-            in_specs=[of_group(x) for x in arrays],
+            in_specs=[of_group(*x) for x in arrays],
             out_specs=pl.BlockSpec((8, height, HEAD_DIM), lambda n, s, g: (n, 0, 0)),
         ),
         compiler_params=pltpu.CompilerParams(vmem_limit_bytes=60 * 1024 * 1024),
         cost_estimate=pl.CostEstimate(flops=0, bytes_accessed=64 * height * 512, transcendentals=0),
-    )(within, group.astype(jnp.int32).reshape(1), *arrays)
+    )(within, group.astype(jnp.int32).reshape(1), *[x for x, _ in arrays])
 
 
 def exchange(x, axes):
@@ -528,16 +535,17 @@
     sums, mine, squares = lax.optimization_barrier((sums, mine, squares))
     squares = exchange(squares, COL)
     halves = ring_end(theirs, arrived, sums)
-    mine_arrived = ring_start(mine)
+    own_first, own_second, right, left, go_right, go_left = mine
+    from_left, from_right = to_right(go_right), to_left(go_left)
     halves, squares = lax.optimization_barrier((halves, squares))
     got = swap(add_halves(*halves), "xl")
     factor = lax.rsqrt(jnp.sum(squares, axis=0).reshape(-1) / D + 1e-05)
-    halves = ring_end(mine, mine_arrived, ring_middle(mine, *mine_arrived[:2]))
+    third_left, third_right = to_right(add_pieces(right, from_left)), to_left(add_pieces(left, from_right))
+    halves = (own_first, third_left, from_right), (own_second, third_right, from_left)
     hidden = gated(halves, got, factor)
     first, hidden_got = lax.optimization_barrier((gather_start(hidden), swap(hidden, "xl")))
     got_left, got_right = to_right(hidden_got), to_left(hidden_got)
     mine_far = to_right(first[0])
-    got_left, got_right, mine_far = lax.optimization_barrier((got_left, got_right, mine_far))
     got_far = to_left(got_right)
     near = (hidden, hidden_got, first[1], got_right, first[0], got_left)
     kept, give = down_product(near, down_weight)

time: 325 us -> 330 us (1.015)
  blocking collectives: 40.3 us -> 70.8 us
  waiting for transfers between devices: 155 us -> 137 us
  starting transfers between devices: 58.1 us -> 46.4 us
  Pallas kernels: 52.4 us -> 56.5 us
    all_to_all x2 -> x3, blocking collectives: 40.3 us -> 70.8 us  [exchange(): return lax.all_to_all(x, axes, split_axis=0, concat_axis=0, tiled=True)]
    ppermute x9 -> x8, waiting for transfers between devices: 43.3 us -> 14.7 us  [to_right(): return lax.ppermute(x, 'y', [(i, (i + 1) % 4) for i in range(4)])]
    ppermute x8, waiting for transfers between devices: 10.2 us -> 25.5 us  [swap(): return lax.ppermute(x, axis, [(0, 1), (1, 0)])]
    ppermute x9 -> x8, starting transfers between devices: 21.8 us -> 13.1 us  [to_left(): return lax.ppermute(x, 'y', [(i, (i + 3) % 4) for i in range(4)])]
    all_to_all x5 -> x4, waiting for transfers between devices: 86.1 us -> 77.8 us  [exchange(): return lax.all_to_all(x, axes, split_axis=0, concat_axis=0, tiled=True)]
    all_to_all x5 -> x4, starting transfers between devices: 33.9 us -> 28.5 us  [exchange(): return lax.all_to_all(x, axes, split_axis=0, concat_axis=0, tiled=True)]
    ppermute x9 -> x8, waiting for transfers between devices: 15.7 us -> 19.3 us  [to_left(): return lax.ppermute(x, 'y', [(i, (i + 3) % 4) for i in range(4)])]
  transfers between devices with their start and end apart: 31 -> 28, of which waited for: 23 -> 18; matrix products, arithmetic and copies ran while one was open for 4% -> 3% of each run, Pallas kernels for 6% -> 7%
where the time goes in v9:
time: 330 us; the launch traced here: 328 us
  waiting for transfers between devices  137 us (42%)
  blocking collectives  70.8 us (21%)
  Pallas kernels  56.5 us (17%)
  starting transfers between devices  46.4 us (14%)
  local copies, waits for them, and re-layouts  10 us (3%)
  other arithmetic  6.99 us (2%)
    all_to_all x4, waiting for transfers between devices, exchange(): return lax.all_to_all(x, axes, split_axis=0, concat_axis=0, tiled=True)  77.8 us
    all_to_all x3, blocking collectives, exchange(): return lax.all_to_all(x, axes, split_axis=0, concat_axis=0, tiled=True)  70.8 us
    all_to_all x4, starting transfers between devices, exchange(): return lax.all_to_all(x, axes, split_axis=0, concat_axis=0, tiled=True)  28.5 us
    ppermute x8, waiting for transfers between devices, swap(): return lax.ppermute(x, axis, [(0, 1), (1, 0)])  25.5 us
    ppermute x8, waiting for transfers between devices, to_left(): return lax.ppermute(x, 'y', [(i, (i + 3) % 4) for i in range(4)])  19.3 us
    pallas_call x2, Pallas kernels, attend(): pl.pallas_call(functools.partial(attend_kernel, scale, per_step, local_bl...  16.7 us
    pallas_call x1, Pallas kernels, partial_columns(): pl.pallas_call(columns_kernel, out_shape=(jax.ShapeDtypeStruct((tokens, 2...  14.7 us
    ppermute x8, waiting for transfers between devices, to_right(): return lax.ppermute(x, 'y', [(i, (i + 1) % 4) for i in range(4)])  14.7 us
  transfers between devices with their start and end apart: 28, of which 18 were waited for; matrix products, arithmetic and copies ran while one was open for 3% of the time, Pallas kernels for 7%

profile of v9, /device:TPU:0, one launch (start us, length us, event | category | flops | bytes accessed | tf_op | source)
XLA Modules:
  0.0 328.4 jit_solution(2641123664856115188)
XLA Ops:
  1.6 7.2 %shard_map.118 = bf16[64,224,128]{2,1,0:T(8,128)(2,1)} custom-call(s32[8,8]{1,0:T(8,128)} %bitcast.31, s32[1]{0:T(128)} %bitcast.4.group_ref, bf16[64,128,128]{2,1,0:T(8,128)(2,1)} %bitcast.26, bf16[64,128,128]{2,1,0:T(8,128)(2,1)} %bitcast.28, bf16[8,128,128]{2,1,0:T(8,128)(2,1)} %near_keys_ref.1, bf16[8,128,128]{2,1,0:T(8,128)(2,1)} %near_values_ref.1), custom_call_target="tpu_custom_call" | custom-call | bytes 7340032 | tf_op jit(solution)/shard_map/pallas_call | solution.py:432
  8.8 11.9 %all-to-all-start = ((bf16[64,224,128]{2,1,0:T(8,128)(2,1)}), bf16[64,224,128]{2,1,0:T(8,128)(2,1)}, u32[]{:S(2)}, u32[]{:S(2)}) async-start(bf16[64,224,128]{2,1,0:T(8,128)(2,1)} %shard_map.118), calls=%async_computation | async-start | bytes 7340032 | tf_op jit(solution)/shard_map/all_to_all | solution.py:447
  21.0 2.3 gather_fusion
  23.2 2.3 gather_fusion.1
  26.7 40.3 %all-to-all-done.refs_4_ = bf16[64,224,128]{2,1,0:T(8,128)(2,1)} async-done(((bf16[64,224,128]{2,1,0:T(8,128)(2,1)}), bf16[64,224,128]{2,1,0:T(8,128)(2,1)}, u32[]{:S(2)}, u32[]{:S(2)}) %all-to-all-start) | async-done | bytes 3670048 | tf_op jit(solution)/shard_map/all_to_all | solution.py:447
  67.1 7.0 %all-to-all-start.1 = ((bf16[64,64,128]{2,1,0:T(8,128)(2,1)}), bf16[64,64,128]{2,1,0:T(8,128)(2,1)S(1)}, u32[]{:S(2)}, u32[]{:S(2)}) async-start(bf16[64,64,128]{2,1,0:T(8,128)(2,1)} %pad_maximum_fusion), calls=%async_computation.1 | async-start | bytes 2097152 | tf_op jit(solution)/shard_map/all_to_all | solution.py:447
  75.5 12.7 %shard_map.119 = (f32[136,512]{1,0:T(8,128)S(1)}, f32[136,512]{1,0:T(8,128)S(1)}, s32[65]{0:T(128)S(1)}) custom-call(s32[64]{0:T(128)S(1)} %dynamic-slice_bitcast_fusion.refs_0_, s32[2]{0:T(128)S(1)} %pad_add_fusion.refs_1_, bf16[128,512]{1,0:T(8,128)(2,1)S(1)} %copy-done.11, bf16[128,512]{1,0:T(8,128)(2,1)S(1)} %collective-permute-done.refs_3_.refs_2_, ...), custom_call_target="tpu_custom_call" | custom-call | flops 1174405120 | bytes 3670016 | tf_op jit(solution)/shard_map/pallas_call | solution.py:134
  88.2 3.7 %all-to-all-done.1.refs_3_ = bf16[64,64,128]{2,1,0:T(8,128)(2,1)S(1)} async-done(((bf16[64,64,128]{2,1,0:T(8,128)(2,1)}), bf16[64,64,128]{2,1,0:T(8,128)(2,1)S(1)}, u32[]{:S(2)}, u32[]{:S(2)}) %all-to-all-start.1) | async-done | bytes 1048608 | tf_op jit(solution)/shard_map/all_to_all | solution.py:447
  91.9 4.0 %shard_map.120 = (f32[136,512]{1,0:T(8,128)S(1)}, f32[136,512]{1,0:T(8,128)S(1)}) custom-call(s32[65]{0:T(128)S(1)} %get-tuple-element.47.refs_0_, bf16[128,512]{1,0:T(8,128)(2,1)S(1)} %copy-done.11, bf16[128,512]{1,0:T(8,128)(2,1)S(1)} %collective-permute-done.refs_3_.refs_2_, bf16[64,64,128]{2,1,0:T(8,128)(2,1)S(1)} %all-to-all-done.1.refs_3_, ...), custom_call_target="tpu_custom_call" | custom-call | flops 335544320 | bytes 1048576 | tf_op jit(solution)/shard_map/pallas_call | solution.py:134
  98.8 3.6 %all-to-all-start.2 = ((bf16[8,128,512]{2,1,0:T(8,128)(2,1)}), bf16[8,128,512]{2,1,0:T(8,128)(2,1)S(1)}, u32[]{:S(2)}, u32[]{:S(2)}) async-start(bf16[8,128,512]{2,1,0:T(8,128)(2,1)} %shard_map.121), calls=%async_computation.2 | async-start | bytes 2097152 | tf_op jit(solution)/shard_map/all_to_all | solution.py:447
  102.3 16.3 %all-to-all-done.2 = bf16[8,128,512]{2,1,0:T(8,128)(2,1)S(1)} async-done(((bf16[8,128,512]{2,1,0:T(8,128)(2,1)}), bf16[8,128,512]{2,1,0:T(8,128)(2,1)S(1)}, u32[]{:S(2)}, u32[]{:S(2)}) %all-to-all-start.2) | async-done | bytes 1048608 | tf_op jit(solution)/shard_map/all_to_all | solution.py:447
  119.4 2.6 collective-permute-done.2.refs_1_
  123.7 6.1 %all-to-all-start.3 = ((bf16[8,64,1024]{2,1,0:T(8,128)(2,1)}), bf16[8,64,1024]{2,1,0:T(8,128)(2,1)S(1)}, u32[]{:S(2)}, u32[]{:S(2)}) async-start(bf16[8,64,1024]{2,1,0:T(8,128)(2,1)} %bitcast.12), calls=%async_computation.3 | async-start | bytes 2097152 | tf_op jit(solution)/shard_map/all_to_all | solution.py:447
  129.9 17.5 %all-to-all-done.3 = bf16[8,64,1024]{2,1,0:T(8,128)(2,1)S(1)} async-done(((bf16[8,64,1024]{2,1,0:T(8,128)(2,1)}), bf16[8,64,1024]{2,1,0:T(8,128)(2,1)S(1)}, u32[]{:S(2)}, u32[]{:S(2)}) %all-to-all-start.3) | async-done | bytes 1048608 | tf_op jit(solution)/shard_map/all_to_all | solution.py:447
  147.8 19.9 %all_to_all.35 = bf16[8,64,1024]{2,1,0:T(8,128)(2,1)S(1)} all-to-all(bf16[8,64,1024]{2,1,0:T(8,128)(2,1)S(1)} %broadcast_in_dim.4), channel_id=1, replica_groups=mesh['z'=4,'xh'=2,'core'=2,'y'=4,'xl'=2] {'z','xh'}, dimensions={0} | all-to-all | bytes 2097152 | tf_op jit(solution)/shard_map/all_to_all | solution.py:447
  168.3 2.0 collective-permute-done.3
  171.3 14.7 %shard_map.124 = (bf16[64,3584]{1,0:T(8,128)(2,1)}, bf16[64,3584]{1,0:T(8,128)(2,1)}, bf16[64,3584]{1,0:T(8,128)(2,1)}, bf16[64,3584]{1,0:T(8,128)(2,1)}, bf16[6...) custom-call(s32[2]{0:T(128)} %pad_add_fusion.1.place_ref, ...), custom_call_target="tpu_custom_call" | custom-call | flops 7516192768 | bytes 16777216 | tf_op jit(solution)/shard_map/pallas_call | solution.py:263
  188.1 2.1 collective-permute-start.10
  190.2 2.2 multiply_reduce_fusion.1
  192.5 7.2 %collective-permute-done.5.b_ref = bf16[64,3584]{1,0:T(8,128)(2,1)S(1)} collective-permute-done((bf16[64,3584]{1,0:T(8,128)(2,1)}, bf16[64,3584]{1,0:T(8,128)(2,1)S(1)}, u32[]{:S(2)}, u32[]{:S(2)}) %collective-permute-start.5) | collective-permute-done | bytes 458784 | tf_op jit(solution)/shard_map/ppermute | solution.py:392
  202.7 3.2 collective-permute-start.13
  206.0 3.5 %collective-permute-done.10.refs_1_ = bf16[64,3584]{1,0:T(8,128)(2,1)S(1)} collective-permute-done((bf16[64,3584]{1,0:T(8,128)(2,1)}, bf16[64,3584]{1,0:T(8,128)(2,1)S(1)}, u32[]{:S(2)}, u32[]{:S(2)}) %collective-permute-start.10) | collective-permute-done | bytes 458784 | tf_op jit(solution)/shard_map/ppermute | solution.py:392
  209.6 30.5 %all_to_all.36 = f32[8,1,128]{2,1,0:T(1,128)S(1)} all-to-all(f32[8,1,128]{2,1,0:T(1,128)S(1)} %reshape.135), channel_id=1, replica_groups=mesh['z'=4,'xh'=2,'core'=2,'y'=4,'xl'=2] {'y','xl'}, dimensions={0} | all-to-all | bytes 8192 | tf_op jit(solution)/shard_map/all_to_all | solution.py:447
  241.3 2.6 shard_map.129
  249.5 15.8 %collective-permute-done.14.refs_6_ = bf16[2,64,3584]{2,1,0:T(8,128)(2,1)S(1)} collective-permute-done((bf16[2,64,3584]{2,1,0:T(8,128)(2,1)}, bf16[2,64,3584]{2,1,0:T(8,128)(2,1)S(1)}, u32[]{:S(2)}, u32[]{:S(2)}) %collective-permute-start.14) | collective-permute-done | bytes 917536 | tf_op jit(solution)/shard_map/ppermute | solution.py:451
  266.4 2.2 shard_map.130.refs_0_
  268.6 3.2 collective-permute-start.16
  272.4 7.8 %collective-permute-done.15.refs_4_ = bf16[128,1792]{1,0:T(8,128)(2,1)S(1)} collective-permute-done((bf16[128,1792]{1,0:T(8,128)(2,1)S(1)}, bf16[128,1792]{1,0:T(8,128)(2,1)S(1)}, u32[]{:S(2)}, u32[]{:S(2)}) %collective-permute-start.15) | collective-permute-done | bytes 458784 | tf_op jit(solution)/shard_map/ppermute | solution.py:388
  283.8 8.6 %collective-permute-done.18.refs_3_ = bf16[128,1792]{1,0:T(8,128)(2,1)S(1)} collective-permute-done((bf16[128,1792]{1,0:T(8,128)(2,1)S(1)}, bf16[128,1792]{1,0:T(8,128)(2,1)S(1)}, u32[]{:S(2)}, u32[]{:S(2)}) %collective-permute-start.18) | collective-permute-done | bytes 458784 | tf_op jit(solution)/shard_map/ppermute | solution.py:392
  293.9 4.0 %collective-permute-done.19.refs_5_ = bf16[128,1792]{1,0:T(8,128)(2,1)S(1)} collective-permute-done((bf16[128,1792]{1,0:T(8,128)(2,1)S(1)}, bf16[128,1792]{1,0:T(8,128)(2,1)S(1)}, u32[]{:S(2)}, u32[]{:S(2)}) %collective-permute-start.19) | collective-permute-done | bytes 458784 | tf_op jit(solution)/shard_map/ppermute | solution.py:388
  297.9 3.6 %shard_map.131 = (f32[6,64,1024]{2,1,0:T(8,128)S(1)}, bf16[6,64,1024]{2,1,0:T(8,128)(2,1)S(1)}) custom-call(bf16[128,1792]{1,0:T(8,128)(2,1)S(1)} %shard_map.130.refs_0_, bf16[128,1792]{1,0:T(8,128)(2,1)S(1)} %collective-permute-done.17.refs_1_, bf16[128,1792]{1,0:T(8,128)(2,1)S(1)} %collective-permute-done.16.refs_2_, ...), custom_call_target="tpu_custom_call" | custom-call | flops 2818572288 | bytes 8781824 | tf_op jit(solution)/shard_map/pallas_call | solution.py:350
  307.1 20.3 %all_to_all.37 = bf16[8,64,1024]{2,1,0:T(8,128)(2,1)S(1)} all-to-all(bf16[8,64,1024]{2,1,0:T(8,128)(2,1)S(1)} %shard_map.133), channel_id=1, replica_groups=mesh['z'=4,'xh'=2,'core'=2,'y'=4,'xl'=2] {'z','xh'}, dimensions={0} | all-to-all | bytes 2097152 | tf_op jit(solution)/shard_map/all_to_all | solution.py:447
  (108 shorter events, 37.1 us)
Async XLA Ops:
  8.8 58.2 %all-to-all-start = ((bf16[64,224,128]{2,1,0:T(8,128)(2,1)}), bf16[64,224,128]{2,1,0:T(8,128)(2,1)}, u32[]{:S(2)}, u32[]{:S(2)}) async-start(bf16[64,224,128]{2,1,0:T(8,128)(2,1)} %shard_map.118), calls=%async_computation | async-start | bytes 7340032 | tf_op jit(solution)/shard_map/all_to_all | solution.py:447
  25.5 48.5 %copy-start.11 = (bf16[128,512]{1,0:T(8,128)(2,1)S(1)}, bf16[128,512]{1,0:T(8,128)(2,1)}, u32[]{:S(2)}) copy-start(bf16[128,512]{1,0:T(8,128)(2,1)} %refs_1_.1) | copy-start | bytes 393220
  67.1 24.9 %all-to-all-start.1 = ((bf16[64,64,128]{2,1,0:T(8,128)(2,1)}), bf16[64,64,128]{2,1,0:T(8,128)(2,1)S(1)}, u32[]{:S(2)}, u32[]{:S(2)}) async-start(bf16[64,64,128]{2,1,0:T(8,128)(2,1)} %pad_maximum_fusion), calls=%async_computation.1 | async-start | bytes 2097152 | tf_op jit(solution)/shard_map/all_to_all | solution.py:447
  74.0 1.4 collective-permute-start
  95.9 1.6 collective-permute-start.1
  98.8 19.8 %all-to-all-start.2 = ((bf16[8,128,512]{2,1,0:T(8,128)(2,1)}), bf16[8,128,512]{2,1,0:T(8,128)(2,1)S(1)}, u32[]{:S(2)}, u32[]{:S(2)}) async-start(bf16[8,128,512]{2,1,0:T(8,128)(2,1)} %shard_map.121), calls=%async_computation.2 | async-start | bytes 2097152 | tf_op jit(solution)/shard_map/all_to_all | solution.py:447
  119.3 2.7 collective-permute-start.2
  123.7 23.7 %all-to-all-start.3 = ((bf16[8,64,1024]{2,1,0:T(8,128)(2,1)}), bf16[8,64,1024]{2,1,0:T(8,128)(2,1)S(1)}, u32[]{:S(2)}, u32[]{:S(2)}) async-start(bf16[8,64,1024]{2,1,0:T(8,128)(2,1)} %bitcast.12), calls=%async_computation.3 | async-start | bytes 2097152 | tf_op jit(solution)/shard_map/all_to_all | solution.py:447
  167.6 2.7 collective-permute-start.3
  186.0 13.6 %collective-permute-start.5 = (bf16[64,3584]{1,0:T(8,128)(2,1)}, bf16[64,3584]{1,0:T(8,128)(2,1)S(1)}, u32[]{:S(2)}, u32[]{:S(2)}) collective-permute-start(bf16[64,3584]{1,0:T(8,128)(2,1)} %get-tuple-element.55), channel_id=1, source_target_pairs={{0,6},{2,0},{4,2},{6,4},{1,7},{3,1},{5,3},{7,5},{8,14},{10,8},{12,... | collective-permute-start | bytes 1376264 | tf_op jit(solution)/shard_map/ppermute | solution.py:392
  187.0 14.8 %collective-permute-start.4 = (bf16[64,3584]{1,0:T(8,128)(2,1)}, bf16[64,3584]{1,0:T(8,128)(2,1)S(1)}, u32[]{:S(2)}, u32[]{:S(2)}) collective-permute-start(bf16[64,3584]{1,0:T(8,128)(2,1)} %get-tuple-element.53), channel_id=1, source_target_pairs={{0,2},{2,4},{4,6},{6,0},{1,3},{3,5},{5,7},{7,1},{8,10},{10,12},{12... | collective-permute-start | bytes 1376264 | tf_op jit(solution)/shard_map/ppermute | solution.py:388
  188.1 21.4 %collective-permute-start.10 = (bf16[64,3584]{1,0:T(8,128)(2,1)}, bf16[64,3584]{1,0:T(8,128)(2,1)S(1)}, u32[]{:S(2)}, u32[]{:S(2)}) collective-permute-start(bf16[64,3584]{1,0:T(8,128)(2,1)} %get-tuple-element.69), channel_id=1, source_target_pairs={{0,6},{2,0},{4,2},{6,4},{1,7},{3,1},{5,3},{7,5},{8,14},{10,8},{12,... | collective-permute-start | bytes 1376264 | tf_op jit(solution)/shard_map/ppermute | solution.py:392
  190.2 51.1 %copy-start.6 = (bf16[64,3584]{1,0:T(8,128)(2,1)S(1)}, bf16[64,3584]{1,0:T(8,128)(2,1)}, u32[]{:S(2)}) copy-start(bf16[64,3584]{1,0:T(8,128)(2,1)} %get-tuple-element.75.refs_0_) | copy-start | bytes 1376260
  190.2 51.1 %copy-start.7 = (bf16[64,3584]{1,0:T(8,128)(2,1)S(1)}, bf16[64,3584]{1,0:T(8,128)(2,1)}, u32[]{:S(2)}) copy-start(bf16[64,3584]{1,0:T(8,128)(2,1)} %get-tuple-element.78.refs_3_) | copy-start | bytes 1376260
  190.2 51.1 %collective-permute-start.12 = (bf16[64,3584]{1,0:T(8,128)(2,1)}, bf16[64,3584]{1,0:T(8,128)(2,1)}, u32[]{:S(2)}, u32[]{:S(2)}) collective-permute-start(bf16[64,3584]{1,0:T(8,128)(2,1)} %get-tuple-element.72), channel_id=1, source_target_pairs={{0,2},{2,4},{4,6},{6,0},{1,3},{3,5},{5,7},{7,1},{8,10},{10,12},{12... | collective-permute-start | bytes 1376264 | tf_op jit(solution)/shard_map/ppermute | solution.py:388
  202.7 38.6 %collective-permute-start.11 = (bf16[64,3584]{1,0:T(8,128)(2,1)}, bf16[64,3584]{1,0:T(8,128)(2,1)}, u32[]{:S(2)}, u32[]{:S(2)}) collective-permute-start(bf16[64,3584]{1,0:T(8,128)(2,1)} %shard_map.125), channel_id=1, source_target_pairs={{0,2},{2,4},{4,6},{6,0},{1,3},{3,5},{5,7},{7,1},{8,10},{10,12},{12... | collective-permute-start | bytes 1376264 | tf_op jit(solution)/shard_map/ppermute | solution.py:388
  202.7 38.6 %collective-permute-start.13 = (bf16[64,3584]{1,0:T(8,128)(2,1)}, bf16[64,3584]{1,0:T(8,128)(2,1)}, u32[]{:S(2)}, u32[]{:S(2)}) collective-permute-start(bf16[64,3584]{1,0:T(8,128)(2,1)} %shard_map.126), channel_id=1, source_target_pairs={{0,6},{2,0},{4,2},{6,4},{1,7},{3,1},{5,3},{7,5},{8,14},{10,8},{12,... | collective-permute-start | bytes 1376264 | tf_op jit(solution)/shard_map/ppermute | solution.py:392
  206.0 38.6 %collective-permute-start.8 = (bf16[2,64,3584]{2,1,0:T(8,128)(2,1)}, bf16[2,64,3584]{2,1,0:T(8,128)(2,1)S(1)}, u32[]{:S(2)}, u32[]{:S(2)}) collective-permute-start(bf16[2,64,3584]{2,1,0:T(8,128)(2,1)} %get-tuple-element.65), channel_id=1, source_target_pairs={{0,6},{2,0},{4,2},{6,4},{1,7},{3,1},{5,3},{7,5},{8,14},{10,8},{12,... | collective-permute-start | bytes 2752520 | tf_op jit(solution)/shard_map/ppermute | solution.py:392
  209.5 37.4 %collective-permute-start.6 = (bf16[2,64,3584]{2,1,0:T(8,128)(2,1)}, bf16[2,64,3584]{2,1,0:T(8,128)(2,1)S(1)}, u32[]{:S(2)}, u32[]{:S(2)}) collective-permute-start(bf16[2,64,3584]{2,1,0:T(8,128)(2,1)} %get-tuple-element.64), channel_id=1, source_target_pairs={{0,2},{2,4},{4,6},{6,0},{1,3},{3,5},{5,7},{7,1},{8,10},{10,12},{12... | collective-permute-start | bytes 2752520 | tf_op jit(solution)/shard_map/ppermute | solution.py:388
  243.9 21.4 %collective-permute-start.14 = (bf16[2,64,3584]{2,1,0:T(8,128)(2,1)}, bf16[2,64,3584]{2,1,0:T(8,128)(2,1)S(1)}, u32[]{:S(2)}, u32[]{:S(2)}) collective-permute-start(bf16[2,64,3584]{2,1,0:T(8,128)(2,1)} %shard_map.129), channel_id=1, source_target_pairs={{0,1},{1,0},{2,3},{3,2},{4,5},{5,4},{6,7},{7,6},{8,9},{9,8},{10,11... | collective-permute-start | bytes 2752520 | tf_op jit(solution)/shard_map/ppermute | solution.py:451
  246.4 19.0 %collective-permute-start.9 = (bf16[64,3584]{1,0:T(8,128)(2,1)}, bf16[64,3584]{1,0:T(8,128)(2,1)}, u32[]{:S(2)}, u32[]{:S(2)}) collective-permute-start(bf16[64,3584]{1,0:T(8,128)(2,1)} %shard_map.128), channel_id=1, source_target_pairs={{0,6},{2,0},{4,2},{6,4},{1,7},{3,1},{5,3},{7,5},{8,14},{10,8},{12,... | collective-permute-start | bytes 1376264 | tf_op jit(solution)/shard_map/ppermute | solution.py:392
  247.8 17.5 %collective-permute-start.7 = (bf16[64,3584]{1,0:T(8,128)(2,1)}, bf16[64,3584]{1,0:T(8,128)(2,1)}, u32[]{:S(2)}, u32[]{:S(2)}) collective-permute-start(bf16[64,3584]{1,0:T(8,128)(2,1)} %shard_map.127), channel_id=1, source_target_pairs={{0,2},{2,4},{4,6},{6,0},{1,3},{3,5},{5,7},{7,1},{8,10},{10,12},{12... | collective-permute-start | bytes 1376264 | tf_op jit(solution)/shard_map/ppermute | solution.py:388
  249.5 48.3 %copy-start.1 = (bf16[1792,1024]{1,0:T(8,128)(2,1)S(1)}, bf16[1792,1024]{1,0:T(8,128)(2,1)}, u32[]{:S(2)}) copy-start(bf16[1792,1024]{1,0:T(8,128)(2,1)} %refs_2_.3) | copy-start | bytes 11010052
  268.5 11.7 %collective-permute-start.15 = (bf16[128,1792]{1,0:T(8,128)(2,1)S(1)}, bf16[128,1792]{1,0:T(8,128)(2,1)S(1)}, u32[]{:S(2)}, u32[]{:S(2)}) collective-permute-start(bf16[128,1792]{1,0:T(8,128)(2,1)S(1)} %shard_map.130.refs_0_), channel_id=1, source_target_pairs={{0,2},{2,4},{4,6},{6,0},{1,3},{3,5},{5,7},{7,1},{8,10},{10,12},{12... | collective-permute-start | bytes 1376264 | tf_op jit(solution)/shard_map/ppermute | solution.py:388
  268.6 11.6 %collective-permute-start.16 = (bf16[128,1792]{1,0:T(8,128)(2,1)S(1)}, bf16[128,1792]{1,0:T(8,128)(2,1)S(1)}, u32[]{:S(2)}, u32[]{:S(2)}) collective-permute-start(bf16[128,1792]{1,0:T(8,128)(2,1)S(1)} %shard_map.130.refs_0_), channel_id=1, source_target_pairs={{0,6},{2,0},{4,2},{6,4},{1,7},{3,1},{5,3},{7,5},{8,14},{10,8},{12,... | collective-permute-start | bytes 1376264 | tf_op jit(solution)/shard_map/ppermute | solution.py:392
  271.8 9.9 %collective-permute-start.17 = (bf16[128,1792]{1,0:T(8,128)(2,1)S(1)}, bf16[128,1792]{1,0:T(8,128)(2,1)S(1)}, u32[]{:S(2)}, u32[]{:S(2)}) collective-permute-start(bf16[128,1792]{1,0:T(8,128)(2,1)S(1)} %shard_map.130.refs_0_), channel_id=1, source_target_pairs={{0,1},{1,0},{2,3},{3,2},{4,5},{5,4},{6,7},{7,6},{8,9},{9,8},{10,11... | collective-permute-start | bytes 1376264 | tf_op jit(solution)/shard_map/ppermute | solution.py:451
  281.7 10.7 %collective-permute-start.18 = (bf16[128,1792]{1,0:T(8,128)(2,1)S(1)}, bf16[128,1792]{1,0:T(8,128)(2,1)S(1)}, u32[]{:S(2)}, u32[]{:S(2)}) collective-permute-start(bf16[128,1792]{1,0:T(8,128)(2,1)S(1)} %collective-permute-done.17.refs_1_), channel_id=1, source_target_pairs={{0,6},{2,0},{4,2},{6,4},{1,7},{3,1},{5,3},{7,5},{8,14},{10,8},{12,... | collective-permute-start | bytes 1376264 | tf_op jit(solution)/shard_map/ppermute | solution.py:392
  283.2 14.7 %collective-permute-start.19 = (bf16[128,1792]{1,0:T(8,128)(2,1)S(1)}, bf16[128,1792]{1,0:T(8,128)(2,1)S(1)}, u32[]{:S(2)}, u32[]{:S(2)}) collective-permute-start(bf16[128,1792]{1,0:T(8,128)(2,1)S(1)} %collective-permute-done.17.refs_1_), channel_id=1, source_target_pairs={{0,2},{2,4},{4,6},{6,0},{1,3},{3,5},{5,7},{7,1},{8,10},{10,12},{12... | collective-permute-start | bytes 1376264 | tf_op jit(solution)/shard_map/ppermute | solution.py:388
  283.7 19.4 %collective-permute-start.21 = (bf16[128,1792]{1,0:T(8,128)(2,1)S(1)}, bf16[128,1792]{1,0:T(8,128)(2,1)S(1)}, u32[]{:S(2)}, u32[]{:S(2)}) collective-permute-start(bf16[128,1792]{1,0:T(8,128)(2,1)S(1)} %collective-permute-done.15.refs_4_), channel_id=1, source_target_pairs={{0,2},{2,4},{4,6},{6,0},{1,3},{3,5},{5,7},{7,1},{8,10},{10,12},{12... | collective-permute-start | bytes 1376264 | tf_op jit(solution)/shard_map/ppermute | solution.py:388
  292.4 10.8 %collective-permute-start.22 = (bf16[128,1792]{1,0:T(8,128)(2,1)S(1)}, bf16[128,1792]{1,0:T(8,128)(2,1)S(1)}, u32[]{:S(2)}, u32[]{:S(2)}) collective-permute-start(bf16[128,1792]{1,0:T(8,128)(2,1)S(1)} %collective-permute-done.18.refs_3_), channel_id=1, source_target_pairs={{0,6},{2,0},{4,2},{6,4},{1,7},{3,1},{5,3},{7,5},{8,14},{10,8},{12,... | collective-permute-start | bytes 1376264 | tf_op jit(solution)/shard_map/ppermute | solution.py:392
  301.5 4.9 %collective-permute-start.20 = (bf16[6,64,1024]{2,1,0:T(8,128)(2,1)S(1)}, bf16[6,64,1024]{2,1,0:T(8,128)(2,1)S(1)}, u32[]{:S(2)}, u32[]{:S(2)}) collective-permute-start(bf16[6,64,1024]{2,1,0:T(8,128)(2,1)S(1)} %get-tuple-element.86), channel_id=1, source_target_pairs={{0,8},{8,0},{1,9},{9,1},{2,10},{10,2},{3,11},{11,3},{4,12},{12,4},... | collective-permute-start | bytes 2359304 | tf_op jit(solution)/shard_map/ppermute | solution.py:451
  304.8 1.6 collective-permute-start.23
  (14 other events, 152.1 us)

commit v10 on v9

--- a/solution.py
+++ b/solution.py
@@ -40,7 +40,7 @@
     own_ref, send_ref = refs[6:8] if last else refs[5:7]
     q_ref, top_ref, sum_ref, acc_ref = refs[-4:]
     length = order_ref.shape[0] - 1
-    part_rows = (chunk_ref.shape[1] - (0 if last else BLK // 4)) // 2
+    part_rows = (chunk_ref.shape[1] - (0 if last else BLK // 8)) // 2
     heads = own_q_ref.shape[1] // HEAD_DIM
     rows = heads * BLK
     for h in range(heads):
@@ -97,22 +97,21 @@
 
     lax.fori_loop(0, (count + per_step - 1) // per_step, far, 0)
 
-    def near(j, carry):
-        which = core + 2 * j
-        shift = (block - which) * BLK
-        key_pos = lax.broadcasted_iota(jnp.int32, (BLK, rows), 0)
-        token = lax.broadcasted_iota(jnp.int32, (BLK, rows), 1) % BLK
-        bias = jnp.where(key_pos <= token + shift, 0.0, NEG)
+    def near(which, carry):
+        part = BLK // 16
+        index = lax.broadcasted_iota(jnp.int32, (BLK // 2, rows), 0)
+        key_pos = index // part * (2 * part) + core * part + index % part
+        token = lax.broadcasted_iota(jnp.int32, (BLK // 2, rows), 1) % BLK
+        bias = jnp.where(key_pos <= token + (block - which) * BLK, 0.0, NEG)
         at = 2 * part_rows
-        eighth = BLK // 8
-        keys = jnp.concatenate([chunk_ref[i * 8 + which, at : at + eighth] for i in range(8)], axis=0)
-        values = jnp.concatenate([chunk_ref[i * 8 + which, at + eighth :] for i in range(8)], axis=0)
+        keys = jnp.concatenate([chunk_ref[i * 8 + which, at : at + part] for i in range(8)], axis=0)
+        values = jnp.concatenate([chunk_ref[i * 8 + which, at + part :] for i in range(8)], axis=0)
         for half in range(2):
             update(half, keys, values, bias)
         return carry
 
     if not last:
-        lax.fori_loop(0, (block - core + 2) // 2, near, 0)
+        lax.fori_loop(0, block + 1, near, 0)
     for half, ref in ((0, own_ref), (1, send_ref)):
         ref[0:HEAD_DIM, :] = acc_ref[half]
         ref[HEAD_DIM : HEAD_DIM + 1, :] = top_ref[half]
@@ -410,25 +409,24 @@
     return to_right(mine), to_left(mine)
 
 
-def pack_kernel(within_ref, group_ref, keys_ref, values_ref, near_keys_ref, near_values_ref, out_ref):
-    eighth = BLK // 8
-    rows = (out_ref.shape[1] - 2 * eighth) // 2
-    goal = pl.program_id(0)
-    near = pl.ds(pl.multiple_of(group_ref[0] * eighth, eighth), eighth)
+def pack_kernel(within_ref, first_ref, keys_ref, values_ref, near_keys_ref, near_values_ref, out_ref):
+    part = BLK // 16
+    rows = (out_ref.shape[1] - 2 * part) // 2
+    near = pl.ds(pl.multiple_of(first_ref[0], part), part)
     for i in range(out_ref.shape[0]):
-        at = within_ref[goal, i]
+        at = within_ref[pl.program_id(0), i]
         out_ref[i, 0:rows] = keys_ref[at, 0:rows]
         out_ref[i, rows : 2 * rows] = values_ref[at, 0:rows]
-        out_ref[i, 2 * rows : 2 * rows + eighth] = near_keys_ref[0, near]
-        out_ref[i, 2 * rows + eighth :] = near_values_ref[0, near]
-
-
-def pack(within, group, keys, values, near_keys, near_values, rows):
+        out_ref[i, 2 * rows : 2 * rows + part] = near_keys_ref[0, near]
+        out_ref[i, 2 * rows + part :] = near_values_ref[0, near]
+
+
+def pack(within, place, keys, values, near_keys, near_values, rows):
     def of_group(x, height):
         return pl.BlockSpec((x.shape[0] // KV_HEADS, height, HEAD_DIM), lambda n, s, g: (n, 0, 0))
 
     arrays = ((keys, rows), (values, rows), (near_keys, BLK), (near_values, BLK))
-    height = 2 * rows + BLK // 4
+    height = 2 * rows + BLK // 8
     return pl.pallas_call(
         pack_kernel,
         out_shape=jax.ShapeDtypeStruct((64, height, HEAD_DIM), bf16),
@@ -440,7 +438,7 @@
         ),
         compiler_params=pltpu.CompilerParams(vmem_limit_bytes=60 * 1024 * 1024),
         cost_estimate=pl.CostEstimate(flops=0, bytes_accessed=64 * height * 512, transcendentals=0),
-    )(within, group.astype(jnp.int32).reshape(1), *[x for x, _ in arrays])
+    )(within, (place * (BLK // 16)).astype(jnp.int32).reshape(1), *[x for x, _ in arrays])
 
 
 def exchange(x, axes):
@@ -495,7 +493,7 @@
 
     blocked = (KV_HEADS * local_blocks, BLK, HEAD_DIM)
     first = pack(
-        within.T, group, cache_keys.reshape(blocked), cache_values.reshape(blocked),
+        within.T, 2 * group + core, cache_keys.reshape(blocked), cache_values.reshape(blocked),
         stretch_keys, stretch_values, 3 * piece,
     )
     first = exchange(first, CHIP)
@@ -529,15 +527,16 @@
     columns = partial_columns(
         where, own_rows.reshape(by_pair), other_rows.reshape(by_pair), gate_weight, up_weight
     )
+    columns, squares = lax.optimization_barrier((columns, squares))
     theirs, mine = columns[:8], columns[8:]
+    squares = exchange(squares, COL)
     arrived = ring_start(theirs)
-    sums = ring_middle(theirs, *arrived[:2])
-    sums, mine, squares = lax.optimization_barrier((sums, mine, squares))
-    squares = exchange(squares, COL)
+    steps, squares = lax.optimization_barrier((arrived[:2], squares))
+    sums = ring_middle(theirs, *steps)
+    sums, mine = lax.optimization_barrier((sums, mine))
     halves = ring_end(theirs, arrived, sums)
     own_first, own_second, right, left, go_right, go_left = mine
     from_left, from_right = to_right(go_right), to_left(go_left)
-    halves, squares = lax.optimization_barrier((halves, squares))
     got = swap(add_halves(*halves), "xl")
     factor = lax.rsqrt(jnp.sum(squares, axis=0).reshape(-1) / D + 1e-05)
     third_left, third_right = to_right(add_pieces(right, from_left)), to_left(add_pieces(left, from_right))

time: 330 us -> 328 us (level)
  blocking collectives: 70.8 us -> 40.2 us
  waiting for transfers between devices: 137 us -> 150 us
  starting transfers between devices: 46.4 us -> 58.8 us
  local copies, waits for them, and re-layouts: 10 us -> 15.9 us
    all_to_all x3 -> x2, blocking collectives: 70.8 us -> 40.2 us  [exchange(): return lax.all_to_all(x, axes, split_axis=0, concat_axis=0, tiled=True)]
    ppermute x8, waiting for transfers between devices: 25.5 us -> 9.83 us  [swap(): return lax.ppermute(x, axis, [(0, 1), (1, 0)])]
    ppermute x8, waiting for transfers between devices: 19.3 us -> 31.3 us  [to_left(): return lax.ppermute(x, 'y', [(i, (i + 3) % 4) for i in range(4)])]
    ppermute x8, waiting for transfers between devices: 14.7 us -> 23.8 us  [to_right(): return lax.ppermute(x, 'y', [(i, (i + 1) % 4) for i in range(4)])]
    all_to_all x4 -> x5, waiting for transfers between devices: 77.8 us -> 85.4 us  [exchange(): return lax.all_to_all(x, axes, split_axis=0, concat_axis=0, tiled=True)]
    all_to_all x4 -> x5, starting transfers between devices: 28.5 us -> 35.6 us  [exchange(): return lax.all_to_all(x, axes, split_axis=0, concat_axis=0, tiled=True)]
    ppermute x8, starting transfers between devices: 13.1 us -> 18.2 us  [to_left(): return lax.ppermute(x, 'y', [(i, (i + 3) % 4) for i in range(4)])]
    unnamed x37 -> x45, local copies, waits for them, and re-layouts: 3.14 us -> 7.46 us
  transfers between devices with their start and end apart: 28 -> 29, of which waited for: 18 -> 19; matrix products, arithmetic and copies ran while one was open for 3% -> 4% of each run, Pallas kernels for 7% -> 6%
where the time goes in v10:
time: 328 us; the launch traced here: 326 us
  waiting for transfers between devices  150 us (46%)
  starting transfers between devices  58.8 us (18%)
  Pallas kernels  54.2 us (17%)
  blocking collectives  40.2 us (12%)
  local copies, waits for them, and re-layouts  15.9 us (5%)
  other arithmetic  6.55 us (2%)
    all_to_all x5, waiting for transfers between devices, exchange(): return lax.all_to_all(x, axes, split_axis=0, concat_axis=0, tiled=True)  85.4 us
    all_to_all x2, blocking collectives, exchange(): return lax.all_to_all(x, axes, split_axis=0, concat_axis=0, tiled=True)  40.2 us
    all_to_all x5, starting transfers between devices, exchange(): return lax.all_to_all(x, axes, split_axis=0, concat_axis=0, tiled=True)  35.6 us
    ppermute x8, waiting for transfers between devices, to_left(): return lax.ppermute(x, 'y', [(i, (i + 3) % 4) for i in range(4)])  31.3 us
    ppermute x8, waiting for transfers between devices, to_right(): return lax.ppermute(x, 'y', [(i, (i + 1) % 4) for i in range(4)])  23.8 us
    ppermute x8, starting transfers between devices, to_left(): return lax.ppermute(x, 'y', [(i, (i + 3) % 4) for i in range(4)])  18.2 us
    pallas_call x2, Pallas kernels, attend(): pl.pallas_call(functools.partial(attend_kernel, scale, per_step, local_bl...  16.3 us
    pallas_call x1, Pallas kernels, partial_columns(): pl.pallas_call(columns_kernel, out_shape=(jax.ShapeDtypeStruct((tokens, 2...  14.8 us
  transfers between devices with their start and end apart: 29, of which 19 were waited for; matrix products, arithmetic and copies ran while one was open for 4% of the time, Pallas kernels for 6%

profile of v10, /device:TPU:0, one launch (start us, length us, event | category | flops | bytes accessed | tf_op | source)
XLA Modules:
  0.0 326.3 jit_solution(7661623557065241325)
XLA Ops:
  1.6 7.1 %shard_map.118 = bf16[64,208,128]{2,1,0:T(8,128)(2,1)} custom-call(s32[8,8]{1,0:T(8,128)} %bitcast.31, s32[1]{0:T(128)} %bitcast.4.first_ref, bf16[64,128,128]{2,1,0:T(8,128)(2,1)} %bitcast.26, bf16[64,128,128]{2,1,0:T(8,128)(2,1)} %bitcast.28, bf16[8,128,128]{2,1,0:T(8,128)(2,1)} %near_keys_ref.1, bf16[8,128,128]{2,1,0:T(8,128)(2,1)} %near_values_ref.1), custom_call_target="tpu_custom_call" | custom-call | bytes 6815744 | tf_op jit(solution)/shard_map/pallas_call | solution.py:430
  8.8 11.6 %all-to-all-start = ((bf16[64,208,128]{2,1,0:T(8,128)(2,1)}), bf16[64,208,128]{2,1,0:T(8,128)(2,1)S(1)}, u32[]{:S(2)}, u32[]{:S(2)}) async-start(bf16[64,208,128]{2,1,0:T(8,128)(2,1)} %shard_map.118), calls=%async_computation | async-start | bytes 6815744 | tf_op jit(solution)/shard_map/all_to_all | solution.py:445
  20.7 3.0 gather_fusion
  23.7 3.0 gather_fusion.1
  26.7 2.3 pad_maximum_fusion
  29.0 34.8 %all-to-all-done.refs_4_ = bf16[64,208,128]{2,1,0:T(8,128)(2,1)S(1)} async-done(((bf16[64,208,128]{2,1,0:T(8,128)(2,1)}), bf16[64,208,128]{2,1,0:T(8,128)(2,1)S(1)}, u32[]{:S(2)}, u32[]{:S(2)}) %all-to-all-start) | async-done | bytes 3407904 | tf_op jit(solution)/shard_map/all_to_all | solution.py:445
  63.8 7.1 %all-to-all-start.1 = ((bf16[64,64,128]{2,1,0:T(8,128)(2,1)}), bf16[64,64,128]{2,1,0:T(8,128)(2,1)}, u32[]{:S(2)}, u32[]{:S(2)}) async-start(bf16[64,64,128]{2,1,0:T(8,128)(2,1)} %pad_maximum_fusion), calls=%async_computation.1 | async-start | bytes 2097152 | tf_op jit(solution)/shard_map/all_to_all | solution.py:445
  72.5 11.5 %shard_map.119 = (f32[136,512]{1,0:T(8,128)S(1)}, f32[136,512]{1,0:T(8,128)S(1)}, s32[65]{0:T(128)S(1)}) custom-call(s32[64]{0:T(128)S(1)} %dynamic-slice_bitcast_fusion.refs_0_, s32[2]{0:T(128)S(1)} %pad_add_fusion.refs_1_, bf16[128,512]{1,0:T(8,128)(2,1)S(1)} %copy-done.11, bf16[128,512]{1,0:T(8,128)(2,1)} %collective-permute-done.refs_3_.refs_2_, ...), custom_call_target="tpu_custom_call" | custom-call | flops 1090519040 | bytes 3407872 | tf_op jit(solution)/shard_map/pallas_call | solution.py:133
  85.5 3.2 all-to-all-done.1.refs_3_
  90.6 4.8 %shard_map.120 = (f32[136,512]{1,0:T(8,128)S(1)}, f32[136,512]{1,0:T(8,128)S(1)}) custom-call(s32[65]{0:T(128)S(1)} %get-tuple-element.57.refs_0_, bf16[128,512]{1,0:T(8,128)(2,1)S(1)} %copy-done.11, bf16[128,512]{1,0:T(8,128)(2,1)} %collective-permute-done.refs_3_.refs_2_, bf16[64,64,128]{2,1,0:T(8,128)(2,1)} %all-to-all-done.1.refs_3_, ...), custom_call_target="tpu_custom_call" | custom-call | flops 335544320 | bytes 1048576 | tf_op jit(solution)/shard_map/pallas_call | solution.py:133
  98.2 6.1 %all-to-all-start.2 = ((bf16[8,128,512]{2,1,0:T(8,128)(2,1)}), bf16[8,128,512]{2,1,0:T(8,128)(2,1)S(1)}, u32[]{:S(2)}, u32[]{:S(2)}) async-start(bf16[8,128,512]{2,1,0:T(8,128)(2,1)} %shard_map.121), calls=%async_computation.2 | async-start | bytes 2097152 | tf_op jit(solution)/shard_map/all_to_all | solution.py:445
  104.4 16.0 %all-to-all-done.2 = bf16[8,128,512]{2,1,0:T(8,128)(2,1)S(1)} async-done(((bf16[8,128,512]{2,1,0:T(8,128)(2,1)}), bf16[8,128,512]{2,1,0:T(8,128)(2,1)S(1)}, u32[]{:S(2)}, u32[]{:S(2)}) %all-to-all-start.2) | async-done | bytes 1048608 | tf_op jit(solution)/shard_map/all_to_all | solution.py:445
  121.2 2.6 collective-permute-done.2.refs_1_
  125.6 7.4 %all-to-all-start.3 = ((bf16[8,64,1024]{2,1,0:T(8,128)(2,1)}), bf16[8,64,1024]{2,1,0:T(8,128)(2,1)S(1)}, u32[]{:S(2)}, u32[]{:S(2)}) async-start(bf16[8,64,1024]{2,1,0:T(8,128)(2,1)} %bitcast.12), calls=%async_computation.3 | async-start | bytes 2097152 | tf_op jit(solution)/shard_map/all_to_all | solution.py:445
  133.0 17.5 %all-to-all-done.3 = bf16[8,64,1024]{2,1,0:T(8,128)(2,1)S(1)} async-done(((bf16[8,64,1024]{2,1,0:T(8,128)(2,1)}), bf16[8,64,1024]{2,1,0:T(8,128)(2,1)S(1)}, u32[]{:S(2)}, u32[]{:S(2)}) %all-to-all-start.3) | async-done | bytes 1048608 | tf_op jit(solution)/shard_map/all_to_all | solution.py:445
  150.9 19.9 %all_to_all.35 = bf16[8,64,1024]{2,1,0:T(8,128)(2,1)S(1)} all-to-all(bf16[8,64,1024]{2,1,0:T(8,128)(2,1)S(1)} %broadcast_in_dim.4), channel_id=1, replica_groups=mesh['z'=4,'xh'=2,'core'=2,'y'=4,'xl'=2] {'z','xh'}, dimensions={0} | all-to-all | bytes 2097152 | tf_op jit(solution)/shard_map/all_to_all | solution.py:445
  174.4 14.8 %shard_map.124 = (bf16[64,3584]{1,0:T(8,128)(2,1)}, bf16[64,3584]{1,0:T(8,128)(2,1)}, bf16[64,3584]{1,0:T(8,128)(2,1)}, bf16[64,3584]{1,0:T(8,128)(2,1)}, bf16[6...) custom-call(s32[2]{0:T(128)} %pad_add_fusion.1.place_ref, ...), custom_call_target="tpu_custom_call" | custom-call | flops 7516192768 | bytes 16777216 | tf_op jit(solution)/shard_map/pallas_call | solution.py:262
  189.5 3.2 collective-permute-start.5
  193.4 3.3 %all-to-all-start.5 = ((f32[8,1,128]{2,1,0:T(1,128)}), f32[8,1,128]{2,1,0:T(1,128)S(1)}, u32[]{:S(2)}, u32[]{:S(2)}) async-start(f32[8,1,128]{2,1,0:T(1,128)} %reshape.135), calls=%async_computation.5 | async-start | bytes 8192 | tf_op jit(solution)/shard_map/all_to_all | solution.py:445
  198.8 13.9 %all-to-all-done.5 = f32[8,1,128]{2,1,0:T(1,128)S(1)} async-done(((f32[8,1,128]{2,1,0:T(1,128)}), f32[8,1,128]{2,1,0:T(1,128)S(1)}, u32[]{:S(2)}, u32[]{:S(2)}) %all-to-all-start.5) | async-done | bytes 4128 | tf_op jit(solution)/shard_map/all_to_all | solution.py:445
  217.8 2.3 collective-permute-start.13
  222.1 9.3 %collective-permute-done.11.refs_2_ = bf16[64,3584]{1,0:T(8,128)(2,1)S(1)} collective-permute-done((bf16[64,3584]{1,0:T(8,128)(2,1)S(1)}, bf16[64,3584]{1,0:T(8,128)(2,1)S(1)}, u32[]{:S(2)}, u32[]{:S(2)}) %collective-permute-start.11) | collective-permute-done | bytes 458784 | tf_op jit(solution)/shard_map/ppermute | solution.py:387
  231.4 2.3 shard_map.129
  234.0 14.7 %collective-permute-done.8.b_ref.refs_2_ = bf16[2,64,3584]{2,1,0:T(8,128)(2,1)S(1)} collective-permute-done((bf16[2,64,3584]{2,1,0:T(8,128)(2,1)}, bf16[2,64,3584]{2,1,0:T(8,128)(2,1)S(1)}, u32[]{:S(2)}, u32[]{:S(2)}) %collective-permute-start.8) | collective-permute-done | bytes 917536 | tf_op jit(solution)/shard_map/ppermute | solution.py:391
  249.6 3.6 %collective-permute-start.9 = (bf16[64,3584]{1,0:T(8,128)(2,1)}, bf16[64,3584]{1,0:T(8,128)(2,1)}, u32[]{:S(2)}, u32[]{:S(2)}) collective-permute-start(bf16[64,3584]{1,0:T(8,128)(2,1)} %shard_map.128), channel_id=1, source_target_pairs={{0,6},{2,0},{4,2},{6,4},{1,7},{3,1},{5,3},{7,5},{8,14},{10,8},{12,... | collective-permute-start | bytes 1376264 | tf_op jit(solution)/shard_map/ppermute | solution.py:391
  254.3 7.2 %collective-permute-done.9.refs_4_ = bf16[64,3584]{1,0:T(8,128)(2,1)} collective-permute-done((bf16[64,3584]{1,0:T(8,128)(2,1)}, bf16[64,3584]{1,0:T(8,128)(2,1)}, u32[]{:S(2)}, u32[]{:S(2)}) %collective-permute-start.9) | collective-permute-done | bytes 458784 | tf_op jit(solution)/shard_map/ppermute | solution.py:391
  261.4 4.3 %collective-permute-done.7.refs_1_ = bf16[64,3584]{1,0:T(8,128)(2,1)} collective-permute-done((bf16[64,3584]{1,0:T(8,128)(2,1)}, bf16[64,3584]{1,0:T(8,128)(2,1)}, u32[]{:S(2)}, u32[]{:S(2)}) %collective-permute-start.7) | collective-permute-done | bytes 458784 | tf_op jit(solution)/shard_map/ppermute | solution.py:387
  269.0 3.2 collective-permute-start.16
  272.5 6.9 %collective-permute-done.15.refs_4_ = bf16[128,1792]{1,0:T(8,128)(2,1)S(1)} collective-permute-done((bf16[128,1792]{1,0:T(8,128)(2,1)S(1)}, bf16[128,1792]{1,0:T(8,128)(2,1)S(1)}, u32[]{:S(2)}, u32[]{:S(2)}) %collective-permute-start.15) | collective-permute-done | bytes 458784 | tf_op jit(solution)/shard_map/ppermute | solution.py:387
  282.9 9.4 %collective-permute-done.18.refs_3_ = bf16[128,1792]{1,0:T(8,128)(2,1)S(1)} collective-permute-done((bf16[128,1792]{1,0:T(8,128)(2,1)S(1)}, bf16[128,1792]{1,0:T(8,128)(2,1)S(1)}, u32[]{:S(2)}, u32[]{:S(2)}) %collective-permute-start.18) | collective-permute-done | bytes 458784 | tf_op jit(solution)/shard_map/ppermute | solution.py:391
  296.2 3.6 %shard_map.131 = (f32[6,64,1024]{2,1,0:T(8,128)S(1)}, bf16[6,64,1024]{2,1,0:T(8,128)(2,1)S(1)}) custom-call(bf16[128,1792]{1,0:T(8,128)(2,1)S(1)} %shard_map.130.refs_0_, bf16[128,1792]{1,0:T(8,128)(2,1)S(1)} %collective-permute-done.17.refs_1_, bf16[128,1792]{1,0:T(8,128)(2,1)S(1)} %collective-permute-done.16.refs_2_, ...), custom_call_target="tpu_custom_call" | custom-call | flops 2818572288 | bytes 8781824 | tf_op jit(solution)/shard_map/pallas_call | solution.py:349
  305.1 20.3 %all_to_all.36 = bf16[8,64,1024]{2,1,0:T(8,128)(2,1)S(1)} all-to-all(bf16[8,64,1024]{2,1,0:T(8,128)(2,1)S(1)} %shard_map.133), channel_id=1, replica_groups=mesh['z'=4,'xh'=2,'core'=2,'y'=4,'xl'=2] {'z','xh'}, dimensions={0} | all-to-all | bytes 2097152 | tf_op jit(solution)/shard_map/all_to_all | solution.py:445
  (117 shorter events, 45.5 us)
Async XLA Ops:
  8.8 55.0 %all-to-all-start = ((bf16[64,208,128]{2,1,0:T(8,128)(2,1)}), bf16[64,208,128]{2,1,0:T(8,128)(2,1)S(1)}, u32[]{:S(2)}, u32[]{:S(2)}) async-start(bf16[64,208,128]{2,1,0:T(8,128)(2,1)} %shard_map.118), calls=%async_computation | async-start | bytes 6815744 | tf_op jit(solution)/shard_map/all_to_all | solution.py:445
  26.7 44.2 %copy-start.11 = (bf16[128,512]{1,0:T(8,128)(2,1)S(1)}, bf16[128,512]{1,0:T(8,128)(2,1)}, u32[]{:S(2)}) copy-start(bf16[128,512]{1,0:T(8,128)(2,1)} %refs_1_.1) | copy-start | bytes 393220
  63.8 24.9 %all-to-all-start.1 = ((bf16[64,64,128]{2,1,0:T(8,128)(2,1)}), bf16[64,64,128]{2,1,0:T(8,128)(2,1)}, u32[]{:S(2)}, u32[]{:S(2)}) async-start(bf16[64,64,128]{2,1,0:T(8,128)(2,1)} %pad_maximum_fusion), calls=%async_computation.1 | async-start | bytes 2097152 | tf_op jit(solution)/shard_map/all_to_all | solution.py:445
  71.0 1.6 collective-permute-start
  95.4 1.6 collective-permute-start.1
  98.2 22.2 %all-to-all-start.2 = ((bf16[8,128,512]{2,1,0:T(8,128)(2,1)}), bf16[8,128,512]{2,1,0:T(8,128)(2,1)S(1)}, u32[]{:S(2)}, u32[]{:S(2)}) async-start(bf16[8,128,512]{2,1,0:T(8,128)(2,1)} %shard_map.121), calls=%async_computation.2 | async-start | bytes 2097152 | tf_op jit(solution)/shard_map/all_to_all | solution.py:445
  121.1 2.7 collective-permute-start.2
  125.6 25.0 %all-to-all-start.3 = ((bf16[8,64,1024]{2,1,0:T(8,128)(2,1)}), bf16[8,64,1024]{2,1,0:T(8,128)(2,1)S(1)}, u32[]{:S(2)}, u32[]{:S(2)}) async-start(bf16[8,64,1024]{2,1,0:T(8,128)(2,1)} %bitcast.12), calls=%async_computation.3 | async-start | bytes 2097152 | tf_op jit(solution)/shard_map/all_to_all | solution.py:445
  170.8 2.7 collective-permute-start.3
  189.2 42.2 %copy-start.6 = (bf16[64,3584]{1,0:T(8,128)(2,1)S(1)}, bf16[64,3584]{1,0:T(8,128)(2,1)}, u32[]{:S(2)}) copy-start(bf16[64,3584]{1,0:T(8,128)(2,1)} %get-tuple-element.95.refs_0_) | copy-start | bytes 1376260
  189.2 42.2 %copy-start.7 = (bf16[64,3584]{1,0:T(8,128)(2,1)S(1)}, bf16[64,3584]{1,0:T(8,128)(2,1)}, u32[]{:S(2)}) copy-start(bf16[64,3584]{1,0:T(8,128)(2,1)} %get-tuple-element.98.refs_3_) | copy-start | bytes 1376260
  189.2 24.7 %collective-permute-start.4 = (bf16[64,3584]{1,0:T(8,128)(2,1)}, bf16[64,3584]{1,0:T(8,128)(2,1)S(1)}, u32[]{:S(2)}, u32[]{:S(2)}) collective-permute-start(bf16[64,3584]{1,0:T(8,128)(2,1)} %get-tuple-element.77), channel_id=1, source_target_pairs={{0,2},{2,4},{4,6},{6,0},{1,3},{3,5},{5,7},{7,1},{8,10},{10,12},{12... | collective-permute-start | bytes 1376264 | tf_op jit(solution)/shard_map/ppermute | solution.py:387
  189.5 24.5 %collective-permute-start.5 = (bf16[64,3584]{1,0:T(8,128)(2,1)}, bf16[64,3584]{1,0:T(8,128)(2,1)S(1)}, u32[]{:S(2)}, u32[]{:S(2)}) collective-permute-start(bf16[64,3584]{1,0:T(8,128)(2,1)} %get-tuple-element.78), channel_id=1, source_target_pairs={{0,6},{2,0},{4,2},{6,4},{1,7},{3,1},{5,3},{7,5},{8,14},{10,8},{12,... | collective-permute-start | bytes 1376264 | tf_op jit(solution)/shard_map/ppermute | solution.py:391
  192.7 29.3 %collective-permute-start.10 = (bf16[64,3584]{1,0:T(8,128)(2,1)}, bf16[64,3584]{1,0:T(8,128)(2,1)S(1)}, u32[]{:S(2)}, u32[]{:S(2)}) collective-permute-start(bf16[64,3584]{1,0:T(8,128)(2,1)} %get-tuple-element.96), channel_id=1, source_target_pairs={{0,6},{2,0},{4,2},{6,4},{1,7},{3,1},{5,3},{7,5},{8,14},{10,8},{12,... | collective-permute-start | bytes 1376264 | tf_op jit(solution)/shard_map/ppermute | solution.py:391
  193.4 19.3 %all-to-all-start.5 = ((f32[8,1,128]{2,1,0:T(1,128)}), f32[8,1,128]{2,1,0:T(1,128)S(1)}, u32[]{:S(2)}, u32[]{:S(2)}) async-start(f32[8,1,128]{2,1,0:T(1,128)} %reshape.135), calls=%async_computation.5 | async-start | bytes 8192 | tf_op jit(solution)/shard_map/all_to_all | solution.py:445
  196.7 25.3 %collective-permute-start.12 = (bf16[64,3584]{1,0:T(8,128)(2,1)}, bf16[64,3584]{1,0:T(8,128)(2,1)}, u32[]{:S(2)}, u32[]{:S(2)}) collective-permute-start(bf16[64,3584]{1,0:T(8,128)(2,1)} %get-tuple-element.99), channel_id=1, source_target_pairs={{0,2},{2,4},{4,6},{6,0},{1,3},{3,5},{5,7},{7,1},{8,10},{10,12},{12... | collective-permute-start | bytes 1376264 | tf_op jit(solution)/shard_map/ppermute | solution.py:387
  216.2 15.2 %collective-permute-start.11 = (bf16[64,3584]{1,0:T(8,128)(2,1)S(1)}, bf16[64,3584]{1,0:T(8,128)(2,1)S(1)}, u32[]{:S(2)}, u32[]{:S(2)}) collective-permute-start(bf16[64,3584]{1,0:T(8,128)(2,1)S(1)} %shard_map.125), channel_id=1, source_target_pairs={{0,2},{2,4},{4,6},{6,0},{1,3},{3,5},{5,7},{7,1},{8,10},{10,12},{12... | collective-permute-start | bytes 1376264 | tf_op jit(solution)/shard_map/ppermute | solution.py:387
  217.8 13.6 %collective-permute-start.13 = (bf16[64,3584]{1,0:T(8,128)(2,1)S(1)}, bf16[64,3584]{1,0:T(8,128)(2,1)S(1)}, u32[]{:S(2)}, u32[]{:S(2)}) collective-permute-start(bf16[64,3584]{1,0:T(8,128)(2,1)S(1)} %shard_map.126), channel_id=1, source_target_pairs={{0,6},{2,0},{4,2},{6,4},{1,7},{3,1},{5,3},{7,5},{8,14},{10,8},{12,... | collective-permute-start | bytes 1376264 | tf_op jit(solution)/shard_map/ppermute | solution.py:391
  220.0 28.6 %collective-permute-start.8 = (bf16[2,64,3584]{2,1,0:T(8,128)(2,1)}, bf16[2,64,3584]{2,1,0:T(8,128)(2,1)S(1)}, u32[]{:S(2)}, u32[]{:S(2)}) collective-permute-start(bf16[2,64,3584]{2,1,0:T(8,128)(2,1)} %get-tuple-element.92), channel_id=1, source_target_pairs={{0,6},{2,0},{4,2},{6,4},{1,7},{3,1},{5,3},{7,5},{8,14},{10,8},{12,... | collective-permute-start | bytes 2752520 | tf_op jit(solution)/shard_map/ppermute | solution.py:391
  222.0 31.2 %collective-permute-start.6 = (bf16[2,64,3584]{2,1,0:T(8,128)(2,1)}, bf16[2,64,3584]{2,1,0:T(8,128)(2,1)S(1)}, u32[]{:S(2)}, u32[]{:S(2)}) collective-permute-start(bf16[2,64,3584]{2,1,0:T(8,128)(2,1)} %get-tuple-element.91), channel_id=1, source_target_pairs={{0,2},{2,4},{4,6},{6,0},{1,3},{3,5},{5,7},{7,1},{8,10},{10,12},{12... | collective-permute-start | bytes 2752520 | tf_op jit(solution)/shard_map/ppermute | solution.py:387
  233.7 20.6 %collective-permute-start.14 = (bf16[2,64,3584]{2,1,0:T(8,128)(2,1)}, bf16[2,64,3584]{2,1,0:T(8,128)(2,1)S(1)}, u32[]{:S(2)}, u32[]{:S(2)}) collective-permute-start(bf16[2,64,3584]{2,1,0:T(8,128)(2,1)} %shard_map.129), channel_id=1, source_target_pairs={{0,1},{1,0},{2,3},{3,2},{4,5},{5,4},{6,7},{7,6},{8,9},{9,8},{10,11... | collective-permute-start | bytes 2752520 | tf_op jit(solution)/shard_map/ppermute | solution.py:449
  249.6 11.8 %collective-permute-start.9 = (bf16[64,3584]{1,0:T(8,128)(2,1)}, bf16[64,3584]{1,0:T(8,128)(2,1)}, u32[]{:S(2)}, u32[]{:S(2)}) collective-permute-start(bf16[64,3584]{1,0:T(8,128)(2,1)} %shard_map.128), channel_id=1, source_target_pairs={{0,6},{2,0},{4,2},{6,4},{1,7},{3,1},{5,3},{7,5},{8,14},{10,8},{12,... | collective-permute-start | bytes 1376264 | tf_op jit(solution)/shard_map/ppermute | solution.py:391
  254.1 11.7 %collective-permute-start.7 = (bf16[64,3584]{1,0:T(8,128)(2,1)}, bf16[64,3584]{1,0:T(8,128)(2,1)}, u32[]{:S(2)}, u32[]{:S(2)}) collective-permute-start(bf16[64,3584]{1,0:T(8,128)(2,1)} %shard_map.127), channel_id=1, source_target_pairs={{0,2},{2,4},{4,6},{6,0},{1,3},{3,5},{5,7},{7,1},{8,10},{10,12},{12... | collective-permute-start | bytes 1376264 | tf_op jit(solution)/shard_map/ppermute | solution.py:387
  268.9 10.5 %collective-permute-start.15 = (bf16[128,1792]{1,0:T(8,128)(2,1)S(1)}, bf16[128,1792]{1,0:T(8,128)(2,1)S(1)}, u32[]{:S(2)}, u32[]{:S(2)}) collective-permute-start(bf16[128,1792]{1,0:T(8,128)(2,1)S(1)} %shard_map.130.refs_0_), channel_id=1, source_target_pairs={{0,2},{2,4},{4,6},{6,0},{1,3},{3,5},{5,7},{7,1},{8,10},{10,12},{12... | collective-permute-start | bytes 1376264 | tf_op jit(solution)/shard_map/ppermute | solution.py:387
  269.0 10.4 %collective-permute-start.16 = (bf16[128,1792]{1,0:T(8,128)(2,1)S(1)}, bf16[128,1792]{1,0:T(8,128)(2,1)S(1)}, u32[]{:S(2)}, u32[]{:S(2)}) collective-permute-start(bf16[128,1792]{1,0:T(8,128)(2,1)S(1)} %shard_map.130.refs_0_), channel_id=1, source_target_pairs={{0,6},{2,0},{4,2},{6,4},{1,7},{3,1},{5,3},{7,5},{8,14},{10,8},{12,... | collective-permute-start | bytes 1376264 | tf_op jit(solution)/shard_map/ppermute | solution.py:391
  272.2 8.7 %collective-permute-start.17 = (bf16[128,1792]{1,0:T(8,128)(2,1)S(1)}, bf16[128,1792]{1,0:T(8,128)(2,1)S(1)}, u32[]{:S(2)}, u32[]{:S(2)}) collective-permute-start(bf16[128,1792]{1,0:T(8,128)(2,1)S(1)} %shard_map.130.refs_0_), channel_id=1, source_target_pairs={{0,1},{1,0},{2,3},{3,2},{4,5},{5,4},{6,7},{7,6},{8,9},{9,8},{10,11... | collective-permute-start | bytes 1376264 | tf_op jit(solution)/shard_map/ppermute | solution.py:449
  280.9 11.5 %collective-permute-start.18 = (bf16[128,1792]{1,0:T(8,128)(2,1)S(1)}, bf16[128,1792]{1,0:T(8,128)(2,1)S(1)}, u32[]{:S(2)}, u32[]{:S(2)}) collective-permute-start(bf16[128,1792]{1,0:T(8,128)(2,1)S(1)} %collective-permute-done.17.refs_1_), channel_id=1, source_target_pairs={{0,6},{2,0},{4,2},{6,4},{1,7},{3,1},{5,3},{7,5},{8,14},{10,8},{12,... | collective-permute-start | bytes 1376264 | tf_op jit(solution)/shard_map/ppermute | solution.py:391
  282.9 13.3 %collective-permute-start.19 = (bf16[128,1792]{1,0:T(8,128)(2,1)S(1)}, bf16[128,1792]{1,0:T(8,128)(2,1)S(1)}, u32[]{:S(2)}, u32[]{:S(2)}) collective-permute-start(bf16[128,1792]{1,0:T(8,128)(2,1)S(1)} %collective-permute-done.17.refs_1_), channel_id=1, source_target_pairs={{0,2},{2,4},{4,6},{6,0},{1,3},{3,5},{5,7},{7,1},{8,10},{10,12},{12... | collective-permute-start | bytes 1376264 | tf_op jit(solution)/shard_map/ppermute | solution.py:387
  282.9 18.2 %collective-permute-start.21 = (bf16[128,1792]{1,0:T(8,128)(2,1)S(1)}, bf16[128,1792]{1,0:T(8,128)(2,1)S(1)}, u32[]{:S(2)}, u32[]{:S(2)}) collective-permute-start(bf16[128,1792]{1,0:T(8,128)(2,1)S(1)} %collective-permute-done.15.refs_4_), channel_id=1, source_target_pairs={{0,2},{2,4},{4,6},{6,0},{1,3},{3,5},{5,7},{7,1},{8,10},{10,12},{12... | collective-permute-start | bytes 1376264 | tf_op jit(solution)/shard_map/ppermute | solution.py:387
  292.3 8.8 %collective-permute-start.22 = (bf16[128,1792]{1,0:T(8,128)(2,1)S(1)}, bf16[128,1792]{1,0:T(8,128)(2,1)S(1)}, u32[]{:S(2)}, u32[]{:S(2)}) collective-permute-start(bf16[128,1792]{1,0:T(8,128)(2,1)S(1)} %collective-permute-done.18.refs_3_), channel_id=1, source_target_pairs={{0,6},{2,0},{4,2},{6,4},{1,7},{3,1},{5,3},{7,5},{8,14},{10,8},{12,... | collective-permute-start | bytes 1376264 | tf_op jit(solution)/shard_map/ppermute | solution.py:391
  299.8 4.5 %collective-permute-start.20 = (bf16[6,64,1024]{2,1,0:T(8,128)(2,1)S(1)}, bf16[6,64,1024]{2,1,0:T(8,128)(2,1)S(1)}, u32[]{:S(2)}, u32[]{:S(2)}) collective-permute-start(bf16[6,64,1024]{2,1,0:T(8,128)(2,1)S(1)} %get-tuple-element.106), channel_id=1, source_target_pairs={{0,8},{8,0},{1,9},{9,1},{2,10},{10,2},{3,11},{11,3},{4,12},{12,4},... | collective-permute-start | bytes 2359304 | tf_op jit(solution)/shard_map/ppermute | solution.py:449
  302.8 1.6 collective-permute-start.23
  (19 other events, 248.5 us)

commit v11 on v8

--- a/solution.py
+++ b/solution.py
@@ -417,10 +417,10 @@
 
 
 def pack(within, group, keys, values, near_keys, near_values, rows):
-    def of_group(x):
-        return pl.BlockSpec((x.shape[0] // KV_HEADS, *x.shape[1:]), lambda n, s, g: (n, 0, 0))
-
-    arrays = (keys, values, near_keys, near_values)
+    def of_group(x, height):
+        return pl.BlockSpec((x.shape[0] // KV_HEADS, height, HEAD_DIM), lambda n, s, g: (n, 0, 0))
+
+    arrays = ((keys, rows), (values, rows), (near_keys, BLK), (near_values, BLK))
     height = 2 * rows + BLK // 4
     return pl.pallas_call(
         pack_kernel,
@@ -428,12 +428,12 @@
         grid_spec=pltpu.PrefetchScalarGridSpec(
             num_scalar_prefetch=2,
             grid=(8,),
-            in_specs=[of_group(x) for x in arrays],
+            in_specs=[of_group(*x) for x in arrays],
             out_specs=pl.BlockSpec((8, height, HEAD_DIM), lambda n, s, g: (n, 0, 0)),
         ),
         compiler_params=pltpu.CompilerParams(vmem_limit_bytes=60 * 1024 * 1024),
         cost_estimate=pl.CostEstimate(flops=0, bytes_accessed=64 * height * 512, transcendentals=0),
-    )(within, group.astype(jnp.int32).reshape(1), *arrays)
+    )(within, group.astype(jnp.int32).reshape(1), *[x for x, _ in arrays])
 
 
 def exchange(x, axes):
@@ -537,7 +537,6 @@
     first, hidden_got = lax.optimization_barrier((gather_start(hidden), swap(hidden, "xl")))
     got_left, got_right = to_right(hidden_got), to_left(hidden_got)
     mine_far = to_right(first[0])
-    got_left, got_right, mine_far = lax.optimization_barrier((got_left, got_right, mine_far))
     got_far = to_left(got_right)
     near = (hidden, hidden_got, first[1], got_right, first[0], got_left)
     kept, give = down_product(near, down_weight)

time: 325 us -> 319 us (0.982)
  waiting for transfers between devices: 155 us -> 148 us
    ppermute x9, waiting for transfers between devices: 43.3 us -> 32.9 us  [to_right(): return lax.ppermute(x, 'y', [(i, (i + 1) % 4) for i in range(4)])]
    ppermute x9, waiting for transfers between devices: 15.7 us -> 19.5 us  [to_left(): return lax.ppermute(x, 'y', [(i, (i + 3) % 4) for i in range(4)])]
  transfers between devices with their start and end apart: 31 -> 31, of which waited for: 23 -> 23; matrix products, arithmetic and copies ran while one was open for 4% -> 4% of each run, Pallas kernels for 6% -> 7%
where the time goes in v11:
time: 319 us; the launch traced here: 317 us
  waiting for transfers between devices  148 us (46%)
  starting transfers between devices  57.8 us (18%)
  Pallas kernels  53.5 us (17%)
  blocking collectives  40.3 us (13%)
  local copies, waits for them, and re-layouts  10.4 us (3%)
  other arithmetic  6.98 us (2%)
    all_to_all x5, waiting for transfers between devices, exchange(): return lax.all_to_all(x, axes, split_axis=0, concat_axis=0, tiled=True)  85.2 us
    all_to_all x2, blocking collectives, exchange(): return lax.all_to_all(x, axes, split_axis=0, concat_axis=0, tiled=True)  40.3 us
    all_to_all x5, starting transfers between devices, exchange(): return lax.all_to_all(x, axes, split_axis=0, concat_axis=0, tiled=True)  33.9 us
    ppermute x9, waiting for transfers between devices, to_right(): return lax.ppermute(x, 'y', [(i, (i + 1) % 4) for i in range(4)])  32.9 us
    ppermute x9, starting transfers between devices, to_left(): return lax.ppermute(x, 'y', [(i, (i + 3) % 4) for i in range(4)])  21.6 us
    ppermute x9, waiting for transfers between devices, to_left(): return lax.ppermute(x, 'y', [(i, (i + 3) % 4) for i in range(4)])  19.5 us
    pallas_call x2, Pallas kernels, attend(): pl.pallas_call(functools.partial(attend_kernel, scale, per_step, local_bl...  15.6 us
    pallas_call x1, Pallas kernels, partial_columns(): pl.pallas_call(columns_kernel, out_shape=(jax.ShapeDtypeStruct((tokens, 2...  14.8 us
  transfers between devices with their start and end apart: 31, of which 23 were waited for; matrix products, arithmetic and copies ran while one was open for 4% of the time, Pallas kernels for 7%

profile of v11, /device:TPU:0, one launch (start us, length us, event | category | flops | bytes accessed | tf_op | source)
XLA Modules:
  0.0 317.3 jit_solution(4029107688314174351)
XLA Ops:
  1.6 7.2 %shard_map.118 = bf16[64,224,128]{2,1,0:T(8,128)(2,1)} custom-call(s32[8,8]{1,0:T(8,128)} %bitcast.29, s32[1]{0:T(128)} %bitcast.4.group_ref, bf16[64,128,128]{2,1,0:T(8,128)(2,1)} %bitcast.25, bf16[64,128,128]{2,1,0:T(8,128)(2,1)} %bitcast.27, bf16[8,128,128]{2,1,0:T(8,128)(2,1)} %near_keys_ref.1, bf16[8,128,128]{2,1,0:T(8,128)(2,1)} %near_values_ref.1), custom_call_target="tpu_custom_call" | custom-call | bytes 7340032 | tf_op jit(solution)/shard_map/pallas_call | solution.py:425
  8.8 11.9 %all-to-all-start = ((bf16[64,224,128]{2,1,0:T(8,128)(2,1)}), bf16[64,224,128]{2,1,0:T(8,128)(2,1)}, u32[]{:S(2)}, u32[]{:S(2)}) async-start(bf16[64,224,128]{2,1,0:T(8,128)(2,1)} %shard_map.118), calls=%async_computation | async-start | bytes 7340032 | tf_op jit(solution)/shard_map/all_to_all | solution.py:440
  26.7 40.3 %all-to-all-done.refs_4_ = bf16[64,224,128]{2,1,0:T(8,128)(2,1)} async-done(((bf16[64,224,128]{2,1,0:T(8,128)(2,1)}), bf16[64,224,128]{2,1,0:T(8,128)(2,1)}, u32[]{:S(2)}, u32[]{:S(2)}) %all-to-all-start) | async-done | bytes 3670048 | tf_op jit(solution)/shard_map/all_to_all | solution.py:440
  67.1 6.9 %all-to-all-start.1 = ((bf16[64,64,128]{2,1,0:T(8,128)(2,1)}), bf16[64,64,128]{2,1,0:T(8,128)(2,1)S(1)}, u32[]{:S(2)}, u32[]{:S(2)}) async-start(bf16[64,64,128]{2,1,0:T(8,128)(2,1)} %pad_maximum_fusion), calls=%async_computation.1 | async-start | bytes 2097152 | tf_op jit(solution)/shard_map/all_to_all | solution.py:440
  75.5 12.7 %shard_map.119 = (f32[136,512]{1,0:T(8,128)S(1)}, f32[136,512]{1,0:T(8,128)S(1)}, s32[65]{0:T(128)S(1)}) custom-call(s32[64]{0:T(128)S(1)} %dynamic-slice_bitcast_fusion.refs_0_, s32[2]{0:T(128)S(1)} %pad_add_fusion.refs_1_, bf16[128,512]{1,0:T(8,128)(2,1)S(1)} %copy-done.13, bf16[128,512]{1,0:T(8,128)(2,1)S(1)} %collective-permute-done.refs_3_.refs_2_, ...), custom_call_target="tpu_custom_call" | custom-call | flops 1174405120 | bytes 3670016 | tf_op jit(solution)/shard_map/pallas_call | solution.py:134
  88.2 3.7 %all-to-all-done.1.refs_3_ = bf16[64,64,128]{2,1,0:T(8,128)(2,1)S(1)} async-done(((bf16[64,64,128]{2,1,0:T(8,128)(2,1)}), bf16[64,64,128]{2,1,0:T(8,128)(2,1)S(1)}, u32[]{:S(2)}, u32[]{:S(2)}) %all-to-all-start.1) | async-done | bytes 1048608 | tf_op jit(solution)/shard_map/all_to_all | solution.py:440
  91.9 2.9 shard_map.120
  97.6 4.2 %all-to-all-start.2 = ((bf16[8,128,512]{2,1,0:T(8,128)(2,1)}), bf16[8,128,512]{2,1,0:T(8,128)(2,1)S(1)}, u32[]{:S(2)}, u32[]{:S(2)}) async-start(bf16[8,128,512]{2,1,0:T(8,128)(2,1)} %shard_map.121), calls=%async_computation.2 | async-start | bytes 2097152 | tf_op jit(solution)/shard_map/all_to_all | solution.py:440
  101.8 16.3 %all-to-all-done.2 = bf16[8,128,512]{2,1,0:T(8,128)(2,1)S(1)} async-done(((bf16[8,128,512]{2,1,0:T(8,128)(2,1)}), bf16[8,128,512]{2,1,0:T(8,128)(2,1)S(1)}, u32[]{:S(2)}, u32[]{:S(2)}) %all-to-all-start.2) | async-done | bytes 1048608 | tf_op jit(solution)/shard_map/all_to_all | solution.py:440
  118.9 2.6 collective-permute-done.2.refs_1_
  123.3 7.6 %all-to-all-start.3 = ((bf16[8,64,1024]{2,1,0:T(8,128)(2,1)}), bf16[8,64,1024]{2,1,0:T(8,128)(2,1)S(1)}, u32[]{:S(2)}, u32[]{:S(2)}) async-start(bf16[8,64,1024]{2,1,0:T(8,128)(2,1)} %bitcast.12), calls=%async_computation.3 | async-start | bytes 2097152 | tf_op jit(solution)/shard_map/all_to_all | solution.py:440
  130.9 17.5 %all-to-all-done.3 = bf16[8,64,1024]{2,1,0:T(8,128)(2,1)S(1)} async-done(((bf16[8,64,1024]{2,1,0:T(8,128)(2,1)}), bf16[8,64,1024]{2,1,0:T(8,128)(2,1)S(1)}, u32[]{:S(2)}, u32[]{:S(2)}) %all-to-all-start.3) | async-done | bytes 1048608 | tf_op jit(solution)/shard_map/all_to_all | solution.py:440
  148.8 20.0 %all_to_all.35 = bf16[8,64,1024]{2,1,0:T(8,128)(2,1)} all-to-all(bf16[8,64,1024]{2,1,0:T(8,128)(2,1)S(1)} %broadcast_in_dim.4), channel_id=1, replica_groups=mesh['z'=4,'xh'=2,'core'=2,'y'=4,'xl'=2] {'z','xh'}, dimensions={0} | all-to-all | bytes 2097152 | tf_op jit(solution)/shard_map/all_to_all | solution.py:440
  169.3 2.4 collective-permute-done.3
  171.7 14.8 %shard_map.124 = (bf16[64,3584]{1,0:T(8,128)(2,1)}, bf16[64,3584]{1,0:T(8,128)(2,1)}, bf16[64,3584]{1,0:T(8,128)(2,1)}, bf16[64,3584]{1,0:T(8,128)(2,1)}, bf16[6...) custom-call(s32[2]{0:T(128)} %pad_add_fusion.1.place_ref, ...), custom_call_target="tpu_custom_call" | custom-call | flops 7516192768 | bytes 16777216 | tf_op jit(solution)/shard_map/pallas_call | solution.py:259
  188.7 2.4 collective-permute-start.12
  193.3 6.9 %collective-permute-done.5.refs_1_ = bf16[64,3584]{1,0:T(8,128)(2,1)S(1)} collective-permute-done((bf16[64,3584]{1,0:T(8,128)(2,1)}, bf16[64,3584]{1,0:T(8,128)(2,1)S(1)}, u32[]{:S(2)}, u32[]{:S(2)}) %collective-permute-start.5) | collective-permute-done | bytes 458784 | tf_op jit(solution)/shard_map/ppermute | solution.py:385
  200.3 2.3 collective-permute-done.4.refs_1_
  203.6 3.2 %collective-permute-start.15 = (bf16[64,3584]{1,0:T(8,128)(2,1)S(1)}, bf16[64,3584]{1,0:T(8,128)(2,1)S(1)}, u32[]{:S(2)}, u32[]{:S(2)}) collective-permute-start(bf16[64,3584]{1,0:T(8,128)(2,1)S(1)} %shard_map.126), channel_id=1, source_target_pairs={{0,6},{2,0},{4,2},{6,4},{1,7},{3,1},{5,3},{7,5},{8,14},{10,8},{12,... | collective-permute-start | bytes 1376264 | tf_op jit(solution)/shard_map/ppermute | solution.py:385
  207.5 3.3 %all-to-all-start.5 = ((f32[8,1,128]{2,1,0:T(1,128)}), f32[8,1,128]{2,1,0:T(1,128)S(1)}, u32[]{:S(2)}, u32[]{:S(2)}) async-start(f32[8,1,128]{2,1,0:T(1,128)} %reshape.135), calls=%async_computation.5 | async-start | bytes 8192 | tf_op jit(solution)/shard_map/all_to_all | solution.py:440
  210.8 3.2 collective-permute-start.10
  214.0 7.4 %all-to-all-done.5 = f32[8,1,128]{2,1,0:T(1,128)S(1)} async-done(((f32[8,1,128]{2,1,0:T(1,128)}), f32[8,1,128]{2,1,0:T(1,128)S(1)}, u32[]{:S(2)}, u32[]{:S(2)}) %all-to-all-start.5) | async-done | bytes 4128 | tf_op jit(solution)/shard_map/all_to_all | solution.py:440
  225.0 3.2 %collective-permute-start.6 = (bf16[64,3584]{1,0:T(8,128)(2,1)}, bf16[64,3584]{1,0:T(8,128)(2,1)S(1)}, u32[]{:S(2)}, u32[]{:S(2)}) collective-permute-start(bf16[64,3584]{1,0:T(8,128)(2,1)} %get-tuple-element.69), channel_id=1, source_target_pairs={{0,6},{2,0},{4,2},{6,4},{1,7},{3,1},{5,3},{7,5},{8,14},{10,8},{12,... | collective-permute-start | bytes 1376264 | tf_op jit(solution)/shard_map/ppermute | solution.py:385
  234.9 2.6 collective-permute-done.7.refs_1_
  239.6 7.8 %collective-permute-done.9.refs_4_ = bf16[64,3584]{1,0:T(8,128)(2,1)} collective-permute-done((bf16[64,3584]{1,0:T(8,128)(2,1)}, bf16[64,3584]{1,0:T(8,128)(2,1)}, u32[]{:S(2)}, u32[]{:S(2)}) %collective-permute-start.9) | collective-permute-done | bytes 458784 | tf_op jit(solution)/shard_map/ppermute | solution.py:381
  248.7 6.4 %collective-permute-done.8.refs_2_ = bf16[64,3584]{1,0:T(8,128)(2,1)} collective-permute-done((bf16[64,3584]{1,0:T(8,128)(2,1)}, bf16[64,3584]{1,0:T(8,128)(2,1)}, u32[]{:S(2)}, u32[]{:S(2)}) %collective-permute-start.8) | collective-permute-done | bytes 458784 | tf_op jit(solution)/shard_map/ppermute | solution.py:381
  257.5 3.2 %collective-permute-start.18 = (bf16[128,1792]{1,0:T(8,128)(2,1)S(1)}, bf16[128,1792]{1,0:T(8,128)(2,1)S(1)}, u32[]{:S(2)}, u32[]{:S(2)}) collective-permute-start(bf16[128,1792]{1,0:T(8,128)(2,1)S(1)} %shard_map.130.refs_0_), channel_id=1, source_target_pairs={{0,6},{2,0},{4,2},{6,4},{1,7},{3,1},{5,3},{7,5},{8,14},{10,8},{12,... | collective-permute-start | bytes 1376264 | tf_op jit(solution)/shard_map/ppermute | solution.py:385
  260.9 8.2 %collective-permute-done.17.refs_4_ = bf16[128,1792]{1,0:T(8,128)(2,1)S(1)} collective-permute-done((bf16[128,1792]{1,0:T(8,128)(2,1)S(1)}, bf16[128,1792]{1,0:T(8,128)(2,1)S(1)}, u32[]{:S(2)}, u32[]{:S(2)}) %collective-permute-start.17) | collective-permute-done | bytes 458784 | tf_op jit(solution)/shard_map/ppermute | solution.py:381
  272.7 8.6 %collective-permute-done.20.refs_3_ = bf16[128,1792]{1,0:T(8,128)(2,1)S(1)} collective-permute-done((bf16[128,1792]{1,0:T(8,128)(2,1)S(1)}, bf16[128,1792]{1,0:T(8,128)(2,1)S(1)}, u32[]{:S(2)}, u32[]{:S(2)}) %collective-permute-start.20) | collective-permute-done | bytes 458784 | tf_op jit(solution)/shard_map/ppermute | solution.py:385
  282.8 4.0 %collective-permute-done.21.refs_5_ = bf16[128,1792]{1,0:T(8,128)(2,1)S(1)} collective-permute-done((bf16[128,1792]{1,0:T(8,128)(2,1)S(1)}, bf16[128,1792]{1,0:T(8,128)(2,1)S(1)}, u32[]{:S(2)}, u32[]{:S(2)}) %collective-permute-start.21) | collective-permute-done | bytes 458784 | tf_op jit(solution)/shard_map/ppermute | solution.py:381
  286.8 3.6 %shard_map.131 = (f32[6,64,1024]{2,1,0:T(8,128)S(1)}, bf16[6,64,1024]{2,1,0:T(8,128)(2,1)S(1)}) custom-call(bf16[128,1792]{1,0:T(8,128)(2,1)S(1)} %shard_map.130.refs_0_, bf16[128,1792]{1,0:T(8,128)(2,1)S(1)} %collective-permute-done.19.refs_1_, bf16[128,1792]{1,0:T(8,128)(2,1)S(1)} %collective-permute-done.18.refs_2_, ...), custom_call_target="tpu_custom_call" | custom-call | flops 2818572288 | bytes 8781824 | tf_op jit(solution)/shard_map/pallas_call | solution.py:343
  296.1 20.3 %all_to_all.36 = bf16[8,64,1024]{2,1,0:T(8,128)(2,1)S(1)} all-to-all(bf16[8,64,1024]{2,1,0:T(8,128)(2,1)S(1)} %shard_map.133), channel_id=1, replica_groups=mesh['z'=4,'xh'=2,'core'=2,'y'=4,'xl'=2] {'z','xh'}, dimensions={0} | all-to-all | bytes 2097152 | tf_op jit(solution)/shard_map/all_to_all | solution.py:440
  (113 shorter events, 49.2 us)
Async XLA Ops:
  8.8 58.2 %all-to-all-start = ((bf16[64,224,128]{2,1,0:T(8,128)(2,1)}), bf16[64,224,128]{2,1,0:T(8,128)(2,1)}, u32[]{:S(2)}, u32[]{:S(2)}) async-start(bf16[64,224,128]{2,1,0:T(8,128)(2,1)} %shard_map.118), calls=%async_computation | async-start | bytes 7340032 | tf_op jit(solution)/shard_map/all_to_all | solution.py:440
  25.5 48.5 %copy-start.13 = (bf16[128,512]{1,0:T(8,128)(2,1)S(1)}, bf16[128,512]{1,0:T(8,128)(2,1)}, u32[]{:S(2)}) copy-start(bf16[128,512]{1,0:T(8,128)(2,1)} %refs_1_.1) | copy-start | bytes 393220
  67.1 24.8 %all-to-all-start.1 = ((bf16[64,64,128]{2,1,0:T(8,128)(2,1)}), bf16[64,64,128]{2,1,0:T(8,128)(2,1)S(1)}, u32[]{:S(2)}, u32[]{:S(2)}) async-start(bf16[64,64,128]{2,1,0:T(8,128)(2,1)} %pad_maximum_fusion), calls=%async_computation.1 | async-start | bytes 2097152 | tf_op jit(solution)/shard_map/all_to_all | solution.py:440
  74.0 1.4 collective-permute-start
  94.8 1.6 collective-permute-start.1
  97.6 20.5 %all-to-all-start.2 = ((bf16[8,128,512]{2,1,0:T(8,128)(2,1)}), bf16[8,128,512]{2,1,0:T(8,128)(2,1)S(1)}, u32[]{:S(2)}, u32[]{:S(2)}) async-start(bf16[8,128,512]{2,1,0:T(8,128)(2,1)} %shard_map.121), calls=%async_computation.2 | async-start | bytes 2097152 | tf_op jit(solution)/shard_map/all_to_all | solution.py:440
  118.8 2.7 collective-permute-start.2
  123.3 25.1 %all-to-all-start.3 = ((bf16[8,64,1024]{2,1,0:T(8,128)(2,1)}), bf16[8,64,1024]{2,1,0:T(8,128)(2,1)S(1)}, u32[]{:S(2)}, u32[]{:S(2)}) async-start(bf16[8,64,1024]{2,1,0:T(8,128)(2,1)} %bitcast.12), calls=%async_computation.3 | async-start | bytes 2097152 | tf_op jit(solution)/shard_map/all_to_all | solution.py:440
  168.7 3.0 collective-permute-start.3
  186.6 13.6 %collective-permute-start.5 = (bf16[64,3584]{1,0:T(8,128)(2,1)}, bf16[64,3584]{1,0:T(8,128)(2,1)S(1)}, u32[]{:S(2)}, u32[]{:S(2)}) collective-permute-start(bf16[64,3584]{1,0:T(8,128)(2,1)} %get-tuple-element.59), channel_id=1, source_target_pairs={{0,6},{2,0},{4,2},{6,4},{1,7},{3,1},{5,3},{7,5},{8,14},{10,8},{12,... | collective-permute-start | bytes 1376264 | tf_op jit(solution)/shard_map/ppermute | solution.py:385
  187.8 14.8 %collective-permute-start.4 = (bf16[64,3584]{1,0:T(8,128)(2,1)}, bf16[64,3584]{1,0:T(8,128)(2,1)S(1)}, u32[]{:S(2)}, u32[]{:S(2)}) collective-permute-start(bf16[64,3584]{1,0:T(8,128)(2,1)} %get-tuple-element.57), channel_id=1, source_target_pairs={{0,2},{2,4},{4,6},{6,0},{1,3},{3,5},{5,7},{7,1},{8,10},{10,12},{12... | collective-permute-start | bytes 1376264 | tf_op jit(solution)/shard_map/ppermute | solution.py:381
  188.7 33.9 %collective-permute-start.12 = (bf16[64,3584]{1,0:T(8,128)(2,1)}, bf16[64,3584]{1,0:T(8,128)(2,1)S(1)}, u32[]{:S(2)}, u32[]{:S(2)}) collective-permute-start(bf16[64,3584]{1,0:T(8,128)(2,1)} %get-tuple-element.77), channel_id=1, source_target_pairs={{0,6},{2,0},{4,2},{6,4},{1,7},{3,1},{5,3},{7,5},{8,14},{10,8},{12,... | collective-permute-start | bytes 1376264 | tf_op jit(solution)/shard_map/ppermute | solution.py:385
  191.1 31.5 %collective-permute-start.14 = (bf16[64,3584]{1,0:T(8,128)(2,1)}, bf16[64,3584]{1,0:T(8,128)(2,1)S(1)}, u32[]{:S(2)}, u32[]{:S(2)}) collective-permute-start(bf16[64,3584]{1,0:T(8,128)(2,1)} %get-tuple-element.80), channel_id=1, source_target_pairs={{0,2},{2,4},{4,6},{6,0},{1,3},{3,5},{5,7},{7,1},{8,10},{10,12},{12... | collective-permute-start | bytes 1376264 | tf_op jit(solution)/shard_map/ppermute | solution.py:381
  203.6 19.0 %collective-permute-start.13 = (bf16[64,3584]{1,0:T(8,128)(2,1)}, bf16[64,3584]{1,0:T(8,128)(2,1)S(1)}, u32[]{:S(2)}, u32[]{:S(2)}) collective-permute-start(bf16[64,3584]{1,0:T(8,128)(2,1)} %shard_map.125), channel_id=1, source_target_pairs={{0,2},{2,4},{4,6},{6,0},{1,3},{3,5},{5,7},{7,1},{8,10},{10,12},{12... | collective-permute-start | bytes 1376264 | tf_op jit(solution)/shard_map/ppermute | solution.py:381
  203.6 19.1 %collective-permute-start.15 = (bf16[64,3584]{1,0:T(8,128)(2,1)S(1)}, bf16[64,3584]{1,0:T(8,128)(2,1)S(1)}, u32[]{:S(2)}, u32[]{:S(2)}) collective-permute-start(bf16[64,3584]{1,0:T(8,128)(2,1)S(1)} %shard_map.126), channel_id=1, source_target_pairs={{0,6},{2,0},{4,2},{6,4},{1,7},{3,1},{5,3},{7,5},{8,14},{10,8},{12,... | collective-permute-start | bytes 1376264 | tf_op jit(solution)/shard_map/ppermute | solution.py:385
  207.5 13.8 %all-to-all-start.5 = ((f32[8,1,128]{2,1,0:T(1,128)}), f32[8,1,128]{2,1,0:T(1,128)S(1)}, u32[]{:S(2)}, u32[]{:S(2)}) async-start(f32[8,1,128]{2,1,0:T(1,128)} %reshape.135), calls=%async_computation.5 | async-start | bytes 8192 | tf_op jit(solution)/shard_map/all_to_all | solution.py:440
  210.8 19.1 %collective-permute-start.10 = (bf16[64,3584]{1,0:T(8,128)(2,1)}, bf16[64,3584]{1,0:T(8,128)(2,1)}, u32[]{:S(2)}, u32[]{:S(2)}) collective-permute-start(bf16[64,3584]{1,0:T(8,128)(2,1)} %get-tuple-element.75), channel_id=1, source_target_pairs={{0,6},{2,0},{4,2},{6,4},{1,7},{3,1},{5,3},{7,5},{8,14},{10,8},{12,... | collective-permute-start | bytes 1376264 | tf_op jit(solution)/shard_map/ppermute | solution.py:385
  222.6 14.9 %collective-permute-start.7 = (bf16[64,3584]{1,0:T(8,128)(2,1)}, bf16[64,3584]{1,0:T(8,128)(2,1)S(1)}, u32[]{:S(2)}, u32[]{:S(2)}) collective-permute-start(bf16[64,3584]{1,0:T(8,128)(2,1)} %get-tuple-element.71), channel_id=1, source_target_pairs={{0,2},{2,4},{4,6},{6,0},{1,3},{3,5},{5,7},{7,1},{8,10},{10,12},{12... | collective-permute-start | bytes 1376264 | tf_op jit(solution)/shard_map/ppermute | solution.py:381
  224.8 30.3 %collective-permute-start.16 = (bf16[2,64,3584]{2,1,0:T(8,128)(2,1)S(1)}, bf16[2,64,3584]{2,1,0:T(8,128)(2,1)S(1)}, u32[]{:S(2)}, u32[]{:S(2)}) collective-permute-start(bf16[2,64,3584]{2,1,0:T(8,128)(2,1)S(1)} %shard_map.129), channel_id=1, source_target_pairs={{0,1},{1,0},{2,3},{3,2},{4,5},{5,4},{6,7},{7,6},{8,9},{9,8},{10,11... | collective-permute-start | bytes 2752520 | tf_op jit(solution)/shard_map/ppermute | solution.py:444
  225.0 14.5 %collective-permute-start.6 = (bf16[64,3584]{1,0:T(8,128)(2,1)}, bf16[64,3584]{1,0:T(8,128)(2,1)S(1)}, u32[]{:S(2)}, u32[]{:S(2)}) collective-permute-start(bf16[64,3584]{1,0:T(8,128)(2,1)} %get-tuple-element.69), channel_id=1, source_target_pairs={{0,6},{2,0},{4,2},{6,4},{1,7},{3,1},{5,3},{7,5},{8,14},{10,8},{12,... | collective-permute-start | bytes 1376264 | tf_op jit(solution)/shard_map/ppermute | solution.py:385
  228.3 19.1 %collective-permute-start.9 = (bf16[64,3584]{1,0:T(8,128)(2,1)}, bf16[64,3584]{1,0:T(8,128)(2,1)}, u32[]{:S(2)}, u32[]{:S(2)}) collective-permute-start(bf16[64,3584]{1,0:T(8,128)(2,1)} %get-tuple-element.73), channel_id=1, source_target_pairs={{0,2},{2,4},{4,6},{6,0},{1,3},{3,5},{5,7},{7,1},{8,10},{10,12},{12... | collective-permute-start | bytes 1376264 | tf_op jit(solution)/shard_map/ppermute | solution.py:381
  232.8 15.9 %collective-permute-start.11 = (bf16[64,3584]{1,0:T(8,128)(2,1)}, bf16[64,3584]{1,0:T(8,128)(2,1)}, u32[]{:S(2)}, u32[]{:S(2)}) collective-permute-start(bf16[64,3584]{1,0:T(8,128)(2,1)} %shard_map.128), channel_id=1, source_target_pairs={{0,6},{2,0},{4,2},{6,4},{1,7},{3,1},{5,3},{7,5},{8,14},{10,8},{12,... | collective-permute-start | bytes 1376264 | tf_op jit(solution)/shard_map/ppermute | solution.py:385
  238.4 16.8 %collective-permute-start.8 = (bf16[64,3584]{1,0:T(8,128)(2,1)}, bf16[64,3584]{1,0:T(8,128)(2,1)}, u32[]{:S(2)}, u32[]{:S(2)}) collective-permute-start(bf16[64,3584]{1,0:T(8,128)(2,1)} %shard_map.127), channel_id=1, source_target_pairs={{0,2},{2,4},{4,6},{6,0},{1,3},{3,5},{5,7},{7,1},{8,10},{10,12},{12... | collective-permute-start | bytes 1376264 | tf_op jit(solution)/shard_map/ppermute | solution.py:381
  257.4 11.7 %collective-permute-start.17 = (bf16[128,1792]{1,0:T(8,128)(2,1)S(1)}, bf16[128,1792]{1,0:T(8,128)(2,1)S(1)}, u32[]{:S(2)}, u32[]{:S(2)}) collective-permute-start(bf16[128,1792]{1,0:T(8,128)(2,1)S(1)} %shard_map.130.refs_0_), channel_id=1, source_target_pairs={{0,2},{2,4},{4,6},{6,0},{1,3},{3,5},{5,7},{7,1},{8,10},{10,12},{12... | collective-permute-start | bytes 1376264 | tf_op jit(solution)/shard_map/ppermute | solution.py:381
  257.5 11.6 %collective-permute-start.18 = (bf16[128,1792]{1,0:T(8,128)(2,1)S(1)}, bf16[128,1792]{1,0:T(8,128)(2,1)S(1)}, u32[]{:S(2)}, u32[]{:S(2)}) collective-permute-start(bf16[128,1792]{1,0:T(8,128)(2,1)S(1)} %shard_map.130.refs_0_), channel_id=1, source_target_pairs={{0,6},{2,0},{4,2},{6,4},{1,7},{3,1},{5,3},{7,5},{8,14},{10,8},{12,... | collective-permute-start | bytes 1376264 | tf_op jit(solution)/shard_map/ppermute | solution.py:385
  260.7 9.9 %collective-permute-start.19 = (bf16[128,1792]{1,0:T(8,128)(2,1)S(1)}, bf16[128,1792]{1,0:T(8,128)(2,1)S(1)}, u32[]{:S(2)}, u32[]{:S(2)}) collective-permute-start(bf16[128,1792]{1,0:T(8,128)(2,1)S(1)} %shard_map.130.refs_0_), channel_id=1, source_target_pairs={{0,1},{1,0},{2,3},{3,2},{4,5},{5,4},{6,7},{7,6},{8,9},{9,8},{10,11... | collective-permute-start | bytes 1376264 | tf_op jit(solution)/shard_map/ppermute | solution.py:444
  270.6 10.7 %collective-permute-start.20 = (bf16[128,1792]{1,0:T(8,128)(2,1)S(1)}, bf16[128,1792]{1,0:T(8,128)(2,1)S(1)}, u32[]{:S(2)}, u32[]{:S(2)}) collective-permute-start(bf16[128,1792]{1,0:T(8,128)(2,1)S(1)} %collective-permute-done.19.refs_1_), channel_id=1, source_target_pairs={{0,6},{2,0},{4,2},{6,4},{1,7},{3,1},{5,3},{7,5},{8,14},{10,8},{12,... | collective-permute-start | bytes 1376264 | tf_op jit(solution)/shard_map/ppermute | solution.py:385
  272.1 14.7 %collective-permute-start.21 = (bf16[128,1792]{1,0:T(8,128)(2,1)S(1)}, bf16[128,1792]{1,0:T(8,128)(2,1)S(1)}, u32[]{:S(2)}, u32[]{:S(2)}) collective-permute-start(bf16[128,1792]{1,0:T(8,128)(2,1)S(1)} %collective-permute-done.19.refs_1_), channel_id=1, source_target_pairs={{0,2},{2,4},{4,6},{6,0},{1,3},{3,5},{5,7},{7,1},{8,10},{10,12},{12... | collective-permute-start | bytes 1376264 | tf_op jit(solution)/shard_map/ppermute | solution.py:381
  272.6 19.5 %collective-permute-start.23 = (bf16[128,1792]{1,0:T(8,128)(2,1)S(1)}, bf16[128,1792]{1,0:T(8,128)(2,1)S(1)}, u32[]{:S(2)}, u32[]{:S(2)}) collective-permute-start(bf16[128,1792]{1,0:T(8,128)(2,1)S(1)} %collective-permute-done.17.refs_4_), channel_id=1, source_target_pairs={{0,2},{2,4},{4,6},{6,0},{1,3},{3,5},{5,7},{7,1},{8,10},{10,12},{12... | collective-permute-start | bytes 1376264 | tf_op jit(solution)/shard_map/ppermute | solution.py:381
  281.3 10.8 %collective-permute-start.24 = (bf16[128,1792]{1,0:T(8,128)(2,1)S(1)}, bf16[128,1792]{1,0:T(8,128)(2,1)S(1)}, u32[]{:S(2)}, u32[]{:S(2)}) collective-permute-start(bf16[128,1792]{1,0:T(8,128)(2,1)S(1)} %collective-permute-done.20.refs_3_), channel_id=1, source_target_pairs={{0,6},{2,0},{4,2},{6,4},{1,7},{3,1},{5,3},{7,5},{8,14},{10,8},{12,... | collective-permute-start | bytes 1376264 | tf_op jit(solution)/shard_map/ppermute | solution.py:385
  290.4 4.9 %collective-permute-start.22 = (bf16[6,64,1024]{2,1,0:T(8,128)(2,1)S(1)}, bf16[6,64,1024]{2,1,0:T(8,128)(2,1)S(1)}, u32[]{:S(2)}, u32[]{:S(2)}) collective-permute-start(bf16[6,64,1024]{2,1,0:T(8,128)(2,1)S(1)} %get-tuple-element.94), channel_id=1, source_target_pairs={{0,8},{8,0},{1,9},{9,1},{2,10},{10,2},{3,11},{11,3},{4,12},{12,4},... | collective-permute-start | bytes 2359304 | tf_op jit(solution)/shard_map/ppermute | solution.py:444
  293.7 1.6 collective-permute-start.25
  (17 other events, 312.8 us)

commit v12 on v11

--- a/solution.py
+++ b/solution.py
@@ -529,10 +529,10 @@
     squares = exchange(squares, COL)
     halves = ring_end(theirs, arrived, sums)
     mine_arrived = ring_start(mine)
-    halves, squares = lax.optimization_barrier((halves, squares))
     got = swap(add_halves(*halves), "xl")
+    steps, squares = lax.optimization_barrier((mine_arrived[:2], squares))
+    halves = ring_end(mine, mine_arrived, ring_middle(mine, *steps))
     factor = lax.rsqrt(jnp.sum(squares, axis=0).reshape(-1) / D + 1e-05)
-    halves = ring_end(mine, mine_arrived, ring_middle(mine, *mine_arrived[:2]))
     hidden = gated(halves, got, factor)
     first, hidden_got = lax.optimization_barrier((gather_start(hidden), swap(hidden, "xl")))
     got_left, got_right = to_right(hidden_got), to_left(hidden_got)

time: 319 us -> 325 us (1.019)
    ppermute x9, waiting for transfers between devices: 32.9 us -> 22.8 us  [to_right(): return lax.ppermute(x, 'y', [(i, (i + 1) % 4) for i in range(4)])]
    ppermute x9, waiting for transfers between devices: 19.5 us -> 29.6 us  [to_left(): return lax.ppermute(x, 'y', [(i, (i + 3) % 4) for i in range(4)])]
    all_to_all x5, waiting for transfers between devices: 85.2 us -> 90.3 us  [exchange(): return lax.all_to_all(x, axes, split_axis=0, concat_axis=0, tiled=True)]
  transfers between devices with their start and end apart: 31 -> 31, of which waited for: 23 -> 21; matrix products, arithmetic and copies ran while one was open for 4% -> 4% of each run, Pallas kernels for 7% -> 7%
where the time goes in v12:
time: 325 us; the launch traced here: 323 us
  waiting for transfers between devices  151 us (46%)
  starting transfers between devices  59.4 us (18%)
  Pallas kernels  54.9 us (17%)
  blocking collectives  40.2 us (12%)
  local copies, waits for them, and re-layouts  9.6 us (3%)
  other arithmetic  7.07 us (2%)
    all_to_all x5, waiting for transfers between devices, exchange(): return lax.all_to_all(x, axes, split_axis=0, concat_axis=0, tiled=True)  90.3 us
    all_to_all x2, blocking collectives, exchange(): return lax.all_to_all(x, axes, split_axis=0, concat_axis=0, tiled=True)  40.2 us
    all_to_all x5, starting transfers between devices, exchange(): return lax.all_to_all(x, axes, split_axis=0, concat_axis=0, tiled=True)  31.9 us
    ppermute x9, waiting for transfers between devices, to_left(): return lax.ppermute(x, 'y', [(i, (i + 3) % 4) for i in range(4)])  29.6 us
    ppermute x9, starting transfers between devices, to_left(): return lax.ppermute(x, 'y', [(i, (i + 3) % 4) for i in range(4)])  23 us
    ppermute x9, waiting for transfers between devices, to_right(): return lax.ppermute(x, 'y', [(i, (i + 1) % 4) for i in range(4)])  22.8 us
    pallas_call x2, Pallas kernels, attend(): pl.pallas_call(functools.partial(attend_kernel, scale, per_step, local_bl...  16.7 us
    pallas_call x1, Pallas kernels, partial_columns(): pl.pallas_call(columns_kernel, out_shape=(jax.ShapeDtypeStruct((tokens, 2...  14.8 us
  transfers between devices with their start and end apart: 31, of which 21 were waited for; matrix products, arithmetic and copies ran while one was open for 4% of the time, Pallas kernels for 7%

profile of v12, /device:TPU:0, one launch (start us, length us, event | category | flops | bytes accessed | tf_op | source)
XLA Modules:
  0.0 322.9 jit_solution(7091540134822720759)
XLA Ops:
  1.6 7.2 %shard_map.118 = bf16[64,224,128]{2,1,0:T(8,128)(2,1)} custom-call(s32[8,8]{1,0:T(8,128)} %bitcast.31, s32[1]{0:T(128)} %bitcast.4.group_ref, bf16[64,128,128]{2,1,0:T(8,128)(2,1)} %bitcast.26, bf16[64,128,128]{2,1,0:T(8,128)(2,1)} %bitcast.28, bf16[8,128,128]{2,1,0:T(8,128)(2,1)} %near_keys_ref.1, bf16[8,128,128]{2,1,0:T(8,128)(2,1)} %near_values_ref.1), custom_call_target="tpu_custom_call" | custom-call | bytes 7340032 | tf_op jit(solution)/shard_map/pallas_call | solution.py:425
  8.8 11.9 %all-to-all-start = ((bf16[64,224,128]{2,1,0:T(8,128)(2,1)}), bf16[64,224,128]{2,1,0:T(8,128)(2,1)}, u32[]{:S(2)}, u32[]{:S(2)}) async-start(bf16[64,224,128]{2,1,0:T(8,128)(2,1)} %shard_map.118), calls=%async_computation | async-start | bytes 7340032 | tf_op jit(solution)/shard_map/all_to_all | solution.py:440
  26.7 40.3 %all-to-all-done.refs_4_ = bf16[64,224,128]{2,1,0:T(8,128)(2,1)} async-done(((bf16[64,224,128]{2,1,0:T(8,128)(2,1)}), bf16[64,224,128]{2,1,0:T(8,128)(2,1)}, u32[]{:S(2)}, u32[]{:S(2)}) %all-to-all-start) | async-done | bytes 3670048 | tf_op jit(solution)/shard_map/all_to_all | solution.py:440
  67.1 6.9 %all-to-all-start.1 = ((bf16[64,64,128]{2,1,0:T(8,128)(2,1)}), bf16[64,64,128]{2,1,0:T(8,128)(2,1)S(1)}, u32[]{:S(2)}, u32[]{:S(2)}) async-start(bf16[64,64,128]{2,1,0:T(8,128)(2,1)} %pad_maximum_fusion), calls=%async_computation.1 | async-start | bytes 2097152 | tf_op jit(solution)/shard_map/all_to_all | solution.py:440
  75.5 12.7 %shard_map.119 = (f32[136,512]{1,0:T(8,128)S(1)}, f32[136,512]{1,0:T(8,128)S(1)}, s32[65]{0:T(128)S(1)}) custom-call(s32[64]{0:T(128)S(1)} %dynamic-slice_bitcast_fusion.refs_0_, s32[2]{0:T(128)S(1)} %pad_add_fusion.refs_1_, bf16[128,512]{1,0:T(8,128)(2,1)S(1)} %copy-done.11, bf16[128,512]{1,0:T(8,128)(2,1)S(1)} %collective-permute-done.refs_3_.refs_2_, ...), custom_call_target="tpu_custom_call" | custom-call | flops 1174405120 | bytes 3670016 | tf_op jit(solution)/shard_map/pallas_call | solution.py:134
  88.2 3.7 %all-to-all-done.1.refs_3_ = bf16[64,64,128]{2,1,0:T(8,128)(2,1)S(1)} async-done(((bf16[64,64,128]{2,1,0:T(8,128)(2,1)}), bf16[64,64,128]{2,1,0:T(8,128)(2,1)S(1)}, u32[]{:S(2)}, u32[]{:S(2)}) %all-to-all-start.1) | async-done | bytes 1048608 | tf_op jit(solution)/shard_map/all_to_all | solution.py:440
  91.9 4.0 %shard_map.120 = (f32[136,512]{1,0:T(8,128)S(1)}, f32[136,512]{1,0:T(8,128)S(1)}) custom-call(s32[65]{0:T(128)S(1)} %get-tuple-element.47.refs_0_, bf16[128,512]{1,0:T(8,128)(2,1)S(1)} %copy-done.11, bf16[128,512]{1,0:T(8,128)(2,1)S(1)} %collective-permute-done.refs_3_.refs_2_, bf16[64,64,128]{2,1,0:T(8,128)(2,1)S(1)} %all-to-all-done.1.refs_3_, ...), custom_call_target="tpu_custom_call" | custom-call | flops 335544320 | bytes 1048576 | tf_op jit(solution)/shard_map/pallas_call | solution.py:134
  98.8 4.2 %all-to-all-start.2 = ((bf16[8,128,512]{2,1,0:T(8,128)(2,1)}), bf16[8,128,512]{2,1,0:T(8,128)(2,1)S(1)}, u32[]{:S(2)}, u32[]{:S(2)}) async-start(bf16[8,128,512]{2,1,0:T(8,128)(2,1)} %shard_map.121), calls=%async_computation.2 | async-start | bytes 2097152 | tf_op jit(solution)/shard_map/all_to_all | solution.py:440
  102.9 16.3 %all-to-all-done.2 = bf16[8,128,512]{2,1,0:T(8,128)(2,1)S(1)} async-done(((bf16[8,128,512]{2,1,0:T(8,128)(2,1)}), bf16[8,128,512]{2,1,0:T(8,128)(2,1)S(1)}, u32[]{:S(2)}, u32[]{:S(2)}) %all-to-all-start.2) | async-done | bytes 1048608 | tf_op jit(solution)/shard_map/all_to_all | solution.py:440
  120.0 2.6 collective-permute-done.2.refs_1_
  124.4 5.6 %all-to-all-start.3 = ((bf16[8,64,1024]{2,1,0:T(8,128)(2,1)}), bf16[8,64,1024]{2,1,0:T(8,128)(2,1)S(1)}, u32[]{:S(2)}, u32[]{:S(2)}) async-start(bf16[8,64,1024]{2,1,0:T(8,128)(2,1)} %bitcast.12), calls=%async_computation.3 | async-start | bytes 2097152 | tf_op jit(solution)/shard_map/all_to_all | solution.py:440
  130.0 17.5 %all-to-all-done.3 = bf16[8,64,1024]{2,1,0:T(8,128)(2,1)S(1)} async-done(((bf16[8,64,1024]{2,1,0:T(8,128)(2,1)}), bf16[8,64,1024]{2,1,0:T(8,128)(2,1)S(1)}, u32[]{:S(2)}, u32[]{:S(2)}) %all-to-all-start.3) | async-done | bytes 1048608 | tf_op jit(solution)/shard_map/all_to_all | solution.py:440
  147.9 19.9 %all_to_all.35 = bf16[8,64,1024]{2,1,0:T(8,128)(2,1)S(1)} all-to-all(bf16[8,64,1024]{2,1,0:T(8,128)(2,1)S(1)} %broadcast_in_dim.4), channel_id=1, replica_groups=mesh['z'=4,'xh'=2,'core'=2,'y'=4,'xl'=2] {'z','xh'}, dimensions={0} | all-to-all | bytes 2097152 | tf_op jit(solution)/shard_map/all_to_all | solution.py:440
  171.4 14.8 %shard_map.124 = (bf16[64,3584]{1,0:T(8,128)(2,1)}, bf16[64,3584]{1,0:T(8,128)(2,1)}, bf16[64,3584]{1,0:T(8,128)(2,1)}, bf16[64,3584]{1,0:T(8,128)(2,1)}, bf16[6...) custom-call(s32[2]{0:T(128)} %pad_add_fusion.1.place_ref, ...), custom_call_target="tpu_custom_call" | custom-call | flops 7516192768 | bytes 16777216 | tf_op jit(solution)/shard_map/pallas_call | solution.py:259
  192.8 7.1 %collective-permute-done.5.refs_1_ = bf16[64,3584]{1,0:T(8,128)(2,1)S(1)} collective-permute-done((bf16[64,3584]{1,0:T(8,128)(2,1)}, bf16[64,3584]{1,0:T(8,128)(2,1)S(1)}, u32[]{:S(2)}, u32[]{:S(2)}) %collective-permute-start.5) | collective-permute-done | bytes 458784 | tf_op jit(solution)/shard_map/ppermute | solution.py:385
  202.3 3.2 collective-permute-start.15
  205.5 4.1 %collective-permute-done.12.refs_1_ = bf16[64,3584]{1,0:T(8,128)(2,1)S(1)} collective-permute-done((bf16[64,3584]{1,0:T(8,128)(2,1)}, bf16[64,3584]{1,0:T(8,128)(2,1)S(1)}, u32[]{:S(2)}, u32[]{:S(2)}) %collective-permute-start.12) | collective-permute-done | bytes 458784 | tf_op jit(solution)/shard_map/ppermute | solution.py:385
  211.9 9.8 %collective-permute-done.13.refs_2_ = bf16[64,3584]{1,0:T(8,128)(2,1)S(1)} collective-permute-done((bf16[64,3584]{1,0:T(8,128)(2,1)S(1)}, bf16[64,3584]{1,0:T(8,128)(2,1)S(1)}, u32[]{:S(2)}, u32[]{:S(2)}) %collective-permute-start.13) | collective-permute-done | bytes 458784 | tf_op jit(solution)/shard_map/ppermute | solution.py:381
  223.4 3.3 %all-to-all-start.5 = ((f32[8,1,128]{2,1,0:T(1,128)}), f32[8,1,128]{2,1,0:T(1,128)S(1)}, u32[]{:S(2)}, u32[]{:S(2)}) async-start(f32[8,1,128]{2,1,0:T(1,128)} %reshape.135), calls=%async_computation.5 | async-start | bytes 8192 | tf_op jit(solution)/shard_map/all_to_all | solution.py:440
  230.0 12.5 %all-to-all-done.5 = f32[8,1,128]{2,1,0:T(1,128)S(1)} async-done(((f32[8,1,128]{2,1,0:T(1,128)}), f32[8,1,128]{2,1,0:T(1,128)S(1)}, u32[]{:S(2)}, u32[]{:S(2)}) %all-to-all-start.5) | async-done | bytes 4128 | tf_op jit(solution)/shard_map/all_to_all | solution.py:440
  246.6 2.6 collective-permute-start.11
  251.4 5.3 %collective-permute-done.11.refs_5_ = bf16[64,3584]{1,0:T(8,128)(2,1)} collective-permute-done((bf16[64,3584]{1,0:T(8,128)(2,1)}, bf16[64,3584]{1,0:T(8,128)(2,1)}, u32[]{:S(2)}, u32[]{:S(2)}) %collective-permute-start.11) | collective-permute-done | bytes 458784 | tf_op jit(solution)/shard_map/ppermute | solution.py:385
  256.6 4.7 %collective-permute-done.9.refs_2_ = bf16[64,3584]{1,0:T(8,128)(2,1)S(1)} collective-permute-done((bf16[64,3584]{1,0:T(8,128)(2,1)}, bf16[64,3584]{1,0:T(8,128)(2,1)S(1)}, u32[]{:S(2)}, u32[]{:S(2)}) %collective-permute-start.9) | collective-permute-done | bytes 458784 | tf_op jit(solution)/shard_map/ppermute | solution.py:381
  261.4 2.3 shard_map.130.refs_0_
  263.8 3.2 collective-permute-start.18
  267.5 6.0 %collective-permute-done.17.refs_4_ = bf16[128,1792]{1,0:T(8,128)(2,1)S(1)} collective-permute-done((bf16[128,1792]{1,0:T(8,128)(2,1)S(1)}, bf16[128,1792]{1,0:T(8,128)(2,1)S(1)}, u32[]{:S(2)}, u32[]{:S(2)}) %collective-permute-start.17) | collective-permute-done | bytes 458784 | tf_op jit(solution)/shard_map/ppermute | solution.py:381
  275.5 3.3 %collective-permute-start.20 = (bf16[128,1792]{1,0:T(8,128)(2,1)S(1)}, bf16[128,1792]{1,0:T(8,128)(2,1)S(1)}, u32[]{:S(2)}, u32[]{:S(2)}) collective-permute-start(bf16[128,1792]{1,0:T(8,128)(2,1)S(1)} %collective-permute-done.19.refs_1_), channel_id=1, source_target_pairs={{0,6},{2,0},{4,2},{6,4},{1,7},{3,1},{5,3},{7,5},{8,14},{10,8},{12,... | collective-permute-start | bytes 1376264 | tf_op jit(solution)/shard_map/ppermute | solution.py:385
  278.8 9.2 %collective-permute-done.20.refs_3_ = bf16[128,1792]{1,0:T(8,128)(2,1)S(1)} collective-permute-done((bf16[128,1792]{1,0:T(8,128)(2,1)S(1)}, bf16[128,1792]{1,0:T(8,128)(2,1)S(1)}, u32[]{:S(2)}, u32[]{:S(2)}) %collective-permute-start.20) | collective-permute-done | bytes 458784 | tf_op jit(solution)/shard_map/ppermute | solution.py:385
  288.0 3.7 %collective-permute-start.24 = (bf16[128,1792]{1,0:T(8,128)(2,1)S(1)}, bf16[128,1792]{1,0:T(8,128)(2,1)S(1)}, u32[]{:S(2)}, u32[]{:S(2)}) collective-permute-start(bf16[128,1792]{1,0:T(8,128)(2,1)S(1)} %collective-permute-done.20.refs_3_), channel_id=1, source_target_pairs={{0,6},{2,0},{4,2},{6,4},{1,7},{3,1},{5,3},{7,5},{8,14},{10,8},{12,... | collective-permute-start | bytes 1376264 | tf_op jit(solution)/shard_map/ppermute | solution.py:385
  291.7 3.6 %shard_map.131 = (f32[6,64,1024]{2,1,0:T(8,128)S(1)}, bf16[6,64,1024]{2,1,0:T(8,128)(2,1)S(1)}) custom-call(bf16[128,1792]{1,0:T(8,128)(2,1)S(1)} %shard_map.130.refs_0_, bf16[128,1792]{1,0:T(8,128)(2,1)S(1)} %collective-permute-done.19.refs_1_, bf16[128,1792]{1,0:T(8,128)(2,1)S(1)} %collective-permute-done.18.refs_2_, ...), custom_call_target="tpu_custom_call" | custom-call | flops 2818572288 | bytes 8781824 | tf_op jit(solution)/shard_map/pallas_call | solution.py:343
  295.4 2.3 collective-permute-done.24.refs_1_
  301.7 20.3 %all_to_all.36 = bf16[8,64,1024]{2,1,0:T(8,128)(2,1)S(1)} all-to-all(bf16[8,64,1024]{2,1,0:T(8,128)(2,1)S(1)} %shard_map.133), channel_id=1, replica_groups=mesh['z'=4,'xh'=2,'core'=2,'y'=4,'xl'=2] {'z','xh'}, dimensions={0} | all-to-all | bytes 2097152 | tf_op jit(solution)/shard_map/all_to_all | solution.py:440
  (113 shorter events, 48.2 us)
Async XLA Ops:
  8.8 58.2 %all-to-all-start = ((bf16[64,224,128]{2,1,0:T(8,128)(2,1)}), bf16[64,224,128]{2,1,0:T(8,128)(2,1)}, u32[]{:S(2)}, u32[]{:S(2)}) async-start(bf16[64,224,128]{2,1,0:T(8,128)(2,1)} %shard_map.118), calls=%async_computation | async-start | bytes 7340032 | tf_op jit(solution)/shard_map/all_to_all | solution.py:440
  25.5 48.6 %copy-start.11 = (bf16[128,512]{1,0:T(8,128)(2,1)S(1)}, bf16[128,512]{1,0:T(8,128)(2,1)}, u32[]{:S(2)}) copy-start(bf16[128,512]{1,0:T(8,128)(2,1)} %refs_1_.1) | copy-start | bytes 393220
  67.1 24.8 %all-to-all-start.1 = ((bf16[64,64,128]{2,1,0:T(8,128)(2,1)}), bf16[64,64,128]{2,1,0:T(8,128)(2,1)S(1)}, u32[]{:S(2)}, u32[]{:S(2)}) async-start(bf16[64,64,128]{2,1,0:T(8,128)(2,1)} %pad_maximum_fusion), calls=%async_computation.1 | async-start | bytes 2097152 | tf_op jit(solution)/shard_map/all_to_all | solution.py:440
  74.0 1.4 collective-permute-start
  95.9 1.6 collective-permute-start.1
  98.8 20.5 %all-to-all-start.2 = ((bf16[8,128,512]{2,1,0:T(8,128)(2,1)}), bf16[8,128,512]{2,1,0:T(8,128)(2,1)S(1)}, u32[]{:S(2)}, u32[]{:S(2)}) async-start(bf16[8,128,512]{2,1,0:T(8,128)(2,1)} %shard_map.121), calls=%async_computation.2 | async-start | bytes 2097152 | tf_op jit(solution)/shard_map/all_to_all | solution.py:440
  119.9 2.7 collective-permute-start.2
  124.4 23.1 %all-to-all-start.3 = ((bf16[8,64,1024]{2,1,0:T(8,128)(2,1)}), bf16[8,64,1024]{2,1,0:T(8,128)(2,1)S(1)}, u32[]{:S(2)}, u32[]{:S(2)}) async-start(bf16[8,64,1024]{2,1,0:T(8,128)(2,1)} %bitcast.12), calls=%async_computation.3 | async-start | bytes 2097152 | tf_op jit(solution)/shard_map/all_to_all | solution.py:440
  167.7 2.7 collective-permute-start.3
  186.2 13.6 %collective-permute-start.5 = (bf16[64,3584]{1,0:T(8,128)(2,1)}, bf16[64,3584]{1,0:T(8,128)(2,1)S(1)}, u32[]{:S(2)}, u32[]{:S(2)}) collective-permute-start(bf16[64,3584]{1,0:T(8,128)(2,1)} %get-tuple-element.55), channel_id=1, source_target_pairs={{0,6},{2,0},{4,2},{6,4},{1,7},{3,1},{5,3},{7,5},{8,14},{10,8},{12,... | collective-permute-start | bytes 1376264 | tf_op jit(solution)/shard_map/ppermute | solution.py:385
  187.3 14.8 %collective-permute-start.4 = (bf16[64,3584]{1,0:T(8,128)(2,1)}, bf16[64,3584]{1,0:T(8,128)(2,1)S(1)}, u32[]{:S(2)}, u32[]{:S(2)}) collective-permute-start(bf16[64,3584]{1,0:T(8,128)(2,1)} %get-tuple-element.53), channel_id=1, source_target_pairs={{0,2},{2,4},{4,6},{6,0},{1,3},{3,5},{5,7},{7,1},{8,10},{10,12},{12... | collective-permute-start | bytes 1376264 | tf_op jit(solution)/shard_map/ppermute | solution.py:381
  188.3 21.4 %collective-permute-start.12 = (bf16[64,3584]{1,0:T(8,128)(2,1)}, bf16[64,3584]{1,0:T(8,128)(2,1)S(1)}, u32[]{:S(2)}, u32[]{:S(2)}) collective-permute-start(bf16[64,3584]{1,0:T(8,128)(2,1)} %get-tuple-element.76), channel_id=1, source_target_pairs={{0,6},{2,0},{4,2},{6,4},{1,7},{3,1},{5,3},{7,5},{8,14},{10,8},{12,... | collective-permute-start | bytes 1376264 | tf_op jit(solution)/shard_map/ppermute | solution.py:385
  190.5 21.4 %collective-permute-start.14 = (bf16[64,3584]{1,0:T(8,128)(2,1)}, bf16[64,3584]{1,0:T(8,128)(2,1)S(1)}, u32[]{:S(2)}, u32[]{:S(2)}) collective-permute-start(bf16[64,3584]{1,0:T(8,128)(2,1)} %get-tuple-element.79), channel_id=1, source_target_pairs={{0,2},{2,4},{4,6},{6,0},{1,3},{3,5},{5,7},{7,1},{8,10},{10,12},{12... | collective-permute-start | bytes 1376264 | tf_op jit(solution)/shard_map/ppermute | solution.py:381
  202.2 19.5 %collective-permute-start.13 = (bf16[64,3584]{1,0:T(8,128)(2,1)S(1)}, bf16[64,3584]{1,0:T(8,128)(2,1)S(1)}, u32[]{:S(2)}, u32[]{:S(2)}) collective-permute-start(bf16[64,3584]{1,0:T(8,128)(2,1)S(1)} %shard_map.125), channel_id=1, source_target_pairs={{0,2},{2,4},{4,6},{6,0},{1,3},{3,5},{5,7},{7,1},{8,10},{10,12},{12... | collective-permute-start | bytes 1376264 | tf_op jit(solution)/shard_map/ppermute | solution.py:381
  202.3 19.5 %collective-permute-start.15 = (bf16[64,3584]{1,0:T(8,128)(2,1)S(1)}, bf16[64,3584]{1,0:T(8,128)(2,1)S(1)}, u32[]{:S(2)}, u32[]{:S(2)}) collective-permute-start(bf16[64,3584]{1,0:T(8,128)(2,1)S(1)} %shard_map.126), channel_id=1, source_target_pairs={{0,6},{2,0},{4,2},{6,4},{1,7},{3,1},{5,3},{7,5},{8,14},{10,8},{12,... | collective-permute-start | bytes 1376264 | tf_op jit(solution)/shard_map/ppermute | solution.py:385
  205.5 38.2 %collective-permute-start.7 = (bf16[64,3584]{1,0:T(8,128)(2,1)}, bf16[64,3584]{1,0:T(8,128)(2,1)}, u32[]{:S(2)}, u32[]{:S(2)}) collective-permute-start(bf16[64,3584]{1,0:T(8,128)(2,1)} %get-tuple-element.67), channel_id=1, source_target_pairs={{0,2},{2,4},{4,6},{6,0},{1,3},{3,5},{5,7},{7,1},{8,10},{10,12},{12... | collective-permute-start | bytes 1376264 | tf_op jit(solution)/shard_map/ppermute | solution.py:381
  209.7 34.0 %collective-permute-start.8 = (bf16[64,3584]{1,0:T(8,128)(2,1)}, bf16[64,3584]{1,0:T(8,128)(2,1)}, u32[]{:S(2)}, u32[]{:S(2)}) collective-permute-start(bf16[64,3584]{1,0:T(8,128)(2,1)} %get-tuple-element.68), channel_id=1, source_target_pairs={{0,6},{2,0},{4,2},{6,4},{1,7},{3,1},{5,3},{7,5},{8,14},{10,8},{12,... | collective-permute-start | bytes 1376264 | tf_op jit(solution)/shard_map/ppermute | solution.py:385
  222.2 39.2 %collective-permute-start.16 = (bf16[2,64,3584]{2,1,0:T(8,128)(2,1)S(1)}, bf16[2,64,3584]{2,1,0:T(8,128)(2,1)S(1)}, u32[]{:S(2)}, u32[]{:S(2)}) collective-permute-start(bf16[2,64,3584]{2,1,0:T(8,128)(2,1)S(1)} %shard_map.129), channel_id=1, source_target_pairs={{0,1},{1,0},{2,3},{3,2},{4,5},{5,4},{6,7},{7,6},{8,9},{9,8},{10,11... | collective-permute-start | bytes 2752520 | tf_op jit(solution)/shard_map/ppermute | solution.py:444
  223.4 19.1 %all-to-all-start.5 = ((f32[8,1,128]{2,1,0:T(1,128)}), f32[8,1,128]{2,1,0:T(1,128)S(1)}, u32[]{:S(2)}, u32[]{:S(2)}) async-start(f32[8,1,128]{2,1,0:T(1,128)} %reshape.135), calls=%async_computation.5 | async-start | bytes 8192 | tf_op jit(solution)/shard_map/all_to_all | solution.py:440
  226.7 24.7 %collective-permute-start.10 = (bf16[64,3584]{1,0:T(8,128)(2,1)}, bf16[64,3584]{1,0:T(8,128)(2,1)}, u32[]{:S(2)}, u32[]{:S(2)}) collective-permute-start(bf16[64,3584]{1,0:T(8,128)(2,1)} %get-tuple-element.72), channel_id=1, source_target_pairs={{0,2},{2,4},{4,6},{6,0},{1,3},{3,5},{5,7},{7,1},{8,10},{10,12},{12... | collective-permute-start | bytes 1376264 | tf_op jit(solution)/shard_map/ppermute | solution.py:381
  228.6 22.7 %collective-permute-start.6 = (bf16[64,3584]{1,0:T(8,128)(2,1)}, bf16[64,3584]{1,0:T(8,128)(2,1)}, u32[]{:S(2)}, u32[]{:S(2)}) collective-permute-start(bf16[64,3584]{1,0:T(8,128)(2,1)} %get-tuple-element.65), channel_id=1, source_target_pairs={{0,6},{2,0},{4,2},{6,4},{1,7},{3,1},{5,3},{7,5},{8,14},{10,8},{12,... | collective-permute-start | bytes 1376264 | tf_op jit(solution)/shard_map/ppermute | solution.py:385
  246.6 10.0 %collective-permute-start.11 = (bf16[64,3584]{1,0:T(8,128)(2,1)}, bf16[64,3584]{1,0:T(8,128)(2,1)}, u32[]{:S(2)}, u32[]{:S(2)}) collective-permute-start(bf16[64,3584]{1,0:T(8,128)(2,1)} %shard_map.128), channel_id=1, source_target_pairs={{0,6},{2,0},{4,2},{6,4},{1,7},{3,1},{5,3},{7,5},{8,14},{10,8},{12,... | collective-permute-start | bytes 1376264 | tf_op jit(solution)/shard_map/ppermute | solution.py:385
  251.2 10.2 %collective-permute-start.9 = (bf16[64,3584]{1,0:T(8,128)(2,1)}, bf16[64,3584]{1,0:T(8,128)(2,1)S(1)}, u32[]{:S(2)}, u32[]{:S(2)}) collective-permute-start(bf16[64,3584]{1,0:T(8,128)(2,1)} %shard_map.127), channel_id=1, source_target_pairs={{0,2},{2,4},{4,6},{6,0},{1,3},{3,5},{5,7},{7,1},{8,10},{10,12},{12... | collective-permute-start | bytes 1376264 | tf_op jit(solution)/shard_map/ppermute | solution.py:381
  263.7 9.8 %collective-permute-start.17 = (bf16[128,1792]{1,0:T(8,128)(2,1)S(1)}, bf16[128,1792]{1,0:T(8,128)(2,1)S(1)}, u32[]{:S(2)}, u32[]{:S(2)}) collective-permute-start(bf16[128,1792]{1,0:T(8,128)(2,1)S(1)} %shard_map.130.refs_0_), channel_id=1, source_target_pairs={{0,2},{2,4},{4,6},{6,0},{1,3},{3,5},{5,7},{7,1},{8,10},{10,12},{12... | collective-permute-start | bytes 1376264 | tf_op jit(solution)/shard_map/ppermute | solution.py:381
  263.8 11.3 %collective-permute-start.18 = (bf16[128,1792]{1,0:T(8,128)(2,1)S(1)}, bf16[128,1792]{1,0:T(8,128)(2,1)S(1)}, u32[]{:S(2)}, u32[]{:S(2)}) collective-permute-start(bf16[128,1792]{1,0:T(8,128)(2,1)S(1)} %shard_map.130.refs_0_), channel_id=1, source_target_pairs={{0,6},{2,0},{4,2},{6,4},{1,7},{3,1},{5,3},{7,5},{8,14},{10,8},{12,... | collective-permute-start | bytes 1376264 | tf_op jit(solution)/shard_map/ppermute | solution.py:385
  267.0 8.5 %collective-permute-start.19 = (bf16[128,1792]{1,0:T(8,128)(2,1)S(1)}, bf16[128,1792]{1,0:T(8,128)(2,1)S(1)}, u32[]{:S(2)}, u32[]{:S(2)}) collective-permute-start(bf16[128,1792]{1,0:T(8,128)(2,1)S(1)} %shard_map.130.refs_0_), channel_id=1, source_target_pairs={{0,1},{1,0},{2,3},{3,2},{4,5},{5,4},{6,7},{7,6},{8,9},{9,8},{10,11... | collective-permute-start | bytes 1376264 | tf_op jit(solution)/shard_map/ppermute | solution.py:444
  275.5 12.5 %collective-permute-start.20 = (bf16[128,1792]{1,0:T(8,128)(2,1)S(1)}, bf16[128,1792]{1,0:T(8,128)(2,1)S(1)}, u32[]{:S(2)}, u32[]{:S(2)}) collective-permute-start(bf16[128,1792]{1,0:T(8,128)(2,1)S(1)} %collective-permute-done.19.refs_1_), channel_id=1, source_target_pairs={{0,6},{2,0},{4,2},{6,4},{1,7},{3,1},{5,3},{7,5},{8,14},{10,8},{12,... | collective-permute-start | bytes 1376264 | tf_op jit(solution)/shard_map/ppermute | solution.py:385
  278.8 12.9 %collective-permute-start.21 = (bf16[128,1792]{1,0:T(8,128)(2,1)S(1)}, bf16[128,1792]{1,0:T(8,128)(2,1)S(1)}, u32[]{:S(2)}, u32[]{:S(2)}) collective-permute-start(bf16[128,1792]{1,0:T(8,128)(2,1)S(1)} %collective-permute-done.19.refs_1_), channel_id=1, source_target_pairs={{0,2},{2,4},{4,6},{6,0},{1,3},{3,5},{5,7},{7,1},{8,10},{10,12},{12... | collective-permute-start | bytes 1376264 | tf_op jit(solution)/shard_map/ppermute | solution.py:381
  278.8 16.6 %collective-permute-start.23 = (bf16[128,1792]{1,0:T(8,128)(2,1)S(1)}, bf16[128,1792]{1,0:T(8,128)(2,1)S(1)}, u32[]{:S(2)}, u32[]{:S(2)}) collective-permute-start(bf16[128,1792]{1,0:T(8,128)(2,1)S(1)} %collective-permute-done.17.refs_4_), channel_id=1, source_target_pairs={{0,2},{2,4},{4,6},{6,0},{1,3},{3,5},{5,7},{7,1},{8,10},{10,12},{12... | collective-permute-start | bytes 1376264 | tf_op jit(solution)/shard_map/ppermute | solution.py:381
  288.0 9.7 %collective-permute-start.24 = (bf16[128,1792]{1,0:T(8,128)(2,1)S(1)}, bf16[128,1792]{1,0:T(8,128)(2,1)S(1)}, u32[]{:S(2)}, u32[]{:S(2)}) collective-permute-start(bf16[128,1792]{1,0:T(8,128)(2,1)S(1)} %collective-permute-done.20.refs_3_), channel_id=1, source_target_pairs={{0,6},{2,0},{4,2},{6,4},{1,7},{3,1},{5,3},{7,5},{8,14},{10,8},{12,... | collective-permute-start | bytes 1376264 | tf_op jit(solution)/shard_map/ppermute | solution.py:385
  295.3 5.6 %collective-permute-start.22 = (bf16[6,64,1024]{2,1,0:T(8,128)(2,1)S(1)}, bf16[6,64,1024]{2,1,0:T(8,128)(2,1)S(1)}, u32[]{:S(2)}, u32[]{:S(2)}) collective-permute-start(bf16[6,64,1024]{2,1,0:T(8,128)(2,1)S(1)} %get-tuple-element.86), channel_id=1, source_target_pairs={{0,8},{8,0},{1,9},{9,1},{2,10},{10,2},{3,11},{11,3},{4,12},{12,4},... | collective-permute-start | bytes 2359304 | tf_op jit(solution)/shard_map/ppermute | solution.py:444
  299.3 1.6 collective-permute-start.25
  (17 other events, 333.3 us)

commit v13 on v9

--- a/solution.py
+++ b/solution.py
@@ -529,15 +529,14 @@
     columns = partial_columns(
         where, own_rows.reshape(by_pair), other_rows.reshape(by_pair), gate_weight, up_weight
     )
+    columns, squares = lax.optimization_barrier((columns, exchange(squares, COL)))
     theirs, mine = columns[:8], columns[8:]
     arrived = ring_start(theirs)
     sums = ring_middle(theirs, *arrived[:2])
-    sums, mine, squares = lax.optimization_barrier((sums, mine, squares))
-    squares = exchange(squares, COL)
+    sums, mine = lax.optimization_barrier((sums, mine))
     halves = ring_end(theirs, arrived, sums)
     own_first, own_second, right, left, go_right, go_left = mine
     from_left, from_right = to_right(go_right), to_left(go_left)
-    halves, squares = lax.optimization_barrier((halves, squares))
     got = swap(add_halves(*halves), "xl")
     factor = lax.rsqrt(jnp.sum(squares, axis=0).reshape(-1) / D + 1e-05)
     third_left, third_right = to_right(add_pieces(right, from_left)), to_left(add_pieces(left, from_right))

time: 330 us -> 325 us (0.985)
  blocking collectives: 70.8 us -> 40.2 us
  waiting for transfers between devices: 137 us -> 157 us
  starting transfers between devices: 46.4 us -> 57.5 us
  Pallas kernels: 56.5 us -> 52.5 us
    ppermute x8, waiting for transfers between devices: 14.7 us -> 49.3 us  [to_right(): return lax.ppermute(x, 'y', [(i, (i + 1) % 4) for i in range(4)])]
    all_to_all x3 -> x2, blocking collectives: 70.8 us -> 40.2 us  [exchange(): return lax.all_to_all(x, axes, split_axis=0, concat_axis=0, tiled=True)]
    ppermute x8, waiting for transfers between devices: 25.5 us -> 14 us  [swap(): return lax.ppermute(x, axis, [(0, 1), (1, 0)])]
    all_to_all x4 -> x5, starting transfers between devices: 28.5 us -> 33.9 us  [exchange(): return lax.all_to_all(x, axes, split_axis=0, concat_axis=0, tiled=True)]
    ppermute x8, waiting for transfers between devices: 19.3 us -> 15.9 us  [to_left(): return lax.ppermute(x, 'y', [(i, (i + 3) % 4) for i in range(4)])]
    all_to_all x4 -> x5, waiting for transfers between devices: 77.8 us -> 77.6 us  [exchange(): return lax.all_to_all(x, axes, split_axis=0, concat_axis=0, tiled=True)]
  transfers between devices with their start and end apart: 28 -> 29, of which waited for: 18 -> 22; matrix products, arithmetic and copies ran while one was open for 3% -> 2% of each run, Pallas kernels for 7% -> 11%
where the time goes in v13:
time: 325 us; the launch traced here: 324 us
  waiting for transfers between devices  157 us (48%)
  starting transfers between devices  57.5 us (18%)
  Pallas kernels  52.5 us (16%)
  blocking collectives  40.2 us (12%)
  local copies, waits for them, and re-layouts  10.7 us (3%)
  other arithmetic  5.52 us (2%)
    all_to_all x5, waiting for transfers between devices, exchange(): return lax.all_to_all(x, axes, split_axis=0, concat_axis=0, tiled=True)  77.6 us
    ppermute x8, waiting for transfers between devices, to_right(): return lax.ppermute(x, 'y', [(i, (i + 1) % 4) for i in range(4)])  49.3 us
    all_to_all x2, blocking collectives, exchange(): return lax.all_to_all(x, axes, split_axis=0, concat_axis=0, tiled=True)  40.2 us
    all_to_all x5, starting transfers between devices, exchange(): return lax.all_to_all(x, axes, split_axis=0, concat_axis=0, tiled=True)  33.9 us
    ppermute x8, waiting for transfers between devices, to_left(): return lax.ppermute(x, 'y', [(i, (i + 3) % 4) for i in range(4)])  15.9 us
    pallas_call x2, Pallas kernels, attend(): pl.pallas_call(functools.partial(attend_kernel, scale, per_step, local_bl...  15.6 us
    ppermute x8, starting transfers between devices, to_left(): return lax.ppermute(x, 'y', [(i, (i + 3) % 4) for i in range(4)])  15.5 us
    pallas_call x1, Pallas kernels, partial_columns(): pl.pallas_call(columns_kernel, out_shape=(jax.ShapeDtypeStruct((tokens, 2...  14.8 us
  transfers between devices with their start and end apart: 29, of which 22 were waited for; matrix products, arithmetic and copies ran while one was open for 2% of the time, Pallas kernels for 11%

profile of v13, /device:TPU:0, one launch (start us, length us, event | category | flops | bytes accessed | tf_op | source)
XLA Modules:
  0.0 323.6 jit_solution(8330913781699857379)
XLA Ops:
  1.6 7.2 %shard_map.118 = bf16[64,224,128]{2,1,0:T(8,128)(2,1)} custom-call(s32[8,8]{1,0:T(8,128)} %bitcast.31, s32[1]{0:T(128)} %bitcast.4.group_ref, bf16[64,128,128]{2,1,0:T(8,128)(2,1)} %bitcast.28, bf16[64,128,128]{2,1,0:T(8,128)(2,1)} %bitcast.26, bf16[8,128,128]{2,1,0:T(8,128)(2,1)} %near_keys_ref.1, bf16[8,128,128]{2,1,0:T(8,128)(2,1)} %near_values_ref.1), custom_call_target="tpu_custom_call" | custom-call | bytes 7340032 | tf_op jit(solution)/shard_map/pallas_call | solution.py:432
  8.8 11.9 %all-to-all-start = ((bf16[64,224,128]{2,1,0:T(8,128)(2,1)}), bf16[64,224,128]{2,1,0:T(8,128)(2,1)}, u32[]{:S(2)}, u32[]{:S(2)}) async-start(bf16[64,224,128]{2,1,0:T(8,128)(2,1)} %shard_map.118), calls=%async_computation | async-start | bytes 7340032 | tf_op jit(solution)/shard_map/all_to_all | solution.py:447
  21.0 2.3 gather_fusion.1
  23.2 2.3 gather_fusion
  26.7 40.3 %all-to-all-done.refs_4_ = bf16[64,224,128]{2,1,0:T(8,128)(2,1)} async-done(((bf16[64,224,128]{2,1,0:T(8,128)(2,1)}), bf16[64,224,128]{2,1,0:T(8,128)(2,1)}, u32[]{:S(2)}, u32[]{:S(2)}) %all-to-all-start) | async-done | bytes 3670048 | tf_op jit(solution)/shard_map/all_to_all | solution.py:447
  67.0 7.0 %all-to-all-start.1 = ((bf16[64,64,128]{2,1,0:T(8,128)(2,1)}), bf16[64,64,128]{2,1,0:T(8,128)(2,1)S(1)}, u32[]{:S(2)}, u32[]{:S(2)}) async-start(bf16[64,64,128]{2,1,0:T(8,128)(2,1)} %pad_maximum_fusion), calls=%async_computation.1 | async-start | bytes 2097152 | tf_op jit(solution)/shard_map/all_to_all | solution.py:447
  75.4 12.7 %shard_map.119 = (f32[136,512]{1,0:T(8,128)S(1)}, f32[136,512]{1,0:T(8,128)S(1)}, s32[65]{0:T(128)S(1)}) custom-call(s32[64]{0:T(128)S(1)} %dynamic-slice_bitcast_fusion.refs_0_, s32[2]{0:T(128)S(1)} %pad_add_fusion.refs_1_, bf16[128,512]{1,0:T(8,128)(2,1)S(1)} %copy-done.11, bf16[128,512]{1,0:T(8,128)(2,1)S(1)} %collective-permute-done.refs_3_.refs_2_, ...), custom_call_target="tpu_custom_call" | custom-call | flops 1174405120 | bytes 3670016 | tf_op jit(solution)/shard_map/pallas_call | solution.py:134
  88.2 3.7 %all-to-all-done.1.refs_3_ = bf16[64,64,128]{2,1,0:T(8,128)(2,1)S(1)} async-done(((bf16[64,64,128]{2,1,0:T(8,128)(2,1)}), bf16[64,64,128]{2,1,0:T(8,128)(2,1)S(1)}, u32[]{:S(2)}, u32[]{:S(2)}) %all-to-all-start.1) | async-done | bytes 1048608 | tf_op jit(solution)/shard_map/all_to_all | solution.py:447
  91.9 2.9 shard_map.120
  97.6 4.4 %all-to-all-start.2 = ((bf16[8,128,512]{2,1,0:T(8,128)(2,1)}), bf16[8,128,512]{2,1,0:T(8,128)(2,1)S(1)}, u32[]{:S(2)}, u32[]{:S(2)}) async-start(bf16[8,128,512]{2,1,0:T(8,128)(2,1)} %shard_map.121), calls=%async_computation.2 | async-start | bytes 2097152 | tf_op jit(solution)/shard_map/all_to_all | solution.py:447
  102.1 16.0 %all-to-all-done.2 = bf16[8,128,512]{2,1,0:T(8,128)(2,1)S(1)} async-done(((bf16[8,128,512]{2,1,0:T(8,128)(2,1)}), bf16[8,128,512]{2,1,0:T(8,128)(2,1)S(1)}, u32[]{:S(2)}, u32[]{:S(2)}) %all-to-all-start.2) | async-done | bytes 1048608 | tf_op jit(solution)/shard_map/all_to_all | solution.py:447
  118.9 2.6 collective-permute-done.2.refs_1_
  123.2 7.2 %all-to-all-start.3 = ((bf16[8,64,1024]{2,1,0:T(8,128)(2,1)}), bf16[8,64,1024]{2,1,0:T(8,128)(2,1)S(1)}, u32[]{:S(2)}, u32[]{:S(2)}) async-start(bf16[8,64,1024]{2,1,0:T(8,128)(2,1)} %bitcast.12), calls=%async_computation.3 | async-start | bytes 2097152 | tf_op jit(solution)/shard_map/all_to_all | solution.py:447
  130.4 17.5 %all-to-all-done.3 = bf16[8,64,1024]{2,1,0:T(8,128)(2,1)S(1)} async-done(((bf16[8,64,1024]{2,1,0:T(8,128)(2,1)}), bf16[8,64,1024]{2,1,0:T(8,128)(2,1)S(1)}, u32[]{:S(2)}, u32[]{:S(2)}) %all-to-all-start.3) | async-done | bytes 1048608 | tf_op jit(solution)/shard_map/all_to_all | solution.py:447
  148.3 19.9 %all_to_all.35 = bf16[8,64,1024]{2,1,0:T(8,128)(2,1)S(1)} all-to-all(bf16[8,64,1024]{2,1,0:T(8,128)(2,1)S(1)} %broadcast_in_dim.4), channel_id=1, replica_groups=mesh['z'=4,'xh'=2,'core'=2,'y'=4,'xl'=2] {'z','xh'}, dimensions={0} | all-to-all | bytes 2097152 | tf_op jit(solution)/shard_map/all_to_all | solution.py:447
  172.2 3.5 %all-to-all-start.5 = ((f32[8,1,128]{2,1,0:T(1,128)}), f32[8,1,128]{2,1,0:T(1,128)S(1)}, u32[]{:S(2)}, u32[]{:S(2)}) async-start(f32[8,1,128]{2,1,0:T(1,128)} %reshape.135), calls=%async_computation.5 | async-start | bytes 8192 | tf_op jit(solution)/shard_map/all_to_all | solution.py:447
  175.7 14.8 %shard_map.124 = (bf16[64,3584]{1,0:T(8,128)(2,1)}, bf16[64,3584]{1,0:T(8,128)(2,1)}, bf16[64,3584]{1,0:T(8,128)(2,1)}, bf16[64,3584]{1,0:T(8,128)(2,1)}, bf16[6...) custom-call(s32[2]{0:T(128)} %pad_add_fusion.1.place_ref, ...), custom_call_target="tpu_custom_call" | custom-call | flops 7516192768 | bytes 16777216 | tf_op jit(solution)/shard_map/pallas_call | solution.py:263
  197.1 9.5 %collective-permute-done.4.b_ref = bf16[64,3584]{1,0:T(8,128)(2,1)S(1)} collective-permute-done((bf16[64,3584]{1,0:T(8,128)(2,1)}, bf16[64,3584]{1,0:T(8,128)(2,1)S(1)}, u32[]{:S(2)}, u32[]{:S(2)}) %collective-permute-start.4) | collective-permute-done | bytes 458784 | tf_op jit(solution)/shard_map/ppermute | solution.py:388
  209.9 2.3 collective-permute-start.13
  212.2 4.8 %collective-permute-done.10.refs_1_ = bf16[64,3584]{1,0:T(8,128)(2,1)S(1)} collective-permute-done((bf16[64,3584]{1,0:T(8,128)(2,1)}, bf16[64,3584]{1,0:T(8,128)(2,1)S(1)}, u32[]{:S(2)}, u32[]{:S(2)}) %collective-permute-start.10) | collective-permute-done | bytes 458784 | tf_op jit(solution)/shard_map/ppermute | solution.py:392
  217.0 2.7 collective-permute-start.8
  219.7 6.5 %collective-permute-done.11.refs_2_ = bf16[64,3584]{1,0:T(8,128)(2,1)S(1)} collective-permute-done((bf16[64,3584]{1,0:T(8,128)(2,1)S(1)}, bf16[64,3584]{1,0:T(8,128)(2,1)S(1)}, u32[]{:S(2)}, u32[]{:S(2)}) %collective-permute-start.11) | collective-permute-done | bytes 458784 | tf_op jit(solution)/shard_map/ppermute | solution.py:388
  229.6 15.5 %collective-permute-done.6.b_ref.refs_5_ = bf16[2,64,3584]{2,1,0:T(8,128)(2,1)S(1)} collective-permute-done((bf16[2,64,3584]{2,1,0:T(8,128)(2,1)}, bf16[2,64,3584]{2,1,0:T(8,128)(2,1)S(1)}, u32[]{:S(2)}, u32[]{:S(2)}) %collective-permute-start.6) | collective-permute-done | bytes 917536 | tf_op jit(solution)/shard_map/ppermute | solution.py:388
  247.2 3.0 collective-permute-start.9
  250.4 8.9 %collective-permute-done.7.refs_1_ = bf16[64,3584]{1,0:T(8,128)(2,1)} collective-permute-done((bf16[64,3584]{1,0:T(8,128)(2,1)}, bf16[64,3584]{1,0:T(8,128)(2,1)}, u32[]{:S(2)}, u32[]{:S(2)}) %collective-permute-start.7) | collective-permute-done | bytes 458784 | tf_op jit(solution)/shard_map/ppermute | solution.py:388
  263.8 3.7 %collective-permute-start.16 = (bf16[128,1792]{1,0:T(8,128)(2,1)S(1)}, bf16[128,1792]{1,0:T(8,128)(2,1)S(1)}, u32[]{:S(2)}, u32[]{:S(2)}) collective-permute-start(bf16[128,1792]{1,0:T(8,128)(2,1)S(1)} %shard_map.130.refs_0_), channel_id=1, source_target_pairs={{0,6},{2,0},{4,2},{6,4},{1,7},{3,1},{5,3},{7,5},{8,14},{10,8},{12,... | collective-permute-start | bytes 1376264 | tf_op jit(solution)/shard_map/ppermute | solution.py:392
  267.5 5.8 %collective-permute-done.17.refs_1_ = bf16[128,1792]{1,0:T(8,128)(2,1)S(1)} collective-permute-done((bf16[128,1792]{1,0:T(8,128)(2,1)S(1)}, bf16[128,1792]{1,0:T(8,128)(2,1)S(1)}, u32[]{:S(2)}, u32[]{:S(2)}) %collective-permute-start.17) | collective-permute-done | bytes 458784 | tf_op jit(solution)/shard_map/ppermute | solution.py:451
  275.0 3.4 %collective-permute-done.15.refs_4_ = bf16[128,1792]{1,0:T(8,128)(2,1)S(1)} collective-permute-done((bf16[128,1792]{1,0:T(8,128)(2,1)S(1)}, bf16[128,1792]{1,0:T(8,128)(2,1)S(1)}, u32[]{:S(2)}, u32[]{:S(2)}) %collective-permute-start.15) | collective-permute-done | bytes 458784 | tf_op jit(solution)/shard_map/ppermute | solution.py:388
  280.4 8.6 %collective-permute-done.18.refs_3_ = bf16[128,1792]{1,0:T(8,128)(2,1)S(1)} collective-permute-done((bf16[128,1792]{1,0:T(8,128)(2,1)S(1)}, bf16[128,1792]{1,0:T(8,128)(2,1)S(1)}, u32[]{:S(2)}, u32[]{:S(2)}) %collective-permute-start.18) | collective-permute-done | bytes 458784 | tf_op jit(solution)/shard_map/ppermute | solution.py:392
  289.3 4.0 %collective-permute-done.19.refs_5_ = bf16[128,1792]{1,0:T(8,128)(2,1)S(1)} collective-permute-done((bf16[128,1792]{1,0:T(8,128)(2,1)S(1)}, bf16[128,1792]{1,0:T(8,128)(2,1)S(1)}, u32[]{:S(2)}, u32[]{:S(2)}) %collective-permute-start.19) | collective-permute-done | bytes 458784 | tf_op jit(solution)/shard_map/ppermute | solution.py:388
  293.3 3.6 %shard_map.131 = (f32[6,64,1024]{2,1,0:T(8,128)S(1)}, bf16[6,64,1024]{2,1,0:T(8,128)(2,1)S(1)}) custom-call(bf16[128,1792]{1,0:T(8,128)(2,1)S(1)} %shard_map.130.refs_0_, bf16[128,1792]{1,0:T(8,128)(2,1)S(1)} %collective-permute-done.17.refs_1_, bf16[128,1792]{1,0:T(8,128)(2,1)S(1)} %collective-permute-done.16.refs_2_, ...), custom_call_target="tpu_custom_call" | custom-call | flops 2818572288 | bytes 8781824 | tf_op jit(solution)/shard_map/pallas_call | solution.py:350
  302.4 20.3 %all_to_all.36 = bf16[8,64,1024]{2,1,0:T(8,128)(2,1)S(1)} all-to-all(bf16[8,64,1024]{2,1,0:T(8,128)(2,1)S(1)} %shard_map.133), channel_id=1, replica_groups=mesh['z'=4,'xh'=2,'core'=2,'y'=4,'xl'=2] {'z','xh'}, dimensions={0} | all-to-all | bytes 2097152 | tf_op jit(solution)/shard_map/all_to_all | solution.py:447
  (109 shorter events, 44.3 us)
Async XLA Ops:
  8.8 58.2 %all-to-all-start = ((bf16[64,224,128]{2,1,0:T(8,128)(2,1)}), bf16[64,224,128]{2,1,0:T(8,128)(2,1)}, u32[]{:S(2)}, u32[]{:S(2)}) async-start(bf16[64,224,128]{2,1,0:T(8,128)(2,1)} %shard_map.118), calls=%async_computation | async-start | bytes 7340032 | tf_op jit(solution)/shard_map/all_to_all | solution.py:447
  25.5 48.5 %copy-start.11 = (bf16[128,512]{1,0:T(8,128)(2,1)S(1)}, bf16[128,512]{1,0:T(8,128)(2,1)}, u32[]{:S(2)}) copy-start(bf16[128,512]{1,0:T(8,128)(2,1)} %refs_1_.1) | copy-start | bytes 393220
  67.0 24.9 %all-to-all-start.1 = ((bf16[64,64,128]{2,1,0:T(8,128)(2,1)}), bf16[64,64,128]{2,1,0:T(8,128)(2,1)S(1)}, u32[]{:S(2)}, u32[]{:S(2)}) async-start(bf16[64,64,128]{2,1,0:T(8,128)(2,1)} %pad_maximum_fusion), calls=%async_computation.1 | async-start | bytes 2097152 | tf_op jit(solution)/shard_map/all_to_all | solution.py:447
  74.0 1.4 collective-permute-start
  94.8 1.6 collective-permute-start.1
  97.6 20.5 %all-to-all-start.2 = ((bf16[8,128,512]{2,1,0:T(8,128)(2,1)}), bf16[8,128,512]{2,1,0:T(8,128)(2,1)S(1)}, u32[]{:S(2)}, u32[]{:S(2)}) async-start(bf16[8,128,512]{2,1,0:T(8,128)(2,1)} %shard_map.121), calls=%async_computation.2 | async-start | bytes 2097152 | tf_op jit(solution)/shard_map/all_to_all | solution.py:447
  118.8 2.7 collective-permute-start.2
  123.2 24.7 %all-to-all-start.3 = ((bf16[8,64,1024]{2,1,0:T(8,128)(2,1)}), bf16[8,64,1024]{2,1,0:T(8,128)(2,1)S(1)}, u32[]{:S(2)}, u32[]{:S(2)}) async-start(bf16[8,64,1024]{2,1,0:T(8,128)(2,1)} %bitcast.12), calls=%async_computation.3 | async-start | bytes 2097152 | tf_op jit(solution)/shard_map/all_to_all | solution.py:447
  168.2 2.7 collective-permute-start.3
  172.2 18.4 %all-to-all-start.5 = ((f32[8,1,128]{2,1,0:T(1,128)}), f32[8,1,128]{2,1,0:T(1,128)S(1)}, u32[]{:S(2)}, u32[]{:S(2)}) async-start(f32[8,1,128]{2,1,0:T(1,128)} %reshape.135), calls=%async_computation.5 | async-start | bytes 8192 | tf_op jit(solution)/shard_map/all_to_all | solution.py:447
  191.8 14.8 %collective-permute-start.4 = (bf16[64,3584]{1,0:T(8,128)(2,1)}, bf16[64,3584]{1,0:T(8,128)(2,1)S(1)}, u32[]{:S(2)}, u32[]{:S(2)}) collective-permute-start(bf16[64,3584]{1,0:T(8,128)(2,1)} %get-tuple-element.74), channel_id=1, source_target_pairs={{0,2},{2,4},{4,6},{6,0},{1,3},{3,5},{5,7},{7,1},{8,10},{10,12},{12... | collective-permute-start | bytes 1376264 | tf_op jit(solution)/shard_map/ppermute | solution.py:388
  193.6 14.2 %collective-permute-start.5 = (bf16[64,3584]{1,0:T(8,128)(2,1)}, bf16[64,3584]{1,0:T(8,128)(2,1)S(1)}, u32[]{:S(2)}, u32[]{:S(2)}) collective-permute-start(bf16[64,3584]{1,0:T(8,128)(2,1)} %get-tuple-element.76), channel_id=1, source_target_pairs={{0,6},{2,0},{4,2},{6,4},{1,7},{3,1},{5,3},{7,5},{8,14},{10,8},{12,... | collective-permute-start | bytes 1376264 | tf_op jit(solution)/shard_map/ppermute | solution.py:392
  195.1 22.0 %collective-permute-start.10 = (bf16[64,3584]{1,0:T(8,128)(2,1)}, bf16[64,3584]{1,0:T(8,128)(2,1)S(1)}, u32[]{:S(2)}, u32[]{:S(2)}) collective-permute-start(bf16[64,3584]{1,0:T(8,128)(2,1)} %get-tuple-element.90), channel_id=1, source_target_pairs={{0,6},{2,0},{4,2},{6,4},{1,7},{3,1},{5,3},{7,5},{8,14},{10,8},{12,... | collective-permute-start | bytes 1376264 | tf_op jit(solution)/shard_map/ppermute | solution.py:392
  196.8 22.9 %collective-permute-start.12 = (bf16[64,3584]{1,0:T(8,128)(2,1)}, bf16[64,3584]{1,0:T(8,128)(2,1)S(1)}, u32[]{:S(2)}, u32[]{:S(2)}) collective-permute-start(bf16[64,3584]{1,0:T(8,128)(2,1)} %get-tuple-element.93), channel_id=1, source_target_pairs={{0,2},{2,4},{4,6},{6,0},{1,3},{3,5},{5,7},{7,1},{8,10},{10,12},{12... | collective-permute-start | bytes 1376264 | tf_op jit(solution)/shard_map/ppermute | solution.py:388
  208.9 37.4 %copy-start.4 = (bf16[64,3584]{1,0:T(8,128)(2,1)S(1)}, bf16[64,3584]{1,0:T(8,128)(2,1)}, u32[]{:S(2)}) copy-start(bf16[64,3584]{1,0:T(8,128)(2,1)} %get-tuple-element.88.a_ref) | copy-start | bytes 1376260
  208.9 17.4 %collective-permute-start.11 = (bf16[64,3584]{1,0:T(8,128)(2,1)S(1)}, bf16[64,3584]{1,0:T(8,128)(2,1)S(1)}, u32[]{:S(2)}, u32[]{:S(2)}) collective-permute-start(bf16[64,3584]{1,0:T(8,128)(2,1)S(1)} %shard_map.125), channel_id=1, source_target_pairs={{0,2},{2,4},{4,6},{6,0},{1,3},{3,5},{5,7},{7,1},{8,10},{10,12},{12... | collective-permute-start | bytes 1376264 | tf_op jit(solution)/shard_map/ppermute | solution.py:388
  209.9 17.0 %collective-permute-start.13 = (bf16[64,3584]{1,0:T(8,128)(2,1)S(1)}, bf16[64,3584]{1,0:T(8,128)(2,1)S(1)}, u32[]{:S(2)}, u32[]{:S(2)}) collective-permute-start(bf16[64,3584]{1,0:T(8,128)(2,1)S(1)} %shard_map.126), channel_id=1, source_target_pairs={{0,6},{2,0},{4,2},{6,4},{1,7},{3,1},{5,3},{7,5},{8,14},{10,8},{12,... | collective-permute-start | bytes 1376264 | tf_op jit(solution)/shard_map/ppermute | solution.py:392
  212.2 32.9 %collective-permute-start.6 = (bf16[2,64,3584]{2,1,0:T(8,128)(2,1)}, bf16[2,64,3584]{2,1,0:T(8,128)(2,1)S(1)}, u32[]{:S(2)}, u32[]{:S(2)}) collective-permute-start(bf16[2,64,3584]{2,1,0:T(8,128)(2,1)} %get-tuple-element.85), channel_id=1, source_target_pairs={{0,2},{2,4},{4,6},{6,0},{1,3},{3,5},{5,7},{7,1},{8,10},{10,12},{12... | collective-permute-start | bytes 2752520 | tf_op jit(solution)/shard_map/ppermute | solution.py:388
  217.0 29.2 %collective-permute-start.8 = (bf16[2,64,3584]{2,1,0:T(8,128)(2,1)}, bf16[2,64,3584]{2,1,0:T(8,128)(2,1)S(1)}, u32[]{:S(2)}, u32[]{:S(2)}) collective-permute-start(bf16[2,64,3584]{2,1,0:T(8,128)(2,1)} %get-tuple-element.86), channel_id=1, source_target_pairs={{0,6},{2,0},{4,2},{6,4},{1,7},{3,1},{5,3},{7,5},{8,14},{10,8},{12,... | collective-permute-start | bytes 2752520 | tf_op jit(solution)/shard_map/ppermute | solution.py:392
  228.1 22.2 %collective-permute-start.14 = (bf16[2,64,3584]{2,1,0:T(8,128)(2,1)}, bf16[2,64,3584]{2,1,0:T(8,128)(2,1)S(1)}, u32[]{:S(2)}, u32[]{:S(2)}) collective-permute-start(bf16[2,64,3584]{2,1,0:T(8,128)(2,1)} %shard_map.129), channel_id=1, source_target_pairs={{0,1},{1,0},{2,3},{3,2},{4,5},{5,4},{6,7},{7,6},{8,9},{9,8},{10,11... | collective-permute-start | bytes 2752520 | tf_op jit(solution)/shard_map/ppermute | solution.py:451
  246.0 13.3 %collective-permute-start.7 = (bf16[64,3584]{1,0:T(8,128)(2,1)}, bf16[64,3584]{1,0:T(8,128)(2,1)}, u32[]{:S(2)}, u32[]{:S(2)}) collective-permute-start(bf16[64,3584]{1,0:T(8,128)(2,1)} %shard_map.127), channel_id=1, source_target_pairs={{0,2},{2,4},{4,6},{6,0},{1,3},{3,5},{5,7},{7,1},{8,10},{10,12},{12... | collective-permute-start | bytes 1376264 | tf_op jit(solution)/shard_map/ppermute | solution.py:388
  247.2 12.3 %collective-permute-start.9 = (bf16[64,3584]{1,0:T(8,128)(2,1)}, bf16[64,3584]{1,0:T(8,128)(2,1)}, u32[]{:S(2)}, u32[]{:S(2)}) collective-permute-start(bf16[64,3584]{1,0:T(8,128)(2,1)} %shard_map.128), channel_id=1, source_target_pairs={{0,6},{2,0},{4,2},{6,4},{1,7},{3,1},{5,3},{7,5},{8,14},{10,8},{12,... | collective-permute-start | bytes 1376264 | tf_op jit(solution)/shard_map/ppermute | solution.py:392
  250.3 43.0 %copy-start.1 = (bf16[1792,1024]{1,0:T(8,128)(2,1)S(1)}, bf16[1792,1024]{1,0:T(8,128)(2,1)}, u32[]{:S(2)}) copy-start(bf16[1792,1024]{1,0:T(8,128)(2,1)} %refs_2_.3) | copy-start | bytes 11010052
  262.6 10.7 %collective-permute-start.17 = (bf16[128,1792]{1,0:T(8,128)(2,1)S(1)}, bf16[128,1792]{1,0:T(8,128)(2,1)S(1)}, u32[]{:S(2)}, u32[]{:S(2)}) collective-permute-start(bf16[128,1792]{1,0:T(8,128)(2,1)S(1)} %shard_map.130.refs_0_), channel_id=1, source_target_pairs={{0,1},{1,0},{2,3},{3,2},{4,5},{5,4},{6,7},{7,6},{8,9},{9,8},{10,11... | collective-permute-start | bytes 1376264 | tf_op jit(solution)/shard_map/ppermute | solution.py:451
  263.8 11.1 %collective-permute-start.16 = (bf16[128,1792]{1,0:T(8,128)(2,1)S(1)}, bf16[128,1792]{1,0:T(8,128)(2,1)S(1)}, u32[]{:S(2)}, u32[]{:S(2)}) collective-permute-start(bf16[128,1792]{1,0:T(8,128)(2,1)S(1)} %shard_map.130.refs_0_), channel_id=1, source_target_pairs={{0,6},{2,0},{4,2},{6,4},{1,7},{3,1},{5,3},{7,5},{8,14},{10,8},{12,... | collective-permute-start | bytes 1376264 | tf_op jit(solution)/shard_map/ppermute | solution.py:392
  267.5 10.9 %collective-permute-start.15 = (bf16[128,1792]{1,0:T(8,128)(2,1)S(1)}, bf16[128,1792]{1,0:T(8,128)(2,1)S(1)}, u32[]{:S(2)}, u32[]{:S(2)}) collective-permute-start(bf16[128,1792]{1,0:T(8,128)(2,1)S(1)} %shard_map.130.refs_0_), channel_id=1, source_target_pairs={{0,2},{2,4},{4,6},{6,0},{1,3},{3,5},{5,7},{7,1},{8,10},{10,12},{12... | collective-permute-start | bytes 1376264 | tf_op jit(solution)/shard_map/ppermute | solution.py:388
  278.4 10.7 %collective-permute-start.18 = (bf16[128,1792]{1,0:T(8,128)(2,1)S(1)}, bf16[128,1792]{1,0:T(8,128)(2,1)S(1)}, u32[]{:S(2)}, u32[]{:S(2)}) collective-permute-start(bf16[128,1792]{1,0:T(8,128)(2,1)S(1)} %collective-permute-done.17.refs_1_), channel_id=1, source_target_pairs={{0,6},{2,0},{4,2},{6,4},{1,7},{3,1},{5,3},{7,5},{8,14},{10,8},{12,... | collective-permute-start | bytes 1376264 | tf_op jit(solution)/shard_map/ppermute | solution.py:392
  278.7 14.7 %collective-permute-start.19 = (bf16[128,1792]{1,0:T(8,128)(2,1)S(1)}, bf16[128,1792]{1,0:T(8,128)(2,1)S(1)}, u32[]{:S(2)}, u32[]{:S(2)}) collective-permute-start(bf16[128,1792]{1,0:T(8,128)(2,1)S(1)} %collective-permute-done.17.refs_1_), channel_id=1, source_target_pairs={{0,2},{2,4},{4,6},{6,0},{1,3},{3,5},{5,7},{7,1},{8,10},{10,12},{12... | collective-permute-start | bytes 1376264 | tf_op jit(solution)/shard_map/ppermute | solution.py:388
  280.4 18.0 %collective-permute-start.21 = (bf16[128,1792]{1,0:T(8,128)(2,1)S(1)}, bf16[128,1792]{1,0:T(8,128)(2,1)S(1)}, u32[]{:S(2)}, u32[]{:S(2)}) collective-permute-start(bf16[128,1792]{1,0:T(8,128)(2,1)S(1)} %collective-permute-done.15.refs_4_), channel_id=1, source_target_pairs={{0,2},{2,4},{4,6},{6,0},{1,3},{3,5},{5,7},{7,1},{8,10},{10,12},{12... | collective-permute-start | bytes 1376264 | tf_op jit(solution)/shard_map/ppermute | solution.py:388
  289.1 9.4 %collective-permute-start.22 = (bf16[128,1792]{1,0:T(8,128)(2,1)S(1)}, bf16[128,1792]{1,0:T(8,128)(2,1)S(1)}, u32[]{:S(2)}, u32[]{:S(2)}) collective-permute-start(bf16[128,1792]{1,0:T(8,128)(2,1)S(1)} %collective-permute-done.18.refs_3_), channel_id=1, source_target_pairs={{0,6},{2,0},{4,2},{6,4},{1,7},{3,1},{5,3},{7,5},{8,14},{10,8},{12,... | collective-permute-start | bytes 1376264 | tf_op jit(solution)/shard_map/ppermute | solution.py:392
  296.9 4.7 %collective-permute-start.20 = (bf16[6,64,1024]{2,1,0:T(8,128)(2,1)S(1)}, bf16[6,64,1024]{2,1,0:T(8,128)(2,1)S(1)}, u32[]{:S(2)}, u32[]{:S(2)}) collective-permute-start(bf16[6,64,1024]{2,1,0:T(8,128)(2,1)S(1)} %get-tuple-element.100), channel_id=1, source_target_pairs={{0,8},{8,0},{1,9},{9,1},{2,10},{10,2},{3,11},{11,3},{4,12},{12,4},... | collective-permute-start | bytes 2359304 | tf_op jit(solution)/shard_map/ppermute | solution.py:451
  300.0 1.6 collective-permute-start.23
  (15 other events, 248.1 us)
